TPU v7x, 32 devices: a whole 2x2x4 slice. The times are simulated.
32 devices in a mesh: dp: 8 (over y, x, core), tensor: 4 (over z).
Axes of the slice: x: 2, y: 2, z: 4, core: 2. Of those that a mesh axis runs over, the one named last changes fastest.
Arguments:
- tokens: bfloat16 [2, 8, 1024, 2048], P(None, 'dp', 'tensor'), may hold values from -6 to 6
- parents: int32 [2, 8, 4], P(None, 'dp'), may hold values from 0 to 2, as said below
- cotangent: bfloat16 [2, 8, 1024, 2048], P(None, 'dp', 'tensor'), may hold values from -6 to 6
- first_gain: bfloat16 [2048], P('dp'), may hold values from 0.5 to 1.5
- first_shift: bfloat16 [2048], P('dp'), may hold values from -1.75 to 1.75
- w_query: bfloat16 [2048, 2048], P('dp', 'tensor'), may hold values from -0.125 to 0.125
- b_query: bfloat16 [32, 64], P('tensor', 'dp'), may hold values from -3 to 3
- w_key: bfloat16 [2048, 2048], P('dp', 'tensor'), may hold values from -0.125 to 0.125
- w_value: bfloat16 [2048, 2048], P('dp', 'tensor'), may hold values from -0.125 to 0.125
- b_value: bfloat16 [32, 64], P('tensor', 'dp'), may hold values from -0.3125 to 0.3125
- w_out: bfloat16 [2048, 2048], P('tensor', 'dp'), may hold values from -1 to 1
- b_out: bfloat16 [2048], P('dp'), may hold values from -1.75 to 1.75
- second_gain: bfloat16 [2048], P('dp'), may hold values from 0.5 to 1.5
- second_shift: bfloat16 [2048], P('dp'), may hold values from -1.75 to 1.75
- w_expand: bfloat16 [2048, 8192], P('dp', 'tensor'), may hold values from -0.125 to 0.125
- b_expand: bfloat16 [128, 64], P('tensor', 'dp'), may hold values from -3 to 3
- w_reduce: bfloat16 [8192, 2048], P('tensor', 'dp'), may hold values from -0.0625 to 0.0625
- b_reduce: bfloat16 [2048], P('dp'), may hold values from -1.75 to 1.75
Outputs:
- layer_out: bfloat16 [2, 8, 1024, 2048], P(None, 'dp', 'tensor')
- input_grad: bfloat16 [2, 8, 1024, 2048], P(None, 'dp', 'tensor')
- grad_first_gain: float32 [2048], P('dp')
- grad_first_shift: float32 [2048], P('dp')
- grad_w_query: float32 [2048, 2048], P('dp', 'tensor')
- grad_b_query: float32 [32, 64], P('tensor', 'dp')
- grad_w_key: float32 [2048, 2048], P('dp', 'tensor')
- grad_w_value: float32 [2048, 2048], P('dp', 'tensor')
- grad_b_value: float32 [32, 64], P('tensor', 'dp')
- grad_w_out: float32 [2048, 2048], P('tensor', 'dp')
- grad_b_out: float32 [2048], P('dp')
- grad_second_gain: float32 [2048], P('dp')
- grad_second_shift: float32 [2048], P('dp')
- grad_w_expand: float32 [2048, 8192], P('dp', 'tensor')
- grad_b_expand: float32 [128, 64], P('tensor', 'dp')
- grad_w_reduce: float32 [8192, 2048], P('tensor', 'dp')
- grad_b_reduce: float32 [2048], P('dp')
Inputs may be any that keep to these rules, and one draw needn't show every extreme that they name: `parents`: block 0 of every tree names itself; every later block j names an earlier block (0 to j - 1) as its parent, so block 1 always hangs on block 0.
All inputs are finite; a program needn't handle non-finite values.
Results may differ from a plain program's by a relative error of at most 0.024.
Values may be sent and summed in bfloat16 or wider, within the bound.
A program may use at most 320 MiB of HBM per device.

v0:
```python
from functools import reduce
import math

import jax
import jax.numpy as jnp
from jax import lax
from jax.sharding import PartitionSpec as P

HEAD_DIM = 64
BLOCK = 256


HIGHEST = lax.Precision.HIGHEST


def layer_norm(rows, gain, shift):
    center = rows - jnp.mean(rows, -1, keepdims=True)
    spread = jnp.mean(center * center, -1, keepdims=True)
    return center * lax.rsqrt(spread + 1e-05) * gain + shift


def ancestry(parent_list):
    count = parent_list.shape[0]
    blocks = jnp.arange(count, dtype=jnp.int32)
    upward = (parent_list[:, None] == blocks[None, :]).astype(jnp.float32)
    unit_matrix = jnp.eye(count, dtype=jnp.float32)
    ancestors = unit_matrix
    for hop_index in range(count):
        ancestors = jnp.maximum(
            unit_matrix,
            jnp.dot(upward, ancestors, precision=HIGHEST, preferred_element_type=jnp.float32),
        )
    return ancestors


def visible(ancestors, first_row, row_count, total_rows, block_len):
    count = ancestors.shape[0]
    blocks = jnp.arange(count, dtype=jnp.int32)
    query_pos = first_row + jnp.arange(row_count, dtype=jnp.int32)
    key_pos = jnp.arange(total_rows, dtype=jnp.int32)
    query_hot = (query_pos[:, None] // block_len == blocks[None, :]).astype(jnp.float32)
    key_hot = (key_pos[:, None] // block_len == blocks[None, :]).astype(jnp.float32)
    linked = jnp.dot(
        jnp.dot(query_hot, ancestors, precision=HIGHEST, preferred_element_type=jnp.float32),
        key_hot.T,
        precision=HIGHEST,
        preferred_element_type=jnp.float32,
    )
    return (linked > 0.5) & (key_pos[None, :] <= query_pos[:, None])


def block_scores(query_blk, key_all, allowed):
    scores = jnp.einsum("qhd,khd->hqk", query_blk, key_all, preferred_element_type=jnp.float32) * (
        1.0 / math.sqrt(HEAD_DIM)
    )
    return jnp.where(allowed[None], scores, -1e30)


def forward_tree(x_low, parent_list, full):
    (
        w_q,
        w_k,
        w_v,
        w_o,
        w_e,
        w_r,
        gain_one,
        shift_one,
        bias_out,
        gain_two,
        shift_two,
        bias_red,
        bias_q,
        bias_v,
        bias_e,
    ) = full
    x_rows = x_low.astype(jnp.float32)
    local_rows = x_rows.shape[0]
    total_rows = local_rows * lax.axis_size("tensor")
    heads_here = w_q.shape[1] // HEAD_DIM
    row_block = math.gcd(total_rows, 512)
    normed_one = layer_norm(
        x_rows, gain_one.astype(jnp.float32), shift_one.astype(jnp.float32)
    ).astype(jnp.bfloat16)
    seq_one = lax.all_gather(normed_one, "tensor", axis=0, tiled=True)
    query = (
        jnp.dot(seq_one, w_q, preferred_element_type=jnp.float32)
        + bias_q.reshape(-1).astype(jnp.float32)
    ).astype(jnp.bfloat16)
    key_rows = jnp.dot(seq_one, w_k, preferred_element_type=jnp.float32).astype(jnp.bfloat16)
    value = (
        jnp.dot(seq_one, w_v, preferred_element_type=jnp.float32)
        + bias_v.reshape(-1).astype(jnp.float32)
    ).astype(jnp.bfloat16)
    query_h = query.reshape(total_rows, heads_here, HEAD_DIM)
    key_h = key_rows.reshape(total_rows, heads_here, HEAD_DIM)
    value_h = value.reshape(total_rows, heads_here, HEAD_DIM)
    ancestors = ancestry(parent_list)
    pieces = []
    totals = []
    for first_row in range(0, total_rows, row_block):
        allowed = visible(ancestors, first_row, row_block, total_rows, BLOCK)
        scores = block_scores(query_h[first_row : first_row + row_block], key_h, allowed)
        row_top = jnp.max(scores, -1, keepdims=True)
        log_total = row_top + jnp.log(jnp.sum(jnp.exp(scores - row_top), -1, keepdims=True))
        attn_probs = jnp.exp(scores - log_total).astype(jnp.bfloat16)
        pieces.append(
            jnp.einsum("hqk,khd->qhd", attn_probs, value_h, preferred_element_type=jnp.float32)
        )
        totals.append(log_total)
    attended = (
        jnp.concatenate(pieces, 0).reshape(total_rows, heads_here * HEAD_DIM).astype(jnp.bfloat16)
    )
    log_totals = jnp.concatenate(totals, 1)
    gain_two32 = gain_two.astype(jnp.float32)
    shift_two32 = shift_two.astype(jnp.float32)
    attn_rows = lax.psum_scatter(
        jnp.dot(attended, w_o, preferred_element_type=jnp.float32).astype(jnp.bfloat16),
        "tensor",
        scatter_dimension=0,
        tiled=True,
    ).astype(jnp.float32)
    hidden_one = x_rows + (attn_rows + bias_out.astype(jnp.float32))
    normed_two = layer_norm(hidden_one, gain_two32, shift_two32).astype(jnp.bfloat16)
    seq_two = lax.all_gather(normed_two, "tensor", axis=0, tiled=True)
    pre_act = jnp.dot(seq_two, w_e, preferred_element_type=jnp.float32) + bias_e.reshape(-1).astype(
        jnp.float32
    )
    activated = jax.nn.gelu(pre_act).astype(jnp.bfloat16)
    unit_rows = lax.psum_scatter(
        jnp.dot(activated, w_r, preferred_element_type=jnp.float32).astype(jnp.bfloat16),
        "tensor",
        scatter_dimension=0,
        tiled=True,
    ).astype(jnp.float32)
    result = hidden_one + (unit_rows + bias_red.astype(jnp.float32))
    saved = (
        seq_one,
        query_h,
        key_h,
        value_h,
        log_totals,
        attended,
        hidden_one,
        seq_two,
        pre_act,
        activated,
    )
    return (result, saved)


def backward_tree(x_rows, grad_rows, parent_list, full, saved):
    (
        w_q,
        w_k,
        w_v,
        w_o,
        w_e,
        w_r,
        gain_one,
        shift_one,
        bias_out,
        gain_two,
        shift_two,
        bias_red,
        bias_q,
        bias_v,
        bias_e,
    ) = full
    (
        seq_one,
        query_h,
        key_h,
        value_h,
        log_totals,
        attended,
        hidden_keep,
        seq_two,
        pre_act,
        activated,
    ) = saved
    total_rows = seq_one.shape[0]
    heads_here = w_q.shape[1] // HEAD_DIM
    row_block = math.gcd(total_rows, 512)
    score_scale = 1.0 / math.sqrt(HEAD_DIM)
    grad_out32 = grad_rows.astype(jnp.float32)
    gain_two32 = gain_two.astype(jnp.float32)
    shift_two32 = shift_two.astype(jnp.float32)
    grad_seq = lax.all_gather(grad_rows, "tensor", axis=0, tiled=True)
    g_reduce = jnp.einsum("tf,td->fd", activated, grad_seq, preferred_element_type=jnp.float32)
    g_bias_red = jnp.sum(grad_out32, 0)
    d_activated = jnp.einsum("td,fd->tf", grad_seq, w_r, preferred_element_type=jnp.float32)
    gelu_value, gelu_pull = jax.vjp(jax.nn.gelu, pre_act)
    d_pre = gelu_pull(d_activated)[0].astype(jnp.bfloat16)
    g_expand = jnp.einsum("tc,tf->cf", seq_two, d_pre, preferred_element_type=jnp.float32)
    g_bias_e = jnp.sum(d_pre.astype(jnp.float32), 0).reshape(-1, HEAD_DIM)
    d_normed_two = lax.psum_scatter(
        jnp.einsum("tf,cf->tc", d_pre, w_e, preferred_element_type=jnp.float32).astype(
            jnp.bfloat16
        ),
        "tensor",
        scatter_dimension=0,
        tiled=True,
    ).astype(jnp.float32)
    norm_value, norm_pull = jax.vjp(layer_norm, hidden_keep, gain_two32, shift_two32)
    d_hidden_norm, g_gain_two, g_shift_two = norm_pull(d_normed_two)
    d_hidden_one = grad_out32 + d_hidden_norm
    d_branch = d_hidden_one.astype(jnp.bfloat16)
    branch_seq = lax.all_gather(d_branch, "tensor", axis=0, tiled=True)
    g_bias_out = jnp.sum(d_branch.astype(jnp.float32), 0)
    g_out = jnp.einsum("tc,td->cd", attended, branch_seq, preferred_element_type=jnp.float32)
    d_attended = jnp.einsum(
        "td,cd->tc", branch_seq, w_o, preferred_element_type=jnp.float32
    ).astype(jnp.bfloat16)
    d_attended = d_attended.reshape(total_rows, heads_here, HEAD_DIM)
    ancestors = ancestry(parent_list)
    query_parts = []
    key_parts = []
    value_parts = []
    for first_row in range(0, total_rows, row_block):
        allowed = visible(ancestors, first_row, row_block, total_rows, BLOCK)
        query_blk = query_h[first_row : first_row + row_block]
        d_att_blk = d_attended[first_row : first_row + row_block]
        scores = block_scores(query_blk, key_h, allowed)
        probs_f = jnp.exp(scores - log_totals[:, first_row : first_row + row_block])
        attn_probs = probs_f.astype(jnp.bfloat16)
        d_probs = jnp.einsum("qhd,khd->hqk", d_att_blk, value_h, preferred_element_type=jnp.float32)
        d_scores = (probs_f * (d_probs - jnp.sum(d_probs * probs_f, -1, keepdims=True))).astype(
            jnp.bfloat16
        )
        query_parts.append(
            jnp.einsum("hqk,khd->qhd", d_scores, key_h, preferred_element_type=jnp.float32)
            * score_scale
        )
        key_parts.append(
            jnp.einsum("hqk,qhd->khd", d_scores, query_blk, preferred_element_type=jnp.float32)
            * score_scale
        )
        value_parts.append(
            jnp.einsum("hqk,qhd->khd", attn_probs, d_att_blk, preferred_element_type=jnp.float32)
        )
    width_here = heads_here * HEAD_DIM
    grad_query = (
        jnp.concatenate(query_parts, 0).reshape(total_rows, width_here).astype(jnp.bfloat16)
    )
    grad_key = reduce(jnp.add, key_parts).reshape(total_rows, width_here).astype(jnp.bfloat16)
    grad_value = reduce(jnp.add, value_parts).reshape(total_rows, width_here).astype(jnp.bfloat16)
    g_query = jnp.einsum("tc,te->ce", seq_one, grad_query, preferred_element_type=jnp.float32)
    g_key = jnp.einsum("tc,te->ce", seq_one, grad_key, preferred_element_type=jnp.float32)
    g_value = jnp.einsum("tc,te->ce", seq_one, grad_value, preferred_element_type=jnp.float32)
    g_bias_q = jnp.sum(grad_query.astype(jnp.float32), 0).reshape(heads_here, HEAD_DIM)
    g_bias_v = jnp.sum(grad_value.astype(jnp.float32), 0).reshape(heads_here, HEAD_DIM)
    part_q = jnp.einsum("te,ce->tc", grad_query, w_q, preferred_element_type=jnp.float32)
    part_k = jnp.einsum("te,ce->tc", grad_key, w_k, preferred_element_type=jnp.float32)
    part_v = jnp.einsum("te,ce->tc", grad_value, w_v, preferred_element_type=jnp.float32)
    d_normed_one = lax.psum_scatter(
        (part_q + part_k + part_v).astype(jnp.bfloat16), "tensor", scatter_dimension=0, tiled=True
    ).astype(jnp.float32)
    first_value, first_pull = jax.vjp(
        layer_norm, x_rows, gain_one.astype(jnp.float32), shift_one.astype(jnp.float32)
    )
    d_x_norm, g_gain_one, g_shift_one = first_pull(d_normed_one)
    grad_x = (d_hidden_one + d_x_norm).astype(jnp.bfloat16)
    increments = (
        g_gain_one,
        g_shift_one,
        g_query,
        g_bias_q,
        g_key,
        g_value,
        g_bias_v,
        g_out,
        g_bias_out,
        g_gain_two,
        g_shift_two,
        g_expand,
        g_bias_e,
        g_reduce,
        g_bias_red,
    )
    return (grad_x, increments)


def body(
    tokens,
    parents,
    cotangent,
    first_gain,
    first_shift,
    w_query,
    b_query,
    w_key,
    w_value,
    b_value,
    w_out,
    b_out,
    second_gain,
    second_shift,
    w_expand,
    b_expand,
    w_reduce,
    b_reduce,
):
    micro_count = tokens.shape[0]
    results = []
    grad_inputs = []
    accum = None
    for micro_idx in range(micro_count):
        x_low = tokens[micro_idx, 0]
        parent_list = parents[micro_idx, 0]
        full_fwd = (
            lax.all_gather(w_query, "dp", axis=0, tiled=True),
            lax.all_gather(w_key, "dp", axis=0, tiled=True),
            lax.all_gather(w_value, "dp", axis=0, tiled=True),
            lax.all_gather(w_out, "dp", axis=1, tiled=True),
            lax.all_gather(w_expand, "dp", axis=0, tiled=True),
            lax.all_gather(w_reduce, "dp", axis=1, tiled=True),
            lax.all_gather(first_gain, "dp", axis=0, tiled=True),
            lax.all_gather(first_shift, "dp", axis=0, tiled=True),
            lax.all_gather(b_out, "dp", axis=0, tiled=True),
            lax.all_gather(second_gain, "dp", axis=0, tiled=True),
            lax.all_gather(second_shift, "dp", axis=0, tiled=True),
            lax.all_gather(b_reduce, "dp", axis=0, tiled=True),
            lax.all_gather(b_query, "dp", axis=1, tiled=True),
            lax.all_gather(b_value, "dp", axis=1, tiled=True),
            lax.all_gather(b_expand, "dp", axis=1, tiled=True),
        )
        result, saved = forward_tree(x_low, parent_list, full_fwd)
        full_back = (
            lax.all_gather(w_query, "dp", axis=0, tiled=True),
            lax.all_gather(w_key, "dp", axis=0, tiled=True),
            lax.all_gather(w_value, "dp", axis=0, tiled=True),
            lax.all_gather(w_out, "dp", axis=1, tiled=True),
            lax.all_gather(w_expand, "dp", axis=0, tiled=True),
            lax.all_gather(w_reduce, "dp", axis=1, tiled=True),
            lax.all_gather(first_gain, "dp", axis=0, tiled=True),
            lax.all_gather(first_shift, "dp", axis=0, tiled=True),
            lax.all_gather(b_out, "dp", axis=0, tiled=True),
            lax.all_gather(second_gain, "dp", axis=0, tiled=True),
            lax.all_gather(second_shift, "dp", axis=0, tiled=True),
            lax.all_gather(b_reduce, "dp", axis=0, tiled=True),
            lax.all_gather(b_query, "dp", axis=1, tiled=True),
            lax.all_gather(b_value, "dp", axis=1, tiled=True),
            lax.all_gather(b_expand, "dp", axis=1, tiled=True),
        )
        grad_x, increments = backward_tree(
            x_low.astype(jnp.float32), cotangent[micro_idx, 0], parent_list, full_back, saved
        )
        results.append(result.astype(jnp.bfloat16))
        grad_inputs.append(grad_x)
        if accum is None:
            accum = increments
        else:
            accum = jax.tree.map(lambda left, right: left + right, accum, increments)
    row_grads = (
        lax.psum(accum[0].astype(jnp.bfloat16), "tensor").astype(jnp.float32),
        lax.psum(accum[1].astype(jnp.bfloat16), "tensor").astype(jnp.float32),
        lax.psum(accum[8].astype(jnp.bfloat16), "tensor").astype(jnp.float32),
        lax.psum(accum[9].astype(jnp.bfloat16), "tensor").astype(jnp.float32),
        lax.psum(accum[10].astype(jnp.bfloat16), "tensor").astype(jnp.float32),
        lax.psum(accum[14].astype(jnp.bfloat16), "tensor").astype(jnp.float32),
    )
    summed = (
        lax.psum_scatter(
            accum[2].astype(jnp.bfloat16), "dp", scatter_dimension=0, tiled=True
        ).astype(jnp.float32),
        lax.psum_scatter(
            accum[4].astype(jnp.bfloat16), "dp", scatter_dimension=0, tiled=True
        ).astype(jnp.float32),
        lax.psum_scatter(
            accum[5].astype(jnp.bfloat16), "dp", scatter_dimension=0, tiled=True
        ).astype(jnp.float32),
        lax.psum_scatter(
            accum[7].astype(jnp.bfloat16), "dp", scatter_dimension=1, tiled=True
        ).astype(jnp.float32),
        lax.psum_scatter(
            accum[11].astype(jnp.bfloat16), "dp", scatter_dimension=0, tiled=True
        ).astype(jnp.float32),
        lax.psum_scatter(
            accum[13].astype(jnp.bfloat16), "dp", scatter_dimension=1, tiled=True
        ).astype(jnp.float32),
        lax.psum_scatter(
            row_grads[0].astype(jnp.bfloat16), "dp", scatter_dimension=0, tiled=True
        ).astype(jnp.float32),
        lax.psum_scatter(
            row_grads[1].astype(jnp.bfloat16), "dp", scatter_dimension=0, tiled=True
        ).astype(jnp.float32),
        lax.psum_scatter(
            row_grads[2].astype(jnp.bfloat16), "dp", scatter_dimension=0, tiled=True
        ).astype(jnp.float32),
        lax.psum_scatter(
            row_grads[3].astype(jnp.bfloat16), "dp", scatter_dimension=0, tiled=True
        ).astype(jnp.float32),
        lax.psum_scatter(
            row_grads[4].astype(jnp.bfloat16), "dp", scatter_dimension=0, tiled=True
        ).astype(jnp.float32),
        lax.psum_scatter(
            row_grads[5].astype(jnp.bfloat16), "dp", scatter_dimension=0, tiled=True
        ).astype(jnp.float32),
        lax.psum_scatter(
            accum[3].astype(jnp.bfloat16), "dp", scatter_dimension=1, tiled=True
        ).astype(jnp.float32),
        lax.psum_scatter(
            accum[6].astype(jnp.bfloat16), "dp", scatter_dimension=1, tiled=True
        ).astype(jnp.float32),
        lax.psum_scatter(
            accum[12].astype(jnp.bfloat16), "dp", scatter_dimension=1, tiled=True
        ).astype(jnp.float32),
    )
    layer_out = jnp.stack(results, 0)[:, None]
    input_grad = jnp.stack(grad_inputs, 0)[:, None]
    return (
        layer_out,
        input_grad,
        summed[6],
        summed[7],
        summed[0],
        summed[12],
        summed[1],
        summed[2],
        summed[13],
        summed[3],
        summed[8],
        summed[9],
        summed[10],
        summed[4],
        summed[14],
        summed[5],
        summed[11],
    )


def solution(mesh):
    in_specs = (
        P(None, "dp", "tensor", None),
        P(None, "dp", None),
        P(None, "dp", "tensor", None),
        P("dp"),
        P("dp"),
        P("dp", "tensor"),
        P("tensor", "dp"),
        P("dp", "tensor"),
        P("dp", "tensor"),
        P("tensor", "dp"),
        P("tensor", "dp"),
        P("dp"),
        P("dp"),
        P("dp"),
        P("dp", "tensor"),
        P("tensor", "dp"),
        P("tensor", "dp"),
        P("dp"),
    )
    out_specs = (
        P(None, "dp", "tensor", None),
        P(None, "dp", "tensor", None),
        P("dp"),
        P("dp"),
        P("dp", "tensor"),
        P("tensor", "dp"),
        P("dp", "tensor"),
        P("dp", "tensor"),
        P("tensor", "dp"),
        P("tensor", "dp"),
        P("dp"),
        P("dp"),
        P("dp"),
        P("dp", "tensor"),
        P("tensor", "dp"),
        P("tensor", "dp"),
        P("dp"),
    )
    return jax.shard_map(body, mesh=mesh, in_specs=in_specs, out_specs=out_specs, check_vma=False)
```

profile of v0, /device:TPU:0, one launch (start us, length us, event | category | flops | bytes accessed | tf_op | source)
XLA Modules:
  0.0 1978.3 jit_solution(4986389479940705640)
XLA Ops:
  9.3 10.3 all-gather.3
  19.7 8.9 all-gather.2
  37.6 7.7 all_gather.50
  45.4 9.6 all_gather.52
  58.3 65.3 %all-gather.23.cloned.1.call-done = bf16[1024,2048]{1,0:T(8,128)(2,1)} async-done(((bf16[256,2048]{1,0:T(8,128)(2,1)}), bf16[1024,2048]{1,0:T(8,128)(2,1)}) %all-gather.23.cloned.1.call-update) | async-done | bytes 4194320 | tf_op jit(solution)/shard_map/all_gather | solution.py:85
  129.8 22.1 %all-gather.29.cloned.1.call-done = bf16[2048,512]{1,0:T(8,128)(2,1)} async-done(((bf16[256,512]{1,0:T(8,128)(2,1)}), bf16[2048,512]{1,0:T(8,128)(2,1)}) %all-gather.29.cloned.1.call-update) | async-done | bytes 2097168 | tf_op jit(solution)/shard_map/all_gather | solution.py:313
  175.1 6.5 all-gather.25.cloned.1.call-done
  187.0 8.5 fusion.86
  200.7 10.8 all-gather.31.cloned.1.call-done
  211.5 5.9 convolution_convert_fusion.5
  218.1 8.8 all-gather.4
  227.0 67.4 %reduce-scatter.18.cloned.1.call-done = bf16[256,2048]{1,0:T(8,128)(2,1)} async-done(((bf16[1024,2048]{1,0:T(8,128)(2,1)}), bf16[256,2048]{1,0:T(8,128)(2,1)}) %reduce-scatter.18.cloned.1.call-update) | async-done | bytes 1048592 | tf_op jit(solution)/shard_map/reduce_scatter | solution.py:117
  302.8 76.4 %all-gather.39.cloned.1.call-done = bf16[1024,2048]{1,0:T(8,128)(2,1)} async-done(((bf16[256,2048]{1,0:T(8,128)(2,1)}), bf16[1024,2048]{1,0:T(8,128)(2,1)}) %all-gather.39.cloned.1.call-update) | async-done | bytes 4194320 | tf_op jit(solution)/shard_map/all_gather | solution.py:85
  394.7 7.4 fusion.3
  402.1 8.1 exponential_reduce_fusion
  417.5 8.0 fusion.88
  432.0 8.9 all-gather.6
  440.9 9.3 all-gather.5
  450.2 56.4 %reduce-scatter.22.cloned.1.call-done = bf16[256,2048]{1,0:T(8,128)(2,1)} async-done(((bf16[1024,2048]{1,0:T(8,128)(2,1)}), bf16[256,2048]{1,0:T(8,128)(2,1)}) %reduce-scatter.22.cloned.1.call-update) | async-done | bytes 1048592 | tf_op jit(solution)/shard_map/reduce_scatter | solution.py:117
  517.9 8.9 all_gather.114
  526.9 36.6 %all-gather.35.cloned.1.call-done = bf16[2048,2048]{1,0:T(8,128)(2,1)} async-done(((bf16[256,2048]{1,0:T(8,128)(2,1)}), bf16[2048,2048]{1,0:T(8,128)(2,1)}) %all-gather.35.cloned.1.call-update) | async-done | bytes 8388624 | tf_op jit(solution)/shard_map/all_gather | solution.py:316
  563.5 82.8 %all-gather.41.cloned.1.call-done = bf16[1024,2048]{1,0:T(8,128)(2,1)} async-done(((bf16[256,2048]{1,0:T(8,128)(2,1)}), bf16[1024,2048]{1,0:T(8,128)(2,1)}) %all-gather.41.cloned.1.call-update) | async-done | bytes 4194320 | tf_op jit(solution)/shard_map/all_gather | solution.py:125
  646.3 14.6 fusion.146
  660.9 66.9 %all-gather.49.cloned.1.call-done = bf16[1,1,1024,2048]{3,2,1,0:T(8,128)(2,1)} async-done(((bf16[1,1,256,2048]{3,2,1,0:T(8,128)(2,1)}), bf16[1,1,1024,2048]{3,2,1,0:T(8,128)(2,1)}) %all-gather.49.cloned.1.call-update) | async-done | bytes 4194320 | tf_op jit(solution)/shard_map/all_gather | solution.py:189
  727.8 56.2 %all-gather.37.cloned.1.call-done = bf16[2048,2048]{1,0:T(8,128)(2,1)} async-done(((bf16[2048,256]{1,0:T(8,128)(2,1)}), bf16[2048,2048]{1,0:T(8,128)(2,1)}) %all-gather.37.cloned.1.call-update) | async-done | bytes 8388624 | tf_op jit(solution)/shard_map/all_gather | solution.py:317
  784.0 19.4 convert_reduce_fusion
  805.3 13.1 convolution_convert_fusion
  818.5 48.5 %all-gather.33.cloned.1.call-done = bf16[1024,2048]{1,0:T(8,128)(2,1)} async-done(((bf16[256,2048]{1,0:T(8,128)(2,1)}), bf16[1024,2048]{1,0:T(8,128)(2,1)}) %all-gather.33.cloned.1.call-update) | async-done | bytes 4194320 | tf_op jit(solution)/shard_map/all_gather | solution.py:125
  867.0 14.5 fusion.145
  881.5 66.8 %all-gather.47.cloned.1.call-done = bf16[1,1,1024,2048]{3,2,1,0:T(8,128)(2,1)} async-done(((bf16[1,1,256,2048]{3,2,1,0:T(8,128)(2,1)}), bf16[1,1,1024,2048]{3,2,1,0:T(8,128)(2,1)}) %all-gather.47.cloned.1.call-update) | async-done | bytes 4194320 | tf_op jit(solution)/shard_map/all_gather | solution.py:189
  948.3 19.2 convert_reduce_fusion.1
  969.6 13.2 convolution_convert_fusion.1
  982.9 16.1 convolution_convert_fusion.2
  999.1 16.1 convolution_convert_fusion.4
  1015.9 9.0 all-gather.7
  1025.8 79.5 %reduce-scatter.26.cloned.1.call-done = bf16[256,2048]{1,0:T(8,128)(2,1)} async-done(((bf16[1024,2048]{1,0:T(8,128)(2,1)}), bf16[256,2048]{1,0:T(8,128)(2,1)}) %reduce-scatter.26.cloned.1.call-update) | async-done | bytes 1048592 | tf_op jit(solution)/shard_map/reduce_scatter | solution.py:197
  1109.9 74.8 %reduce-scatter.24.cloned.1.call-done = bf16[256,2048]{1,0:T(8,128)(2,1)} async-done(((bf16[1024,2048]{1,0:T(8,128)(2,1)}), bf16[256,2048]{1,0:T(8,128)(2,1)}) %reduce-scatter.24.cloned.1.call-update) | async-done | bytes 1048592 | tf_op jit(solution)/shard_map/reduce_scatter | solution.py:130
  1189.3 74.9 %reduce-scatter.20.cloned.1.call-done = bf16[256,2048]{1,0:T(8,128)(2,1)} async-done(((bf16[1024,2048]{1,0:T(8,128)(2,1)}), bf16[256,2048]{1,0:T(8,128)(2,1)}) %reduce-scatter.20.cloned.1.call-update) | async-done | bytes 1048592 | tf_op jit(solution)/shard_map/reduce_scatter | solution.py:130
  1271.4 17.5 fusion.25
  1288.8 21.4 %add_convert_fusion = bf16[2048,2048]{1,0:T(8,128)(2,1)} fusion(f32[2048,2048]{1,0:T(8,128)} %fusion.25, bf16[1,1,1024,2048]{3,2,1,0:T(8,128)(2,1)S(1)} %copy-done.132, f32[1024,2048]{1,0:T(8,128)} %fusion.146, f32[2048]{0:T(1024)S(1)} %reshape.410), kind=kOutput, calls=%fused_computation | convolution fusion | flops 8619294720 | bytes 37756928 | tf_op jit(solution)/shard_map/tf,td->fd/dot_general | solution.py:190
  1310.3 16.0 fusion.157
  1326.3 14.7 add_convert_fusion.1
  1341.1 11.1 all-gather.45.cloned.1.call-done
  1357.6 75.9 %all-gather.43.cloned.1.call-done = bf16[1024,2048]{1,0:T(8,128)(2,1)} async-done(((bf16[256,2048]{1,0:T(8,128)(2,1)}), bf16[1024,2048]{1,0:T(8,128)(2,1)}) %all-gather.43.cloned.1.call-update) | async-done | bytes 4194320 | tf_op jit(solution)/shard_map/all_gather | solution.py:209
  1439.1 17.4 multiply_reduce_fusion
  1459.1 9.0 multiply_convert_fusion
  1480.5 9.6 fusion.133
  1490.2 10.4 fusion.130
  1500.6 10.2 convert_reduce_fusion.12
  1510.9 13.3 multiply_reduce_fusion.1
  1524.3 10.6 convert_reduce_fusion.13
  1537.4 11.4 multiply_convert_fusion.1
  1555.3 7.1 fusion.78
  1562.5 16.1 multiply_reduce_fusion.2
  1579.5 11.0 multiply_reduce_fusion.3
  1593.0 13.4 multiply_convert_fusion.2
  1612.5 11.2 multiply_convert_fusion.3
  1626.5 6.3 fusion.80
  1701.1 14.7 reduce-scatter.34.cloned.1.call-done
  1717.6 42.9 %reduce-scatter.36.cloned.1.call-done = bf16[256,512]{1,0:T(8,128)(2,1)} async-done(((bf16[2048,512]{1,0:T(8,128)(2,1)}), bf16[256,512]{1,0:T(8,128)(2,1)}) %reduce-scatter.36.cloned.1.call-update) | async-done | bytes 262160 | tf_op jit(solution)/shard_map/reduce_scatter | solution.py:367
  1762.3 77.1 %reduce-scatter.32.cloned.1.call-done = bf16[256,2048]{1,0:T(8,128)(2,1)} async-done(((bf16[1024,2048]{1,0:T(8,128)(2,1)}), bf16[256,2048]{1,0:T(8,128)(2,1)}) %reduce-scatter.32.cloned.1.call-update) | async-done | bytes 1048592 | tf_op jit(solution)/shard_map/reduce_scatter | solution.py:256
  1839.5 79.7 %reduce-scatter.28.cloned.1.call-done = bf16[256,2048]{1,0:T(8,128)(2,1)} async-done(((bf16[1024,2048]{1,0:T(8,128)(2,1)}), bf16[256,2048]{1,0:T(8,128)(2,1)}) %reduce-scatter.28.cloned.1.call-update) | async-done | bytes 1048592 | tf_op jit(solution)/shard_map/reduce_scatter | solution.py:256
  1924.1 24.3 %all-reduce.9 = (bf16[2048]{0:T(1024)(128)(2,1)S(1)}, bf16[2048]{0:T(1024)(128)(2,1)S(1)}, bf16[8,64]{1,0:T(8,128)(2,1)S(1)}, bf16[8,64]{1,0:T(8,128)(2,1)S(1)},...) all-reduce(bf16[2048]{0:T(1024)(128)(2,1)S(1)} %add_convert_fusion., ...), channel_id=12, replica_groups=mesh['dp'=8,'tensor'=4] {'dp'}, use_global_device_ids=true, to_apply=%region_39.40.clone | all-reduce | flops 15360 | bytes 61440
  1948.9 11.2 all-reduce.10
  (572 shorter events, 259.1 us)
Async XLA Ops:
  7.2 29.5 %copy-start.121 = (bf16[8,8]{1,0:T(8,128)(2,1)S(1)}, bf16[8,8]{1,0:T(8,128)(2,1)}, u32[]{:S(2)}) copy-start(bf16[8,8]{1,0:T(8,128)(2,1)} %param.24) | copy-start | bytes 388
  7.2 29.6 %copy-start.122 = (bf16[8,8]{1,0:T(8,128)(2,1)S(1)}, bf16[8,8]{1,0:T(8,128)(2,1)}, u32[]{:S(2)}) copy-start(bf16[8,8]{1,0:T(8,128)(2,1)} %param.27) | copy-start | bytes 388
  7.2 51.0 %all-gather.27.cloned.1.call-start = ((), (), s32[]{:S(2)}) async-start(), calls=%async_computation.16 | async-start | bytes 2359296 | tf_op jit(solution)/shard_map/all_gather | solution.py:312
  8.0 115.6 %all-gather.23.cloned.1.call-start = ((), (), s32[]{:S(2)}) async-start(), calls=%async_computation.14 | async-start | bytes 5242880 | tf_op jit(solution)/shard_map/all_gather | solution.py:85
  28.6 267.8 %copy-start.66 = (f32[8,1,256]{2,1,0:T(1,128)}, f32[8,1,256]{2,1,0:T(1,128)S(1)}, u32[]{:S(2)}) copy-start(f32[8,1,256]{2,1,0:T(1,128)S(1)} %convert_element_type.587) | copy-start | bytes 24580
  33.9 118.0 %all-gather.29.cloned.1.call-start = ((), (), s32[]{:S(2)}) async-start(), calls=%async_computation.17 | async-start | bytes 2359296 | tf_op jit(solution)/shard_map/all_gather | solution.py:313
  34.7 146.9 %all-gather.25.cloned.1.call-start = ((), (), s32[]{:S(2)}) async-start(), calls=%async_computation.15 | async-start | bytes 2359296 | tf_op jit(solution)/shard_map/all_gather | solution.py:314
  35.2 176.3 %all-gather.31.cloned.1.call-start = ((), (), s32[]{:S(2)}) async-start(), calls=%async_computation.18 | async-start | bytes 2359296 | tf_op jit(solution)/shard_map/all_gather | solution.py:315
  35.8 258.6 %reduce-scatter.18.cloned.1.call-start = ((), (), s32[]{:S(2)}) async-start(), calls=%async_computation.19 | async-start | bytes 5242880 | tf_op jit(solution)/shard_map/reduce_scatter | solution.py:117
  56.6 139.0 %copy-start.22 = (pred[512,1024]{1,0:T(8,128)(4,1)}, pred[512,1024]{1,0:T(8,128)(4,1)S(1)}, u32[]{:S(2)}) copy-start(pred[512,1024]{1,0:T(8,128)(4,1)S(1)} %fusion.72) | copy-start | bytes 1572868
  58.2 128.8 %copy-start.25 = (pred[512,1024]{1,0:T(8,128)(4,1)}, pred[512,1024]{1,0:T(8,128)(4,1)S(1)}, u32[]{:S(2)}) copy-start(pred[512,1024]{1,0:T(8,128)(4,1)S(1)} %fusion.70) | copy-start | bytes 1572868
  217.5 161.7 %all-gather.39.cloned.1.call-start = ((), (), s32[]{:S(2)}) async-start(), calls=%async_computation.24 | async-start | bytes 5242880 | tf_op jit(solution)/shard_map/all_gather | solution.py:85
  227.0 283.1 %copy-start.64 = (f32[8,1,256]{2,1,0:T(1,128)}, f32[8,1,256]{2,1,0:T(1,128)S(1)}, u32[]{:S(2)}) copy-start(f32[8,1,256]{2,1,0:T(1,128)S(1)} %convert_element_type.589) | copy-start | bytes 24580
  227.0 74.2 %copy-start.83 = (f32[256]{0:T(256)}, f32[256]{0:T(256)S(1)}, u32[]{:S(2)}) copy-start(f32[256]{0:T(256)S(1)} %broadcast_multiply_fusion.1) | copy-start | bytes 3076
  297.8 208.8 %reduce-scatter.22.cloned.1.call-start = ((), (), s32[]{:S(2)}) async-start(), calls=%async_computation.25 | async-start | bytes 5242880 | tf_op jit(solution)/shard_map/reduce_scatter | solution.py:117
  301.2 111.6 %copy-start.27 = (pred[512,1024]{1,0:T(8,128)(4,1)}, pred[512,1024]{1,0:T(8,128)(4,1)S(1)}, u32[]{:S(2)}) copy-start(pred[512,1024]{1,0:T(8,128)(4,1)S(1)} %fusion.71) | copy-start | bytes 1572868
  302.8 114.6 %copy-start.30 = (pred[512,1024]{1,0:T(8,128)(4,1)}, pred[512,1024]{1,0:T(8,128)(4,1)S(1)}, u32[]{:S(2)}) copy-start(pred[512,1024]{1,0:T(8,128)(4,1)S(1)} %fusion.69) | copy-start | bytes 1572868
  431.1 75.5 %copy-start.11 = (bf16[256,2048]{1,0:T(8,128)(2,1)S(1)}, bf16[256,2048]{1,0:T(8,128)(2,1)}, u32[]{:S(2)}) copy-start(bf16[256,2048]{1,0:T(8,128)(2,1)} %reduce-scatter.18.cloned.1.call-done) | copy-start | bytes 3145732
  431.2 132.3 %all-gather.35.cloned.1.call-start = ((), (), s32[]{:S(2)}) async-start(), calls=%async_computation.21 | async-start | bytes 9437184 | tf_op jit(solution)/shard_map/all_gather | solution.py:316
  431.9 214.4 %all-gather.41.cloned.1.call-start = ((), (), s32[]{:S(2)}) async-start(), calls=%async_computation.26 | async-start | bytes 5242880 | tf_op jit(solution)/shard_map/all_gather | solution.py:125
  450.2 62.5 %copy-start.68 = (f32[8,1,256]{2,1,0:T(1,128)}, f32[8,1,256]{2,1,0:T(1,128)S(1)}, u32[]{:S(2)}) copy-start(f32[8,1,256]{2,1,0:T(1,128)S(1)} %convert_element_type.590) | copy-start | bytes 24580
  450.2 62.5 %copy-start.95 = (f32[256]{0:T(256)}, f32[256]{0:T(256)S(1)}, u32[]{:S(2)}) copy-start(f32[256]{0:T(256)S(1)} %broadcast_multiply_fusion.2) | copy-start | bytes 3076
  512.7 215.0 %all-gather.49.cloned.1.call-start = ((), (), s32[]{:S(2)}) async-start(), calls=%async_computation.41 | async-start | bytes 5242880 | tf_op jit(solution)/shard_map/all_gather | solution.py:189
  515.9 268.1 %all-gather.37.cloned.1.call-start = ((), (), s32[]{:S(2)}) async-start(), calls=%async_computation.22 | async-start | bytes 9437184 | tf_op jit(solution)/shard_map/all_gather | solution.py:317
  516.5 350.5 %all-gather.33.cloned.1.call-start = ((), (), s32[]{:S(2)}) async-start(), calls=%async_computation.20 | async-start | bytes 5242880 | tf_op jit(solution)/shard_map/all_gather | solution.py:125
  517.2 431.1 %all-gather.47.cloned.1.call-start = ((), (), s32[]{:S(2)}) async-start(), calls=%async_computation.40 | async-start | bytes 5242880 | tf_op jit(solution)/shard_map/all_gather | solution.py:189
  517.8 507.9 %reduce-scatter.30.cloned.1.call-start = ((), (), s32[]{:S(2)}) async-start(), calls=%async_computation.31 | async-start | bytes 5242880 | tf_op jit(solution)/shard_map/reduce_scatter | solution.py:197
  818.4 286.9 %reduce-scatter.26.cloned.1.call-start = ((), (), s32[]{:S(2)}) async-start(), calls=%async_computation.28 | async-start | bytes 5242880 | tf_op jit(solution)/shard_map/reduce_scatter | solution.py:197
  982.9 201.9 %reduce-scatter.24.cloned.1.call-start = ((), (), s32[]{:S(2)}) async-start(), calls=%async_computation.27 | async-start | bytes 5242880 | tf_op jit(solution)/shard_map/reduce_scatter | solution.py:130
  999.1 265.2 %reduce-scatter.20.cloned.1.call-start = ((), (), s32[]{:S(2)}) async-start(), calls=%async_computation.23 | async-start | bytes 5242880 | tf_op jit(solution)/shard_map/reduce_scatter | solution.py:130
  1015.2 90.1 %copy-start.4 = (bf16[2,1,256,2048]{3,2,1,0:T(8,128)(2,1)S(1)}, bf16[2,1,256,2048]{3,2,1,0:T(8,128)(2,1)}, u32[]{:S(2)}) copy-start(bf16[2,1,256,2048]{3,2,1,0:T(8,128)(2,1)} %param.18) | copy-start | bytes 6291460
  1015.2 90.1 %copy-start.12 = (bf16[256,2048]{1,0:T(8,128)(2,1)S(1)}, bf16[256,2048]{1,0:T(8,128)(2,1)}, u32[]{:S(2)}) copy-start(bf16[256,2048]{1,0:T(8,128)(2,1)} %reduce-scatter.18.cloned.1.call-done) | copy-start | bytes 3145732
  1015.2 90.1 %copy-start.65 = (f32[8,1,256]{2,1,0:T(1,128)S(1)}, f32[8,1,256]{2,1,0:T(1,128)}, u32[]{:S(2)}) copy-start(f32[8,1,256]{2,1,0:T(1,128)} %copy-done.64) | copy-start | bytes 24580
  1015.2 90.1 %copy-start.69 = (f32[8,1,256]{2,1,0:T(1,128)S(1)}, f32[8,1,256]{2,1,0:T(1,128)}, u32[]{:S(2)}) copy-start(f32[8,1,256]{2,1,0:T(1,128)} %copy-done.68) | copy-start | bytes 24580
  1015.3 90.1 %copy-start.94 = (f32[256]{0:T(256)S(1)}, f32[256]{0:T(256)}, u32[]{:S(2)}) copy-start(f32[256]{0:T(256)} %copy-done.93) | copy-start | bytes 3076
  1015.3 90.1 %copy-start.96 = (f32[256]{0:T(256)S(1)}, f32[256]{0:T(256)}, u32[]{:S(2)}) copy-start(f32[256]{0:T(256)} %copy-done.95) | copy-start | bytes 3076
  1015.3 90.1 %copy-start.102 = (f32[256]{0:T(256)S(1)}, f32[256]{0:T(256)}, u32[]{:S(2)}) copy-start(f32[256]{0:T(256)} %copy-done.101) | copy-start | bytes 3076
  1015.3 90.1 %copy-start.104 = (f32[256]{0:T(256)S(1)}, f32[256]{0:T(256)}, u32[]{:S(2)}) copy-start(f32[256]{0:T(256)} %copy-done.103) | copy-start | bytes 3076
  1015.3 94.6 %copy-start.108 = (f32[256]{0:T(256)S(1)}, f32[256]{0:T(256)}, u32[]{:S(2)}) copy-start(f32[256]{0:T(256)} %copy-done.107) | copy-start | bytes 3076
  1015.3 336.8 %all-gather.45.cloned.1.call-start = ((), (), s32[]{:S(2)}) async-start(), calls=%async_computation.32 | async-start | bytes 5242880 | tf_op jit(solution)/shard_map/all_gather | solution.py:209
  1109.9 79.4 %copy-start.110 = (f32[256]{0:T(256)S(1)}, f32[256]{0:T(256)}, u32[]{:S(2)}) copy-start(f32[256]{0:T(256)} %copy-done.109) | copy-start | bytes 3076
  1189.3 81.4 %copy-start.113 = (f32[256]{0:T(256)}, f32[256]{0:T(256)S(1)}, u32[]{:S(2)}) copy-start(f32[256]{0:T(256)S(1)} %negate_multiply_fusion.1) | copy-start | bytes 3076
  1270.7 162.7 %all-gather.43.cloned.1.call-start = ((), (), s32[]{:S(2)}) async-start(), calls=%async_computation.29 | async-start | bytes 5242880 | tf_op jit(solution)/shard_map/all_gather | solution.py:209
  1271.3 420.4 %reduce-scatter.44.cloned.1.call-start = ((), (), s32[]{:S(2)}) async-start(), calls=%async_computation.39 | async-start | bytes 9437184 | tf_op jit(solution)/shard_map/reduce_scatter | solution.py:379
  1310.2 384.4 %reduce-scatter.42.cloned.1.call-start = ((), (), s32[]{:S(2)}) async-start(), calls=%async_computation.38 | async-start | bytes 9437184 | tf_op jit(solution)/shard_map/reduce_scatter | solution.py:376
  1341.0 356.5 %reduce-scatter.40.cloned.1.call-start = ((), (), s32[]{:S(2)}) async-start(), calls=%async_computation.37 | async-start | bytes 2359296 | tf_op jit(solution)/shard_map/reduce_scatter | solution.py:373
  1357.6 81.5 %copy-start.52 = (bf16[512,512]{0,1:T(8,128)(2,1)}, bf16[512,512]{0,1:T(8,128)(2,1)S(1)}, u32[]{:S(2)}) copy-start(bf16[512,512]{0,1:T(8,128)(2,1)S(1)} %get-tuple-element.183) | copy-start | bytes 1572868
  1357.6 81.5 %copy-start.31 = (pred[512,1024]{1,0:T(8,128)(4,1)S(1)}, pred[512,1024]{1,0:T(8,128)(4,1)}, u32[]{:S(2)}) copy-start(pred[512,1024]{1,0:T(8,128)(4,1)} %copy-done.30) | copy-start | bytes 1572868
  1524.2 175.1 %reduce-scatter.38.cloned.1.call-start = ((), (), s32[]{:S(2)}) async-start(), calls=%async_computation.36 | async-start | bytes 2359296 | tf_op jit(solution)/shard_map/reduce_scatter | solution.py:370
  1590.5 125.3 %reduce-scatter.34.cloned.1.call-start = ((), (), s32[]{:S(2)}) async-start(), calls=%async_computation.34 | async-start | bytes 2359296 | tf_op jit(solution)/shard_map/reduce_scatter | solution.py:364
  1642.2 118.4 %reduce-scatter.36.cloned.1.call-start = ((), (), s32[]{:S(2)}) async-start(), calls=%async_computation.35 | async-start | bytes 2359296 | tf_op jit(solution)/shard_map/reduce_scatter | solution.py:367
  1661.8 177.7 %reduce-scatter.32.cloned.1.call-start = ((), (), s32[]{:S(2)}) async-start(), calls=%async_computation.33 | async-start | bytes 5242880 | tf_op jit(solution)/shard_map/reduce_scatter | solution.py:256
  1673.0 246.2 %reduce-scatter.28.cloned.1.call-start = ((), (), s32[]{:S(2)}) async-start(), calls=%async_computation.30 | async-start | bytes 5242880 | tf_op jit(solution)/shard_map/reduce_scatter | solution.py:256
  1691.7 227.5 %copy-start.5 = (bf16[2,1,256,2048]{3,2,1,0:T(8,128)(2,1)S(1)}, bf16[2,1,256,2048]{3,2,1,0:T(8,128)(2,1)}, u32[]{:S(2)}) copy-start(bf16[2,1,256,2048]{3,2,1,0:T(8,128)(2,1)} %param.18) | copy-start | bytes 6291460
  1691.7 227.5 %copy-start.67 = (f32[8,1,256]{2,1,0:T(1,128)S(1)}, f32[8,1,256]{2,1,0:T(1,128)}, u32[]{:S(2)}) copy-start(f32[8,1,256]{2,1,0:T(1,128)} %copy-done.66) | copy-start | bytes 24580
  1691.7 227.5 %copy-start.84 = (f32[256]{0:T(256)S(1)}, f32[256]{0:T(256)}, u32[]{:S(2)}) copy-start(f32[256]{0:T(256)} %copy-done.83) | copy-start | bytes 3076
  1691.7 227.5 %copy-start.86 = (f32[256]{0:T(256)S(1)}, f32[256]{0:T(256)}, u32[]{:S(2)}) copy-start(f32[256]{0:T(256)} %copy-done.85) | copy-start | bytes 3076
  1697.5 224.5 %copy-start.112 = (f32[256]{0:T(256)S(1)}, f32[256]{0:T(256)}, u32[]{:S(2)}) copy-start(f32[256]{0:T(256)} %copy-done.111) | copy-start | bytes 3076
  1697.5 224.5 %copy-start.106 = (f32[256]{0:T(256)S(1)}, f32[256]{0:T(256)}, u32[]{:S(2)}) copy-start(f32[256]{0:T(256)} %copy-done.105) | copy-start | bytes 3076
  1697.5 224.6 %copy-start.98 = (f32[256]{0:T(256)S(1)}, f32[256]{0:T(256)}, u32[]{:S(2)}) copy-start(f32[256]{0:T(256)} %copy-done.97) | copy-start | bytes 3076
  1697.5 224.6 %copy-start.100 = (f32[256]{0:T(256)S(1)}, f32[256]{0:T(256)}, u32[]{:S(2)}) copy-start(f32[256]{0:T(256)} %copy-done.99) | copy-start | bytes 3076
  1762.3 203.3 %copy-start.114 = (f32[256]{0:T(256)S(1)}, f32[256]{0:T(256)}, u32[]{:S(2)}) copy-start(f32[256]{0:T(256)} %copy-done.113) | copy-start | bytes 3076
  1762.3 203.3 %copy-start.116 = (f32[256]{0:T(256)S(1)}, f32[256]{0:T(256)}, u32[]{:S(2)}) copy-start(f32[256]{0:T(256)} %copy-done.115) | copy-start | bytes 3076
  1839.5 82.6 %copy-start.20 = (bf16[256,2048]{1,0:T(8,128)(2,1)S(1)}, bf16[256,2048]{1,0:T(8,128)(2,1)}, u32[]{:S(2)}) copy-start(bf16[256,2048]{1,0:T(8,128)(2,1)} %reduce-scatter.32.cloned.1.call-done) | copy-start | bytes 3145732
  (137 other events, 1112.4 us)
Sparse Core Ops, SparseCore 0:
  10.0 30.6 all-gather.26
  42.7 80.7 all-gather.22
  125.4 26.4 all-gather.28
  153.6 27.9 all-gather.24
  183.3 28.1 all-gather.30
  217.6 76.7 reduce-scatter.17
  297.9 81.2 all-gather.38
  431.3 75.2 reduce-scatter.21
  508.5 54.9 all-gather.34
  565.5 80.7 all-gather.40
  648.4 79.2 all-gather.48
  729.5 54.4 all-gather.36
  786.2 80.7 all-gather.32
  868.9 79.3 all-gather.46
  950.4 75.2 reduce-scatter.29
  1028.0 77.2 reduce-scatter.25
  1107.4 77.2 reduce-scatter.23
  1187.0 77.2 reduce-scatter.19
  1270.9 81.2 all-gather.44
  1354.1 79.2 all-gather.42
  1436.9 69.8 reduce-scatter.43
  1510.6 71.3 reduce-scatter.41
  1585.3 41.1 reduce-scatter.39
  1630.0 41.2 reduce-scatter.37
  1674.6 41.1 reduce-scatter.33
  1719.3 41.2 reduce-scatter.35
  1762.7 76.7 reduce-scatter.31
  1841.9 77.2 reduce-scatter.27
where the time goes:
time: 1980 us
  waiting for transfers between devices  1200 us (61%)
  matrix products  472 us (24%)
  other arithmetic  131 us (7%)
  blocking collectives  117 us (6%)
  local copies, waits for them, and re-layouts  38.7 us (2%)
    reduce_scatter x2, waiting for transfers between devices, backward_tree(): lax.psum_scatter((part_q + part_k + part_v).astype(jnp.bfloat16), 'tensor...  157 us
    reduce_scatter x2, waiting for transfers between devices, forward_tree(): lax.psum_scatter(jnp.dot(activated, w_r, preferred_element_type=jnp.float...  150 us
    all_gather x2, waiting for transfers between devices, forward_tree(): seq_one = lax.all_gather(normed_one, 'tensor', axis=0, tiled=True)  142 us
    all_gather x2, waiting for transfers between devices, backward_tree(): grad_seq = lax.all_gather(grad_rows, 'tensor', axis=0, tiled=True)  134 us
    all_gather x2, waiting for transfers between devices, forward_tree(): seq_two = lax.all_gather(normed_two, 'tensor', axis=0, tiled=True)  131 us
    reduce_scatter x2, waiting for transfers between devices, forward_tree(): lax.psum_scatter(jnp.dot(attended, w_o, preferred_element_type=jnp.float3...  124 us
    all_gather x2, waiting for transfers between devices, backward_tree(): branch_seq = lax.all_gather(d_branch, 'tensor', axis=0, tiled=True)  86.9 us
    reduce_scatter x2, waiting for transfers between devices, backward_tree(): lax.psum_scatter(jnp.einsum('tf,cf->tc', d_pre, w_e, preferred_element_ty...  80.4 us
  transfers between devices with their start and end apart: 28, of which 23 were waited for; matrix products, arithmetic and copies ran while one was open for 27% of the time, Pallas kernels for 0%

commit v1 on v0

v1 whole, which is shorter than its diff:
```python
import functools
import math

import jax
import jax.numpy as jnp
from jax import lax
from jax.experimental import pallas as pl
from jax.experimental.pallas import tpu as pltpu
from jax.sharding import PartitionSpec as P

HEAD_DIM = 64
BLOCK = 256

F32 = jnp.float32
BF16 = jnp.bfloat16
MESH = pl.DeviceIdType.MESH
GELU = math.sqrt(2.0 / math.pi)


def layer_norm(rows, gain, shift):
    center = rows - jnp.mean(rows, -1, keepdims=True)
    spread = jnp.mean(center * center, -1, keepdims=True)
    return center * lax.rsqrt(spread + 1e-05) * gain + shift


def chain_gather(own):
    n = lax.axis_size("tensor")
    me = lax.axis_index("tensor")
    from_left, from_right = [own], [own]
    for step in range(1, n):
        up = [(i, i + 1) for i in range(step - 1, n - 1)]
        down = [(n - 1 - i, n - 2 - i) for i in range(step - 1, n - 1)]
        from_left.append(lax.ppermute(from_left[-1], "tensor", up))
        from_right.append(lax.ppermute(from_right[-1], "tensor", down))
    full = jnp.zeros((n,) + own.shape, own.dtype)
    full = lax.dynamic_update_slice_in_dim(full, own[None], me, 0)
    for step in range(1, n):
        piece = jnp.where(me >= step, from_left[step], from_right[n - step])
        full = lax.dynamic_update_slice_in_dim(full, piece[None], lax.rem(me - step + n, n), 0)
    return full.reshape(n * own.shape[0], own.shape[1])


def line_gather(own):
    return lax.all_gather(own, "tensor", axis=0, tiled=True)


def line_scatter(parts):
    return lax.psum_scatter(parts, "tensor", scatter_dimension=0, tiled=True).astype(F32)


def far_pairs(hop):
    n = lax.axis_size("tensor")
    return [(i, (i + hop) % n) for i in range(n)]


def far_gather(own):
    n = lax.axis_size("tensor")
    return [own] + [lax.ppermute(own, "tensor", far_pairs(hop)) for hop in range(1, n)]


def far_scatter(parts):
    n = lax.axis_size("tensor")
    total = parts[0].astype(F32)
    for hop in range(1, n):
        total = total + lax.ppermute(parts[hop], "tensor", far_pairs(n - hop)).astype(F32)
    return total


def after(value, *others):
    return lax.optimization_barrier((value,) + others)[0]


PAIR = 2 * HEAD_DIM
NEVER = -1e30


def over(left, right, on_left, on_right):
    return lax.dot_general(
        left, right, (((on_left,), (on_right,)), ((), ())), preferred_element_type=F32
    )


def lane_of(shape, head):
    lane = lax.broadcasted_iota(jnp.int32, shape, 1)
    return (lane < HEAD_DIM) if head == 0 else (lane >= HEAD_DIM)


def sight(parents_ref, row, col):
    at = jnp.int32(row)
    seen = at == col
    for hop in range(row - col):
        at = parents_ref[at]
        seen = seen | (at == col)
    return jnp.where(seen, 0.0, NEVER).astype(F32)


def masked_scores(parents_ref, q_head, k_ref, row):
    scores = []
    for col in range(row + 1):
        part = over(q_head, k_ref[col * BLOCK : (col + 1) * BLOCK, :], 1, 1)
        if col == row:
            below = lax.broadcasted_iota(jnp.int32, part.shape, 1) <= lax.broadcasted_iota(
                jnp.int32, part.shape, 0
            )
            part = jnp.where(below, part, NEVER)
        else:
            part = part + sight(parents_ref, row, col)
        scores.append(part)
    return scores


def row_reduce(parts, fold, reduce):
    return reduce(functools.reduce(fold, parts), axis=-1, keepdims=True)


def attend_kernel(parents_ref, q_ref, k_ref, v_ref, out_ref):
    blocks = q_ref.shape[0] // BLOCK
    scale = 1.0 / math.sqrt(HEAD_DIM)
    for row in range(blocks):
        here = slice(row * BLOCK, (row + 1) * BLOCK)
        heads = []
        for head in range(2):
            q_head = q_ref[here, :].astype(F32) * scale
            q_head = jnp.where(lane_of(q_head.shape, head), q_head, 0.0).astype(BF16)
            scores = masked_scores(parents_ref, q_head, k_ref, row)
            top = row_reduce(scores, jnp.maximum, jnp.max)
            probs = [jnp.exp(s - top) for s in scores]
            total = row_reduce(probs, jnp.add, jnp.sum)
            out = None
            for col in range(row + 1):
                term = over(
                    probs[col].astype(BF16), v_ref[col * BLOCK : (col + 1) * BLOCK, :], 1, 0
                )
                out = term if out is None else out + term
            heads.append(out / total)
        mixed = jnp.where(lane_of(heads[0].shape, 0), heads[0], heads[1])
        out_ref[here, :] = mixed.astype(out_ref.dtype)


def attend(parents, qkv, width):
    rows = qkv.shape[0]
    pairs = width // PAIR
    spec = lambda part: pl.BlockSpec((rows, PAIR), lambda p, parents: (0, part * pairs + p))
    blocks = rows // BLOCK
    work = pairs * 2 * (blocks * (blocks + 1) // 2) * BLOCK * BLOCK
    return pl.pallas_call(
        attend_kernel,
        out_shape=jax.ShapeDtypeStruct((rows, width), BF16),
        grid_spec=pltpu.PrefetchScalarGridSpec(
            num_scalar_prefetch=1,
            grid=(pairs,),
            in_specs=[spec(0), spec(1), spec(2)],
            out_specs=pl.BlockSpec((rows, PAIR), lambda p, parents: (0, p)),
        ),
        compiler_params=pltpu.CompilerParams(vmem_limit_bytes=48 << 20),
        cost_estimate=pl.CostEstimate(
            flops=work * PAIR * 4, bytes_accessed=rows * width * 8, transcendentals=work
        ),
        name="attend",
    )(parents, qkv, qkv, qkv)


def attend_back_kernel(parents_ref, q_ref, k_ref, v_ref, g_ref, out_ref, dq_s, dk_s, dv_s):
    part = pl.program_id(1)
    blocks = q_ref.shape[0] // BLOCK
    scale = 1.0 / math.sqrt(HEAD_DIM)

    @pl.when(part == 0)
    def _():
        for row in range(blocks):
            here = slice(row * BLOCK, (row + 1) * BLOCK)
            dq_heads = []
            for head in range(2):
                lanes = lane_of((BLOCK, PAIR), head)
                q_head = jnp.where(lanes, q_ref[here, :].astype(F32) * scale, 0.0).astype(BF16)
                g_head = jnp.where(lanes, g_ref[here, :].astype(F32), 0.0).astype(BF16)
                scores = masked_scores(parents_ref, q_head, k_ref, row)
                top = row_reduce(scores, jnp.maximum, jnp.max)
                probs = [jnp.exp(s - top) for s in scores]
                rest = 1.0 / row_reduce(probs, jnp.add, jnp.sum)
                probs = [p * rest for p in probs]
                d_probs = [
                    over(g_head, v_ref[col * BLOCK : (col + 1) * BLOCK, :], 1, 1)
                    for col in range(row + 1)
                ]
                level = row_reduce([p * d for p, d in zip(probs, d_probs)], jnp.add, jnp.sum)
                dq = None
                for col in range(row + 1):
                    there = slice(col * BLOCK, (col + 1) * BLOCK)
                    d_scores = (probs[col] * (d_probs[col] - level)).astype(BF16)
                    term = over(d_scores, k_ref[there, :], 1, 0)
                    dq = term if dq is None else dq + term
                    dk = over(d_scores, q_head, 0, 0)
                    dv = over(probs[col].astype(BF16), g_head, 0, 0)
                    if row == col and head == 0:
                        dk_s[there, :] = dk
                        dv_s[there, :] = dv
                    else:
                        dk_s[there, :] += dk
                        dv_s[there, :] += dv
                dq_heads.append(dq * scale)
            dq_s[here, :] = jnp.where(lane_of((BLOCK, PAIR), 0), dq_heads[0], dq_heads[1]).astype(
                BF16
            )
        out_ref[...] = dq_s[...]

    @pl.when(part == 1)
    def _():
        out_ref[...] = dk_s[...].astype(BF16)

    @pl.when(part == 2)
    def _():
        out_ref[...] = dv_s[...].astype(BF16)


def attend_back(parents, qkv, grad, width):
    rows = qkv.shape[0]
    pairs = width // PAIR
    spec = lambda part: pl.BlockSpec((rows, PAIR), lambda p, c, parents: (0, part * pairs + p))
    blocks = rows // BLOCK
    work = pairs * 2 * (blocks * (blocks + 1) // 2) * BLOCK * BLOCK
    return pl.pallas_call(
        attend_back_kernel,
        out_shape=jax.ShapeDtypeStruct((rows, 3 * width), BF16),
        grid_spec=pltpu.PrefetchScalarGridSpec(
            num_scalar_prefetch=1,
            grid=(pairs, 3),
            in_specs=[
                spec(0),
                spec(1),
                spec(2),
                pl.BlockSpec((rows, PAIR), lambda p, c, parents: (0, p)),
            ],
            out_specs=pl.BlockSpec((rows, PAIR), lambda p, c, parents: (0, c * pairs + p)),
            scratch_shapes=[
                pltpu.VMEM((rows, PAIR), BF16),
                pltpu.VMEM((rows, PAIR), F32),
                pltpu.VMEM((rows, PAIR), F32),
            ],
        ),
        compiler_params=pltpu.CompilerParams(vmem_limit_bytes=48 << 20),
        cost_estimate=pl.CostEstimate(
            flops=work * PAIR * 10, bytes_accessed=rows * width * 14, transcendentals=work
        ),
        name="attend_back",
    )(parents, qkv, qkv, qkv, grad)


def cube_place():
    levels = lax.axis_size("dp").bit_length() - 2
    me = lax.axis_index("dp")
    core = me % 2
    flips = []
    for bit in range(1, levels + 1):
        flips.append((1 << bit) * (1 - 2 * ((me // (1 << bit)) % 2)))
    steps = [
        flips[l] * (1 - core) + flips[levels - 1 - l] * core for l in range(levels)
    ]
    return levels, me, steps, 1 - 2 * core


def ffn_kernel(
    n2_ref, dy_ref, wet_ref, wr_ref, be_ref,
    sum_ref, seq_ref, act_ref, dpre_ref,
    wet, wr, seq, dy_st, act_st, dpre_st, keep, give, core_in, fold_in,
    w_sem, own_sem, dy_sem, seq_sem, st_sem,
    ag_send, ag_recv, agc_send, agc_recv, rsc_send, rsc_recv, fold_send, fold_recv,
):
    levels, me, steps, core_step = cube_place()
    tensor = lax.axis_index("tensor")
    count = 1 << levels
    rows, model = n2_ref.shape
    units = wet_ref.shape[0]

    def at(index):
        return (index, tensor)

    def owner(piece):
        mine, other = me, me + core_step
        for l in range(levels):
            if piece >> l & 1:
                mine = mine + steps[l]
                other = other + steps[levels - 1 - l]
        return mine, other

    barrier = pltpu.get_barrier_semaphore()
    for step in steps + [core_step]:
        pl.semaphore_signal(barrier, inc=1, device_id=at(me + step), device_id_type=MESH)
    load_own = pltpu.make_async_copy(n2_ref, seq.at[0, pl.ds(0, rows)], own_sem)
    load_own.start()
    load_wet = pltpu.make_async_copy(wet_ref, wet, w_sem.at[0])
    load_wr = pltpu.make_async_copy(wr_ref, wr, w_sem.at[1])
    load_wet.start()
    load_wr.start()

    def load_dy(piece, slot):
        mine, other = owner(piece)
        out = []
        for half, index in enumerate((mine, other)):
            out.append(
                pltpu.make_async_copy(
                    dy_ref.at[pl.ds(pl.multiple_of(index * rows, rows), rows)],
                    dy_st.at[slot, pl.ds(half * rows, rows)],
                    dy_sem.at[slot, half],
                )
            )
        return out

    def remote(src, dst, send, recv, to):
        return pltpu.make_async_remote_copy(
            src_ref=src, dst_ref=dst, send_sem=send, recv_sem=recv,
            device_id=at(to), device_id_type=MESH,
        )

    def gather_copy(piece, level):
        there = piece + (1 << level)
        return remote(
            seq.at[piece, pl.ds(0, rows)], seq.at[there, pl.ds(0, rows)],
            ag_send.at[there], ag_recv.at[there], me + steps[level],
        )

    def gather_core(piece):
        return remote(
            seq.at[piece, pl.ds(0, rows)], seq.at[piece, pl.ds(rows, rows)],
            agc_send.at[piece], agc_recv.at[piece], me + core_step,
        )

    order = [0] + sorted(range(1, count), key=lambda p: (-(p.bit_length()), p))
    slots = {piece: i % 2 for i, piece in enumerate(order)}
    loads = {order[0]: load_dy(order[0], 0)}
    for c in loads[order[0]]:
        c.start()

    load_own.wait()
    pl.semaphore_wait(barrier, levels + 1)
    sends = []
    for level in range(levels):
        sends.append(gather_copy(0, level))
        sends[-1].start()
    sends.append(gather_core(0))
    sends[-1].start()
    load_wet.wait()
    load_wr.wait()

    arrived = {0}

    def take(piece):
        if piece in arrived:
            return
        low = piece - (1 << (piece.bit_length() - 1))
        gather_copy(low, piece.bit_length() - 1).wait_recv()
        arrived.add(piece)
        for level in range(piece.bit_length(), levels):
            sends.append(gather_copy(piece, level))
            sends[-1].start()
        sends.append(gather_core(piece))
        sends[-1].start()

    stores = {}
    outs = {}
    core_sends = {}
    folds = {}
    done_core = set()

    def add(piece, other):
        @pl.loop(0, rows // 16)
        def _(i):
            part = pl.ds(pl.multiple_of(i * 16, 16), 16)
            keep[piece, part] = (
                keep[piece, part].astype(F32) + other[part].astype(F32)
            ).astype(BF16)

    def add_core(piece):
        if piece in done_core:
            return
        core_copy(piece).wait_recv()
        add(piece, core_in.at[piece])
        done_core.add(piece)

    def core_copy(piece):
        return remote(
            give.at[slots[piece]], core_in.at[piece],
            rsc_send.at[piece], rsc_recv.at[piece], me + core_step,
        )

    def fold_copy(piece):
        level = piece.bit_length() - 1
        low = piece - (1 << level)
        return remote(
            keep.at[piece], fold_in.at[piece - 1],
            fold_send.at[piece - 1], fold_recv.at[piece - 1], me + steps[level],
        )

    def fold(piece):
        add_core(piece)
        for level in range(levels - 1, piece.bit_length() - 1, -1):
            above = piece + (1 << level)
            fold_copy(above).wait_recv()
            add(piece, fold_in.at[above - 1])
        if piece:
            folds[piece] = fold_copy(piece)
            folds[piece].start()

    chunk = 256
    wide = 512
    for turn, piece in enumerate(order):
        slot = turn % 2
        for earlier in range(1, piece + 1):
            take(earlier)
        gather_core(piece).wait_recv()
        for c in loads[piece]:
            c.wait()
        if turn + 1 < count:
            loads[order[turn + 1]] = load_dy(order[turn + 1], 1 - slot)
            for c in loads[order[turn + 1]]:
                c.start()
        if turn >= 2:
            for c in stores[turn - 2]:
                c.wait()
            core_sends[order[turn - 2]].wait_send()

        @pl.loop(0, units // chunk)
        def _(i):
            cols = pl.ds(pl.multiple_of(i * chunk, chunk), chunk)
            pre = over(seq[piece], wet[cols, :], 1, 1) + be_ref[:, cols]
            d_act = over(dy_st[slot], wr[cols, :], 1, 1)
            square = pre * pre
            t = jnp.tanh(GELU * pre * (1.0 + 0.044715 * square))
            act_st[slot, :, cols] = (0.5 * pre * (1.0 + t)).astype(BF16)
            slope = 0.5 * (1.0 + t) + (0.5 * GELU) * pre * (1.0 - t * t) * (
                1.0 + (3 * 0.044715) * square
            )
            dpre_st[slot, :, cols] = (d_act * slope).astype(BF16)

        @pl.loop(0, model // wide)
        def _(i):
            cols = pl.ds(pl.multiple_of(i * wide, wide), wide)
            cols_out = pl.ds(pl.multiple_of(model + i * wide, wide), wide)
            d_two = over(dpre_st[slot], wet[:, cols], 1, 0).astype(BF16)
            keep[piece, :, cols] = d_two[:rows]
            give[slot, :, cols] = d_two[rows:]
            out = over(act_st[slot], wr[:, cols], 1, 0).astype(BF16)
            keep[piece, :, cols_out] = out[:rows]
            give[slot, :, cols_out] = out[rows:]

        core_sends[piece] = core_copy(piece)
        core_sends[piece].start()
        mine, other = owner(piece)
        stores[turn] = []
        for half, index in enumerate((mine, other)):
            to = pl.ds(pl.multiple_of(index * rows, rows), rows)
            part = pl.ds(half * rows, rows)
            stores[turn].append(
                pltpu.make_async_copy(act_st.at[slot, part], act_ref.at[to], st_sem.at[0, slot, half])
            )
            stores[turn].append(
                pltpu.make_async_copy(dpre_st.at[slot, part], dpre_ref.at[to], st_sem.at[1, slot, half])
            )
            stores[turn].append(
                pltpu.make_async_copy(seq.at[piece, part], seq_ref.at[to], seq_sem.at[piece, half])
            )
        for c in stores[turn]:
            c.start()
        if piece.bit_length() == levels:
            fold(piece)
    for level in range(levels - 2, -1, -1):
        for piece in range((1 << level), 2 << level):
            fold(piece)
    add_core(0)
    for level in range(levels):
        fold_copy(1 << level).wait_recv()

    @pl.loop(0, rows // 16)
    def _(i):
        part = pl.ds(pl.multiple_of(i * 16, 16), 16)
        total = keep[0, part].astype(F32)
        for level in range(levels):
            total = total + fold_in[(1 << level) - 1, part].astype(F32)
        sum_ref[part] = total

    for s in sends:
        s.wait_send()
    for turn in range(max(0, count - 2), count):
        for c in stores[turn]:
            c.wait()
        core_sends[order[turn]].wait_send()
    for s in folds.values():
        s.wait_send()


def ffn(n2, dy_all, wet, wr, bias_e):
    rows, model = n2.shape
    units = wet.shape[0]
    dp = lax.axis_size("dp")
    count = dp // 2
    dma = pltpu.SemaphoreType.DMA
    anywhere = pl.BlockSpec(memory_space=pl.ANY)
    vmem = pl.BlockSpec(memory_space=pltpu.VMEM)
    flops = 8 * dp * rows * model * units
    return pl.pallas_call(
        ffn_kernel,
        out_shape=(
            jax.ShapeDtypeStruct((rows, 2 * model), F32),
            jax.ShapeDtypeStruct((dp * rows, model), BF16),
            jax.ShapeDtypeStruct((dp * rows, units), BF16),
            jax.ShapeDtypeStruct((dp * rows, units), BF16),
        ),
        in_specs=[anywhere, anywhere, anywhere, anywhere, vmem],
        out_specs=(vmem, anywhere, anywhere, anywhere),
        scratch_shapes=[
            pltpu.VMEM((units, model), BF16),
            pltpu.VMEM((units, model), BF16),
            pltpu.VMEM((count, 2 * rows, model), BF16),
            pltpu.VMEM((2, 2 * rows, model), BF16),
            pltpu.VMEM((2, 2 * rows, units), BF16),
            pltpu.VMEM((2, 2 * rows, units), BF16),
            pltpu.VMEM((count, rows, 2 * model), BF16),
            pltpu.VMEM((2, rows, 2 * model), BF16),
            pltpu.VMEM((count, rows, 2 * model), BF16),
            pltpu.VMEM((count - 1, rows, 2 * model), BF16),
            dma((2,)), dma, dma((2, 2)), dma((count, 2)), dma((2, 2, 2)),
            dma((count,)), dma((count,)), dma((count,)), dma((count,)),
            dma((count,)), dma((count,)), dma((count - 1,)), dma((count - 1,)),
        ],
        compiler_params=pltpu.CompilerParams(
            collective_id=1, has_side_effects=True, vmem_limit_bytes=62 << 20
        ),
        cost_estimate=pl.CostEstimate(
            flops=flops, bytes_accessed=8 * dp * rows * (model + units), transcendentals=dp * rows * units
        ),
        name="ffn_plane",
    )(n2, dy_all, wet, wr, bias_e)


def body(
    tokens,
    parents,
    cotangent,
    first_gain,
    first_shift,
    w_query,
    b_query,
    w_key,
    w_value,
    b_value,
    w_out,
    b_out,
    second_gain,
    second_shift,
    w_expand,
    b_expand,
    w_reduce,
    b_reduce,
):
    micro_count = tokens.shape[0]
    dp = lax.axis_size("dp")
    tn = lax.axis_size("tensor")
    dp_me = lax.axis_index("dp")
    tn_me = lax.axis_index("tensor")
    width = w_query.shape[1]
    model = w_query.shape[0] * dp
    units = w_expand.shape[1]
    mine = units // dp
    micros = range(micro_count)

    cut = first_gain.shape[0]
    bq_rows, bq_cols = b_query.shape
    be_rows, be_cols = b_expand.shape
    be_all = lax.all_gather(b_expand.reshape(-1), "tensor", axis=0, tiled=True)
    small = jnp.concatenate(
        [first_gain, first_shift, b_out, second_gain, second_shift, b_reduce]
        + [b_query.reshape(-1), b_value.reshape(-1), be_all]
    )
    small = lax.all_gather(small, "dp", axis=0, tiled=False)
    gain_one, shift_one, bias_out, gain_two, shift_two, bias_red = [
        small[:, i * cut : (i + 1) * cut].reshape(1, model).astype(F32) for i in range(6)
    ]
    at = 6 * cut
    bias_qkv = []
    for i in range(2):
        part = small[:, at : at + bq_rows * bq_cols].reshape(dp, bq_rows, bq_cols)
        bias_qkv.append(part.transpose(1, 0, 2).reshape(1, width).astype(F32))
        at += bq_rows * bq_cols
    bias_qkv = jnp.concatenate([bias_qkv[0], jnp.zeros((1, width), F32), bias_qkv[1]], 1)
    bias_e = small[:, at:].reshape(dp, tn, dp, be_rows // dp, be_cols)
    bias_e = lax.dynamic_index_in_dim(bias_e, dp_me, 2, keepdims=False)
    bias_e = bias_e.transpose(1, 2, 0, 3).reshape(tn, mine)
    turned = [
        lax.dynamic_index_in_dim(bias_e, lax.rem(tn_me - hop + tn, tn), 0, keepdims=True)
        for hop in range(tn)
    ]
    bias_e = jnp.concatenate(turned, 1).astype(F32)

    x_low = [tokens[m, 0] for m in micros]
    dy_low = [cotangent[m, 0] for m in micros]
    rows_here = x_low[0].shape[0]
    total = rows_here * tn
    seq_x = [chain_gather(after(x_low[0], small))]
    w_attn = jnp.concatenate([w_query, w_key, w_value, w_out.T], axis=1)
    w_attn = lax.all_gather(after(w_attn, small), "dp", axis=0, tiled=True)
    w_qkv = w_attn[:, : 3 * width]
    w_ot = w_attn[:, 3 * width :]
    for m in range(1, micro_count):
        seq_x.append(line_gather(after(x_low[m], seq_x[-1])))

    ffn_w = jnp.stack([w_expand.T, w_reduce], 0)
    ffn_w = lax.all_to_all(after(ffn_w, small), "dp", split_axis=1, concat_axis=2, tiled=True)
    ffn_w = far_gather(after(ffn_w, seq_x[0]))
    w_et = jnp.concatenate([p[0] for p in ffn_w], 0)
    w_r = jnp.concatenate([p[1] for p in ffn_w], 0)

    seq_grad = [
        lax.all_gather(after(dy_low[m], w_attn), "dp", axis=0, tiled=True) for m in micros
    ]

    seq_one, qkv, attended, hidden, normed_two = [], [], [], [], []
    for m in micros:
        seq_one.append(layer_norm(seq_x[m].astype(F32), gain_one, shift_one).astype(BF16))
        qkv.append(
            (jnp.dot(seq_one[m], w_qkv, preferred_element_type=F32) + bias_qkv).astype(BF16)
        )
        attended.append(attend(parents[m, 0], qkv[m], width))
        branch = line_scatter(over(attended[m], w_ot, 1, 1).astype(BF16))
        hidden.append(x_low[m].astype(F32) + (branch + bias_out))
        normed_two.append(layer_norm(hidden[m], gain_two, shift_two).astype(BF16))

    layer_out, seq_two, activated, d_pre, d_hidden, d_branch = [], [], [], [], [], []
    g_gain_two = g_shift_two = g_bias_red = g_bias_out = g_bias_e = 0.0
    for m in micros:
        sums, seq, act, dpre = ffn(normed_two[m], seq_grad[m], w_et, w_r, bias_e)
        seq_two.append(seq)
        activated.append(act)
        d_pre.append(dpre)
        d_two = sums[:, :model]
        layer_out.append((hidden[m] + (sums[:, model:] + bias_red)).astype(BF16))
        grad32 = dy_low[m].astype(F32)
        norm_value, norm_pull = jax.vjp(layer_norm, hidden[m], gain_two, shift_two)
        d_norm, g_gain, g_shift = norm_pull(d_two)
        d_hidden.append(grad32 + d_norm)
        d_branch.append(d_hidden[m].astype(BF16))
        g_gain_two = g_gain_two + g_gain
        g_shift_two = g_shift_two + g_shift
        g_bias_red = g_bias_red + jnp.sum(grad32, 0, keepdims=True)
        g_bias_out = g_bias_out + jnp.sum(d_branch[m].astype(F32), 0, keepdims=True)
        g_bias_e = g_bias_e + jnp.sum(dpre.astype(F32), 0)

    def outer(left, right):
        out = None
        for a, b in zip(left, right):
            term = over(a, b, 0, 0)
            out = term if out is None else out + term
        return out.astype(BF16)

    g_r = outer(activated, seq_grad)
    g_et = outer(d_pre, seq_two)
    g_ffn = far_scatter(
        [
            jnp.stack([g_et[i * mine : (i + 1) * mine], g_r[i * mine : (i + 1) * mine]], 0)
            for i in range(tn)
        ]
    ).astype(BF16)
    g_ffn = lax.all_to_all(g_ffn, "dp", split_axis=2, concat_axis=1, tiled=True).astype(F32)
    g_expand = g_ffn[0].T
    g_reduce = g_ffn[1]

    input_grad, d_qkv, seq_branch = [], [], []
    g_gain_one = g_shift_one = g_bias_qkv = 0.0
    for m in micros:
        seq_branch.append(line_gather(d_branch[m]))
        d_att = jnp.dot(seq_branch[m], w_ot, preferred_element_type=F32).astype(BF16)
        d_qkv.append(attend_back(parents[m, 0], qkv[m], d_att, width))
        g_bias_qkv = g_bias_qkv + jnp.sum(d_qkv[m].astype(F32), 0)
        d_one = line_scatter(over(d_qkv[m], w_qkv, 1, 1).astype(BF16))
        first_value, first_pull = jax.vjp(
            layer_norm, x_low[m].astype(F32), gain_one, shift_one
        )
        d_x, g_gain, g_shift = first_pull(d_one)
        input_grad.append((d_hidden[m] + d_x).astype(BF16))
        g_gain_one = g_gain_one + g_gain
        g_shift_one = g_shift_one + g_shift

    g_attn = jnp.concatenate(
        [
            outer(seq_one, d_qkv),
            outer(seq_branch, attended),
        ],
        axis=1,
    )
    g_attn = lax.psum_scatter(g_attn, "dp", scatter_dimension=0, tiled=True).astype(F32)
    g_query, g_key, g_value = [g_attn[:, i * width : (i + 1) * width] for i in range(3)]
    g_out = g_attn[:, 3 * width :].T

    rows = jnp.concatenate(
        [g_gain_one, g_shift_one, g_bias_out, g_gain_two, g_shift_two, g_bias_red], 0
    ).reshape(-1)
    place = jnp.zeros((tn, width), F32)
    row_q = lax.dynamic_update_slice(place, g_bias_qkv[None, :width], (tn_me, 0)).reshape(-1)
    row_v = lax.dynamic_update_slice(place, g_bias_qkv[None, 2 * width :], (tn_me, 0)).reshape(-1)
    g_bias_e = g_bias_e.reshape(tn, 1, 1, mine)
    row_e = jnp.zeros((tn, dp, mine), F32)
    for hop in range(tn):
        row_e = lax.dynamic_update_slice(
            row_e, g_bias_e[hop], (lax.rem(tn_me - hop + tn, tn), dp_me, 0)
        )
    row_e = row_e.reshape(-1)
    sums = lax.psum(jnp.concatenate([rows, row_q, row_v, row_e]), ("dp", "tensor"))
    n_rows = 6 * model
    six = lax.dynamic_slice_in_dim(sums[:n_rows].reshape(6, model), dp_me * cut, cut, 1)

    def block(flat, row_count):
        table = flat.reshape(tn, row_count, HEAD_DIM)
        cols = HEAD_DIM // dp
        table = lax.dynamic_slice(table, (tn_me, 0, dp_me * cols), (1, row_count, cols))
        return table[0]

    heads_all = tn * width
    g_bq = block(sums[n_rows : n_rows + heads_all], bq_rows)
    g_bv = block(sums[n_rows + heads_all : n_rows + 2 * heads_all], bq_rows)
    g_be = block(sums[n_rows + 2 * heads_all :], be_rows)

    return (
        jnp.stack(layer_out, 0)[:, None],
        jnp.stack(input_grad, 0)[:, None],
        six[0],
        six[1],
        g_query,
        g_bq,
        g_key,
        g_value,
        g_bv,
        g_out,
        six[2],
        six[3],
        six[4],
        g_expand,
        g_be,
        g_reduce,
        six[5],
    )


def solution(mesh):
    in_specs = (
        P(None, "dp", "tensor", None),
        P(None, "dp", None),
        P(None, "dp", "tensor", None),
        P("dp"),
        P("dp"),
        P("dp", "tensor"),
        P("tensor", "dp"),
        P("dp", "tensor"),
        P("dp", "tensor"),
        P("tensor", "dp"),
        P("tensor", "dp"),
        P("dp"),
        P("dp"),
        P("dp"),
        P("dp", "tensor"),
        P("tensor", "dp"),
        P("tensor", "dp"),
        P("dp"),
    )
    out_specs = (
        P(None, "dp", "tensor", None),
        P(None, "dp", "tensor", None),
        P("dp"),
        P("dp"),
        P("dp", "tensor"),
        P("tensor", "dp"),
        P("dp", "tensor"),
        P("dp", "tensor"),
        P("tensor", "dp"),
        P("tensor", "dp"),
        P("dp"),
        P("dp"),
        P("dp"),
        P("dp", "tensor"),
        P("tensor", "dp"),
        P("tensor", "dp"),
        P("dp"),
    )
    return jax.shard_map(body, mesh=mesh, in_specs=in_specs, out_specs=out_specs, check_vma=False)
```

time: 1980 us -> 1510 us (0.76)
  waiting for transfers between devices: 1200 us -> 723 us
  Pallas kernels: 0 us -> 370 us
  matrix products: 472 us -> 146 us
  blocking collectives: 117 us -> 52 us
  local copies, waits for them, and re-layouts: 38.7 us -> 90.2 us
  other arithmetic: 131 us -> 83.6 us
  starting transfers between devices: 2.42 us -> 25.7 us
    all_gather x14 -> x6, waiting for transfers between devices: 626 us -> 137 us  [the longest x3 130 us: line_gather(): return lax.all_gather(own, 'tensor', axis=0, tiled=True)]
    reduce_scatter x14 -> x5, waiting for transfers between devices: 568 us -> 82.2 us  [the longest x4 56.4 us: line_scatter(): lax.psum_scatter(parts, 'tensor', scatter_dimension=0, tiled=True)]
    ppermute x0 -> x12, waiting for transfers between devices: none -> 480 us  [the longest x3 236 us: far_gather(): lax.ppermute(own, 'tensor', far_pairs(hop))]
    pallas_call x0 -> x6, Pallas kernels: none -> 370 us  [the longest x2 272 us: ffn(): pl.pallas_call(ffn_kernel, out_shape=(jax.ShapeDtypeStruct((rows, 2 * mod...]
    dot_general x76 -> x16, matrix products: 472 us -> 146 us  [the longest x12 115 us: over(): lax.dot_general(left, right, (((on_left,), (on_right,)), ((), ())), prefe...]
    all_gather x9 -> x2, blocking collectives: 81.3 us -> 21.9 us  [the longest x1 12.6 us: body(): be_all = lax.all_gather(b_expand.reshape(-1), 'tensor', axis=0, tiled=True)]
    convert_element_type x37 -> x7, other arithmetic: 68.4 us -> 14.4 us  [the longest x1 4.67 us: body(): layer_norm(seq_x[m].astype(F32), gain_one, shift_one).astype(BF16)]
    all_to_all x0 -> x1, blocking collectives: none -> 30.1 us  [body(): lax.all_to_all(after(ffn_w, small), 'dp', split_axis=1, concat_axis=2, ti...]
  transfers between devices with their start and end apart: 28 -> 25, of which waited for: 23 -> 14; matrix products, arithmetic and copies ran while one was open for 27% -> 18% of each run, Pallas kernels for 0% -> 16%
where the time goes in v1:
time: 1510 us
  waiting for transfers between devices  723 us (48%)
  Pallas kernels  370 us (25%)
  matrix products  146 us (10%)
  local copies, waits for them, and re-layouts  90.2 us (6%)
  other arithmetic  83.6 us (6%)
  blocking collectives  52 us (3%)
  starting transfers between devices  25.7 us (2%)
  between operations  15.9 us (1%)
    pallas_call x2, Pallas kernels, ffn(): pl.pallas_call(ffn_kernel, out_shape=(jax.ShapeDtypeStruct((rows, 2 * mod...  272 us
    ppermute x3, waiting for transfers between devices, far_gather(): lax.ppermute(own, 'tensor', far_pairs(hop))  236 us
    ppermute x3, waiting for transfers between devices, far_scatter(): lax.ppermute(parts[hop], 'tensor', far_pairs(n - hop)).astype(F32)  179 us
    all_gather x3, waiting for transfers between devices, line_gather(): return lax.all_gather(own, 'tensor', axis=0, tiled=True)  130 us
    dot_general x12, matrix products, over(): lax.dot_general(left, right, (((on_left,), (on_right,)), ((), ())), prefe...  115 us
    pallas_call x2, Pallas kernels, attend_back(): pl.pallas_call(attend_back_kernel, out_shape=jax.ShapeDtypeStruct((rows,...  70.1 us
    ppermute x3, waiting for transfers between devices, chain_gather(): from_right.append(lax.ppermute(from_right[-1], 'tensor', down))  64.5 us
    reduce_scatter x4, waiting for transfers between devices, line_scatter(): lax.psum_scatter(parts, 'tensor', scatter_dimension=0, tiled=True)  56.4 us
  transfers between devices with their start and end apart: 25, of which 14 were waited for; matrix products, arithmetic and copies ran while one was open for 18% of the time, Pallas kernels for 16%

profile of v1, /device:TPU:0, one launch (start us, length us, event | category | flops | bytes accessed | tf_op | source)
XLA Modules:
  0.0 1507.2 jit_solution(16720917885337806856)
XLA Ops:
  9.6 12.6 all-gather.1
  22.3 4.1 concatenate.35
  26.4 9.3 all-gather.2
  43.6 5.5 collective-permute-start
  49.2 20.5 %collective-permute-done.1 = bf16[256,2048]{1,0:T(8,128)(2,1)S(1)} collective-permute-done((bf16[256,2048]{1,0:T(8,128)(2,1)S(1)}, bf16[256,2048]{1,0:T(8,128)(2,1)S(1)}, u32[]{:S(2)}, u32[]{:S(2)}) %collective-permute-start.1) | collective-permute-done | bytes 1048608 | tf_op jit(solution)/shard_map/ppermute | solution.py:34
  72.7 23.7 %collective-permute-done.2 = bf16[256,2048]{1,0:T(8,128)(2,1)} collective-permute-done((bf16[256,2048]{1,0:T(8,128)(2,1)S(1)}, bf16[256,2048]{1,0:T(8,128)(2,1)}, u32[]{:S(2)}, u32[]{:S(2)}) %collective-permute-start.2) | collective-permute-done | bytes 1048608 | tf_op jit(solution)/shard_map/ppermute | solution.py:34
  102.0 20.4 %collective-permute-done.3 = bf16[256,2048]{1,0:T(8,128)(2,1)} collective-permute-done((bf16[256,2048]{1,0:T(8,128)(2,1)}, bf16[256,2048]{1,0:T(8,128)(2,1)}, u32[]{:S(2)}, u32[]{:S(2)}) %collective-permute-start.3) | collective-permute-done | bytes 1048608 | tf_op jit(solution)/shard_map/ppermute | solution.py:34
  122.3 2.6 bitcast_dynamic-update-slice_fusion.2
  124.9 2.7 bitcast_dynamic-update-slice_fusion.1
  129.9 2.8 convert_reduce_fusion.1
  132.7 3.8 fusion.7
  136.6 4.7 add_convert_fusion.3
  141.3 10.1 add_convert_fusion.5.q_ref.k_ref.v_ref
  151.4 14.2 attend.2
  166.7 5.9 convolution_convert_fusion.1
  173.1 34.2 %all-gather.14.cloned.1.call-done = bf16[1024,2048]{1,0:T(8,128)(2,1)} async-done(((bf16[256,2048]{1,0:T(8,128)(2,1)}), bf16[1024,2048]{1,0:T(8,128)(2,1)}) %all-gather.14.cloned.1.call-update) | async-done | bytes 4194320 | tf_op jit(solution)/shard_map/all_gather | solution.py:44
  207.2 3.0 convert_reduce_fusion
  212.0 9.9 add_convert_fusion.4.q_ref.k_ref.v_ref
  221.9 14.2 attend.3
  237.0 6.0 convolution_convert_fusion
  243.1 3.1 slice_bitcast_fusion.18
  250.8 12.8 copy.104
  263.7 30.1 %all_to_all.27 = bf16[2,2048,256]{2,0,1:T(2,128)(2,1)S(1)} all-to-all(bf16[2,2048,256]{2,0,1:T(2,128)(2,1)S(1)} %copy.104), channel_id=1, replica_groups=mesh['dp'=8,'tensor'=4] {'dp'}, dimensions={1} | all-to-all | bytes 4194304 | tf_op jit(solution)/shard_map/all_to_all | solution.py:607
  296.3 4.2 all_to_all.23
  306.4 86.2 %collective-permute-done.8 = bf16[2,256,2048]{2,1,0:T(8,128)(2,1)} collective-permute-done((bf16[2,256,2048]{2,1,0:T(8,128)(2,1)}, bf16[2,256,2048]{2,1,0:T(8,128)(2,1)}, u32[]{:S(2)}, u32[]{:S(2)}) %collective-permute-start.8) | collective-permute-done | bytes 2097184 | tf_op jit(solution)/shard_map/ppermute | solution.py:58
  394.4 149.4 %collective-permute-done.7 = bf16[2,256,2048]{2,1,0:T(8,128)(2,1)} collective-permute-done((bf16[2,256,2048]{2,1,0:T(8,128)(2,1)}, bf16[2,256,2048]{2,1,0:T(8,128)(2,1)}, u32[]{:S(2)}, u32[]{:S(2)}) %collective-permute-start.7) | collective-permute-done | bytes 2097184 | tf_op jit(solution)/shard_map/ppermute | solution.py:58
  557.7 2.6 add_convert_fusion.13
  560.3 7.0 all-gather.12.cloned.1.call-done.dy_ref
  567.3 149.8 %ffn_plane.2 = (f32[256,4096]{1,0:T(8,128)}, bf16[2048,2048]{1,0:T(8,128)(2,1)}, bf16[2048,1024]{1,0:T(8,128)(2,1)}, bf16[2048,1024]{1,0:T(8,128)(2,1)}) custom-call(bf16[256,2048]{1,0:T(8,128)(2,1)} %get-tuple-element.182.n2_ref, bf16[2048,2048]{1,0:T(8,128)(2,1)} %all-gather.12.cloned.1.call-done.dy_ref, bf16[1024,2048]{1,0:T(8,128)(2,1)} %pad_maximum_fusion.1.wet_ref, ...), custom_call_target="tpu_custom_call" | custom-call | flops 34359738368 | bytes 50331648 | tf_op jit(solution)/shard_map/ffn_plane/pallas_call | solution.py:500
  717.1 122.2 %ffn_plane.3 = (f32[256,4096]{1,0:T(8,128)}, bf16[2048,2048]{1,0:T(8,128)(2,1)}, bf16[2048,1024]{1,0:T(8,128)(2,1)}, bf16[2048,1024]{1,0:T(8,128)(2,1)}) custom-call(bf16[256,2048]{1,0:T(8,128)(2,1)} %get-tuple-element.183.n2_ref, bf16[2048,2048]{1,0:T(8,128)(2,1)} %all-gather.16.cloned.1.call-done.dy_ref, bf16[1024,2048]{1,0:T(8,128)(2,1)} %pad_maximum_fusion.1.wet_ref, ...), custom_call_target="tpu_custom_call" | custom-call | flops 34359738368 | bytes 50331648 | tf_op jit(solution)/shard_map/ffn_plane/pallas_call | solution.py:500
  839.4 4.8 multiply_reduce_fusion.1
  852.6 81.8 %all-gather.20.cloned.1.call-done = bf16[1024,2048]{1,0:T(8,128)(2,1)} async-done(((bf16[256,2048]{1,0:T(8,128)(2,1)}), bf16[1024,2048]{1,0:T(8,128)(2,1)}) %all-gather.20.cloned.1.call-update) | async-done | bytes 4194320 | tf_op jit(solution)/shard_map/all_gather | solution.py:44
  934.5 5.4 convolution_convert_fusion.2.g_ref
  939.8 34.7 %attend_back.3 = bf16[1024,1536]{1,0:T(8,128)(2,1)S(1)} custom-call(s32[4]{0:T(128)S(1)} %get-tuple-element.235.parents_ref, bf16[1024,1536]{1,0:T(8,128)(2,1)} %copy-done.1, bf16[1024,1536]{1,0:T(8,128)(2,1)} %copy-done.1, bf16[1024,1536]{1,0:T(8,128)(2,1)} %copy-done.1, bf16[1024,512]{1,0:T(8,128)(2,1)S(1)} %convolution_convert_fusion.2.g_ref), custom_call_target="tpu_custom_call" | custom-call | flops 6710886400 | bytes 7340032 | tf_op jit(solution)/shard_map/attend_back/pallas_call | solution.py:222
  974.6 8.2 fusion.17
  982.9 3.1 convert_reduce_fusion.3
  987.4 15.0 fusion.73
  1002.3 13.6 all-gather.18.cloned.1.call-done
  1015.9 5.4 convolution_convert_fusion.3.g_ref
  1021.3 35.4 %attend_back.2 = bf16[1024,1536]{1,0:T(8,128)(2,1)S(1)} custom-call(s32[4]{0:T(128)S(1)} %copy-done.9, bf16[1024,1536]{1,0:T(8,128)(2,1)} %copy-done, bf16[1024,1536]{1,0:T(8,128)(2,1)} %copy-done, bf16[1024,1536]{1,0:T(8,128)(2,1)} %copy-done, bf16[1024,512]{1,0:T(8,128)(2,1)S(1)} %convolution_convert_fusion.3.g_ref), custom_call_target="tpu_custom_call" | custom-call | flops 6710886400 | bytes 7340032 | tf_op jit(solution)/shard_map/attend_back/pallas_call | solution.py:222
  1058.4 8.2 fusion.14
  1066.6 15.9 %add_convert_fusion.2 = bf16[1024,2048]{1,0:T(8,128)(2,1)} fusion(f32[1024,2048]{1,0:T(8,128)} %fusion.73, bf16[2048,1024]{1,0:T(8,128)(2,1)} %get-tuple-element.42, bf16[2048,2048]{1,0:T(8,128)(2,1)} %get-tuple-element.44), kind=kOutput, calls=%fused_computation.15 | convolution fusion | flops 8594128896 | bytes 25165824 | tf_op jit(solution)/shard_map/dot_general | solution.py:78
  1085.1 5.0 fusion.72
  1090.1 3.9 add_convert_fusion.7
  1094.1 9.7 fusion.71
  1103.8 12.9 add_convert_fusion
  1116.7 56.4 %reduce-scatter.10.cloned.1.call-done = bf16[256,2048]{1,0:T(8,128)(2,1)} async-done(((bf16[1024,2048]{1,0:T(8,128)(2,1)}), bf16[256,2048]{1,0:T(8,128)(2,1)}) %reduce-scatter.10.cloned.1.call-update) | async-done | bytes 1048592 | tf_op jit(solution)/shard_map/reduce_scatter | solution.py:48
  1173.1 3.7 fusion.31
  1179.8 8.3 pad_maximum_fusion
  1188.1 13.0 fusion.74
  1201.2 11.6 add_convert_fusion.1
  1213.7 2.6 collective-permute-start.9
  1219.2 43.3 %collective-permute-done.9 = bf16[2,256,2048]{2,1,0:T(8,128)(2,1)S(1)} collective-permute-done((bf16[2,256,2048]{2,1,0:T(8,128)(2,1)S(1)}, bf16[2,256,2048]{2,1,0:T(8,128)(2,1)S(1)}, u32[]{:S(2)}, u32[]{:S(2)}) %collective-permute-start.9) | collective-permute-done | bytes 2097184 | tf_op jit(solution)/shard_map/ppermute | solution.py:65
  1262.5 136.1 %collective-permute-done.10 = bf16[2,256,2048]{2,1,0:T(8,128)(2,1)S(1)} collective-permute-done((bf16[2,256,2048]{2,1,0:T(8,128)(2,1)S(1)}, bf16[2,256,2048]{2,1,0:T(8,128)(2,1)S(1)}, u32[]{:S(2)}, u32[]{:S(2)}) %collective-permute-start.10) | collective-permute-done | bytes 2097184 | tf_op jit(solution)/shard_map/ppermute | solution.py:65
  1398.6 3.2 add_convert_fusion.6
  1401.8 6.1 copy.107
  1407.9 4.6 all-to-all-start.1
  1412.5 3.1 maximum_bitcast_fusion
  1415.6 23.6 %all-to-all-done.1 = bf16[2,256,2048]{1,0,2:T(2,128)(2,1)} async-done(((bf16[2,256,2048]{1,0,2:T(2,128)(2,1)}), bf16[2,256,2048]{1,0,2:T(2,128)(2,1)}, u32[]{:S(2)}, u32[]{:S(2)}) %all-to-all-start.1) | async-done | bytes 2097184 | tf_op jit(solution)/shard_map/all_to_all | solution.py:662
  1439.2 3.1 convert_bitcast_fusion
  1442.3 6.1 fusion.65
  1448.4 6.1 copy.110
  1454.5 3.1 copy.108
  1468.9 25.8 %reduce-scatter.14.cloned.1.call-done = bf16[256,2048]{0,1:T(8,128)(2,1)} async-done(((bf16[2048,2048]{0,1:T(8,128)(2,1)}), bf16[256,2048]{0,1:T(8,128)(2,1)}) %reduce-scatter.14.cloned.1.call-update) | async-done | bytes 1048592 | tf_op jit(solution)/shard_map/reduce_scatter | solution.py:689
  (286 shorter events, 91.2 us)
Async XLA Ops:
  7.2 134.1 %all-gather.10.cloned.1.call-start = ((), (), s32[]{:S(2)}) async-start(), calls=%async_computation.7 | async-start | bytes 9437184 | tf_op jit(solution)/shard_map/all_gather | solution.py:600
  36.8 4.4 copy-start.10
  41.1 166.1 %all-gather.14.cloned.1.call-start = ((), (), s32[]{:S(2)}) async-start(), calls=%async_computation.10 | async-start | bytes 5242880 | tf_op jit(solution)/shard_map/all_gather | solution.py:44
  42.3 27.3 %collective-permute-start.1 = (bf16[256,2048]{1,0:T(8,128)(2,1)S(1)}, bf16[256,2048]{1,0:T(8,128)(2,1)S(1)}, u32[]{:S(2)}, u32[]{:S(2)}) collective-permute-start(bf16[256,2048]{1,0:T(8,128)(2,1)S(1)} %get-tuple-element.32), channel_id=1, source_target_pairs={{3,2},{2,1},{1,0},{7,6},{6,5},{5,4},{11,10},{10,9},{9,8},{15,14},{... | collective-permute-start | bytes 3145736 | tf_op jit(solution)/shard_map/ppermute | solution.py:34
  43.6 27.3 %collective-permute-start = (bf16[256,2048]{1,0:T(8,128)(2,1)S(1)}, bf16[256,2048]{1,0:T(8,128)(2,1)}, u32[]{:S(2)}, u32[]{:S(2)}) collective-permute-start(bf16[256,2048]{1,0:T(8,128)(2,1)S(1)} %get-tuple-element.32), channel_id=1, source_target_pairs={{0,1},{1,2},{2,3},{4,5},{5,6},{6,7},{8,9},{9,10},{10,11},{12,13},{... | collective-permute-start | bytes 3145736 | tf_op jit(solution)/shard_map/ppermute | solution.py:33
  69.6 26.7 %collective-permute-start.2 = (bf16[256,2048]{1,0:T(8,128)(2,1)S(1)}, bf16[256,2048]{1,0:T(8,128)(2,1)}, u32[]{:S(2)}, u32[]{:S(2)}) collective-permute-start(bf16[256,2048]{1,0:T(8,128)(2,1)S(1)} %collective-permute-done.1), channel_id=1, source_target_pairs={{2,1},{1,0},{6,5},{5,4},{10,9},{9,8},{14,13},{13,12},{18,17},{17,1... | collective-permute-start | bytes 3145736 | tf_op jit(solution)/shard_map/ppermute | solution.py:34
  70.9 30.3 %collective-permute-start.4 = (bf16[256,2048]{1,0:T(8,128)(2,1)}, bf16[256,2048]{1,0:T(8,128)(2,1)}, u32[]{:S(2)}, u32[]{:S(2)}) collective-permute-start(bf16[256,2048]{1,0:T(8,128)(2,1)} %collective-permute-done), channel_id=1, source_target_pairs={{1,2},{2,3},{5,6},{6,7},{9,10},{10,11},{13,14},{14,15},{17,18},{18... | collective-permute-start | bytes 3145736 | tf_op jit(solution)/shard_map/ppermute | solution.py:33
  96.3 26.0 %collective-permute-start.3 = (bf16[256,2048]{1,0:T(8,128)(2,1)}, bf16[256,2048]{1,0:T(8,128)(2,1)}, u32[]{:S(2)}, u32[]{:S(2)}) collective-permute-start(bf16[256,2048]{1,0:T(8,128)(2,1)} %collective-permute-done.2), channel_id=1, source_target_pairs={{1,0},{5,4},{9,8},{13,12},{17,16},{21,20},{25,24},{29,28}} | collective-permute-start | bytes 3145736 | tf_op jit(solution)/shard_map/ppermute | solution.py:34
  101.2 26.4 %collective-permute-start.5 = (bf16[256,2048]{1,0:T(8,128)(2,1)}, bf16[256,2048]{1,0:T(8,128)(2,1)S(1)}, u32[]{:S(2)}, u32[]{:S(2)}) collective-permute-start(bf16[256,2048]{1,0:T(8,128)(2,1)} %collective-permute-done.4), channel_id=1, source_target_pairs={{2,3},{6,7},{10,11},{14,15},{18,19},{22,23},{26,27},{30,31}} | collective-permute-start | bytes 3145736 | tf_op jit(solution)/shard_map/ppermute | solution.py:33
  129.1 423.2 %reduce-scatter.6.cloned.1.call-start = ((), (), s32[]{:S(2)}) async-start(), calls=%async_computation.8 | async-start | bytes 5242880 | tf_op jit(solution)/shard_map/reduce_scatter | solution.py:48
  129.8 82.1 %copy-start.38 = (f32[1,2,8,128]{3,1,2,0:T(2,128)}, f32[1,2,8,128]{3,1,2,0:T(2,128)S(1)}, u32[]{:S(2)}) copy-start(f32[1,2,8,128]{3,1,2,0:T(2,128)S(1)} %copy.121) | copy-start | bytes 24580
  129.8 82.1 %copy-start.36 = (f32[1,2,8,128]{3,1,2,0:T(2,128)}, f32[1,2,8,128]{3,1,2,0:T(2,128)S(1)}, u32[]{:S(2)}) copy-start(f32[1,2,8,128]{3,1,2,0:T(2,128)S(1)} %copy.120) | copy-start | bytes 24580
  129.9 21.5 %copy-start.8 = (s32[4]{0:T(128)}, s32[4]{0:T(128)S(1)}, u32[]{:S(2)}) copy-start(s32[4]{0:T(128)S(1)} %get-tuple-element.236.parents_ref) | copy-start | bytes 52
  151.4 14.2 copy-start
  172.6 381.4 %reduce-scatter.8.cloned.1.call-start = ((), (), s32[]{:S(2)}) async-start(), calls=%async_computation.11 | async-start | bytes 5242880 | tf_op jit(solution)/shard_map/reduce_scatter | solution.py:48
  207.2 3.4 copy-start.23
  211.9 9.9 copy-start.46
  221.9 14.2 copy-start.1
  243.0 324.3 %all-gather.12.cloned.1.call-start = ((), (), s32[]{:S(2)}) async-start(), calls=%async_computation.9 | async-start | bytes 9437184 | tf_op jit(solution)/shard_map/all_gather | solution.py:613
  246.2 470.9 %all-gather.16.cloned.1.call-start = ((), (), s32[]{:S(2)}) async-start(), calls=%async_computation.12 | async-start | bytes 9437184 | tf_op jit(solution)/shard_map/all_gather | solution.py:613
  246.8 687.6 %all-gather.20.cloned.1.call-start = ((), (), s32[]{:S(2)}) async-start(), calls=%async_computation.15 | async-start | bytes 5242880 | tf_op jit(solution)/shard_map/all_gather | solution.py:44
  300.5 92.1 %collective-permute-start.8 = (bf16[2,256,2048]{2,1,0:T(8,128)(2,1)}, bf16[2,256,2048]{2,1,0:T(8,128)(2,1)}, u32[]{:S(2)}, u32[]{:S(2)}) collective-permute-start(bf16[2,256,2048]{2,1,0:T(8,128)(2,1)} %all_to_all.23), channel_id=1, source_target_pairs={{0,3},{1,0},{2,1},{3,2},{4,7},{5,4},{6,5},{7,6},{8,11},{9,8},{10,9... | collective-permute-start | bytes 6291464 | tf_op jit(solution)/shard_map/ppermute | solution.py:58
  301.4 242.4 %collective-permute-start.7 = (bf16[2,256,2048]{2,1,0:T(8,128)(2,1)}, bf16[2,256,2048]{2,1,0:T(8,128)(2,1)}, u32[]{:S(2)}, u32[]{:S(2)}) collective-permute-start(bf16[2,256,2048]{2,1,0:T(8,128)(2,1)} %all_to_all.23), channel_id=1, source_target_pairs={{0,2},{1,3},{2,0},{3,1},{4,6},{5,7},{6,4},{7,5},{8,10},{9,11},{10,... | collective-permute-start | bytes 6291464 | tf_op jit(solution)/shard_map/ppermute | solution.py:58
  301.4 244.2 %collective-permute-start.6 = (bf16[2,256,2048]{2,1,0:T(8,128)(2,1)}, bf16[2,256,2048]{2,1,0:T(8,128)(2,1)}, u32[]{:S(2)}, u32[]{:S(2)}) collective-permute-start(bf16[2,256,2048]{2,1,0:T(8,128)(2,1)} %all_to_all.23), channel_id=1, source_target_pairs={{0,1},{1,2},{2,3},{3,0},{4,5},{5,6},{6,7},{7,4},{8,9},{9,10},{10,1... | collective-permute-start | bytes 6291464 | tf_op jit(solution)/shard_map/ppermute | solution.py:58
  717.1 122.2 %copy-start.14 = (bf16[256,2048]{1,0:T(8,128)(2,1)S(1)}, bf16[256,2048]{1,0:T(8,128)(2,1)}, u32[]{:S(2)}) copy-start(bf16[256,2048]{1,0:T(8,128)(2,1)} %reduce-scatter.8.cloned.1.call-done) | copy-start | bytes 3145732
  839.4 4.9 copy-start.11
  839.4 5.0 copy-start.26
  846.4 2.9 copy-start.17
  846.4 2.9 copy-start.42
  851.8 164.1 %all-gather.18.cloned.1.call-start = ((), (), s32[]{:S(2)}) async-start(), calls=%async_computation.13 | async-start | bytes 5242880 | tf_op jit(solution)/shard_map/all_gather | solution.py:44
  852.6 264.1 %reduce-scatter.12.cloned.1.call-start = ((), (), s32[]{:S(2)}) async-start(), calls=%async_computation.16 | async-start | bytes 5242880 | tf_op jit(solution)/shard_map/reduce_scatter | solution.py:48
  934.5 40.1 %slice-start = ((s8[8388608]{0:T(1024)(128)(4,1)}), s8[4194304]{0:T(1024)(128)(4,1)S(1)}, s32[]{:S(2)}) async-start(s8[8388608]{0:T(1024)(128)(4,1)} %bitcast.326), calls=%async_computation.19 | async-start | bytes 8388608
  939.8 34.7 %slice-start.1 = ((s8[8388608]{0:T(1024)(128)(4,1)}), s8[4194304]{0:T(1024)(128)(4,1)S(1)}, s32[]{:S(2)}) async-start(s8[8388608]{0:T(1024)(128)(4,1)} %bitcast.326), calls=%async_computation.20 | async-start | bytes 8388608
  982.8 190.3 %reduce-scatter.10.cloned.1.call-start = ((), (), s32[]{:S(2)}) async-start(), calls=%async_computation.14 | async-start | bytes 5242880 | tf_op jit(solution)/shard_map/reduce_scatter | solution.py:48
  982.9 3.5 copy-start.32
  1002.3 19.0 %copy-start.9 = (s32[4]{0:T(128)S(1)}, s32[4]{0:T(128)}, u32[]{:S(2)}) copy-start(s32[4]{0:T(128)} %copy-done.8) | copy-start | bytes 52
  1015.9 42.4 %slice-start.2 = ((s8[8388608]{0:T(1024)(128)(4,1)}), s8[4194304]{0:T(1024)(128)(4,1)S(1)}, s32[]{:S(2)}) async-start(s8[8388608]{0:T(1024)(128)(4,1)} %bitcast.328), calls=%async_computation.21 | async-start | bytes 8388608
  1021.3 37.1 %slice-start.3 = ((s8[8388608]{0:T(1024)(128)(4,1)}), s8[4194304]{0:T(1024)(128)(4,1)S(1)}, s32[]{:S(2)}) async-start(s8[8388608]{0:T(1024)(128)(4,1)} %bitcast.328), calls=%async_computation.22 | async-start | bytes 8388608
  1066.6 397.7 %all-reduce.2.cloned.1.call-start = ((), (), s32[]{:S(2)}) async-start(), calls=%async_computation.17 | async-start | bytes 196608 | tf_op jit(solution)/shard_map/psum | solution.py:706
  1085.1 5.1 copy-start.7
  1085.1 5.1 copy-start.49
  1090.1 3.9 copy-start.4
  1090.1 3.9 copy-start.31
  1094.0 9.8 copy-start.24
  1094.0 9.8 copy-start.37
  1094.0 9.8 copy-start.39
  1094.0 9.7 copy-start.41
  1094.1 9.7 copy-start.47
  1116.7 60.2 %copy-start.12 = (bf16[2,1,256,2048]{3,2,1,0:T(8,128)(2,1)S(1)}, bf16[2,1,256,2048]{3,2,1,0:T(8,128)(2,1)}, u32[]{:S(2)}) copy-start(bf16[2,1,256,2048]{3,2,1,0:T(8,128)(2,1)} %param.18) | copy-start | bytes 6291460
  1116.7 60.2 %copy-start.27 = (bf16[256,2048]{1,0:T(8,128)(2,1)S(1)}, bf16[256,2048]{1,0:T(8,128)(2,1)}, u32[]{:S(2)}) copy-start(bf16[256,2048]{1,0:T(8,128)(2,1)} %reduce-scatter.12.cloned.1.call-done) | copy-start | bytes 3145732
  1173.1 3.8 copy-start.28
  1179.7 315.0 %reduce-scatter.14.cloned.1.call-start = ((), (), s32[]{:S(2)}) async-start(), calls=%async_computation.18 | async-start | bytes 9437184 | tf_op jit(solution)/shard_map/reduce_scatter | solution.py:689
  1188.1 13.0 copy-start.50
  1201.2 11.6 copy-start.33
  1213.7 48.8 %collective-permute-start.9 = (bf16[2,256,2048]{2,1,0:T(8,128)(2,1)S(1)}, bf16[2,256,2048]{2,1,0:T(8,128)(2,1)S(1)}, u32[]{:S(2)}, u32[]{:S(2)}) collective-permute-start(bf16[2,256,2048]{2,1,0:T(8,128)(2,1)S(1)} %pad_maximum_fusion.4), channel_id=1, source_target_pairs={{0,3},{1,0},{2,1},{3,2},{4,7},{5,4},{6,5},{7,6},{8,11},{9,8},{10,9... | collective-permute-start | bytes 6291464 | tf_op jit(solution)/shard_map/ppermute | solution.py:65
  1216.5 182.1 %collective-permute-start.10 = (bf16[2,256,2048]{2,1,0:T(8,128)(2,1)S(1)}, bf16[2,256,2048]{2,1,0:T(8,128)(2,1)S(1)}, u32[]{:S(2)}, u32[]{:S(2)}) collective-permute-start(bf16[2,256,2048]{2,1,0:T(8,128)(2,1)S(1)} %pad_maximum_fusion.5), channel_id=1, source_target_pairs={{0,2},{1,3},{2,0},{3,1},{4,6},{5,7},{6,4},{7,5},{8,10},{9,11},{10,... | collective-permute-start | bytes 6291464 | tf_op jit(solution)/shard_map/ppermute | solution.py:65
  1217.1 181.4 %collective-permute-start.11 = (bf16[2,256,2048]{2,1,0:T(8,128)(2,1)S(1)}, bf16[2,256,2048]{2,1,0:T(8,128)(2,1)S(1)}, u32[]{:S(2)}, u32[]{:S(2)}) collective-permute-start(bf16[2,256,2048]{2,1,0:T(8,128)(2,1)S(1)} %pad_maximum_fusion.6), channel_id=1, source_target_pairs={{0,1},{1,2},{2,3},{3,0},{4,5},{5,6},{6,7},{7,4},{8,9},{9,10},{10,1... | collective-permute-start | bytes 6291464 | tf_op jit(solution)/shard_map/ppermute | solution.py:65
  1407.9 31.3 %all-to-all-start.1 = ((bf16[2,256,2048]{1,0,2:T(2,128)(2,1)}), bf16[2,256,2048]{1,0,2:T(2,128)(2,1)}, u32[]{:S(2)}, u32[]{:S(2)}) async-start(bf16[2,256,2048]{1,0,2:T(2,128)(2,1)} %copy.107), calls=%async_computation.6 | async-start | bytes 4194304 | tf_op jit(solution)/shard_map/all_to_all | solution.py:662
  1454.5 5.4 copy-start.22
  1454.5 5.4 copy-start.29
  1457.6 3.1 copy-start.20
  1457.6 3.1 copy-start.43
  1457.6 3.1 copy-start.45
  1495.9 3.0 copy-start.30
  (16 other events, 31.1 us)
Sparse Core Ops, SparseCore 0:
  41.2 53.2 all-gather.9
  129.2 78.0 all-gather.13
  209.5 75.2 reduce-scatter.5
  287.1 222.5 reduce-scatter.7
  512.0 55.2 all-gather.11
  569.6 77.0 all-gather.15
  851.9 82.4 all-gather.19
  936.6 79.2 all-gather.17
  1018.2 75.2 reduce-scatter.11
  1095.8 77.2 reduce-scatter.9
  1179.8 239.3 all-reduce.1
  1422.5 72.1 reduce-scatter.13

commit v2 on v1

--- a/solution.py
+++ b/solution.py
@@ -14,6 +14,7 @@
 F32 = jnp.float32
 BF16 = jnp.bfloat16
 MESH = pl.DeviceIdType.MESH
+DMA = pltpu.SemaphoreType.DMA
 GELU = math.sqrt(2.0 / math.pi)
 
 
@@ -23,61 +24,584 @@
     return center * lax.rsqrt(spread + 1e-05) * gain + shift
 
 
-def chain_gather(own):
-    n = lax.axis_size("tensor")
-    me = lax.axis_index("tensor")
-    from_left, from_right = [own], [own]
-    for step in range(1, n):
-        up = [(i, i + 1) for i in range(step - 1, n - 1)]
-        down = [(n - 1 - i, n - 2 - i) for i in range(step - 1, n - 1)]
-        from_left.append(lax.ppermute(from_left[-1], "tensor", up))
-        from_right.append(lax.ppermute(from_right[-1], "tensor", down))
-    full = jnp.zeros((n,) + own.shape, own.dtype)
-    full = lax.dynamic_update_slice_in_dim(full, own[None], me, 0)
-    for step in range(1, n):
-        piece = jnp.where(me >= step, from_left[step], from_right[n - step])
-        full = lax.dynamic_update_slice_in_dim(full, piece[None], lax.rem(me - step + n, n), 0)
-    return full.reshape(n * own.shape[0], own.shape[1])
-
-
-def line_gather(own):
-    return lax.all_gather(own, "tensor", axis=0, tiled=True)
-
-
-def line_scatter(parts):
-    return lax.psum_scatter(parts, "tensor", scatter_dimension=0, tiled=True).astype(F32)
-
-
-def far_pairs(hop):
-    n = lax.axis_size("tensor")
-    return [(i, (i + hop) % n) for i in range(n)]
-
-
-def far_gather(own):
-    n = lax.axis_size("tensor")
-    return [own] + [lax.ppermute(own, "tensor", far_pairs(hop)) for hop in range(1, n)]
-
-
-def far_scatter(parts):
-    n = lax.axis_size("tensor")
-    total = parts[0].astype(F32)
-    for hop in range(1, n):
-        total = total + lax.ppermute(parts[hop], "tensor", far_pairs(n - hop)).astype(F32)
-    return total
-
-
 def after(value, *others):
     return lax.optimization_barrier((value,) + others)[0]
-
-
-PAIR = 2 * HEAD_DIM
-NEVER = -1e30
 
 
 def over(left, right, on_left, on_right):
     return lax.dot_general(
         left, right, (((on_left,), (on_right,)), ((), ())), preferred_element_type=F32
     )
+
+
+def window(index, rows):
+    return pl.ds(pl.multiple_of(index * rows, rows), rows)
+
+
+def remote(src, dst, send, recv, to):
+    return pltpu.make_async_remote_copy(
+        src_ref=src, dst_ref=dst, send_sem=send, recv_sem=recv,
+        device_id=to, device_id_type=MESH,
+    )
+
+
+class Line:
+    def __init__(self):
+        self.n = lax.axis_size("tensor")
+        self.me = lax.axis_index("tensor")
+        self.dp = lax.axis_index("dp")
+
+    def at(self, index):
+        return (self.dp, index)
+
+    def greet(self, barrier):
+        @pl.when(self.me > 0)
+        def _():
+            pl.semaphore_signal(barrier, inc=1, device_id=self.at(self.me - 1), device_id_type=MESH)
+
+        @pl.when(self.me < self.n - 1)
+        def _():
+            pl.semaphore_signal(barrier, inc=1, device_id=self.at(self.me + 1), device_id_type=MESH)
+
+    def peers(self):
+        return (self.me + self.n - 1) // self.n + (2 * self.n - 2 - self.me) // self.n
+
+
+class LineGather:
+    def __init__(self, line, own, full, sems):
+        self.line, self.own, self.full = line, own, full
+        self.rows = own.shape[0]
+        self.local, self.up_send, self.up_recv, self.down_send, self.down_recv = sems
+
+    @staticmethod
+    def sems(n):
+        return [DMA, DMA((n - 1,)), DMA((n - 1,)), DMA((n - 1,)), DMA((n - 1,))]
+
+    def hop(self, step, up):
+        line = self.line
+        if up:
+            shard, to = line.me - (step - 1), line.me + 1
+            send, recv = self.up_send, self.up_recv
+        else:
+            shard, to = line.me + (step - 1), line.me - 1
+            send, recv = self.down_send, self.down_recv
+        there = self.full.at[window(shard, self.rows)]
+        src = self.own if step == 1 else there
+        return remote(src, there, send.at[step - 1], recv.at[step - 1], line.at(to))
+
+    def sends(self, step, up):
+        line = self.line
+        if up:
+            return (line.me < line.n - 1) & (line.me >= step - 1)
+        return (line.me > 0) & (line.me + step - 1 < line.n)
+
+    def takes(self, step, up):
+        line = self.line
+        return (line.me >= step) if up else (line.me + step < line.n)
+
+    def send(self, step):
+        for up in (True, False):
+            @pl.when(self.sends(step, up))
+            def _():
+                self.hop(step, up).start()
+
+    def start(self):
+        self.place = pltpu.make_async_copy(
+            self.own, self.full.at[window(self.line.me, self.rows)], self.local
+        )
+        self.place.start()
+        self.send(1)
+
+    def take(self, step):
+        for up in (True, False):
+            @pl.when(self.takes(step, up))
+            def _():
+                line = self.line
+                shard = (line.me - step) if up else (line.me + step)
+                here = self.full.at[window(shard, self.rows)]
+                send, recv = (
+                    (self.up_send, self.up_recv) if up else (self.down_send, self.down_recv)
+                )
+                remote(
+                    here, here, send.at[step - 1], recv.at[step - 1], line.at(line.me)
+                ).wait_recv()
+        if step < self.line.n - 1:
+            self.send(step + 1)
+
+    def finish(self):
+        for step in range(1, self.line.n):
+            for up in (True, False):
+                @pl.when(self.sends(step, up))
+                def _():
+                    self.hop(step, up).wait_send()
+        pltpu.make_async_copy(
+            self.own, self.full.at[window(self.line.me, self.rows)], self.local
+        ).wait()
+
+
+class LineScatter:
+    def __init__(self, line, parts, out, scratch):
+        self.line, self.parts, self.out = line, parts, out
+        self.rows = out.shape[0]
+        (self.own, self.sum, self.come, self.load, self.own_sem, self.send_sem, self.recv_sem) = scratch
+
+    @staticmethod
+    def scratch(n, rows, d):
+        return [
+            pltpu.VMEM((rows, d), BF16),
+            pltpu.VMEM((2, n - 1, rows, d), BF16),
+            pltpu.VMEM((2, n - 1, rows, d), BF16),
+            DMA((2, n - 1)), DMA, DMA((2, n - 1)), DMA((2, n - 1)),
+        ]
+
+    def sends(self, step, up):
+        line = self.line
+        return (line.me <= step - 1) if up else (line.n - 1 - line.me <= step - 1)
+
+    def load_of(self, step, up):
+        line = self.line
+        chunk = (line.me + line.n - step) if up else (line.me - line.n + step)
+        way = 0 if up else 1
+        return pltpu.make_async_copy(
+            self.parts.at[window(chunk, self.rows)], self.sum.at[way, step - 1], self.load.at[way, step - 1]
+        )
+
+    def hop(self, step, up):
+        line, way = self.line, 0 if up else 1
+        return remote(
+            self.sum.at[way, step - 1], self.come.at[way, step - 1],
+            self.send_sem.at[way, step - 1], self.recv_sem.at[way, step - 1],
+            line.at(line.me + 1 if up else line.me - 1),
+        )
+
+    def wait_from(self, step, up):
+        line, way = self.line, 0 if up else 1
+        remote(
+            self.come.at[way, step - 1], self.come.at[way, step - 1],
+            self.send_sem.at[way, step - 1], self.recv_sem.at[way, step - 1],
+            line.at(line.me),
+        ).wait_recv()
+
+    def own_load(self):
+        return pltpu.make_async_copy(
+            self.parts.at[window(self.line.me, self.rows)], self.own, self.own_sem
+        )
+
+    def prepare(self):
+        self.own_load().start()
+        for step in range(1, self.line.n):
+            for up in (True, False):
+                @pl.when(self.sends(step, up))
+                def _():
+                    self.load_of(step, up).start()
+
+    def step(self, step):
+        line = self.line
+        for up in (True, False):
+            way = 0 if up else 1
+
+            @pl.when(self.sends(step, up))
+            def _():
+                self.load_of(step, up).wait()
+                if step > 1:
+                    inner = (line.me > 0) if up else (line.me < line.n - 1)
+
+                    @pl.when(inner)
+                    def _():
+                        self.wait_from(step - 1, up)
+
+                        @pl.loop(0, self.rows // 16)
+                        def _(i):
+                            part = window(i, 16)
+                            self.sum[way, step - 1, part] = (
+                                self.sum[way, step - 1, part].astype(F32)
+                                + self.come[way, step - 2, part].astype(F32)
+                            ).astype(BF16)
+
+                self.hop(step, up).start()
+
+    def finish(self):
+        line, n = self.line, self.line.n
+        self.own_load().wait()
+
+        @pl.loop(0, self.rows // 16)
+        def _(i):
+            part = window(i, 16)
+            self.out[part] = self.own[part].astype(F32)
+
+        for up in (True, False):
+            way = 0 if up else 1
+
+            @pl.when((line.me > 0) if up else (line.me < n - 1))
+            def _():
+                self.wait_from(n - 1, up)
+
+                @pl.loop(0, self.rows // 16)
+                def _(i):
+                    part = window(i, 16)
+                    self.out[part] += self.come[way, n - 2, part].astype(F32)
+
+        for step in range(1, n):
+            for up in (True, False):
+                @pl.when(self.sends(step, up))
+                def _():
+                    self.hop(step, up).wait_send()
+
+
+class Cube:
+    def __init__(self):
+        self.dp = lax.axis_size("dp")
+        self.levels = levels = self.dp.bit_length() - 2
+        self.count = 1 << levels
+        self.me = me = lax.axis_index("dp")
+        self.tensor = lax.axis_index("tensor")
+        core = me % 2
+        flips = []
+        for bit in range(1, levels + 1):
+            flips.append((1 << bit) * (1 - 2 * ((me // (1 << bit)) % 2)))
+        self.steps = [
+            flips[l] * (1 - core) + flips[levels - 1 - l] * core for l in range(levels)
+        ]
+        self.core_step = 1 - 2 * core
+
+    def at(self, index):
+        return (index, self.tensor)
+
+    def owner(self, piece):
+        mine, other = self.me, self.me + self.core_step
+        for l in range(self.levels):
+            if piece >> l & 1:
+                mine = mine + self.steps[l]
+                other = other + self.steps[self.levels - 1 - l]
+        return mine, other
+
+    def greet(self, barrier):
+        for step in self.steps + [self.core_step]:
+            pl.semaphore_signal(
+                barrier, inc=1, device_id=self.at(self.me + step), device_id_type=MESH
+            )
+
+    def peers(self):
+        return self.levels + 1
+
+
+class CubeGather:
+    def __init__(self, cube, own, full, sems):
+        self.cube, self.own, self.full = cube, own, full
+        self.rows = own.shape[0]
+        self.local, self.send_sem, self.recv_sem, self.core_send, self.core_recv = sems
+        self.arrived, self.sent = {0}, []
+
+    @staticmethod
+    def sems(count):
+        return [DMA, DMA((count,)), DMA((count,)), DMA((count,)), DMA((count,))]
+
+    def slot(self, index):
+        return self.full.at[window(index, self.rows)]
+
+    def src(self, piece):
+        return self.own if piece == 0 else self.slot(self.cube.owner(piece)[0])
+
+    def hop(self, piece, level):
+        cube, there = self.cube, piece + (1 << level)
+        return remote(
+            self.src(piece), self.slot(cube.owner(piece)[0]),
+            self.send_sem.at[there], self.recv_sem.at[there], cube.at(cube.me + cube.steps[level]),
+        )
+
+    def core(self, piece):
+        cube = self.cube
+        return remote(
+            self.src(piece), self.slot(cube.owner(piece)[0]),
+            self.core_send.at[piece], self.core_recv.at[piece], cube.at(cube.me + cube.core_step),
+        )
+
+    def give(self, piece):
+        for level in range(piece.bit_length(), self.cube.levels):
+            self.sent.append(self.hop(piece, level))
+            self.sent[-1].start()
+        self.sent.append(self.core(piece))
+        self.sent[-1].start()
+
+    def start(self):
+        self.place = pltpu.make_async_copy(self.own, self.slot(self.cube.me), self.local)
+        self.place.start()
+        self.give(0)
+
+    def take(self, piece):
+        if piece in self.arrived:
+            return
+        here = self.slot(self.cube.owner(piece)[0])
+        remote(
+            here, here, self.send_sem.at[piece], self.recv_sem.at[piece], self.cube.at(self.cube.me)
+        ).wait_recv()
+        self.arrived.add(piece)
+        self.give(piece)
+
+    def take_core(self, piece):
+        here = self.slot(self.cube.owner(piece)[1])
+        remote(
+            here, here, self.core_send.at[piece], self.core_recv.at[piece], self.cube.at(self.cube.me)
+        ).wait_recv()
+
+    def finish(self):
+        for piece in range(self.cube.count):
+            self.take(piece)
+            self.take_core(piece)
+        for copy in self.sent:
+            copy.wait_send()
+        self.place.wait()
+
+
+class CubeScatter:
+    def __init__(self, cube, parts, out, scratch):
+        self.cube, self.parts, self.out = cube, parts, out
+        self.rows = out.shape[0]
+        (self.keep, self.core_in, self.fold_in, self.load_sem,
+         self.core_send, self.core_recv, self.send_sem, self.recv_sem) = scratch
+
+    @staticmethod
+    def scratch(count, rows, d):
+        return [
+            pltpu.VMEM((count, rows, d), BF16),
+            pltpu.VMEM((count, rows, d), BF16),
+            pltpu.VMEM((count - 1, rows, d), BF16),
+            DMA((count,)), DMA((count,)), DMA((count,)), DMA((count - 1,)), DMA((count - 1,)),
+        ]
+
+    def load(self, piece):
+        return pltpu.make_async_copy(
+            self.parts.at[window(self.cube.owner(piece)[0], self.rows)],
+            self.keep.at[piece], self.load_sem.at[piece],
+        )
+
+    def core(self, piece):
+        cube = self.cube
+        return remote(
+            self.parts.at[window(cube.owner(piece)[1], self.rows)], self.core_in.at[piece],
+            self.core_send.at[piece], self.core_recv.at[piece], cube.at(cube.me + cube.core_step),
+        )
+
+    def hop(self, piece):
+        cube, level = self.cube, piece.bit_length() - 1
+        return remote(
+            self.keep.at[piece], self.fold_in.at[piece - 1],
+            self.send_sem.at[piece - 1], self.recv_sem.at[piece - 1],
+            cube.at(cube.me + cube.steps[level]),
+        )
+
+    def order(self):
+        return sorted(range(self.cube.count), key=lambda p: (-(p.bit_length()), p))
+
+    def start(self):
+        for piece in self.order():
+            self.core(piece).start()
+            self.load(piece).start()
+
+    def add(self, piece, other):
+        @pl.loop(0, self.rows // 16)
+        def _(i):
+            part = window(i, 16)
+            self.keep[piece, part] = (
+                self.keep[piece, part].astype(F32) + other[part].astype(F32)
+            ).astype(BF16)
+
+    def fold(self, piece):
+        self.load(piece).wait()
+        self.core(piece).wait_recv()
+        self.add(piece, self.core_in.at[piece])
+        for level in range(self.cube.levels - 1, piece.bit_length() - 1, -1):
+            above = piece + (1 << level)
+            self.hop(above).wait_recv()
+            self.add(piece, self.fold_in.at[above - 1])
+        if piece:
+            self.hop(piece).start()
+
+    def finish(self):
+        self.fold(0)
+
+        @pl.loop(0, self.rows // 16)
+        def _(i):
+            part = window(i, 16)
+            self.out[part] = self.keep[0, part].astype(F32)
+
+        for piece in range(self.cube.count):
+            self.core(piece).wait_send()
+            if piece:
+                self.hop(piece).wait_send()
+
+
+class CubeExchange:
+    def __init__(self, cube, moves, sems):
+        self.cube, self.moves = cube, moves
+        self.send_sem, self.recv_sem, self.local = sems
+
+    @staticmethod
+    def sems(dp, moves):
+        return [DMA((moves, dp)), DMA((moves, dp)), DMA((moves,))]
+
+    def copies(self):
+        cube = self.cube
+        out = []
+        for k in range(1, cube.dp):
+            to = (cube.me + k) % cube.dp
+            for m, (src, dst) in enumerate(self.moves):
+                out.append(
+                    remote(src(to), dst(cube.me), self.send_sem.at[m, k], self.recv_sem.at[m, k], cube.at(to))
+                )
+        return out
+
+    def locals(self):
+        return [
+            pltpu.make_async_copy(src(self.cube.me), dst(self.cube.me), self.local.at[m])
+            for m, (src, dst) in enumerate(self.moves)
+        ]
+
+    def start(self):
+        for copy in self.copies() + self.locals():
+            copy.start()
+
+    def finish(self):
+        cube = self.cube
+        for copy in self.copies():
+            copy.wait_send()
+        for k in range(1, cube.dp):
+            of = (cube.me - k + cube.dp) % cube.dp
+            for m, (src, dst) in enumerate(self.moves):
+                here = dst(of)
+                remote(here, here, self.send_sem.at[m, k], self.recv_sem.at[m, k], cube.at(of)).wait_recv()
+        for copy in self.locals():
+            copy.wait()
+
+
+ANY = pl.BlockSpec(memory_space=pl.ANY)
+VMEM = pl.BlockSpec(memory_space=pltpu.VMEM)
+
+
+def front_kernel(x_ref, w_ref, we_ref, wr_ref, small_ref, seq_ref, w_out, we_out, wr_out, small_out, *sems):
+    line, cube = Line(), Cube()
+    gather = LineGather(line, x_ref, seq_ref, sems[:5])
+    weights = CubeGather(cube, w_ref, w_out, sems[5:10])
+    mine = wr_out.shape[0]
+    rows, cols = we_ref.shape[0], wr_ref.shape[1]
+    tile = small_ref.shape[0]
+    moves = [
+        (lambda d: small_ref, lambda d: small_out.at[window(d, tile)]),
+        (lambda d: wr_ref.at[window(d, mine)], lambda d: wr_out.at[:, window(d, cols)]),
+        (lambda d: we_ref.at[:, window(d, mine)], lambda d: we_out.at[window(d, rows)]),
+    ]
+    swap = CubeExchange(cube, moves if mine % 128 == 0 else moves[:2], sems[10:13])
+    barrier = pltpu.get_barrier_semaphore()
+    line.greet(barrier)
+    for k in range(1, cube.dp):
+        pl.semaphore_signal(
+            barrier, inc=1, device_id=cube.at((cube.me + k) % cube.dp), device_id_type=MESH
+        )
+    pl.semaphore_wait(barrier, cube.dp - 1 + line.peers())
+    gather.start()
+    weights.start()
+    gather.take(1)
+    for piece in range(1, cube.count):
+        if piece.bit_length() < cube.levels:
+            weights.take(piece)
+    swap.start()
+    gather.take(2)
+    for piece in range(1, cube.count):
+        weights.take(piece)
+    for step in range(3, line.n):
+        gather.take(step)
+    weights.finish()
+    swap.finish()
+    gather.finish()
+
+
+def front(x, w, w_e, w_r, small):
+    dp, n = lax.axis_size("dp"), lax.axis_size("tensor")
+    rows, model = x.shape
+    outs = pl.pallas_call(
+        front_kernel,
+        out_shape=(
+            jax.ShapeDtypeStruct((n * rows, model), BF16),
+            jax.ShapeDtypeStruct((dp * w.shape[0], w.shape[1]), BF16),
+            jax.ShapeDtypeStruct((dp * w_e.shape[0], w_e.shape[1] // dp), BF16),
+            jax.ShapeDtypeStruct((w_r.shape[0] // dp, w_r.shape[1] * dp), BF16),
+            jax.ShapeDtypeStruct((dp * small.shape[0], small.shape[1]), BF16),
+        ),
+        in_specs=[ANY] * 5,
+        out_specs=(ANY,) * 5,
+        scratch_shapes=LineGather.sems(n) + CubeGather.sems(dp // 2) + CubeExchange.sems(dp, 3),
+        compiler_params=pltpu.CompilerParams(collective_id=0, has_side_effects=True),
+        cost_estimate=pl.CostEstimate(flops=80 * 10**9, bytes_accessed=10**7, transcendentals=0),
+        name="front",
+    )(x, w, w_e, w_r, small)
+    seq, w_all, e_all, r_all, small_all = outs
+    if r_all.shape[0] % 128:
+        e_all = lax.all_to_all(w_e, "dp", split_axis=1, concat_axis=0, tiled=True)
+    return seq, w_all, e_all, r_all, small_all
+
+
+def sum_kernel(lines, *refs):
+    line, cube = Line(), Cube()
+    total = len([r for r in refs if r is not None])
+    extra = 1 if total - 2 * lines - 7 * lines > 0 else 0
+    ins, outs = refs[: lines + extra], refs[lines + extra : 2 * (lines + extra)]
+    scratch = refs[2 * (lines + extra) :]
+    sums = [
+        LineScatter(line, ins[i], outs[i], scratch[7 * i : 7 * i + 7]) for i in range(lines)
+    ]
+    plane = CubeScatter(cube, ins[lines], outs[lines], scratch[7 * lines :]) if extra else None
+    for s in sums:
+        s.prepare()
+    barrier = pltpu.get_barrier_semaphore()
+    line.greet(barrier)
+    if extra:
+        cube.greet(barrier)
+    pl.semaphore_wait(barrier, line.peers() + (cube.peers() if extra else 0))
+    if extra:
+        plane.start()
+    pieces = [p for p in plane.order() if p] if extra else []
+    per = -(-len(pieces) // (line.n - 1))
+    for step in range(1, line.n):
+        for s in sums:
+            s.step(step)
+        for piece in pieces[:per]:
+            plane.fold(piece)
+        pieces = pieces[per:]
+    if extra:
+        plane.finish()
+    for s in sums:
+        s.finish()
+
+
+def line_sums(parts, plane_parts, collective_id):
+    dp, n = lax.axis_size("dp"), lax.axis_size("tensor")
+    rows, d = parts[0].shape[0] // n, parts[0].shape[1]
+    out_shape = [jax.ShapeDtypeStruct((rows, d), F32) for _ in parts]
+    scratch = []
+    for _ in parts:
+        scratch += LineScatter.scratch(n, rows, d)
+    operands = list(parts)
+    if plane_parts is not None:
+        rows_p, d_p = plane_parts.shape[0] // dp, plane_parts.shape[1]
+        out_shape.append(jax.ShapeDtypeStruct((rows_p, d_p), F32))
+        scratch += CubeScatter.scratch(dp // 2, rows_p, d_p)
+        operands.append(plane_parts)
+    return pl.pallas_call(
+        functools.partial(sum_kernel, len(parts)),
+        out_shape=tuple(out_shape),
+        in_specs=[ANY] * len(operands),
+        out_specs=(VMEM,) * len(operands),
+        scratch_shapes=scratch,
+        compiler_params=pltpu.CompilerParams(
+            collective_id=collective_id, has_side_effects=True, vmem_limit_bytes=60 << 20
+        ),
+        cost_estimate=pl.CostEstimate(flops=80 * 10**9, bytes_accessed=10**7, transcendentals=0),
+        name="line_sums",
+    )(*operands)
+
+
+PAIR = 2 * HEAD_DIM
+NEVER = -1e30
 
 
 def lane_of(shape, head):
@@ -154,13 +678,32 @@
         ),
         compiler_params=pltpu.CompilerParams(vmem_limit_bytes=48 << 20),
         cost_estimate=pl.CostEstimate(
-            flops=work * PAIR * 4, bytes_accessed=rows * width * 8, transcendentals=work
+            flops=work * PAIR * 24, bytes_accessed=rows * width * 8, transcendentals=work
         ),
         name="attend",
     )(parents, qkv, qkv, qkv)
 
 
-def attend_back_kernel(parents_ref, q_ref, k_ref, v_ref, g_ref, out_ref, dq_s, dk_s, dv_s):
+def attend_back_kernel(host, parents_ref, q_ref, k_ref, v_ref, g_ref, *refs):
+    if host:
+        own_ref, out_ref, full_ref, dq_s, dk_s, dv_s = refs[:6]
+        line = Line()
+        gather = LineGather(line, own_ref, full_ref, refs[6:])
+        pair, pairs = pl.program_id(0), pl.num_programs(0)
+
+        @pl.when((pair == 0) & (pl.program_id(1) == 0))
+        def _():
+            barrier = pltpu.get_barrier_semaphore()
+            line.greet(barrier)
+            pl.semaphore_wait(barrier, line.peers())
+            gather.start()
+
+        @pl.when((pair == pairs - 1) & (pl.program_id(1) == 0))
+        def _():
+            gather.take(1)
+
+    else:
+        out_ref, dq_s, dk_s, dv_s = refs
     part = pl.program_id(1)
     blocks = q_ref.shape[0] // BLOCK
     scale = 1.0 / math.sqrt(HEAD_DIM)
@@ -212,16 +755,35 @@
     def _():
         out_ref[...] = dv_s[...].astype(BF16)
 
-
-def attend_back(parents, qkv, grad, width):
+    if host:
+
+        @pl.when((pair == pairs - 1) & (part == 2))
+        def _():
+            for step in range(2, line.n):
+                gather.take(step)
+            gather.finish()
+
+
+def attend_back(parents, qkv, grad, width, own=None):
     rows = qkv.shape[0]
     pairs = width // PAIR
     spec = lambda part: pl.BlockSpec((rows, PAIR), lambda p, c, parents: (0, part * pairs + p))
     blocks = rows // BLOCK
     work = pairs * 2 * (blocks * (blocks + 1) // 2) * BLOCK * BLOCK
-    return pl.pallas_call(
-        attend_back_kernel,
-        out_shape=jax.ShapeDtypeStruct((rows, 3 * width), BF16),
+    host = own is not None
+    out_shape = [jax.ShapeDtypeStruct((rows, 3 * width), BF16)]
+    out_specs = [pl.BlockSpec((rows, PAIR), lambda p, c, parents: (0, c * pairs + p))]
+    sems = []
+    params = dict(vmem_limit_bytes=48 << 20)
+    if host:
+        n = lax.axis_size("tensor")
+        out_shape.append(jax.ShapeDtypeStruct((n * own.shape[0], own.shape[1]), BF16))
+        out_specs.append(ANY)
+        sems = LineGather.sems(n)
+        params.update(collective_id=4, has_side_effects=True)
+    out = pl.pallas_call(
+        functools.partial(attend_back_kernel, host),
+        out_shape=out_shape,
         grid_spec=pltpu.PrefetchScalarGridSpec(
             num_scalar_prefetch=1,
             grid=(pairs, 3),
@@ -230,68 +792,62 @@
                 spec(1),
                 spec(2),
                 pl.BlockSpec((rows, PAIR), lambda p, c, parents: (0, p)),
-            ],
-            out_specs=pl.BlockSpec((rows, PAIR), lambda p, c, parents: (0, c * pairs + p)),
+            ]
+            + [ANY] * host,
+            out_specs=out_specs,
             scratch_shapes=[
                 pltpu.VMEM((rows, PAIR), BF16),
                 pltpu.VMEM((rows, PAIR), F32),
                 pltpu.VMEM((rows, PAIR), F32),
-            ],
+            ]
+            + sems,
         ),
-        compiler_params=pltpu.CompilerParams(vmem_limit_bytes=48 << 20),
+        compiler_params=pltpu.CompilerParams(**params),
         cost_estimate=pl.CostEstimate(
-            flops=work * PAIR * 10, bytes_accessed=rows * width * 14, transcendentals=work
+            flops=work * PAIR * 60, bytes_accessed=rows * width * 14, transcendentals=work
         ),
         name="attend_back",
-    )(parents, qkv, qkv, qkv, grad)
-
-
-def cube_place():
-    levels = lax.axis_size("dp").bit_length() - 2
-    me = lax.axis_index("dp")
-    core = me % 2
-    flips = []
-    for bit in range(1, levels + 1):
-        flips.append((1 << bit) * (1 - 2 * ((me // (1 << bit)) % 2)))
-    steps = [
-        flips[l] * (1 - core) + flips[levels - 1 - l] * core for l in range(levels)
-    ]
-    return levels, me, steps, 1 - 2 * core
-
-
-def ffn_kernel(
-    n2_ref, dy_ref, wet_ref, wr_ref, be_ref,
-    sum_ref, seq_ref, act_ref, dpre_ref,
-    wet, wr, seq, dy_st, act_st, dpre_st, keep, give, core_in, fold_in,
-    w_sem, own_sem, dy_sem, seq_sem, st_sem,
-    ag_send, ag_recv, agc_send, agc_recv, rsc_send, rsc_recv, fold_send, fold_recv,
-):
-    levels, me, steps, core_step = cube_place()
-    tensor = lax.axis_index("tensor")
-    count = 1 << levels
+    )(parents, qkv, qkv, qkv, grad, *([own] if host else []))
+    return out if host else out[0]
+
+
+def ffn_kernel(host, n2_ref, dy_ref, we_ref, wr_ref, be_ref, *refs):
+    if host:
+        line_own, refs = refs[0], refs[1:]
+    sum_ref, seq_ref, act_ref, dpre_ref = refs[:4]
+    refs = refs[4:]
+    if host:
+        line_full, refs = refs[0], refs[1:]
+    we, wr, seq, dy_st, act_st, dpre_st, keep, give, core_in, fold_in = refs[:10]
+    w_sem, own_sem, dy_sem, seq_sem, st_sem = refs[10:15]
+    ag_send, ag_recv, agc_send, agc_recv, rsc_send, rsc_recv, fold_send, fold_recv = refs[15:23]
+    cube = Cube()
+    levels, me, steps, core_step = cube.levels, cube.me, cube.steps, cube.core_step
+    count, at, owner = cube.count, cube.at, cube.owner
     rows, model = n2_ref.shape
-    units = wet_ref.shape[0]
-
-    def at(index):
-        return (index, tensor)
-
-    def owner(piece):
-        mine, other = me, me + core_step
-        for l in range(levels):
-            if piece >> l & 1:
-                mine = mine + steps[l]
-                other = other + steps[levels - 1 - l]
-        return mine, other
-
+    units = wr_ref.shape[0]
     barrier = pltpu.get_barrier_semaphore()
-    for step in steps + [core_step]:
-        pl.semaphore_signal(barrier, inc=1, device_id=at(me + step), device_id_type=MESH)
+    cube.greet(barrier)
+    hosted = []
+    if host:
+        line = Line()
+        line.greet(barrier)
+        gather = LineGather(line, line_own, line_full, refs[23:])
     load_own = pltpu.make_async_copy(n2_ref, seq.at[0, pl.ds(0, rows)], own_sem)
     load_own.start()
-    load_wet = pltpu.make_async_copy(wet_ref, wet, w_sem.at[0])
-    load_wr = pltpu.make_async_copy(wr_ref, wr, w_sem.at[1])
-    load_wet.start()
-    load_wr.start()
+    parts = we_ref.shape[0] // model
+    mine_units = we_ref.shape[1]
+    loads_w = [pltpu.make_async_copy(wr_ref, wr, w_sem.at[parts])]
+    for part in range(parts):
+        loads_w.append(
+            pltpu.make_async_copy(
+                we_ref.at[pl.ds(part * model, model)],
+                we.at[:, pl.ds(part * mine_units, mine_units)],
+                w_sem.at[part],
+            )
+        )
+    for c in loads_w:
+        c.start()
 
     def load_dy(piece, slot):
         mine, other = owner(piece)
@@ -306,23 +862,17 @@
             )
         return out
 
-    def remote(src, dst, send, recv, to):
-        return pltpu.make_async_remote_copy(
-            src_ref=src, dst_ref=dst, send_sem=send, recv_sem=recv,
-            device_id=at(to), device_id_type=MESH,
-        )
-
     def gather_copy(piece, level):
         there = piece + (1 << level)
         return remote(
             seq.at[piece, pl.ds(0, rows)], seq.at[there, pl.ds(0, rows)],
-            ag_send.at[there], ag_recv.at[there], me + steps[level],
+            ag_send.at[there], ag_recv.at[there], at(me + steps[level]),
         )
 
     def gather_core(piece):
         return remote(
             seq.at[piece, pl.ds(0, rows)], seq.at[piece, pl.ds(rows, rows)],
-            agc_send.at[piece], agc_recv.at[piece], me + core_step,
+            agc_send.at[piece], agc_recv.at[piece], at(me + core_step),
         )
 
     order = [0] + sorted(range(1, count), key=lambda p: (-(p.bit_length()), p))
@@ -332,15 +882,17 @@
         c.start()
 
     load_own.wait()
-    pl.semaphore_wait(barrier, levels + 1)
+    pl.semaphore_wait(barrier, cube.peers() + (line.peers() if host else 0))
+    if host:
+        gather.start()
     sends = []
     for level in range(levels):
         sends.append(gather_copy(0, level))
         sends[-1].start()
     sends.append(gather_core(0))
     sends[-1].start()
-    load_wet.wait()
-    load_wr.wait()
+    for c in loads_w:
+        c.wait()
 
     arrived = {0}
 
@@ -380,7 +932,7 @@
     def core_copy(piece):
         return remote(
             give.at[slots[piece]], core_in.at[piece],
-            rsc_send.at[piece], rsc_recv.at[piece], me + core_step,
+            rsc_send.at[piece], rsc_recv.at[piece], at(me + core_step),
         )
 
     def fold_copy(piece):
@@ -388,7 +940,7 @@
         low = piece - (1 << level)
         return remote(
             keep.at[piece], fold_in.at[piece - 1],
-            fold_send.at[piece - 1], fold_recv.at[piece - 1], me + steps[level],
+            fold_send.at[piece - 1], fold_recv.at[piece - 1], at(me + steps[level]),
         )
 
     def fold(piece):
@@ -422,7 +974,7 @@
         @pl.loop(0, units // chunk)
         def _(i):
             cols = pl.ds(pl.multiple_of(i * chunk, chunk), chunk)
-            pre = over(seq[piece], wet[cols, :], 1, 1) + be_ref[:, cols]
+            pre = over(seq[piece], we[:, cols], 1, 0) + be_ref[:, cols]
             d_act = over(dy_st[slot], wr[cols, :], 1, 1)
             square = pre * pre
             t = jnp.tanh(GELU * pre * (1.0 + 0.044715 * square))
@@ -436,13 +988,15 @@
         def _(i):
             cols = pl.ds(pl.multiple_of(i * wide, wide), wide)
             cols_out = pl.ds(pl.multiple_of(model + i * wide, wide), wide)
-            d_two = over(dpre_st[slot], wet[:, cols], 1, 0).astype(BF16)
+            d_two = over(dpre_st[slot], we[cols, :], 1, 1).astype(BF16)
             keep[piece, :, cols] = d_two[:rows]
             give[slot, :, cols] = d_two[rows:]
             out = over(act_st[slot], wr[:, cols], 1, 0).astype(BF16)
             keep[piece, :, cols_out] = out[:rows]
             give[slot, :, cols_out] = out[rows:]
 
+        if host and turn < line.n - 1:
+            gather.take(turn + 1)
         core_sends[piece] = core_copy(piece)
         core_sends[piece].start()
         mine, other = owner(piece)
@@ -478,6 +1032,10 @@
             total = total + fold_in[(1 << level) - 1, part].astype(F32)
         sum_ref[part] = total
 
+    if host:
+        for step in range(count + 1, line.n):
+            gather.take(step)
+        gather.finish()
     for s in sends:
         s.wait_send()
     for turn in range(max(0, count - 2), count):
@@ -488,27 +1046,30 @@
         s.wait_send()
 
 
-def ffn(n2, dy_all, wet, wr, bias_e):
+def ffn(n2, dy_all, we, wr, bias_e, own=None):
+    host = own is not None
+    n = lax.axis_size("tensor")
     rows, model = n2.shape
-    units = wet.shape[0]
+    units = wr.shape[0]
     dp = lax.axis_size("dp")
     count = dp // 2
-    dma = pltpu.SemaphoreType.DMA
-    anywhere = pl.BlockSpec(memory_space=pl.ANY)
-    vmem = pl.BlockSpec(memory_space=pltpu.VMEM)
-    flops = 8 * dp * rows * model * units
+    dma, anywhere, vmem = DMA, ANY, VMEM
+    operands = [n2, dy_all, we, wr, bias_e] + [own] * host
+    lines = [jax.ShapeDtypeStruct((n * rows, model), BF16)] * host
+    flops = 36 * dp * rows * model * units
     return pl.pallas_call(
-        ffn_kernel,
+        functools.partial(ffn_kernel, host),
         out_shape=(
             jax.ShapeDtypeStruct((rows, 2 * model), F32),
             jax.ShapeDtypeStruct((dp * rows, model), BF16),
             jax.ShapeDtypeStruct((dp * rows, units), BF16),
             jax.ShapeDtypeStruct((dp * rows, units), BF16),
+            *lines,
         ),
-        in_specs=[anywhere, anywhere, anywhere, anywhere, vmem],
-        out_specs=(vmem, anywhere, anywhere, anywhere),
+        in_specs=[anywhere, anywhere, anywhere, anywhere, vmem] + [anywhere] * host,
+        out_specs=(vmem, anywhere, anywhere, anywhere) + (anywhere,) * host,
         scratch_shapes=[
-            pltpu.VMEM((units, model), BF16),
+            pltpu.VMEM((model, units), BF16),
             pltpu.VMEM((units, model), BF16),
             pltpu.VMEM((count, 2 * rows, model), BF16),
             pltpu.VMEM((2, 2 * rows, model), BF16),
@@ -518,18 +1079,19 @@
             pltpu.VMEM((2, rows, 2 * model), BF16),
             pltpu.VMEM((count, rows, 2 * model), BF16),
             pltpu.VMEM((count - 1, rows, 2 * model), BF16),
-            dma((2,)), dma, dma((2, 2)), dma((count, 2)), dma((2, 2, 2)),
+            dma((n + 1,)), dma, dma((2, 2)), dma((count, 2)), dma((2, 2, 2)),
             dma((count,)), dma((count,)), dma((count,)), dma((count,)),
             dma((count,)), dma((count,)), dma((count - 1,)), dma((count - 1,)),
-        ],
+        ]
+        + (LineGather.sems(n) if host else []),
         compiler_params=pltpu.CompilerParams(
-            collective_id=1, has_side_effects=True, vmem_limit_bytes=62 << 20
+            collective_id=2 if host else 1, has_side_effects=True, vmem_limit_bytes=62 << 20
         ),
         cost_estimate=pl.CostEstimate(
             flops=flops, bytes_accessed=8 * dp * rows * (model + units), transcendentals=dp * rows * units
         ),
         name="ffn_plane",
-    )(n2, dy_all, wet, wr, bias_e)
+    )(*operands)
 
 
 def body(
@@ -552,7 +1114,6 @@
     w_reduce,
     b_reduce,
 ):
-    micro_count = tokens.shape[0]
     dp = lax.axis_size("dp")
     tn = lax.axis_size("tensor")
     dp_me = lax.axis_index("dp")
@@ -561,17 +1122,27 @@
     model = w_query.shape[0] * dp
     units = w_expand.shape[1]
     mine = units // dp
-    micros = range(micro_count)
+    micros = range(tokens.shape[0])
+    last = tokens.shape[0] - 1
+    x_low = [tokens[m, 0] for m in micros]
+    dy_low = [cotangent[m, 0] for m in micros]
+    rows_here = x_low[0].shape[0]
+    total = rows_here * tn
 
     cut = first_gain.shape[0]
     bq_rows, bq_cols = b_query.shape
     be_rows, be_cols = b_expand.shape
-    be_all = lax.all_gather(b_expand.reshape(-1), "tensor", axis=0, tiled=True)
     small = jnp.concatenate(
         [first_gain, first_shift, b_out, second_gain, second_shift, b_reduce]
-        + [b_query.reshape(-1), b_value.reshape(-1), be_all]
+        + [b_query.reshape(-1), b_value.reshape(-1), b_expand.reshape(-1)]
     )
-    small = lax.all_gather(small, "dp", axis=0, tiled=False)
+    used = small.shape[0]
+    small = jnp.pad(small, (0, -used % 2048)).reshape(-1, 128)
+    w_attn = jnp.concatenate([w_query, w_key, w_value, w_out.T], axis=1)
+    seq_x0, w_attn, w_e, w_r, small = front(x_low[0], w_attn, w_expand, w_reduce, small)
+    w_qkv = w_attn[:, : 3 * width]
+    w_ot = w_attn[:, 3 * width :]
+    small = small.reshape(dp, -1)[:, :used]
     gain_one, shift_one, bias_out, gain_two, shift_two, bias_red = [
         small[:, i * cut : (i + 1) * cut].reshape(1, model).astype(F32) for i in range(6)
     ]
@@ -582,52 +1153,39 @@
         bias_qkv.append(part.transpose(1, 0, 2).reshape(1, width).astype(F32))
         at += bq_rows * bq_cols
     bias_qkv = jnp.concatenate([bias_qkv[0], jnp.zeros((1, width), F32), bias_qkv[1]], 1)
-    bias_e = small[:, at:].reshape(dp, tn, dp, be_rows // dp, be_cols)
-    bias_e = lax.dynamic_index_in_dim(bias_e, dp_me, 2, keepdims=False)
-    bias_e = bias_e.transpose(1, 2, 0, 3).reshape(tn, mine)
-    turned = [
-        lax.dynamic_index_in_dim(bias_e, lax.rem(tn_me - hop + tn, tn), 0, keepdims=True)
-        for hop in range(tn)
-    ]
-    bias_e = jnp.concatenate(turned, 1).astype(F32)
-
-    x_low = [tokens[m, 0] for m in micros]
-    dy_low = [cotangent[m, 0] for m in micros]
-    rows_here = x_low[0].shape[0]
-    total = rows_here * tn
-    seq_x = [chain_gather(after(x_low[0], small))]
-    w_attn = jnp.concatenate([w_query, w_key, w_value, w_out.T], axis=1)
-    w_attn = lax.all_gather(after(w_attn, small), "dp", axis=0, tiled=True)
-    w_qkv = w_attn[:, : 3 * width]
-    w_ot = w_attn[:, 3 * width :]
-    for m in range(1, micro_count):
-        seq_x.append(line_gather(after(x_low[m], seq_x[-1])))
-
-    ffn_w = jnp.stack([w_expand.T, w_reduce], 0)
-    ffn_w = lax.all_to_all(after(ffn_w, small), "dp", split_axis=1, concat_axis=2, tiled=True)
-    ffn_w = far_gather(after(ffn_w, seq_x[0]))
-    w_et = jnp.concatenate([p[0] for p in ffn_w], 0)
-    w_r = jnp.concatenate([p[1] for p in ffn_w], 0)
-
-    seq_grad = [
-        lax.all_gather(after(dy_low[m], w_attn), "dp", axis=0, tiled=True) for m in micros
-    ]
-
-    seq_one, qkv, attended, hidden, normed_two = [], [], [], [], []
+    bias_e = small[:, at:].reshape(dp, dp, be_rows // dp, be_cols)
+    bias_e = lax.dynamic_index_in_dim(bias_e, dp_me, 1, keepdims=False)
+    bias_e = lax.all_gather(bias_e.transpose(1, 0, 2).reshape(1, mine), "tensor", axis=1, tiled=True)
+    bias_e = bias_e.astype(F32)
+
+    seq_grad = [lax.all_gather(dy_low[0], "dp", axis=0, tiled=True)]
+    seq_x = [seq_x0]
+    for m in micros[1:]:
+        seq_x.append(lax.all_gather(after(x_low[m], seq_x[-1]), "tensor", axis=0, tiled=True))
+    side = 0 if mine % 128 == 0 else 1
+    w_e = lax.all_gather(after(w_e, seq_x[-1]), "tensor", axis=side, tiled=True)
+    w_r = lax.all_gather(after(w_r, w_e), "tensor", axis=0, tiled=True)
+    for m in micros[1:]:
+        seq_grad.append(lax.all_gather(after(dy_low[m], w_r), "dp", axis=0, tiled=True))
+
+    normal_one, seq_one, qkv, attended, hidden, normed_two = [], [], [], [], [], []
     for m in micros:
-        seq_one.append(layer_norm(seq_x[m].astype(F32), gain_one, shift_one).astype(BF16))
+        normal_one.append(layer_norm(seq_x[m].astype(F32), 1.0, 0.0))
+        seq_one.append((normal_one[m] * gain_one + shift_one).astype(BF16))
         qkv.append(
             (jnp.dot(seq_one[m], w_qkv, preferred_element_type=F32) + bias_qkv).astype(BF16)
         )
         attended.append(attend(parents[m, 0], qkv[m], width))
-        branch = line_scatter(over(attended[m], w_ot, 1, 1).astype(BF16))
+        branch = line_sums([over(attended[m], w_ot, 1, 1).astype(BF16)], None, 3)[0]
         hidden.append(x_low[m].astype(F32) + (branch + bias_out))
         normed_two.append(layer_norm(hidden[m], gain_two, shift_two).astype(BF16))
 
-    layer_out, seq_two, activated, d_pre, d_hidden, d_branch = [], [], [], [], [], []
+    layer_out, seq_two, activated, d_pre, d_hidden, d_branch, seq_branch = [], [], [], [], [], [], []
     g_gain_two = g_shift_two = g_bias_red = g_bias_out = g_bias_e = 0.0
     for m in micros:
-        sums, seq, act, dpre = ffn(normed_two[m], seq_grad[m], w_et, w_r, bias_e)
+        own = d_branch[m - 1] if m else None
+        sums, seq, act, dpre, *line = ffn(normed_two[m], seq_grad[m], w_e, w_r, bias_e, own)
+        seq_branch += line
         seq_two.append(seq)
         activated.append(act)
         d_pre.append(dpre)
@@ -652,43 +1210,27 @@
         return out.astype(BF16)
 
     g_r = outer(activated, seq_grad)
-    g_et = outer(d_pre, seq_two)
-    g_ffn = far_scatter(
-        [
-            jnp.stack([g_et[i * mine : (i + 1) * mine], g_r[i * mine : (i + 1) * mine]], 0)
-            for i in range(tn)
-        ]
-    ).astype(BF16)
-    g_ffn = lax.all_to_all(g_ffn, "dp", split_axis=2, concat_axis=1, tiled=True).astype(F32)
-    g_expand = g_ffn[0].T
-    g_reduce = g_ffn[1]
-
-    input_grad, d_qkv, seq_branch = [], [], []
+    g_r_sum = lax.psum_scatter(g_r, "tensor", scatter_dimension=0, tiled=True)
+
+    d_qkv, d_one = [], []
     g_gain_one = g_shift_one = g_bias_qkv = 0.0
     for m in micros:
-        seq_branch.append(line_gather(d_branch[m]))
         d_att = jnp.dot(seq_branch[m], w_ot, preferred_element_type=F32).astype(BF16)
-        d_qkv.append(attend_back(parents[m, 0], qkv[m], d_att, width))
-        g_bias_qkv = g_bias_qkv + jnp.sum(d_qkv[m].astype(F32), 0)
-        d_one = line_scatter(over(d_qkv[m], w_qkv, 1, 1).astype(BF16))
-        first_value, first_pull = jax.vjp(
-            layer_norm, x_low[m].astype(F32), gain_one, shift_one
-        )
-        d_x, g_gain, g_shift = first_pull(d_one)
-        input_grad.append((d_hidden[m] + d_x).astype(BF16))
-        g_gain_one = g_gain_one + g_gain
-        g_shift_one = g_shift_one + g_shift
-
-    g_attn = jnp.concatenate(
-        [
-            outer(seq_one, d_qkv),
-            outer(seq_branch, attended),
-        ],
-        axis=1,
-    )
-    g_attn = lax.psum_scatter(g_attn, "dp", scatter_dimension=0, tiled=True).astype(F32)
-    g_query, g_key, g_value = [g_attn[:, i * width : (i + 1) * width] for i in range(3)]
-    g_out = g_attn[:, 3 * width :].T
+        if m < last:
+            d_att = after(d_att, g_r)
+            d, full = attend_back(parents[m, 0], qkv[m], d_att, width, d_branch[m + 1])
+            seq_branch.append(full)
+        else:
+            g_et = outer(d_pre, seq_two)
+            g_et_sum = lax.psum_scatter(after(g_et, g_r_sum), "tensor", scatter_dimension=0, tiled=True)
+            d_att = after(d_att, g_et)
+            d = attend_back(parents[m, 0], qkv[m], d_att, width)
+        d_qkv.append(d)
+        g_bias_qkv = g_bias_qkv + jnp.sum(d.astype(F32), 0)
+        d_one.append(over(d, w_qkv, 1, 1).astype(BF16))
+        part = d_one[m].astype(F32)
+        g_gain_one = g_gain_one + jnp.sum(part * normal_one[m], 0, keepdims=True)
+        g_shift_one = g_shift_one + jnp.sum(part, 0, keepdims=True)
 
     rows = jnp.concatenate(
         [g_gain_one, g_shift_one, g_bias_out, g_gain_two, g_shift_two, g_bias_red], 0
@@ -696,13 +1238,9 @@
     place = jnp.zeros((tn, width), F32)
     row_q = lax.dynamic_update_slice(place, g_bias_qkv[None, :width], (tn_me, 0)).reshape(-1)
     row_v = lax.dynamic_update_slice(place, g_bias_qkv[None, 2 * width :], (tn_me, 0)).reshape(-1)
-    g_bias_e = g_bias_e.reshape(tn, 1, 1, mine)
-    row_e = jnp.zeros((tn, dp, mine), F32)
-    for hop in range(tn):
-        row_e = lax.dynamic_update_slice(
-            row_e, g_bias_e[hop], (lax.rem(tn_me - hop + tn, tn), dp_me, 0)
-        )
-    row_e = row_e.reshape(-1)
+    row_e = lax.dynamic_update_slice(
+        jnp.zeros((tn, dp, mine), F32), g_bias_e.reshape(tn, 1, mine), (0, dp_me, 0)
+    ).reshape(-1)
     sums = lax.psum(jnp.concatenate([rows, row_q, row_v, row_e]), ("dp", "tensor"))
     n_rows = 6 * model
     six = lax.dynamic_slice_in_dim(sums[:n_rows].reshape(6, model), dp_me * cut, cut, 1)
@@ -717,6 +1255,22 @@
     g_bq = block(sums[n_rows : n_rows + heads_all], bq_rows)
     g_bv = block(sums[n_rows + heads_all : n_rows + 2 * heads_all], bq_rows)
     g_be = block(sums[n_rows + 2 * heads_all :], be_rows)
+
+    g_ffn = jnp.stack([g_et_sum, g_r_sum], 0)
+    g_ffn = lax.all_to_all(g_ffn, "dp", split_axis=2, concat_axis=1, tiled=True).astype(F32)
+    g_expand = g_ffn[0].T
+    g_reduce = g_ffn[1]
+
+    g_attn = jnp.concatenate([outer(seq_one, d_qkv), outer(seq_branch, attended)], axis=1)
+    *d_one, g_attn = line_sums(d_one, g_attn, 5)
+    g_query, g_key, g_value = [g_attn[:, i * width : (i + 1) * width] for i in range(3)]
+    g_out = g_attn[:, 3 * width :].T
+    input_grad = []
+    for m in micros:
+        first_value, first_pull = jax.vjp(
+            lambda rows: layer_norm(rows, gain_one, shift_one), x_low[m].astype(F32)
+        )
+        input_grad.append((d_hidden[m] + first_pull(d_one[m])[0]).astype(BF16))
 
     return (
         jnp.stack(layer_out, 0)[:, None],

time: 1510 us -> 1500 us (level)
  Pallas kernels: 370 us -> 931 us
  waiting for transfers between devices: 723 us -> 261 us
  blocking collectives: 52 us -> 8.25 us
  local copies, waits for them, and re-layouts: 90.2 us -> 57.7 us
  starting transfers between devices: 25.7 us -> 5.04 us
  other arithmetic: 83.6 us -> 65.5 us
    pallas_call x4 -> x8, Pallas kernels: 342 us -> 903 us  [the longest x3 372 us: line_sums(): pl.pallas_call(functools.partial(sum_kernel, len(parts)), out_shape=tuple...]
    ppermute x12 -> x0, waiting for transfers between devices: 480 us -> none  [the longest x3 236 us: far_gather(): lax.ppermute(own, 'tensor', far_pairs(hop))]
    psum x1, waiting for transfers between devices: 0.01 us -> 102 us  [body(): lax.psum(jnp.concatenate([rows, row_q, row_v, row_e]), ('dp', 'tensor'))]
    reduce_scatter x5 -> x2, waiting for transfers between devices: 82.2 us -> 0.02 us  [the longest x1 0.02 us: body(): lax.psum_scatter(after(g_et, g_r_sum), 'tensor', scatter_dimension=0, til...]
    all_to_all x1 -> x0, blocking collectives: 30.1 us -> none  [body(): lax.all_to_all(after(ffn_w, small), 'dp', split_axis=1, concat_axis=2, ti...]
    all_to_all x1, waiting for transfers between devices: 23.6 us -> 0.01 us  [body(): lax.all_to_all(g_ffn, 'dp', split_axis=2, concat_axis=1, tiled=True)]
    all_gather x6 -> x5, waiting for transfers between devices: 137 us -> 159 us  [the longest x1 80.8 us: body(): w_e = lax.all_gather(after(w_e, seq_x[-1]), 'tensor', axis=side, tiled=True)]
    ppermute x12 -> x0, starting transfers between devices: 19.9 us -> none  [the longest x3 7.99 us: chain_gather(): from_left.append(lax.ppermute(from_left[-1], 'tensor', up))]
  transfers between devices with their start and end apart: 25 -> 9, of which waited for: 14 -> 3; matrix products, arithmetic and copies ran while one was open for 18% -> 15% of each run, Pallas kernels for 16% -> 48%
where the time goes in v2:
time: 1500 us
  Pallas kernels  931 us (62%)
  waiting for transfers between devices  261 us (17%)
  matrix products  154 us (10%)
  other arithmetic  65.5 us (4%)
  local copies, waits for them, and re-layouts  57.7 us (4%)
  between operations  15.7 us (1%)
    pallas_call x3, Pallas kernels, line_sums(): pl.pallas_call(functools.partial(sum_kernel, len(parts)), out_shape=tuple...  372 us
    pallas_call x2, Pallas kernels, ffn(): pl.pallas_call(functools.partial(ffn_kernel, host), out_shape=(jax.ShapeD...  278 us
    pallas_call x2, Pallas kernels, attend_back(): pl.pallas_call(functools.partial(attend_back_kernel, host), out_shape=out...  173 us
    dot_general x12, matrix products, over(): lax.dot_general(left, right, (((on_left,), (on_right,)), ((), ())), prefe...  123 us
    psum x1, waiting for transfers between devices, body(): lax.psum(jnp.concatenate([rows, row_q, row_v, row_e]), ('dp', 'tensor'))  102 us
    all_gather x1, waiting for transfers between devices, body(): w_e = lax.all_gather(after(w_e, seq_x[-1]), 'tensor', axis=side, tiled=True)  80.8 us
    pallas_call x1, Pallas kernels, front(): pl.pallas_call(front_kernel, out_shape=(jax.ShapeDtypeStruct((n * rows, m...  79.2 us
    all_gather x1, waiting for transfers between devices, body(): lax.all_gather(after(x_low[m], seq_x[-1]), 'tensor', axis=0, tiled=True)  78.4 us
  transfers between devices with their start and end apart: 9, of which 3 were waited for; matrix products, arithmetic and copies ran while one was open for 15% of the time, Pallas kernels for 48%

profile of v2, /device:TPU:0, one launch (start us, length us, event | category | flops | bytes accessed | tf_op | source)
XLA Modules:
  0.0 1499.1 jit_solution(12073718562175596747)
XLA Ops:
  9.7 4.1 concatenate.19
  15.5 3.1 slice_bitcast_fusion.1
  18.6 1.1 pad_maximum_fusion.2.w_ref
  19.7 79.2 %front.1 = (bf16[1024,2048]{1,0:T(8,128)(2,1)}, bf16[2048,2048]{1,0:T(8,128)(2,1)}, bf16[2048,256]{1,0:T(8,128)(2,1)}, bf16[256,2048]{1,0:T(8,128)(2,1)}, bf16[128,128]{1,0:T(8,128)(2,1)}) custom-call(bf16[256,2048]{1,0:T(8,128)(2,1)} %get-tuple-element.187.x_ref, bf16[256,2048]{1,0:T(8,128)(2,1)} %pad_maximum_fusion.2.w_ref, bf16[256,2048]{1,0:T(8,128)(2,1)} %we_ref.1, ...), custom_call_target="tpu_custom_call" | custom-call | flops 80000000000 | bytes 10000000 | tf_op jit(solution)/shard_map/front/pallas_call | solution.py:521
  99.0 78.4 %all-gather.7.cloned.1.call-done = bf16[1024,2048]{1,0:T(8,128)(2,1)} async-done(((bf16[256,2048]{1,0:T(8,128)(2,1)}), bf16[1024,2048]{1,0:T(8,128)(2,1)}) %all-gather.7.cloned.1.call-update) | async-done | bytes 4194320 | tf_op jit(solution)/shard_map/all_gather | solution.py:1164
  177.5 80.8 %all-gather.9.cloned.1.call-done.we_ref = bf16[8192,256]{1,0:T(8,128)(2,1)} async-done(((bf16[2048,256]{1,0:T(8,128)(2,1)}), bf16[8192,256]{1,0:T(8,128)(2,1)}) %all-gather.9.cloned.1.call-update) | async-done | bytes 4194320 | tf_op jit(solution)/shard_map/all_gather | solution.py:1166
  258.4 1.5 fusion.69
  260.7 2.8 convert_reduce_fusion.3
  263.7 3.8 fusion.11
  270.5 8.2 all_gather.22
  279.4 11.1 add_convert_fusion.4.q_ref.k_ref.v_ref
  290.6 14.2 attend.2
  305.8 5.9 convolution_convert_fusion.1.refs_0_
  311.7 96.2 %line_sums.3 = f32[256,2048]{1,0:T(8,128)} custom-call(bf16[1024,2048]{1,0:T(8,128)(2,1)} %convolution_convert_fusion.1.refs_0_), custom_call_target="tpu_custom_call" | custom-call | flops 80000000000 | bytes 10000000 | tf_op jit(solution)/shard_map/line_sums/pallas_call | solution.py:589
  408.0 3.0 convert_reduce_fusion.2
  411.4 1.2 fusion.10
  412.7 9.8 add_convert_fusion.3.q_ref.k_ref.v_ref
  422.6 14.2 attend.3
  437.8 5.9 convolution_convert_fusion.refs_0_
  443.8 69.5 %line_sums.4 = f32[256,2048]{1,0:T(8,128)} custom-call(bf16[1024,2048]{1,0:T(8,128)(2,1)} %convolution_convert_fusion.refs_0_), custom_call_target="tpu_custom_call" | custom-call | flops 80000000000 | bytes 10000000 | tf_op jit(solution)/shard_map/line_sums/pallas_call | solution.py:589
  513.2 3.1 convert_reduce_fusion.9
  519.0 2.1 add_convert_fusion.11
  521.2 152.1 %ffn_plane.2 = (f32[256,4096]{1,0:T(8,128)}, bf16[2048,2048]{1,0:T(8,128)(2,1)}, bf16[2048,1024]{1,0:T(8,128)(2,1)}, bf16[2048,1024]{1,0:T(8,128)(2,1)}) custom-call(bf16[256,2048]{1,0:T(8,128)(2,1)} %get-tuple-element.205.n2_ref, bf16[2048,2048]{1,0:T(8,128)(2,1)} %bitcast.217, bf16[8192,256]{1,0:T(8,128)(2,1)} %all-gather.9.cloned.1.call-done.we_ref, ...), custom_call_target="tpu_custom_call" | custom-call | flops 154618822656 | bytes 50331648 | tf_op jit(solution)/shard_map/ffn_plane/pallas_call | solution.py:1060
  673.4 3.7 multiply_reduce_fusion.1
  677.2 4.1 fusion.65
  681.3 2.1 convert_reduce_fusion.13
  685.2 1.3 convert_reduce_fusion.5
  686.5 11.6 fusion.73
  698.1 11.7 fusion.53
  709.8 126.1 %ffn_plane.3 = (f32[256,4096]{1,0:T(8,128)}, bf16[2048,2048]{1,0:T(8,128)(2,1)}, bf16[2048,1024]{1,0:T(8,128)(2,1)}, bf16[2048,1024]{1,0:T(8,128)(2,1)}, bf16[1024,2048]{1,0:T(8,128)(2,1)}) custom-call(bf16[256,2048]{1,0:T(8,128)(2,1)} %get-tuple-element.206.n2_ref, bf16[2048,2048]{1,0:T(8,128)(2,1)} %all-gather.13.cloned.1.call-done.dy_ref, ...), custom_call_target="tpu_custom_call" | custom-call | flops 154618822656 | bytes 50331648 | tf_op jit(solution)/shard_map/ffn_plane/pallas_call | solution.py:1060
  835.9 15.5 %add_convert_fusion.2 = bf16[1024,2048]{1,0:T(8,128)(2,1)} fusion(f32[1024,2048]{1,0:T(8,128)} %fusion.53, bf16[2048,1024]{1,0:T(8,128)(2,1)} %get-tuple-element.56, bf16[2048,2048]{1,0:T(8,128)(2,1)} %all-gather.13.cloned.1.call-done.dy_ref), kind=kOutput, calls=%fused_computation.27 | convolution fusion | flops 8594128896 | bytes 25165824 | tf_op jit(solution)/shard_map/dot_general | solution.py:32
  851.6 1.5 copy-done.15
  853.0 2.6 multiply_reduce_fusion
  855.7 1.8 fusion.64
  858.3 4.1 convolution_convert_fusion.3.g_ref
  863.0 139.3 %attend_back.2 = (bf16[1024,1536]{1,0:T(8,128)(2,1)S(1)}, bf16[1024,2048]{1,0:T(8,128)(2,1)}) custom-call(s32[4]{0:T(128)S(1)} %copy-done.5, bf16[1024,1536]{1,0:T(8,128)(2,1)} %copy-done.11, bf16[1024,1536]{1,0:T(8,128)(2,1)} %copy-done.11, bf16[1024,1536]{1,0:T(8,128)(2,1)} %copy-done.11, bf16[1024,512]{1,0:T(8,128)(2,1)S(1)} %convolution_convert_fusion.3.g_ref, ...), custom_call_target="tpu_custom_call" | custom-call | flops 40265318400 | bytes 7340032 | tf_op jit(solution)/shard_map/attend_back/pallas_call | solution.py:784
  1003.0 11.4 convert_reduce_fusion.1
  1015.9 6.3 convolution_convert_fusion.2.g_ref
  1022.2 15.0 add_convert_fusion.1
  1037.1 1.2 copy-done.9
  1038.4 33.9 %attend_back.3 = bf16[1024,1536]{1,0:T(8,128)(2,1)S(1)} custom-call(s32[4]{0:T(128)S(1)} %copy-done.3, bf16[1024,1536]{1,0:T(8,128)(2,1)} %copy-done.10, bf16[1024,1536]{1,0:T(8,128)(2,1)} %copy-done.10, bf16[1024,1536]{1,0:T(8,128)(2,1)} %copy-done.10, bf16[1024,512]{1,0:T(8,128)(2,1)S(1)} %copy-done.9), custom_call_target="tpu_custom_call" | custom-call | flops 40265318400 | bytes 7340032 | tf_op jit(solution)/shard_map/attend_back/pallas_call | solution.py:784
  1072.3 1.6 copy-done
  1075.9 12.3 convert_reduce_fusion
  1088.3 5.1 fusion.74
  1093.4 3.9 add_convert_fusion.5
  1097.3 11.6 fusion.59
  1108.9 12.9 add_convert_fusion
  1121.8 7.4 pad_maximum_fusion.refs_2_
  1129.3 206.8 %line_sums.5 = (f32[256,2048]{1,0:T(8,128)}, f32[256,2048]{1,0:T(8,128)}, f32[256,2048]{1,0:T(8,128)}) custom-call(bf16[1024,2048]{1,0:T(8,128)(2,1)} %get-tuple-element.215.refs_0_, bf16[1024,2048]{1,0:T(8,128)(2,1)} %get-tuple-element.216.refs_1_, bf16[2048,2048]{1,0:T(8,128)(2,1)} %pad_maximum_fusion.refs_2_), custom_call_target="tpu_custom_call" | custom-call | flops 80000000000 | bytes 10000000 | tf_op jit(solution)/shard_map/line_sums/pallas_call | solution.py:589
  1336.1 3.5 fusion.36
  1339.7 1.5 fusion.55
  1341.2 1.5 maximum_bitcast_fusion
  1343.5 1.2 slice_bitcast_fusion.3
  1345.4 3.1 pad_maximum_fusion.1
  1348.5 6.2 copy.82
  1354.6 4.7 all-to-all-start
  1359.4 5.1 fusion.45
  1364.5 1.5 maximum_bitcast_fusion.1
  1367.0 102.0 %all-reduce.3.cloned.1.call-done = f32[24576]{0:T(1024)} async-done(((f32[24576]{0:T(1024)}), f32[24576]{0:T(1024)}) %all-reduce.3.cloned.1.call-update) | async-done | bytes 98320 | tf_op jit(solution)/shard_map/psum | solution.py:1244
  1474.2 3.0 convert_bitcast_fusion
  1477.2 5.4 fusion.68
  1482.6 6.0 copy.85
  1488.6 1.2 copy.83
  1489.8 2.2 copy.102
  (295 shorter events, 29.4 us)
Async XLA Ops:
  7.2 11.4 copy-start.40
  7.2 11.4 copy-start.41
  7.2 11.4 copy-start.42
  7.2 170.2 %all-gather.7.cloned.1.call-start = ((), (), s32[]{:S(2)}) async-start(), calls=%async_computation.3 | async-start | bytes 5242880 | tf_op jit(solution)/shard_map/all_gather | solution.py:1164
  98.9 159.4 %copy-start.18 = (bf16[2,1,256,2048]{3,2,1,0:T(8,128)(2,1)S(1)}, bf16[2,1,256,2048]{3,2,1,0:T(8,128)(2,1)}, u32[]{:S(2)}) copy-start(bf16[2,1,256,2048]{3,2,1,0:T(8,128)(2,1)} %param.20) | copy-start | bytes 6291460
  99.0 159.3 %all-gather.9.cloned.1.call-start = ((), (), s32[]{:S(2)}) async-start(), calls=%async_computation.4 | async-start | bytes 5242880 | tf_op jit(solution)/shard_map/all_gather | solution.py:1166
  177.4 343.7 %all-gather.11.cloned.1.call-start = ((), (), s32[]{:S(2)}) async-start(), calls=%async_computation.5 | async-start | bytes 5242880 | tf_op jit(solution)/shard_map/all_gather | solution.py:1167
  258.3 262.9 %all-gather.15.cloned.1.call-start = ((), (), s32[]{:S(2)}) async-start(), calls=%async_computation.10 | async-start | bytes 9437184 | tf_op jit(solution)/shard_map/all_gather | solution.py:1161
  259.8 3.7 copy-start.56
  259.8 3.8 copy-start.87
  259.9 449.9 %all-gather.13.cloned.1.call-start = ((), (), s32[]{:S(2)}) async-start(), calls=%async_computation.6 | async-start | bytes 9437184 | tf_op jit(solution)/shard_map/all_gather | solution.py:1169
  263.6 26.9 %copy-start.4 = (s32[4]{0:T(128)}, s32[4]{0:T(128)S(1)}, u32[]{:S(2)}) copy-start(s32[4]{0:T(128)S(1)} %get-tuple-element.213.parents_ref) | copy-start | bytes 52
  263.6 158.9 %copy-start.2 = (s32[4]{0:T(128)}, s32[4]{0:T(128)S(1)}, u32[]{:S(2)}) copy-start(s32[4]{0:T(128)S(1)} %get-tuple-element.214.parents_ref) | copy-start | bytes 52
  263.7 26.9 %copy-start.65 = (f32[1024]{0:T(1024)}, f32[1024]{0:T(1024)S(1)}, u32[]{:S(2)}) copy-start(f32[1024]{0:T(1024)S(1)} %broadcast_multiply_fusion.1) | copy-start | bytes 12292
  267.4 23.1 %copy-start.83 = (f32[1024]{0:T(1024)}, f32[1024]{0:T(1024)S(1)}, u32[]{:S(2)}) copy-start(f32[1024]{0:T(1024)S(1)} %add_rsqrt_fusion.1) | copy-start | bytes 12292
  269.9 142.8 %copy-start.81 = (f32[1,2,8,128]{3,1,2,0:T(2,128)}, f32[1,2,8,128]{3,1,2,0:T(2,128)S(1)}, u32[]{:S(2)}) copy-start(f32[1,2,8,128]{3,1,2,0:T(2,128)S(1)} %copy.94) | copy-start | bytes 24580
  269.9 142.8 %copy-start.43 = (f32[1,2,8,128]{3,1,2,0:T(2,128)}, f32[1,2,8,128]{3,1,2,0:T(2,128)S(1)}, u32[]{:S(2)}) copy-start(f32[1,2,8,128]{3,1,2,0:T(2,128)S(1)} %copy.93) | copy-start | bytes 24580
  290.5 14.2 copy-start.11
  411.4 11.1 copy-start.67
  412.7 9.9 copy-start.85
  422.6 14.2 copy-start.10
  443.8 69.5 %copy-start.12 = (bf16[2,1,256,2048]{3,2,1,0:T(8,128)(2,1)S(1)}, bf16[2,1,256,2048]{3,2,1,0:T(8,128)(2,1)}, u32[]{:S(2)}) copy-start(bf16[2,1,256,2048]{3,2,1,0:T(8,128)(2,1)} %param.18) | copy-start | bytes 6291460
  443.8 69.5 %copy-start.57 = (f32[1,2,8,128]{3,1,2,0:T(2,128)S(1)}, f32[1,2,8,128]{3,1,2,0:T(2,128)}, u32[]{:S(2)}) copy-start(f32[1,2,8,128]{3,1,2,0:T(2,128)} %copy.95) | copy-start | bytes 24580
  521.1 608.1 %reduce-scatter.3.cloned.1.call-start = ((), (), s32[]{:S(2)}) async-start(), calls=%async_computation.8 | async-start | bytes 5242880 | tf_op jit(solution)/shard_map/reduce_scatter | solution.py:1213
  521.2 152.2 %copy-start.38 = (f32[1,2,8,128]{3,1,2,0:T(2,128)S(1)}, f32[1,2,8,128]{3,1,2,0:T(2,128)}, u32[]{:S(2)}) copy-start(f32[1,2,8,128]{3,1,2,0:T(2,128)} %copy.96) | copy-start | bytes 24580
  521.2 152.2 %copy-start.61 = (f32[256]{0:T(256)S(1)}, f32[256]{0:T(256)}, u32[]{:S(2)}) copy-start(f32[256]{0:T(256)} %copy-done.60) | copy-start | bytes 3076
  521.2 152.2 %copy-start.72 = (f32[256]{0:T(256)S(1)}, f32[256]{0:T(256)}, u32[]{:S(2)}) copy-start(f32[256]{0:T(256)} %copy-done.71) | copy-start | bytes 3076
  673.4 3.7 copy-start.76
  673.4 3.7 copy-start.17
  673.4 3.7 copy-start.46
  677.1 4.1 copy-start.19
  677.2 9.3 copy-start.90
  681.3 5.2 copy-start.24
  681.3 3.9 copy-start.32
  685.2 13.0 slice-start
  686.5 11.7 slice-start.1
  686.5 11.7 copy-start.91
  851.5 4.2 copy-start.74
  851.5 4.2 copy-start.47
  851.5 493.9 %reduce-scatter.5.cloned.1.call-start = ((), (), s32[]{:S(2)}) async-start(), calls=%async_computation.9 | async-start | bytes 5242880 | tf_op jit(solution)/shard_map/reduce_scatter | solution.py:1225
  851.6 4.1 copy-start.29
  857.5 4.9 copy-start.23
  857.5 4.9 copy-start.77
  858.3 4.1 copy-start.20
  863.0 139.8 %copy-start.25 = (bf16[1024,2048]{1,0:T(8,128)(2,1)S(1)}, bf16[1024,2048]{1,0:T(8,128)(2,1)}, u32[]{:S(2)}) copy-start(bf16[1024,2048]{1,0:T(8,128)(2,1)} %get-tuple-element.43) | copy-start | bytes 12582916
  1003.0 11.4 copy-start.30
  1015.9 6.3 copy-start.31
  1022.2 15.0 copy-start.3
  1075.9 12.3 copy-start.53
  1088.3 5.1 copy-start.8
  1088.3 5.1 copy-start.89
  1093.4 3.9 copy-start.26
  1093.4 3.9 copy-start.44
  1093.4 3.9 copy-start.82
  1097.3 11.6 copy-start.1
  1097.3 11.6 copy-start.28
  1108.9 12.9 copy-start.36
  1129.2 339.7 %all-reduce.3.cloned.1.call-start = ((), (), s32[]{:S(2)}) async-start(), calls=%async_computation.7 | async-start | bytes 196608 | tf_op jit(solution)/shard_map/psum | solution.py:1244
  1129.3 206.8 %copy-start.13 = (bf16[2,1,256,2048]{3,2,1,0:T(8,128)(2,1)S(1)}, bf16[2,1,256,2048]{3,2,1,0:T(8,128)(2,1)}, u32[]{:S(2)}) copy-start(bf16[2,1,256,2048]{3,2,1,0:T(8,128)(2,1)} %param.18) | copy-start | bytes 6291460
  1129.3 206.8 %copy-start.62 = (f32[256]{0:T(256)S(1)}, f32[256]{0:T(256)}, u32[]{:S(2)}) copy-start(f32[256]{0:T(256)} %get-tuple-element.217) | copy-start | bytes 3076
  1129.3 206.8 %copy-start.63 = (f32[256]{0:T(256)S(1)}, f32[256]{0:T(256)}, u32[]{:S(2)}) copy-start(f32[256]{0:T(256)} %get-tuple-element.218) | copy-start | bytes 3076
  1354.6 4.7 copy-start.78
  1354.6 4.8 copy-start.80
  1354.6 119.6 %all-to-all-start = ((bf16[2,256,2048]{1,0,2:T(2,128)(2,1)}), bf16[2,256,2048]{1,0,2:T(2,128)(2,1)}, u32[]{:S(2)}, u32[]{:S(2)}) async-start(bf16[2,256,2048]{1,0,2:T(2,128)(2,1)} %copy.82), calls=%async_computation.2 | async-start | bytes 4194304 | tf_op jit(solution)/shard_map/all_to_all | solution.py:1260
  (39 other events, 71.3 us)
Sparse Core Ops, SparseCore 0:
  99.1 78.2 all-gather.6
  179.0 79.2 all-gather.8
  259.9 97.8 all-gather.10
  359.5 58.5 all-gather.14
  521.2 79.5 all-gather.12
  851.6 110.4 reduce-scatter.2
  1129.4 141.0 reduce-scatter.4
  1345.5 123.3 all-reduce.2

commit v3 on v2

--- a/solution.py
+++ b/solution.py
@@ -540,54 +540,127 @@
     return seq, w_all, e_all, r_all, small_all
 
 
-def sum_kernel(lines, *refs):
+class SmallSum:
+    def __init__(self, line, cube, parts, out, scratch):
+        self.line, self.cube, self.parts, self.out = line, cube, parts, out
+        self.come, self.gather, self.sems, self.line_send, self.line_recv = (
+            scratch[0], scratch[1], scratch[2:5], scratch[5], scratch[6]
+        )
+        moves = [(lambda d: parts.at[d], lambda d: self.come.at[d])]
+        self.swap = CubeExchange(cube, moves, self.sems)
+
+    @staticmethod
+    def scratch(dp, n, rows, d):
+        return [
+            pltpu.VMEM((dp, rows, d), F32),
+            pltpu.VMEM((n, rows, d), F32),
+            *CubeExchange.sems(dp, 1),
+            DMA((n,)), DMA((n,)),
+        ]
+
+    def hop(self, k):
+        line = self.line
+        here = self.gather.at[line.me]
+        return remote(
+            here, here, self.line_send.at[k], self.line_recv.at[k], line.at((line.me + k) % line.n)
+        )
+
+    def middle(self):
+        self.swap.finish()
+        total = self.come[0]
+        for d in range(1, self.cube.dp):
+            total = total + self.come[d]
+        self.gather[self.line.me] = total
+        for k in range(1, self.line.n):
+            self.hop(k).start()
+
+    def finish(self):
+        line = self.line
+        for k in range(1, line.n):
+            here = self.gather.at[(line.me - k + line.n) % line.n]
+            remote(
+                here, here, self.line_send.at[k], self.line_recv.at[k], line.at(line.me)
+            ).wait_recv()
+            self.hop(k).wait_send()
+        total = self.gather[0]
+        for z in range(1, line.n):
+            total = total + self.gather[z]
+        self.out[...] = total
+
+
+def sum_kernel(lines, planes, small, *refs):
     line, cube = Line(), Cube()
-    total = len([r for r in refs if r is not None])
-    extra = 1 if total - 2 * lines - 7 * lines > 0 else 0
-    ins, outs = refs[: lines + extra], refs[lines + extra : 2 * (lines + extra)]
-    scratch = refs[2 * (lines + extra) :]
-    sums = [
-        LineScatter(line, ins[i], outs[i], scratch[7 * i : 7 * i + 7]) for i in range(lines)
-    ]
-    plane = CubeScatter(cube, ins[lines], outs[lines], scratch[7 * lines :]) if extra else None
+    count = lines + planes + small
+    ins, outs, scratch = refs[:count], refs[count : 2 * count], refs[2 * count :]
+    sums, folds = [], []
+    for i in range(lines):
+        sums.append(LineScatter(line, ins[i], outs[i], scratch[:7]))
+        scratch = scratch[7:]
+    for i in range(lines, lines + planes):
+        folds.append(CubeScatter(cube, ins[i], outs[i], scratch[:8]))
+        scratch = scratch[8:]
+    barrier = pltpu.get_barrier_semaphore()
+    if small:
+        for k in range(1, line.n):
+            pl.semaphore_signal(
+                barrier, inc=1, device_id=line.at((line.me + k) % line.n), device_id_type=MESH
+            )
+        for k in range(1, cube.dp):
+            pl.semaphore_signal(
+                barrier, inc=1, device_id=cube.at((cube.me + k) % cube.dp), device_id_type=MESH
+            )
+    else:
+        line.greet(barrier)
+        if planes:
+            cube.greet(barrier)
     for s in sums:
         s.prepare()
-    barrier = pltpu.get_barrier_semaphore()
-    line.greet(barrier)
-    if extra:
-        cube.greet(barrier)
-    pl.semaphore_wait(barrier, line.peers() + (cube.peers() if extra else 0))
-    if extra:
-        plane.start()
-    pieces = [p for p in plane.order() if p] if extra else []
+    if small:
+        pl.semaphore_wait(barrier, line.n - 1 + cube.dp - 1)
+        little = SmallSum(line, cube, ins[-1], outs[-1], scratch)
+        little.swap.start()
+    else:
+        pl.semaphore_wait(barrier, line.peers() + (cube.peers() if planes else 0))
+    pieces = [p for p in folds[0].order() if p] if planes else []
     per = -(-len(pieces) // (line.n - 1))
     for step in range(1, line.n):
         for s in sums:
             s.step(step)
+        if step == 1:
+            for f in folds:
+                f.start()
+            if small:
+                little.middle()
         for piece in pieces[:per]:
-            plane.fold(piece)
+            for f in folds:
+                f.fold(piece)
         pieces = pieces[per:]
-    if extra:
-        plane.finish()
+    for f in folds:
+        f.finish()
     for s in sums:
         s.finish()
-
-
-def line_sums(parts, plane_parts, collective_id):
+    if small:
+        little.finish()
+
+
+def all_sums(line_parts, plane_parts, small_parts, collective_id):
     dp, n = lax.axis_size("dp"), lax.axis_size("tensor")
-    rows, d = parts[0].shape[0] // n, parts[0].shape[1]
-    out_shape = [jax.ShapeDtypeStruct((rows, d), F32) for _ in parts]
-    scratch = []
-    for _ in parts:
+    out_shape, scratch = [], []
+    for part in line_parts:
+        rows, d = part.shape[0] // n, part.shape[1]
+        out_shape.append(jax.ShapeDtypeStruct((rows, d), F32))
         scratch += LineScatter.scratch(n, rows, d)
-    operands = list(parts)
-    if plane_parts is not None:
-        rows_p, d_p = plane_parts.shape[0] // dp, plane_parts.shape[1]
-        out_shape.append(jax.ShapeDtypeStruct((rows_p, d_p), F32))
-        scratch += CubeScatter.scratch(dp // 2, rows_p, d_p)
-        operands.append(plane_parts)
+    for part in plane_parts:
+        rows, d = part.shape[0] // dp, part.shape[1]
+        out_shape.append(jax.ShapeDtypeStruct((rows, d), F32))
+        scratch += CubeScatter.scratch(dp // 2, rows, d)
+    for part in small_parts:
+        rows, d = part.shape[1:]
+        out_shape.append(jax.ShapeDtypeStruct((rows, d), F32))
+        scratch += SmallSum.scratch(dp, n, rows, d)
+    operands = list(line_parts) + list(plane_parts) + list(small_parts)
     return pl.pallas_call(
-        functools.partial(sum_kernel, len(parts)),
+        functools.partial(sum_kernel, len(line_parts), len(plane_parts), len(small_parts)),
         out_shape=tuple(out_shape),
         in_specs=[ANY] * len(operands),
         out_specs=(VMEM,) * len(operands),
@@ -596,7 +669,7 @@
             collective_id=collective_id, has_side_effects=True, vmem_limit_bytes=60 << 20
         ),
         cost_estimate=pl.CostEstimate(flops=80 * 10**9, bytes_accessed=10**7, transcendentals=0),
-        name="line_sums",
+        name="sums",
     )(*operands)
 
 
@@ -814,11 +887,12 @@
 def ffn_kernel(host, n2_ref, dy_ref, we_ref, wr_ref, be_ref, *refs):
     if host:
         line_own, refs = refs[0], refs[1:]
-    sum_ref, seq_ref, act_ref, dpre_ref = refs[:4]
-    refs = refs[4:]
+    sum_ref, seq_ref, act_ref, dpre_ref, part_ref = refs[:5]
+    refs = refs[5:]
     if host:
         line_full, refs = refs[0], refs[1:]
-    we, wr, seq, dy_st, act_st, dpre_st, keep, give, core_in, fold_in = refs[:10]
+    we, wr, seq, dy_st, act_st, dpre_st, part_st, keep, give, core_in, fold_in = refs[:11]
+    refs = refs[1:]
     w_sem, own_sem, dy_sem, seq_sem, st_sem = refs[10:15]
     ag_send, ag_recv, agc_send, agc_recv, rsc_send, rsc_recv, fold_send, fold_recv = refs[15:23]
     cube = Cube()
@@ -987,13 +1061,11 @@
         @pl.loop(0, model // wide)
         def _(i):
             cols = pl.ds(pl.multiple_of(i * wide, wide), wide)
-            cols_out = pl.ds(pl.multiple_of(model + i * wide, wide), wide)
             d_two = over(dpre_st[slot], we[cols, :], 1, 1).astype(BF16)
             keep[piece, :, cols] = d_two[:rows]
             give[slot, :, cols] = d_two[rows:]
             out = over(act_st[slot], wr[:, cols], 1, 0).astype(BF16)
-            keep[piece, :, cols_out] = out[:rows]
-            give[slot, :, cols_out] = out[rows:]
+            part_st[slot, :, cols] = out
 
         if host and turn < line.n - 1:
             gather.take(turn + 1)
@@ -1011,6 +1083,9 @@
                 pltpu.make_async_copy(dpre_st.at[slot, part], dpre_ref.at[to], st_sem.at[1, slot, half])
             )
             stores[turn].append(
+                pltpu.make_async_copy(part_st.at[slot, part], part_ref.at[to], st_sem.at[2, slot, half])
+            )
+            stores[turn].append(
                 pltpu.make_async_copy(seq.at[piece, part], seq_ref.at[to], seq_sem.at[piece, half])
             )
         for c in stores[turn]:
@@ -1060,14 +1135,15 @@
     return pl.pallas_call(
         functools.partial(ffn_kernel, host),
         out_shape=(
-            jax.ShapeDtypeStruct((rows, 2 * model), F32),
+            jax.ShapeDtypeStruct((rows, model), F32),
             jax.ShapeDtypeStruct((dp * rows, model), BF16),
             jax.ShapeDtypeStruct((dp * rows, units), BF16),
             jax.ShapeDtypeStruct((dp * rows, units), BF16),
+            jax.ShapeDtypeStruct((dp * rows, model), BF16),
             *lines,
         ),
         in_specs=[anywhere, anywhere, anywhere, anywhere, vmem] + [anywhere] * host,
-        out_specs=(vmem, anywhere, anywhere, anywhere) + (anywhere,) * host,
+        out_specs=(vmem, anywhere, anywhere, anywhere, anywhere) + (anywhere,) * host,
         scratch_shapes=[
             pltpu.VMEM((model, units), BF16),
             pltpu.VMEM((units, model), BF16),
@@ -1075,11 +1151,12 @@
             pltpu.VMEM((2, 2 * rows, model), BF16),
             pltpu.VMEM((2, 2 * rows, units), BF16),
             pltpu.VMEM((2, 2 * rows, units), BF16),
-            pltpu.VMEM((count, rows, 2 * model), BF16),
-            pltpu.VMEM((2, rows, 2 * model), BF16),
-            pltpu.VMEM((count, rows, 2 * model), BF16),
-            pltpu.VMEM((count - 1, rows, 2 * model), BF16),
-            dma((n + 1,)), dma, dma((2, 2)), dma((count, 2)), dma((2, 2, 2)),
+            pltpu.VMEM((2, 2 * rows, model), BF16),
+            pltpu.VMEM((count, rows, model), BF16),
+            pltpu.VMEM((2, rows, model), BF16),
+            pltpu.VMEM((count, rows, model), BF16),
+            pltpu.VMEM((count - 1, rows, model), BF16),
+            dma((n + 1,)), dma, dma((2, 2)), dma((count, 2)), dma((3, 2, 2)),
             dma((count,)), dma((count,)), dma((count,)), dma((count,)),
             dma((count,)), dma((count,)), dma((count - 1,)), dma((count - 1,)),
         ]
@@ -1161,12 +1238,7 @@
     seq_grad = [lax.all_gather(dy_low[0], "dp", axis=0, tiled=True)]
     seq_x = [seq_x0]
     for m in micros[1:]:
-        seq_x.append(lax.all_gather(after(x_low[m], seq_x[-1]), "tensor", axis=0, tiled=True))
-    side = 0 if mine % 128 == 0 else 1
-    w_e = lax.all_gather(after(w_e, seq_x[-1]), "tensor", axis=side, tiled=True)
-    w_r = lax.all_gather(after(w_r, w_e), "tensor", axis=0, tiled=True)
-    for m in micros[1:]:
-        seq_grad.append(lax.all_gather(after(dy_low[m], w_r), "dp", axis=0, tiled=True))
+        seq_x.append(lax.all_gather(after(x_low[m], seq_x0, seq_grad[0]), "tensor", axis=0, tiled=True))
 
     normal_one, seq_one, qkv, attended, hidden, normed_two = [], [], [], [], [], []
     for m in micros:
@@ -1176,21 +1248,26 @@
             (jnp.dot(seq_one[m], w_qkv, preferred_element_type=F32) + bias_qkv).astype(BF16)
         )
         attended.append(attend(parents[m, 0], qkv[m], width))
-        branch = line_sums([over(attended[m], w_ot, 1, 1).astype(BF16)], None, 3)[0]
+        if m == 0:
+            side = 0 if mine % 128 == 0 else 1
+            w_e = lax.all_gather(after(w_e, qkv[m]), "tensor", axis=side, tiled=True)
+            w_r = lax.all_gather(after(w_r, attended[m]), "tensor", axis=0, tiled=True)
+        else:
+            seq_grad.append(lax.all_gather(after(dy_low[m], attended[m]), "dp", axis=0, tiled=True))
+        branch = all_sums([over(attended[m], w_ot, 1, 1).astype(BF16)], [], [], 3)[0]
         hidden.append(x_low[m].astype(F32) + (branch + bias_out))
         normed_two.append(layer_norm(hidden[m], gain_two, shift_two).astype(BF16))
 
-    layer_out, seq_two, activated, d_pre, d_hidden, d_branch, seq_branch = [], [], [], [], [], [], []
+    out_part, seq_two, activated, d_pre, d_hidden, d_branch, seq_branch = [], [], [], [], [], [], []
     g_gain_two = g_shift_two = g_bias_red = g_bias_out = g_bias_e = 0.0
     for m in micros:
         own = d_branch[m - 1] if m else None
-        sums, seq, act, dpre, *line = ffn(normed_two[m], seq_grad[m], w_e, w_r, bias_e, own)
+        d_two, seq, act, dpre, part, *line = ffn(normed_two[m], seq_grad[m], w_e, w_r, bias_e, own)
         seq_branch += line
         seq_two.append(seq)
         activated.append(act)
         d_pre.append(dpre)
-        d_two = sums[:, :model]
-        layer_out.append((hidden[m] + (sums[:, model:] + bias_red)).astype(BF16))
+        out_part.append(part)
         grad32 = dy_low[m].astype(F32)
         norm_value, norm_pull = jax.vjp(layer_norm, hidden[m], gain_two, shift_two)
         d_norm, g_gain, g_shift = norm_pull(d_two)
@@ -1222,7 +1299,7 @@
             seq_branch.append(full)
         else:
             g_et = outer(d_pre, seq_two)
-            g_et_sum = lax.psum_scatter(after(g_et, g_r_sum), "tensor", scatter_dimension=0, tiled=True)
+            g_et_sum = lax.psum_scatter(g_et, "tensor", scatter_dimension=0, tiled=True)
             d_att = after(d_att, g_et)
             d = attend_back(parents[m, 0], qkv[m], d_att, width)
         d_qkv.append(d)
@@ -1234,27 +1311,19 @@
 
     rows = jnp.concatenate(
         [g_gain_one, g_shift_one, g_bias_out, g_gain_two, g_shift_two, g_bias_red], 0
-    ).reshape(-1)
-    place = jnp.zeros((tn, width), F32)
-    row_q = lax.dynamic_update_slice(place, g_bias_qkv[None, :width], (tn_me, 0)).reshape(-1)
-    row_v = lax.dynamic_update_slice(place, g_bias_qkv[None, 2 * width :], (tn_me, 0)).reshape(-1)
+    )
+    rows = rows.reshape(6, dp, cut).transpose(1, 0, 2).reshape(dp, 6 * cut)
+    row_qv = jnp.concatenate([g_bias_qkv[:width], g_bias_qkv[2 * width :]])
+    row_qv = row_qv.reshape(2 * bq_rows, dp, bq_cols).transpose(1, 0, 2)[:, None]
+    row_qv = lax.dynamic_update_slice(
+        jnp.zeros((dp, tn, 2 * bq_rows, bq_cols), F32), row_qv, (0, tn_me, 0, 0)
+    ).reshape(dp, -1)
+    row_e = g_bias_e.reshape(tn, be_rows // dp, dp, be_cols).transpose(2, 0, 1, 3)[:, :, None]
     row_e = lax.dynamic_update_slice(
-        jnp.zeros((tn, dp, mine), F32), g_bias_e.reshape(tn, 1, mine), (0, dp_me, 0)
-    ).reshape(-1)
-    sums = lax.psum(jnp.concatenate([rows, row_q, row_v, row_e]), ("dp", "tensor"))
-    n_rows = 6 * model
-    six = lax.dynamic_slice_in_dim(sums[:n_rows].reshape(6, model), dp_me * cut, cut, 1)
-
-    def block(flat, row_count):
-        table = flat.reshape(tn, row_count, HEAD_DIM)
-        cols = HEAD_DIM // dp
-        table = lax.dynamic_slice(table, (tn_me, 0, dp_me * cols), (1, row_count, cols))
-        return table[0]
-
-    heads_all = tn * width
-    g_bq = block(sums[n_rows : n_rows + heads_all], bq_rows)
-    g_bv = block(sums[n_rows + heads_all : n_rows + 2 * heads_all], bq_rows)
-    g_be = block(sums[n_rows + 2 * heads_all :], be_rows)
+        jnp.zeros((dp, tn, dp, be_rows // dp, be_cols), F32), row_e, (0, 0, dp_me, 0, 0)
+    ).reshape(dp, -1)
+    little = jnp.concatenate([rows, row_qv, row_e], 1)
+    little = jnp.pad(little, ((0, 0), (0, -little.shape[1] % 1024))).reshape(dp, -1, 128)
 
     g_ffn = jnp.stack([g_et_sum, g_r_sum], 0)
     g_ffn = lax.all_to_all(g_ffn, "dp", split_axis=2, concat_axis=1, tiled=True).astype(F32)
@@ -1262,7 +1331,23 @@
     g_reduce = g_ffn[1]
 
     g_attn = jnp.concatenate([outer(seq_one, d_qkv), outer(seq_branch, attended)], axis=1)
-    *d_one, g_attn = line_sums(d_one, g_attn, 5)
+    out_sum = [
+        lax.psum_scatter(after(part, d_qkv[last]), "dp", scatter_dimension=0, tiled=True).astype(F32)
+        for part in out_part[:last]
+    ]
+    sums = all_sums(d_one, [g_attn, out_part[last]], [little], 5)
+    d_one, (g_attn, out_last, little) = sums[: last + 1], sums[last + 1 :]
+    out_sum.append(out_last)
+    layer_out = [(hidden[m] + (out_sum[m] + bias_red)).astype(BF16) for m in micros]
+    little = little.reshape(-1)
+    six = little[: 6 * cut].reshape(6, cut)
+    at = 6 * cut
+    g_bqv = little[at : at + tn * 2 * bq_rows * bq_cols].reshape(tn, 2 * bq_rows, bq_cols)
+    g_bqv = lax.dynamic_index_in_dim(g_bqv, tn_me, 0, keepdims=False)
+    g_bq, g_bv = g_bqv[:bq_rows], g_bqv[bq_rows:]
+    at += tn * 2 * bq_rows * bq_cols
+    g_be = little[at : at + tn * be_rows * be_cols].reshape(tn, be_rows, be_cols)
+    g_be = lax.dynamic_index_in_dim(g_be, tn_me, 0, keepdims=False)
     g_query, g_key, g_value = [g_attn[:, i * width : (i + 1) * width] for i in range(3)]
     g_out = g_attn[:, 3 * width :].T
     input_grad = []

time: 1500 us -> 1280 us (0.85)
  waiting for transfers between devices: 261 us -> 19.1 us
    all_gather x4, waiting for transfers between devices: 159 us -> 0.06 us  [the longest x1 0.02 us: body(): lax.all_gather(after(x_low[m], seq_x0, seq_grad[0]), 'tensor', axis=0, ti...]
    psum x1 -> x0, waiting for transfers between devices: 102 us -> none  [body(): lax.psum(jnp.concatenate([rows, row_q, row_v, row_e]), ('dp', 'tensor'))]
    pallas_call x3, Pallas kernels: 372 us -> 418 us  [all_sums(): pl.pallas_call(functools.partial(sum_kernel, len(line_parts), len(plane_p...]
    pallas_call x2, Pallas kernels: 278 us -> 234 us  [ffn(): pl.pallas_call(functools.partial(ffn_kernel, host), out_shape=(jax.ShapeD...]
    all_to_all x1, waiting for transfers between devices: 0.01 us -> 18.9 us  [body(): lax.all_to_all(g_ffn, 'dp', split_axis=2, concat_axis=1, tiled=True)]
    pallas_call x1, Pallas kernels: 79.2 us -> 95.8 us  [front(): pl.pallas_call(front_kernel, out_shape=(jax.ShapeDtypeStruct((n * rows, m...]
  transfers between devices with their start and end apart: 9 -> 9, of which waited for: 3 -> 1; matrix products, arithmetic and copies ran while one was open for 15% -> 19% of each run, Pallas kernels for 48% -> 65%
where the time goes in v3:
time: 1280 us; the launch traced here: 1270 us
  Pallas kernels  936 us (73%)
  matrix products  160 us (12%)
  other arithmetic  68.1 us (5%)
  local copies, waits for them, and re-layouts  54.7 us (4%)
  waiting for transfers between devices  19.1 us (1%)
  between operations  16.1 us (1%)
    pallas_call x3, Pallas kernels, all_sums(): pl.pallas_call(functools.partial(sum_kernel, len(line_parts), len(plane_p...  418 us
    pallas_call x2, Pallas kernels, ffn(): pl.pallas_call(functools.partial(ffn_kernel, host), out_shape=(jax.ShapeD...  234 us
    pallas_call x2, Pallas kernels, attend_back(): pl.pallas_call(functools.partial(attend_back_kernel, host), out_shape=out...  160 us
    dot_general x12, matrix products, over(): lax.dot_general(left, right, (((on_left,), (on_right,)), ((), ())), prefe...  127 us
    pallas_call x1, Pallas kernels, front(): pl.pallas_call(front_kernel, out_shape=(jax.ShapeDtypeStruct((n * rows, m...  95.8 us
    pallas_call x2, Pallas kernels, attend(): pl.pallas_call(attend_kernel, out_shape=jax.ShapeDtypeStruct((rows, width...  28.4 us
  transfers between devices with their start and end apart: 9, of which 1 were waited for; matrix products, arithmetic and copies ran while one was open for 19% of the time, Pallas kernels for 65%

profile of v3, /device:TPU:0, one launch (start us, length us, event | category | flops | bytes accessed | tf_op | source)
XLA Modules:
  0.0 1270.4 jit_solution(16726102027809809099)
XLA Ops:
  7.4 3.3 slice_bitcast_fusion
  12.0 1.1 pad_maximum_fusion.2.w_ref
  13.1 1.5 slice_bitcast_fusion.1
  14.6 95.8 %front.1 = (bf16[1024,2048]{1,0:T(8,128)(2,1)}, bf16[2048,2048]{1,0:T(8,128)(2,1)}, bf16[2048,256]{1,0:T(8,128)(2,1)}, bf16[256,2048]{1,0:T(8,128)(2,1)}, bf16[128,128]{1,0:T(8,128)(2,1)}) custom-call(bf16[256,2048]{1,0:T(8,128)(2,1)} %get-tuple-element.193.x_ref, bf16[256,2048]{1,0:T(8,128)(2,1)} %pad_maximum_fusion.2.w_ref, bf16[256,2048]{1,0:T(8,128)(2,1)} %we_ref.1, ...), custom_call_target="tpu_custom_call" | custom-call | flops 80000000000 | bytes 10000000 | tf_op jit(solution)/shard_map/front/pallas_call | solution.py:521
  111.8 3.0 convert_reduce_fusion.3
  115.2 1.2 fusion.11
  116.5 11.1 add_convert_fusion.4.q_ref.k_ref.v_ref
  127.7 1.9 copy-done.13
  129.6 14.2 %attend.2 = bf16[1024,512]{1,0:T(8,128)(2,1)S(1)} custom-call(s32[4]{0:T(128)S(1)} %get-tuple-element.221.parents_ref, bf16[1024,1536]{1,0:T(8,128)(2,1)S(1)} %copy-done.13, bf16[1024,1536]{1,0:T(8,128)(2,1)S(1)} %copy-done.13, bf16[1024,1536]{1,0:T(8,128)(2,1)S(1)} %copy-done.13), custom_call_target="tpu_custom_call" | custom-call | flops 16106127360 | bytes 4194304 | tf_op jit(solution)/shard_map/attend/pallas_call | solution.py:743
  144.8 5.9 convolution_convert_fusion.1.refs_0_
  153.3 11.3 all_gather.21
  165.2 150.3 %sums.3 = f32[256,2048]{1,0:T(8,128)} custom-call(bf16[1024,2048]{1,0:T(8,128)(2,1)} %convolution_convert_fusion.1.refs_0_), custom_call_target="tpu_custom_call" | custom-call | flops 80000000000 | bytes 10000000 | tf_op jit(solution)/shard_map/sums/pallas_call | solution.py:662
  315.6 3.0 convert_reduce_fusion.2
  319.0 1.2 fusion.10
  320.3 9.8 add_convert_fusion.3.q_ref.k_ref.v_ref
  330.2 14.2 %attend.3 = bf16[1024,512]{1,0:T(8,128)(2,1)S(1)} custom-call(s32[4]{0:T(128)S(1)} %get-tuple-element.222.parents_ref, bf16[1024,1536]{1,0:T(8,128)(2,1)S(1)} %add_convert_fusion.3.q_ref.k_ref.v_ref, bf16[1024,1536]{1,0:T(8,128)(2,1)S(1)} %add_convert_fusion.3.q_ref.k_ref.v_ref, bf16[1024,1536]{1,0:T(8,128)(2,1)S(1)} %add_convert_fusion.3.q_ref.k_ref.v_ref), custom_call_target="tpu_custom_call" | custom-call | flops 16106127360 | bytes 4194304 | tf_op jit(solution)/shard_map/attend/pallas_call | solution.py:743
  344.4 6.3 convolution_convert_fusion.refs_0_
  350.6 123.9 %sums.4 = f32[256,2048]{1,0:T(8,128)} custom-call(bf16[1024,2048]{1,0:T(8,128)(2,1)} %convolution_convert_fusion.refs_0_), custom_call_target="tpu_custom_call" | custom-call | flops 80000000000 | bytes 10000000 | tf_op jit(solution)/shard_map/sums/pallas_call | solution.py:662
  474.6 4.4 convert_reduce_fusion.9
  481.2 3.7 add_convert_fusion.11
  484.9 120.2 %ffn_plane.2 = (f32[256,2048]{1,0:T(8,128)}, bf16[2048,2048]{1,0:T(8,128)(2,1)}, bf16[2048,1024]{1,0:T(8,128)(2,1)}, bf16[2048,1024]{1,0:T(8,128)(2,1)}, bf16[2048,2048]{1,0:T(8,128)(2,1)}) custom-call(bf16[256,2048]{1,0:T(8,128)(2,1)} %get-tuple-element.205.n2_ref, bf16[2048,2048]{1,0:T(8,128)(2,1)} %bitcast.206, ...), custom_call_target="tpu_custom_call" | custom-call | flops 154618822656 | bytes 50331648 | tf_op jit(solution)/shard_map/ffn_plane/pallas_call | solution.py:1135
  605.2 3.7 multiply_reduce_fusion.1
  610.5 2.1 convert_reduce_fusion.13
  613.9 3.6 convert_reduce_fusion.5
  617.5 14.0 %fusion.70 = f32[1024,2048]{1,0:T(8,128)} fusion(bf16[2048,1024]{1,0:T(8,128)(2,1)S(1)} %copy-done.37, bf16[2048,2048]{1,0:T(8,128)(2,1)} %get-tuple-element.65), kind=kOutput, calls=%fused_computation.174 | convolution fusion | flops 8589934592 | bytes 20971520 | tf_op jit(solution)/shard_map/dot_general | solution.py:32
  631.5 11.5 fusion.53
  643.0 113.6 %ffn_plane.3 = (f32[256,2048]{1,0:T(8,128)}, bf16[2048,2048]{1,0:T(8,128)(2,1)}, bf16[2048,1024]{1,0:T(8,128)(2,1)}, bf16[2048,1024]{1,0:T(8,128)(2,1)}, bf16[20...) custom-call(bf16[256,2048]{1,0:T(8,128)(2,1)} %get-tuple-element.206.n2_ref, ...), custom_call_target="tpu_custom_call" | custom-call | flops 154618822656 | bytes 50331648 | tf_op jit(solution)/shard_map/ffn_plane/pallas_call | solution.py:1135
  756.6 15.5 %add_convert_fusion.2 = bf16[1024,2048]{1,0:T(8,128)(2,1)} fusion(f32[1024,2048]{1,0:T(8,128)} %fusion.53, bf16[2048,1024]{1,0:T(8,128)(2,1)} %get-tuple-element.60, bf16[2048,2048]{1,0:T(8,128)(2,1)} %all-gather.13.cloned.1.call-done.dy_ref), kind=kOutput, calls=%fused_computation.27 | convolution fusion | flops 8594128896 | bytes 25165824 | tf_op jit(solution)/shard_map/dot_general | solution.py:32
  772.2 3.0 convert_reduce_fusion.4
  777.4 6.3 convolution_convert_fusion.3.g_ref
  785.3 1.4 convert_reduce_fusion.12
  786.7 1.2 copy-done.3
  788.0 1.2 copy-done.11
  789.2 125.5 %attend_back.2 = (bf16[1024,1536]{1,0:T(8,128)(2,1)S(1)}, bf16[1024,2048]{1,0:T(8,128)(2,1)}) custom-call(s32[4]{0:T(128)S(1)} %copy-done.7, bf16[1024,1536]{1,0:T(8,128)(2,1)} %add_convert_fusion.4.q_ref.k_ref.v_ref, bf16[1024,1536]{1,0:T(8,128)(2,1)} %add_convert_fusion.4.q_ref.k_ref.v_ref, bf16[1024,1536]{1,0:T(8,128)(2,1)} %add_convert_fusion.4.q_ref.k_ref.v_ref, ...), custom_call_target="tpu_custom_call" | custom-call | flops 40265318400 | bytes 7340032 | tf_op jit(solution)/shard_map/attend_back/pallas_call | solution.py:857
  914.7 6.3 convolution_convert_fusion.2.g_ref
  921.0 14.6 %add_convert_fusion.1 = bf16[1024,2048]{1,0:T(8,128)(2,1)} fusion(f32[1024,2048]{1,0:T(8,128)} %fusion.70, bf16[2048,1024]{1,0:T(8,128)(2,1)S(1)} %copy-done.36, bf16[2048,2048]{1,0:T(8,128)(2,1)} %get-tuple-element.67), kind=kOutput, calls=%fused_computation.26 | convolution fusion | flops 8594128896 | bytes 25165824 | tf_op jit(solution)/shard_map/dot_general | solution.py:32
  936.2 1.2 copy-done.12
  937.4 34.3 %attend_back.3 = bf16[1024,1536]{1,0:T(8,128)(2,1)S(1)} custom-call(s32[4]{0:T(128)S(1)} %copy-done.5, bf16[1024,1536]{1,0:T(8,128)(2,1)} %copy-done.14, bf16[1024,1536]{1,0:T(8,128)(2,1)} %copy-done.14, bf16[1024,1536]{1,0:T(8,128)(2,1)} %copy-done.14, bf16[1024,512]{1,0:T(8,128)(2,1)S(1)} %copy-done.12), custom_call_target="tpu_custom_call" | custom-call | flops 40265318400 | bytes 7340032 | tf_op jit(solution)/shard_map/attend_back/pallas_call | solution.py:857
  971.8 1.6 copy-done
  974.9 12.0 convert_reduce_fusion.1
  986.9 11.4 convert_reduce_fusion
  999.1 5.1 fusion.71
  1004.3 3.7 add_convert_fusion.5
  1008.0 11.5 fusion.59
  1019.5 1.9 copy-done.2
  1021.4 15.3 %add_convert_fusion = bf16[2048,1536]{1,0:T(8,128)(2,1)} fusion(f32[2048,1536]{1,0:T(8,128)} %fusion.59, bf16[1024,1536]{1,0:T(8,128)(2,1)S(1)} %copy-done.2, bf16[1024,2048]{1,0:T(8,128)(2,1)} %all-gather.11.cloned.1.call-done, f32[1024]{0:T(1024)S(1)} %copy-done.86, f32[1024]{0:T(1024)S(1)} %copy-done.65, f32[2048]{0:T(1024)S(1)} %bitcast.204, ...), kind=kOutput, calls=%fused_computation | convolution fusion | flops 6461325312 | bytes 26238976 | tf_op jit(solution)/shard_map/dot_general | solution.py:32
  1036.7 8.4 pad_maximum_fusion.refs_2_
  1045.0 143.6 %sums.5 = (f32[256,2048]{1,0:T(8,128)}, f32[256,2048]{1,0:T(8,128)}, f32[256,2048]{1,0:T(8,128)}, f32[256,2048]{1,0:T(8,128)}, f32[24,128]{1,0:T(8,128)}) custom-call(bf16[1024,2048]{1,0:T(8,128)(2,1)} %get-tuple-element.223.refs_0_, bf16[1024,2048]{1,0:T(8,128)(2,1)} %get-tuple-element.224.refs_1_, bf16[2048,2048]{1,0:T(8,128)(2,1)} %pad_maximum_fusion.refs_2_, ...), custom_call_target="tpu_custom_call" | custom-call | flops 80000000000 | bytes 10000000 | tf_op jit(solution)/shard_map/sums/pallas_call | solution.py:662
  1190.9 2.8 slice_bitcast_fusion.3
  1194.7 3.5 fusion.36
  1198.3 1.5 fusion.55
  1199.8 3.1 pad_maximum_fusion.1
  1202.8 6.1 copy.89
  1209.0 4.7 all-to-all-start
  1214.9 5.1 fusion.45
  1220.0 1.5 maximum_bitcast_fusion.1
  1221.5 18.9 %all-to-all-done = bf16[2,256,2048]{1,0,2:T(2,128)(2,1)} async-done(((bf16[2,256,2048]{1,0,2:T(2,128)(2,1)}), bf16[2,256,2048]{1,0,2:T(2,128)(2,1)}, u32[]{:S(2)}, u32[]{:S(2)}) %all-to-all-start) | async-done | bytes 2097184 | tf_op jit(solution)/shard_map/all_to_all | solution.py:1329
  1240.4 3.0 convert_bitcast_fusion
  1243.4 5.4 fusion.68
  1248.8 6.0 copy.92
  1254.8 1.2 copy.90
  1256.1 2.2 copy.107
  1258.3 3.4 fusion.43
  1261.7 1.5 maximum_bitcast_fusion
  (318 shorter events, 23.8 us)
Async XLA Ops:
  7.2 3.6 copy-start.89
  7.2 3.7 copy-start.87
  7.2 3.9 copy-start.41
  7.2 4.0 copy-start.96
  7.2 4.0 copy-start.95
  7.3 4.0 copy-start.94
  7.3 4.0 copy-start.93
  7.3 4.0 copy-start.92
  7.3 4.0 copy-start.91
  7.3 4.7 copy-start.42
  7.3 4.7 copy-start.43
  7.3 4.7 copy-start.44
  7.3 103.0 %all-gather.15.cloned.1.call-start = ((), (), s32[]{:S(2)}) async-start(), calls=%async_computation.11 | async-start | bytes 9437184 | tf_op jit(solution)/shard_map/all_gather | solution.py:1238
  10.7 304.9 %all-gather.11.cloned.1.call-start = ((), (), s32[]{:S(2)}) async-start(), calls=%async_computation.6 | async-start | bytes 5242880 | tf_op jit(solution)/shard_map/all_gather | solution.py:1241
  110.4 374.5 %all-gather.7.cloned.1.call-start = ((), (), s32[]{:S(2)}) async-start(), calls=%async_computation.4 | async-start | bytes 5242880 | tf_op jit(solution)/shard_map/all_gather | solution.py:1253
  111.3 209.0 %copy-start.79 = (f32[1,2,8,128]{3,1,2,0:T(2,128)}, f32[1,2,8,128]{3,1,2,0:T(2,128)S(1)}, u32[]{:S(2)}) copy-start(f32[1,2,8,128]{3,1,2,0:T(2,128)S(1)} %copy.101) | copy-start | bytes 24580
  111.3 209.0 %copy-start.45 = (f32[1,2,8,128]{3,1,2,0:T(2,128)}, f32[1,2,8,128]{3,1,2,0:T(2,128)S(1)}, u32[]{:S(2)}) copy-start(f32[1,2,8,128]{3,1,2,0:T(2,128)S(1)} %copy.100) | copy-start | bytes 24580
  116.5 11.1 copy-start.83
  116.5 11.2 copy-start.90
  127.6 357.3 %all-gather.9.cloned.1.call-start = ((), (), s32[]{:S(2)}) async-start(), calls=%async_computation.5 | async-start | bytes 5242880 | tf_op jit(solution)/shard_map/all_gather | solution.py:1254
  127.7 16.1 %copy-start.6 = (s32[4]{0:T(128)}, s32[4]{0:T(128)S(1)}, u32[]{:S(2)}) copy-start(s32[4]{0:T(128)S(1)} %get-tuple-element.221.parents_ref) | copy-start | bytes 52
  127.7 202.4 %copy-start.4 = (s32[4]{0:T(128)}, s32[4]{0:T(128)S(1)}, u32[]{:S(2)}) copy-start(s32[4]{0:T(128)S(1)} %get-tuple-element.222.parents_ref) | copy-start | bytes 52
  129.6 14.3 %copy-start.22 = (bf16[2,1,256,2048]{3,2,1,0:T(8,128)(2,1)S(1)}, bf16[2,1,256,2048]{3,2,1,0:T(8,128)(2,1)}, u32[]{:S(2)}) copy-start(bf16[2,1,256,2048]{3,2,1,0:T(8,128)(2,1)} %param.20) | copy-start | bytes 6291460
  143.8 6.9 copy-start.8
  143.9 499.2 %all-gather.13.cloned.1.call-start = ((), (), s32[]{:S(2)}) async-start(), calls=%async_computation.7 | async-start | bytes 9437184 | tf_op jit(solution)/shard_map/all_gather | solution.py:1256
  320.3 9.8 copy-start.85
  330.1 14.2 %copy-start.14 = (bf16[1024,1536]{1,0:T(8,128)(2,1)}, bf16[1024,1536]{1,0:T(8,128)(2,1)S(1)}, u32[]{:S(2)}) copy-start(bf16[1024,1536]{1,0:T(8,128)(2,1)S(1)} %add_convert_fusion.3.q_ref.k_ref.v_ref) | copy-start | bytes 9437188
  344.4 6.3 copy-start.9
  350.6 123.9 %copy-start.54 = (f32[1,2,8,128]{3,1,2,0:T(2,128)S(1)}, f32[1,2,8,128]{3,1,2,0:T(2,128)}, u32[]{:S(2)}) copy-start(f32[1,2,8,128]{3,1,2,0:T(2,128)} %copy.102) | copy-start | bytes 24580
  480.9 4.0 copy-start.66
  480.9 4.0 copy-start.68
  480.9 718.8 %reduce-scatter.8.cloned.1.call-start = ((), (), s32[]{:S(2)}) async-start(), calls=%async_computation.10 | async-start | bytes 5242880 | tf_op jit(solution)/shard_map/reduce_scatter | solution.py:1290
  484.9 120.2 %copy-start.39 = (f32[1,2,8,128]{3,1,2,0:T(2,128)S(1)}, f32[1,2,8,128]{3,1,2,0:T(2,128)}, u32[]{:S(2)}) copy-start(f32[1,2,8,128]{3,1,2,0:T(2,128)} %copy.103) | copy-start | bytes 24580
  484.9 120.2 %copy-start.58 = (f32[256]{0:T(256)S(1)}, f32[256]{0:T(256)}, u32[]{:S(2)}) copy-start(f32[256]{0:T(256)} %copy-done.57) | copy-start | bytes 3076
  484.9 120.2 %copy-start.69 = (f32[256]{0:T(256)S(1)}, f32[256]{0:T(256)}, u32[]{:S(2)}) copy-start(f32[256]{0:T(256)} %copy-done.68) | copy-start | bytes 3076
  605.2 3.7 copy-start.74
  605.2 3.7 copy-start.19
  605.2 3.7 copy-start.35
  613.9 3.6 copy-start.37
  613.9 17.6 %slice-start = ((s8[8388608]{0:T(1024)(128)(4,1)}), s8[4194304]{0:T(1024)(128)(4,1)S(1)}, s32[]{:S(2)}) async-start(s8[8388608]{0:T(1024)(128)(4,1)} %bitcast.207), calls=%async_computation.12 | async-start | bytes 8388608
  617.5 14.0 %slice-start.1 = ((s8[8388608]{0:T(1024)(128)(4,1)}), s8[4194304]{0:T(1024)(128)(4,1)S(1)}, s32[]{:S(2)}) async-start(s8[8388608]{0:T(1024)(128)(4,1)} %bitcast.207), calls=%async_computation.13 | async-start | bytes 8388608
  617.5 14.0 %copy-start.98 = (bf16[2048,1024]{1,0:T(8,128)(2,1)S(1)}, bf16[2048,1024]{1,0:T(8,128)(2,1)}, u32[]{:S(2)}) copy-start(bf16[2048,1024]{1,0:T(8,128)(2,1)} %get-tuple-element.59) | copy-start | bytes 12582916
  772.2 427.6 %reduce-scatter.6.cloned.1.call-start = ((), (), s32[]{:S(2)}) async-start(), calls=%async_computation.9 | async-start | bytes 5242880 | tf_op jit(solution)/shard_map/reduce_scatter | solution.py:1302
  777.4 6.3 copy-start.72
  777.4 6.3 copy-start.34
  914.7 6.3 copy-start.36
  935.6 322.6 %reduce-scatter.4.cloned.1.call-start = ((), (), s32[]{:S(2)}) async-start(), calls=%async_computation.8 | async-start | bytes 9437184 | tf_op jit(solution)/shard_map/reduce_scatter | solution.py:1335
  974.8 12.1 copy-start.1
  974.8 12.1 copy-start.32
  974.8 12.1 copy-start.65
  974.9 12.1 copy-start.86
  986.9 11.5 copy-start.52
  999.1 5.1 copy-start.10
  999.1 5.1 copy-start.97
  1004.2 3.7 copy-start.30
  1004.3 3.7 copy-start.46
  1004.3 3.7 copy-start.80
  1190.9 3.8 copy-start.21
  1190.9 3.8 copy-start.59
  1190.9 3.8 copy-start.60
  1209.0 5.4 copy-start.70
  1209.0 6.0 copy-start.76
  1209.0 6.0 copy-start.78
  1209.0 31.4 %all-to-all-start = ((bf16[2,256,2048]{1,0,2:T(2,128)(2,1)}), bf16[2,256,2048]{1,0,2:T(2,128)(2,1)}, u32[]{:S(2)}, u32[]{:S(2)}) async-start(bf16[2,256,2048]{1,0,2:T(2,128)(2,1)} %copy.89), calls=%async_computation.3 | async-start | bytes 4194304 | tf_op jit(solution)/shard_map/all_to_all | solution.py:1329
  (46 other events, 95.5 us)
Sparse Core Ops, SparseCore 0:
  10.8 90.9 all-gather.14
  110.5 100.4 all-gather.10
  212.6 116.5 all-gather.6
  330.6 118.6 all-gather.8
  481.0 80.1 all-gather.12
  772.3 99.0 reduce-scatter.7
  935.8 76.1 reduce-scatter.5
  1019.6 86.0 reduce-scatter.3

commit v4 on v3

--- a/solution.py
+++ b/solution.py
@@ -588,44 +588,68 @@
         self.out[...] = total
 
 
-def sum_kernel(lines, planes, small, *refs):
+def sum_kernel(counts, *refs):
+    lines, planes, gathers, swaps, small = counts
     line, cube = Line(), Cube()
-    count = lines + planes + small
-    ins, outs, scratch = refs[:count], refs[count : 2 * count], refs[2 * count :]
-    sums, folds = [], []
-    for i in range(lines):
-        sums.append(LineScatter(line, ins[i], outs[i], scratch[:7]))
-        scratch = scratch[7:]
-    for i in range(lines, lines + planes):
-        folds.append(CubeScatter(cube, ins[i], outs[i], scratch[:8]))
-        scratch = scratch[8:]
+    count = sum(counts)
+    ins, outs, scratch = refs[:count], refs[count : 2 * count], list(refs[2 * count :])
+
+    def take(number):
+        taken = tuple(scratch[:number])
+        del scratch[:number]
+        return taken
+
+    pairs = list(zip(ins, outs))
+    sums = [LineScatter(line, *pairs.pop(0), take(7)) for _ in range(lines)]
+    folds = [CubeScatter(cube, *pairs.pop(0), take(8)) for _ in range(planes)]
+    lanes = [LineGather(line, *pairs.pop(0), take(5)) for _ in range(gathers)]
+    moves = []
+    for _ in range(swaps):
+        src, dst = pairs.pop(0)
+        rows, cols = src.shape[0], dst.shape[1]
+        moves.append(
+            (
+                lambda d, src=src, cols=cols: src.at[:, window(d, cols)],
+                lambda d, dst=dst, rows=rows: dst.at[window(d, rows)],
+            )
+        )
+    swap = CubeExchange(cube, moves, take(3)) if swaps else None
+    little = SmallSum(line, cube, *pairs.pop(0), take(7)) if small else None
     barrier = pltpu.get_barrier_semaphore()
+    peers = 0
     if small:
         for k in range(1, line.n):
             pl.semaphore_signal(
                 barrier, inc=1, device_id=line.at((line.me + k) % line.n), device_id_type=MESH
             )
+        peers = line.n - 1
+    elif lines or gathers:
+        line.greet(barrier)
+        peers = line.peers()
+    if small or swaps:
         for k in range(1, cube.dp):
             pl.semaphore_signal(
                 barrier, inc=1, device_id=cube.at((cube.me + k) % cube.dp), device_id_type=MESH
             )
-    else:
-        line.greet(barrier)
-        if planes:
-            cube.greet(barrier)
+        peers = peers + cube.dp - 1
+    elif planes:
+        cube.greet(barrier)
+        peers = peers + cube.peers()
     for s in sums:
         s.prepare()
+    pl.semaphore_wait(barrier, peers)
     if small:
-        pl.semaphore_wait(barrier, line.n - 1 + cube.dp - 1)
-        little = SmallSum(line, cube, ins[-1], outs[-1], scratch)
         little.swap.start()
-    else:
-        pl.semaphore_wait(barrier, line.peers() + (cube.peers() if planes else 0))
+    for lane in lanes:
+        lane.start()
     pieces = [p for p in folds[0].order() if p] if planes else []
     per = -(-len(pieces) // (line.n - 1))
     for step in range(1, line.n):
         for s in sums:
             s.step(step)
+        if step > 1:
+            for lane in lanes:
+                lane.take(step - 1)
         if step == 1:
             for f in folds:
                 f.start()
@@ -635,41 +659,63 @@
             for f in folds:
                 f.fold(piece)
         pieces = pieces[per:]
+        if step == 1 and swaps:
+            swap.start()
     for f in folds:
         f.finish()
+    for lane in lanes:
+        lane.take(line.n - 1)
+        lane.finish()
     for s in sums:
         s.finish()
+    if swaps:
+        swap.finish()
     if small:
         little.finish()
 
 
-def all_sums(line_parts, plane_parts, small_parts, collective_id):
+def exchange(collective_id, lines=(), planes=(), gathers=(), swaps=(), small=()):
     dp, n = lax.axis_size("dp"), lax.axis_size("tensor")
-    out_shape, scratch = [], []
-    for part in line_parts:
+    out_shape, out_specs, scratch = [], [], []
+    for part in lines:
         rows, d = part.shape[0] // n, part.shape[1]
         out_shape.append(jax.ShapeDtypeStruct((rows, d), F32))
+        out_specs.append(VMEM)
         scratch += LineScatter.scratch(n, rows, d)
-    for part in plane_parts:
+    for part in planes:
         rows, d = part.shape[0] // dp, part.shape[1]
         out_shape.append(jax.ShapeDtypeStruct((rows, d), F32))
+        out_specs.append(VMEM)
         scratch += CubeScatter.scratch(dp // 2, rows, d)
-    for part in small_parts:
+    for part in gathers:
+        rows, d = part.shape
+        out_shape.append(jax.ShapeDtypeStruct((n * rows, d), BF16))
+        out_specs.append(ANY)
+        scratch += LineGather.sems(n)
+    for part in swaps:
+        rows, d = part.shape
+        out_shape.append(jax.ShapeDtypeStruct((dp * rows, d // dp), BF16))
+        out_specs.append(ANY)
+    if swaps:
+        scratch += CubeExchange.sems(dp, len(swaps))
+    for part in small:
         rows, d = part.shape[1:]
         out_shape.append(jax.ShapeDtypeStruct((rows, d), F32))
+        out_specs.append(VMEM)
         scratch += SmallSum.scratch(dp, n, rows, d)
-    operands = list(line_parts) + list(plane_parts) + list(small_parts)
+    counts = tuple(len(g) for g in (lines, planes, gathers, swaps, small))
+    operands = [part for group in (lines, planes, gathers, swaps, small) for part in group]
     return pl.pallas_call(
-        functools.partial(sum_kernel, len(line_parts), len(plane_parts), len(small_parts)),
+        functools.partial(sum_kernel, counts),
         out_shape=tuple(out_shape),
         in_specs=[ANY] * len(operands),
-        out_specs=(VMEM,) * len(operands),
+        out_specs=tuple(out_specs),
         scratch_shapes=scratch,
         compiler_params=pltpu.CompilerParams(
             collective_id=collective_id, has_side_effects=True, vmem_limit_bytes=60 << 20
         ),
         cost_estimate=pl.CostEstimate(flops=80 * 10**9, bytes_accessed=10**7, transcendentals=0),
-        name="sums",
+        name="exchange",
     )(*operands)
 
 
@@ -757,26 +803,7 @@
     )(parents, qkv, qkv, qkv)
 
 
-def attend_back_kernel(host, parents_ref, q_ref, k_ref, v_ref, g_ref, *refs):
-    if host:
-        own_ref, out_ref, full_ref, dq_s, dk_s, dv_s = refs[:6]
-        line = Line()
-        gather = LineGather(line, own_ref, full_ref, refs[6:])
-        pair, pairs = pl.program_id(0), pl.num_programs(0)
-
-        @pl.when((pair == 0) & (pl.program_id(1) == 0))
-        def _():
-            barrier = pltpu.get_barrier_semaphore()
-            line.greet(barrier)
-            pl.semaphore_wait(barrier, line.peers())
-            gather.start()
-
-        @pl.when((pair == pairs - 1) & (pl.program_id(1) == 0))
-        def _():
-            gather.take(1)
-
-    else:
-        out_ref, dq_s, dk_s, dv_s = refs
+def attend_back_kernel(parents_ref, q_ref, k_ref, v_ref, g_ref, out_ref, dq_s, dk_s, dv_s):
     part = pl.program_id(1)
     blocks = q_ref.shape[0] // BLOCK
     scale = 1.0 / math.sqrt(HEAD_DIM)
@@ -828,35 +855,16 @@
     def _():
         out_ref[...] = dv_s[...].astype(BF16)
 
-    if host:
-
-        @pl.when((pair == pairs - 1) & (part == 2))
-        def _():
-            for step in range(2, line.n):
-                gather.take(step)
-            gather.finish()
-
-
-def attend_back(parents, qkv, grad, width, own=None):
+
+def attend_back(parents, qkv, grad, width):
     rows = qkv.shape[0]
     pairs = width // PAIR
     spec = lambda part: pl.BlockSpec((rows, PAIR), lambda p, c, parents: (0, part * pairs + p))
     blocks = rows // BLOCK
     work = pairs * 2 * (blocks * (blocks + 1) // 2) * BLOCK * BLOCK
-    host = own is not None
-    out_shape = [jax.ShapeDtypeStruct((rows, 3 * width), BF16)]
-    out_specs = [pl.BlockSpec((rows, PAIR), lambda p, c, parents: (0, c * pairs + p))]
-    sems = []
-    params = dict(vmem_limit_bytes=48 << 20)
-    if host:
-        n = lax.axis_size("tensor")
-        out_shape.append(jax.ShapeDtypeStruct((n * own.shape[0], own.shape[1]), BF16))
-        out_specs.append(ANY)
-        sems = LineGather.sems(n)
-        params.update(collective_id=4, has_side_effects=True)
-    out = pl.pallas_call(
-        functools.partial(attend_back_kernel, host),
-        out_shape=out_shape,
+    return pl.pallas_call(
+        attend_back_kernel,
+        out_shape=jax.ShapeDtypeStruct((rows, 3 * width), BF16),
         grid_spec=pltpu.PrefetchScalarGridSpec(
             num_scalar_prefetch=1,
             grid=(pairs, 3),
@@ -865,23 +873,20 @@
                 spec(1),
                 spec(2),
                 pl.BlockSpec((rows, PAIR), lambda p, c, parents: (0, p)),
-            ]
-            + [ANY] * host,
-            out_specs=out_specs,
+            ],
+            out_specs=pl.BlockSpec((rows, PAIR), lambda p, c, parents: (0, c * pairs + p)),
             scratch_shapes=[
                 pltpu.VMEM((rows, PAIR), BF16),
                 pltpu.VMEM((rows, PAIR), F32),
                 pltpu.VMEM((rows, PAIR), F32),
-            ]
-            + sems,
+            ],
         ),
-        compiler_params=pltpu.CompilerParams(**params),
+        compiler_params=pltpu.CompilerParams(vmem_limit_bytes=48 << 20),
         cost_estimate=pl.CostEstimate(
             flops=work * PAIR * 60, bytes_accessed=rows * width * 14, transcendentals=work
         ),
         name="attend_back",
-    )(parents, qkv, qkv, qkv, grad, *([own] if host else []))
-    return out if host else out[0]
+    )(parents, qkv, qkv, qkv, grad)
 
 
 def ffn_kernel(host, n2_ref, dy_ref, we_ref, wr_ref, be_ref, *refs):
@@ -906,7 +911,8 @@
     if host:
         line = Line()
         line.greet(barrier)
-        gather = LineGather(line, line_own, line_full, refs[23:])
+        aside = LineScatter(line, line_own, line_full, refs[23:])
+        aside.prepare()
     load_own = pltpu.make_async_copy(n2_ref, seq.at[0, pl.ds(0, rows)], own_sem)
     load_own.start()
     parts = we_ref.shape[0] // model
@@ -958,7 +964,7 @@
     load_own.wait()
     pl.semaphore_wait(barrier, cube.peers() + (line.peers() if host else 0))
     if host:
-        gather.start()
+        aside.step(1)
     sends = []
     for level in range(levels):
         sends.append(gather_copy(0, level))
@@ -1067,8 +1073,8 @@
             out = over(act_st[slot], wr[:, cols], 1, 0).astype(BF16)
             part_st[slot, :, cols] = out
 
-        if host and turn < line.n - 1:
-            gather.take(turn + 1)
+        if host and turn < line.n - 2:
+            aside.step(turn + 2)
         core_sends[piece] = core_copy(piece)
         core_sends[piece].start()
         mine, other = owner(piece)
@@ -1108,9 +1114,9 @@
         sum_ref[part] = total
 
     if host:
-        for step in range(count + 1, line.n):
-            gather.take(step)
-        gather.finish()
+        for step in range(count + 2, line.n):
+            aside.step(step)
+        aside.finish()
     for s in sends:
         s.wait_send()
     for turn in range(max(0, count - 2), count):
@@ -1130,7 +1136,7 @@
     count = dp // 2
     dma, anywhere, vmem = DMA, ANY, VMEM
     operands = [n2, dy_all, we, wr, bias_e] + [own] * host
-    lines = [jax.ShapeDtypeStruct((n * rows, model), BF16)] * host
+    lines = [jax.ShapeDtypeStruct((rows, model), F32)] * host
     flops = 36 * dp * rows * model * units
     return pl.pallas_call(
         functools.partial(ffn_kernel, host),
@@ -1143,7 +1149,7 @@
             *lines,
         ),
         in_specs=[anywhere, anywhere, anywhere, anywhere, vmem] + [anywhere] * host,
-        out_specs=(vmem, anywhere, anywhere, anywhere, anywhere) + (anywhere,) * host,
+        out_specs=(vmem, anywhere, anywhere, anywhere, anywhere) + (vmem,) * host,
         scratch_shapes=[
             pltpu.VMEM((model, units), BF16),
             pltpu.VMEM((units, model), BF16),
@@ -1160,7 +1166,7 @@
             dma((count,)), dma((count,)), dma((count,)), dma((count,)),
             dma((count,)), dma((count,)), dma((count - 1,)), dma((count - 1,)),
         ]
-        + (LineGather.sems(n) if host else []),
+        + (LineScatter.scratch(n, rows, model) if host else []),
         compiler_params=pltpu.CompilerParams(
             collective_id=2 if host else 1, has_side_effects=True, vmem_limit_bytes=62 << 20
         ),
@@ -1237,33 +1243,63 @@
 
     seq_grad = [lax.all_gather(dy_low[0], "dp", axis=0, tiled=True)]
     seq_x = [seq_x0]
-    for m in micros[1:]:
-        seq_x.append(lax.all_gather(after(x_low[m], seq_x0, seq_grad[0]), "tensor", axis=0, tiled=True))
+    side = 0 if mine % 128 == 0 else 1
+    w_e = lax.all_gather(after(w_e, seq_grad[0]), "tensor", axis=side, tiled=True)
 
     normal_one, seq_one, qkv, attended, hidden, normed_two = [], [], [], [], [], []
+    out_part, seq_two, activated, d_pre, d_hidden, d_branch, seq_branch = [], [], [], [], [], [], []
+    d_qkv, d_one, out_sum = [], [], []
+    g_gain_two = g_shift_two = g_bias_red = g_bias_out = g_bias_e = 0.0
+    g_gain_one = g_shift_one = g_bias_qkv = 0.0
     for m in micros:
         normal_one.append(layer_norm(seq_x[m].astype(F32), 1.0, 0.0))
         seq_one.append((normal_one[m] * gain_one + shift_one).astype(BF16))
         qkv.append(
             (jnp.dot(seq_one[m], w_qkv, preferred_element_type=F32) + bias_qkv).astype(BF16)
         )
+        if m == 0:
+            w_r = lax.all_gather(after(w_r, qkv[m]), "tensor", axis=0, tiled=True)
         attended.append(attend(parents[m, 0], qkv[m], width))
+        branch = over(attended[m], w_ot, 1, 1).astype(BF16)
+        if m < last:
+            next_x = lax.all_gather(after(x_low[m + 1], branch), "tensor", axis=0, tiled=True)
         if m == 0:
-            side = 0 if mine % 128 == 0 else 1
-            w_e = lax.all_gather(after(w_e, qkv[m]), "tensor", axis=side, tiled=True)
-            w_r = lax.all_gather(after(w_r, attended[m]), "tensor", axis=0, tiled=True)
+            (branch,) = exchange(3, lines=[branch])
         else:
-            seq_grad.append(lax.all_gather(after(dy_low[m], attended[m]), "dp", axis=0, tiled=True))
-        branch = all_sums([over(attended[m], w_ot, 1, 1).astype(BF16)], [], [], 3)[0]
+            branch, full = exchange(4, lines=[branch], gathers=[d_branch[m - 1]])
+            seq_branch.append(full)
         hidden.append(x_low[m].astype(F32) + (branch + bias_out))
         normed_two.append(layer_norm(hidden[m], gain_two, shift_two).astype(BF16))
-
-    out_part, seq_two, activated, d_pre, d_hidden, d_branch, seq_branch = [], [], [], [], [], [], []
-    g_gain_two = g_shift_two = g_bias_red = g_bias_out = g_bias_e = 0.0
-    for m in micros:
-        own = d_branch[m - 1] if m else None
+        if m < last:
+            seq_grad.append(
+                lax.all_gather(after(dy_low[m + 1], normed_two[m]), "dp", axis=0, tiled=True)
+            )
+
+        def attention_back(k):
+            d_att = jnp.dot(seq_branch[k], w_ot, preferred_element_type=F32).astype(BF16)
+            d_qkv.append(attend_back(parents[k, 0], qkv[k], d_att, width))
+            d_one.append(over(d_qkv[k], w_qkv, 1, 1).astype(BF16))
+            part = d_one[k].astype(F32)
+            return (
+                jnp.sum(part * normal_one[k], 0, keepdims=True),
+                jnp.sum(part, 0, keepdims=True),
+                jnp.sum(d_qkv[k].astype(F32), 0),
+            )
+
+        own = None
+        if m:
+            part, attended[m] = lax.optimization_barrier((out_part[m - 1], attended[m]))
+            part = lax.psum_scatter(part, "dp", scatter_dimension=0, tiled=True)
+            normed_two[m], part = lax.optimization_barrier((normed_two[m], part))
+            out_sum.append(part.astype(F32))
+            gain, shift, bias = attention_back(m - 1)
+            g_gain_one, g_shift_one = g_gain_one + gain, g_shift_one + shift
+            g_bias_qkv = g_bias_qkv + bias
+            own = d_one[m - 1]
+
         d_two, seq, act, dpre, part, *line = ffn(normed_two[m], seq_grad[m], w_e, w_r, bias_e, own)
-        seq_branch += line
+        if m:
+            d_one[m - 1] = line[0]
         seq_two.append(seq)
         activated.append(act)
         d_pre.append(dpre)
@@ -1278,6 +1314,8 @@
         g_bias_red = g_bias_red + jnp.sum(grad32, 0, keepdims=True)
         g_bias_out = g_bias_out + jnp.sum(d_branch[m].astype(F32), 0, keepdims=True)
         g_bias_e = g_bias_e + jnp.sum(dpre.astype(F32), 0)
+        if m < last:
+            seq_x.append(after(next_x, d_branch[m]))
 
     def outer(left, right):
         out = None
@@ -1286,28 +1324,15 @@
             out = term if out is None else out + term
         return out.astype(BF16)
 
+    seq_branch.append(lax.all_gather(d_branch[last], "tensor", axis=0, tiled=True))
     g_r = outer(activated, seq_grad)
-    g_r_sum = lax.psum_scatter(g_r, "tensor", scatter_dimension=0, tiled=True)
-
-    d_qkv, d_one = [], []
-    g_gain_one = g_shift_one = g_bias_qkv = 0.0
-    for m in micros:
-        d_att = jnp.dot(seq_branch[m], w_ot, preferred_element_type=F32).astype(BF16)
-        if m < last:
-            d_att = after(d_att, g_r)
-            d, full = attend_back(parents[m, 0], qkv[m], d_att, width, d_branch[m + 1])
-            seq_branch.append(full)
-        else:
-            g_et = outer(d_pre, seq_two)
-            g_et_sum = lax.psum_scatter(g_et, "tensor", scatter_dimension=0, tiled=True)
-            d_att = after(d_att, g_et)
-            d = attend_back(parents[m, 0], qkv[m], d_att, width)
-        d_qkv.append(d)
-        g_bias_qkv = g_bias_qkv + jnp.sum(d.astype(F32), 0)
-        d_one.append(over(d, w_qkv, 1, 1).astype(BF16))
-        part = d_one[m].astype(F32)
-        g_gain_one = g_gain_one + jnp.sum(part * normal_one[m], 0, keepdims=True)
-        g_shift_one = g_shift_one + jnp.sum(part, 0, keepdims=True)
+    g_r = lax.psum_scatter(after(g_r, d_branch[last]), "tensor", scatter_dimension=0, tiled=True)
+    g_et = outer(d_pre, seq_two)
+    g_et_sum = lax.psum_scatter(g_et, "tensor", scatter_dimension=0, tiled=True)
+    seq_branch[last] = after(seq_branch[last], g_et)
+    gain, shift, bias = attention_back(last)
+    g_gain_one, g_shift_one = g_gain_one + gain, g_shift_one + shift
+    g_bias_qkv = g_bias_qkv + bias
 
     rows = jnp.concatenate(
         [g_gain_one, g_shift_one, g_bias_out, g_gain_two, g_shift_two, g_bias_red], 0
@@ -1325,19 +1350,16 @@
     little = jnp.concatenate([rows, row_qv, row_e], 1)
     little = jnp.pad(little, ((0, 0), (0, -little.shape[1] % 1024))).reshape(dp, -1, 128)
 
-    g_ffn = jnp.stack([g_et_sum, g_r_sum], 0)
-    g_ffn = lax.all_to_all(g_ffn, "dp", split_axis=2, concat_axis=1, tiled=True).astype(F32)
-    g_expand = g_ffn[0].T
-    g_reduce = g_ffn[1]
-
     g_attn = jnp.concatenate([outer(seq_one, d_qkv), outer(seq_branch, attended)], axis=1)
-    out_sum = [
-        lax.psum_scatter(after(part, d_qkv[last]), "dp", scatter_dimension=0, tiled=True).astype(F32)
-        for part in out_part[:last]
-    ]
-    sums = all_sums(d_one, [g_attn, out_part[last]], [little], 5)
-    d_one, (g_attn, out_last, little) = sums[: last + 1], sums[last + 1 :]
+    d_one[last], g_attn, out_last, g_reduce, little = exchange(
+        5, lines=[d_one[last]], planes=[g_attn, out_part[last]], swaps=[g_r], small=[little]
+    )
     out_sum.append(out_last)
+    (g_expand,) = exchange(6, swaps=[after(g_et_sum, little)])
+    g_expand = g_expand.T.astype(F32)
+    g_reduce = g_reduce.astype(F32)
+    g_query, g_key, g_value = [g_attn[:, i * width : (i + 1) * width] for i in range(3)]
+    g_out = g_attn[:, 3 * width :].T
     layer_out = [(hidden[m] + (out_sum[m] + bias_red)).astype(BF16) for m in micros]
     little = little.reshape(-1)
     six = little[: 6 * cut].reshape(6, cut)
@@ -1348,8 +1370,6 @@
     at += tn * 2 * bq_rows * bq_cols
     g_be = little[at : at + tn * be_rows * be_cols].reshape(tn, be_rows, be_cols)
     g_be = lax.dynamic_index_in_dim(g_be, tn_me, 0, keepdims=False)
-    g_query, g_key, g_value = [g_attn[:, i * width : (i + 1) * width] for i in range(3)]
-    g_out = g_attn[:, 3 * width :].T
     input_grad = []
     for m in micros:
         first_value, first_pull = jax.vjp(

time: 1280 us -> 1130 us (0.88)
  Pallas kernels: 936 us -> 782 us
  waiting for transfers between devices: 19.1 us -> 55.7 us
  local copies, waits for them, and re-layouts: 54.7 us -> 34.2 us
    pallas_call x5 -> x6, Pallas kernels: 578 us -> 470 us  [the longest x4 401 us: exchange(): pl.pallas_call(functools.partial(sum_kernel, counts), out_shape=tuple(out...]
    all_gather x4 -> x5, waiting for transfers between devices: 0.06 us -> 54.4 us  [the longest x1 49.5 us: body(): lax.all_gather(after(w_e, seq_grad[0]), 'tensor', axis=side, tiled=True)]
    pallas_call x2, Pallas kernels: 234 us -> 187 us  [ffn(): pl.pallas_call(functools.partial(ffn_kernel, host), out_shape=(jax.ShapeD...]
    all_to_all x1 -> x0, waiting for transfers between devices: 18.9 us -> none  [body(): lax.all_to_all(g_ffn, 'dp', split_axis=2, concat_axis=1, tiled=True)]
  transfers between devices with their start and end apart: 9 -> 9, of which waited for: 1 -> 2; matrix products, arithmetic and copies ran while one was open for 19% -> 17% of each run, Pallas kernels for 65% -> 59%
where the time goes in v4:
time: 1130 us; the launch traced here: 1120 us
  Pallas kernels  782 us (69%)
  matrix products  157 us (14%)
  other arithmetic  66.1 us (6%)
  waiting for transfers between devices  55.7 us (5%)
  local copies, waits for them, and re-layouts  34.2 us (3%)
  between operations  15.8 us (1%)
  blocking collectives  11.4 us (1%)
    pallas_call x4, Pallas kernels, exchange(): pl.pallas_call(functools.partial(sum_kernel, counts), out_shape=tuple(out...  401 us
    pallas_call x2, Pallas kernels, ffn(): pl.pallas_call(functools.partial(ffn_kernel, host), out_shape=(jax.ShapeD...  187 us
    dot_general x12, matrix products, over(): lax.dot_general(left, right, (((on_left,), (on_right,)), ((), ())), prefe...  127 us
    pallas_call x1, Pallas kernels, front(): pl.pallas_call(front_kernel, out_shape=(jax.ShapeDtypeStruct((n * rows, m...  95.8 us
    pallas_call x2, Pallas kernels, attend_back(): pl.pallas_call(attend_back_kernel, out_shape=jax.ShapeDtypeStruct((rows,...  68.9 us
    all_gather x1, waiting for transfers between devices, body(): lax.all_gather(after(w_e, seq_grad[0]), 'tensor', axis=side, tiled=True)  49.5 us
    pallas_call x2, Pallas kernels, attend(): pl.pallas_call(attend_kernel, out_shape=jax.ShapeDtypeStruct((rows, width...  28.4 us
  transfers between devices with their start and end apart: 9, of which 2 were waited for; matrix products, arithmetic and copies ran while one was open for 17% of the time, Pallas kernels for 59%

profile of v4, /device:TPU:0, one launch (start us, length us, event | category | flops | bytes accessed | tf_op | source)
XLA Modules:
  0.0 1123.0 jit_solution(15300639690539643923)
XLA Ops:
  7.4 3.3 slice_bitcast_fusion
  12.0 1.1 pad_maximum_fusion.1.w_ref
  13.1 1.5 slice_bitcast_fusion.1
  14.6 95.8 %front.1 = (bf16[1024,2048]{1,0:T(8,128)(2,1)}, bf16[2048,2048]{1,0:T(8,128)(2,1)}, bf16[2048,256]{1,0:T(8,128)(2,1)}, bf16[256,2048]{1,0:T(8,128)(2,1)}, bf16[128,128]{1,0:T(8,128)(2,1)}) custom-call(bf16[256,2048]{1,0:T(8,128)(2,1)} %get-tuple-element.180.x_ref, bf16[256,2048]{1,0:T(8,128)(2,1)} %pad_maximum_fusion.1.w_ref, bf16[256,2048]{1,0:T(8,128)(2,1)} %we_ref.1, ...), custom_call_target="tpu_custom_call" | custom-call | flops 80000000000 | bytes 10000000 | tf_op jit(solution)/shard_map/front/pallas_call | solution.py:521
  112.3 3.0 convert_reduce_fusion.3
  115.7 1.2 fusion.11
  117.0 11.1 add_convert_fusion.4.q_ref.k_ref.v_ref
  128.9 1.9 copy-done.12
  130.8 14.2 %attend.2 = bf16[1024,512]{1,0:T(8,128)(2,1)S(1)} custom-call(s32[4]{0:T(128)S(1)} %get-tuple-element.206.parents_ref, bf16[1024,1536]{1,0:T(8,128)(2,1)S(1)} %copy-done.12, bf16[1024,1536]{1,0:T(8,128)(2,1)S(1)} %copy-done.12, bf16[1024,1536]{1,0:T(8,128)(2,1)S(1)} %copy-done.12), custom_call_target="tpu_custom_call" | custom-call | flops 16106127360 | bytes 4194304 | tf_op jit(solution)/shard_map/attend/pallas_call | solution.py:789
  145.0 6.4 convolution_convert_fusion.1.refs_0_
  151.5 123.9 %exchange.4 = f32[256,2048]{1,0:T(8,128)} custom-call(bf16[1024,2048]{1,0:T(8,128)(2,1)} %convolution_convert_fusion.1.refs_0_), custom_call_target="tpu_custom_call" | custom-call | flops 80000000000 | bytes 10000000 | tf_op jit(solution)/shard_map/exchange/pallas_call | solution.py:708
  275.4 2.8 convert_reduce_fusion.9
  278.2 1.3 copy-done.13
  280.2 11.4 %all_gather.25 = bf16[1,1024]{1,0:T(2,128)(2,1)S(1)} all-gather(bf16[1,256]{1,0:T(2,128)(2,1)S(1)} %reshape.474), channel_id=1, replica_groups=mesh['dp'=8,'tensor'=4] {'tensor'}, dimensions={1}, use_global_device_ids=true | all-gather | bytes 2560 | tf_op jit(solution)/shard_map/all_gather | solution.py:1241
  292.2 3.0 add_convert_fusion.11.n2_ref
  295.2 49.5 %all-gather.10.cloned.1.call-done.we_ref = bf16[8192,256]{1,0:T(8,128)(2,1)} async-done(((bf16[2048,256]{1,0:T(8,128)(2,1)}), bf16[8192,256]{1,0:T(8,128)(2,1)}) %all-gather.10.cloned.1.call-update) | async-done | bytes 4194320 | tf_op jit(solution)/shard_map/all_gather | solution.py:1247
  344.7 93.7 %ffn_plane.2 = (f32[256,2048]{1,0:T(8,128)}, bf16[2048,2048]{1,0:T(8,128)(2,1)}, bf16[2048,1024]{1,0:T(8,128)(2,1)}, bf16[2048,1024]{1,0:T(8,128)(2,1)}, bf16[2048,2048]{1,0:T(8,128)(2,1)}) custom-call(bf16[256,2048]{1,0:T(8,128)(2,1)} %add_convert_fusion.11.n2_ref, bf16[2048,2048]{1,0:T(8,128)(2,1)} %bitcast.192, ...), custom_call_target="tpu_custom_call" | custom-call | flops 154618822656 | bytes 50331648 | tf_op jit(solution)/shard_map/ffn_plane/pallas_call | solution.py:1141
  438.5 3.7 multiply_reduce_fusion.1
  442.9 1.3 copy-done.27
  444.2 2.1 convert_reduce_fusion.13
  446.3 3.0 convert_reduce_fusion.2
  449.8 1.2 fusion.10
  451.1 9.8 add_convert_fusion.3.q_ref.k_ref.v_ref
  460.9 14.2 %attend.3 = bf16[1024,512]{1,0:T(8,128)(2,1)S(1)} custom-call(s32[4]{0:T(128)S(1)} %get-tuple-element.207.parents_ref, bf16[1024,1536]{1,0:T(8,128)(2,1)S(1)} %add_convert_fusion.3.q_ref.k_ref.v_ref, bf16[1024,1536]{1,0:T(8,128)(2,1)S(1)} %add_convert_fusion.3.q_ref.k_ref.v_ref, bf16[1024,1536]{1,0:T(8,128)(2,1)S(1)} %add_convert_fusion.3.q_ref.k_ref.v_ref), custom_call_target="tpu_custom_call" | custom-call | flops 16106127360 | bytes 4194304 | tf_op jit(solution)/shard_map/attend/pallas_call | solution.py:789
  476.1 6.0 convolution_convert_fusion.refs_0_
  482.0 119.7 %exchange.5 = (f32[256,2048]{1,0:T(8,128)}, bf16[1024,2048]{1,0:T(8,128)(2,1)}) custom-call(bf16[1024,2048]{1,0:T(8,128)(2,1)} %convolution_convert_fusion.refs_0_, bf16[256,2048]{1,0:T(8,128)(2,1)} %get-tuple-element.159.refs_1_), custom_call_target="tpu_custom_call" | custom-call | flops 80000000000 | bytes 10000000 | tf_op jit(solution)/shard_map/exchange/pallas_call | solution.py:708
  601.7 2.0 fusion.65
  604.4 1.4 add_convert_fusion.10.n2_ref
  605.8 1.2 copy-done.110
  607.0 3.9 convolution_convert_fusion.3.g_ref
  611.0 34.2 %attend_back.2 = bf16[1024,1536]{1,0:T(8,128)(2,1)S(1)} custom-call(s32[4]{0:T(128)S(1)} %copy-done.6, bf16[1024,1536]{1,0:T(8,128)(2,1)} %add_convert_fusion.4.q_ref.k_ref.v_ref, bf16[1024,1536]{1,0:T(8,128)(2,1)} %add_convert_fusion.4.q_ref.k_ref.v_ref, bf16[1024,1536]{1,0:T(8,128)(2,1)} %add_convert_fusion.4.q_ref.k_ref.v_ref, ...), custom_call_target="tpu_custom_call" | custom-call | flops 40265318400 | bytes 7340032 | tf_op jit(solution)/shard_map/attend_back/pallas_call | solution.py:865
  645.2 1.7 copy-done
  647.0 11.9 %convert_reduce_fusion.1 = (f32[2048]{0:T(1024)}, f32[2048]{0:T(1024)}, bf16[1024,2048]{1,0:T(8,128)(2,1)}) fusion(f32[1024]{0:T(1024)S(1)} %copy-done.94, f32[1024]{0:T(1024)S(1)} %copy-done.68, bf16[1024,2048]{1,0:T(8,128)(2,1)S(1)} %copy-done.32, bf16[1024,1536]{1,0:T(8,128)(2,1)S(1)} %attend_back.2, bf16[2048,2048]{1,0:T(8,128)(2,1)} %get-tuple-element.54), kind=kOutput, calls=%fused_computation.3 | convolution fusion | flops 6459224064 | bytes 17850368 | tf_op jit(solution)/shard_map/dot_general | solution.py:32
  658.9 93.7 %ffn_plane.3 = (f32[256,2048]{1,0:T(8,128)}, bf16[2048,2048]{1,0:T(8,128)(2,1)}, bf16[2048,1024]{1,0:T(8,128)(2,1)}, bf16[2048,1024]{1,0:T(8,128)(2,1)}, bf16[20...) custom-call(bf16[256,2048]{1,0:T(8,128)(2,1)} %add_convert_fusion.10.n2_ref, ...), custom_call_target="tpu_custom_call" | custom-call | flops 154618822656 | bytes 50331648 | tf_op jit(solution)/shard_map/ffn_plane/pallas_call | solution.py:1141
  752.7 3.1 multiply_reduce_fusion
  757.8 1.4 convert_reduce_fusion.12
  760.2 12.8 %fusion.53 = f32[1024,2048]{1,0:T(8,128)S(1)} fusion(bf16[2048,1024]{1,0:T(8,128)(2,1)} %get-tuple-element.77, bf16[1,1,2048,2048]{3,2,1,0:T(8,128)(2,1)} %all-gather.18.cloned.1.call-done), kind=kOutput, calls=%fused_computation.162 | convolution fusion | flops 8589934592 | bytes 20971520 | tf_op jit(solution)/shard_map/dot_general | solution.py:32
  773.0 13.1 %add_convert_fusion.1 = bf16[1024,2048]{1,0:T(8,128)(2,1)} fusion(f32[1024,2048]{1,0:T(8,128)S(1)} %fusion.53, bf16[2048,1024]{1,0:T(8,128)(2,1)S(1)} %copy-done.111, bf16[2048,2048]{1,0:T(8,128)(2,1)} %all-gather.14.cloned.1.call-done.dy_ref), kind=kOutput, calls=%fused_computation.26 | convolution fusion | flops 8594128896 | bytes 25165824 | tf_op jit(solution)/shard_map/dot_general | solution.py:32
  787.4 6.7 fusion.70
  794.2 14.0 %fusion.69 = f32[1024,2048]{1,0:T(8,128)} fusion(bf16[2048,1024]{1,0:T(8,128)(2,1)S(1)} %copy-done.36, bf16[2048,2048]{1,0:T(8,128)(2,1)} %get-tuple-element.71), kind=kOutput, calls=%fused_computation.172 | convolution fusion | flops 8589934592 | bytes 20971520 | tf_op jit(solution)/shard_map/dot_general | solution.py:32
  808.2 11.6 %fusion.59 = f32[2048,1536]{1,0:T(8,128)} fusion(bf16[1024,1536]{1,0:T(8,128)(2,1)S(1)} %copy-done.1, bf16[1024,2048]{1,0:T(8,128)(2,1)S(1)} %copy-done.33, f32[2048]{0:T(1024)S(1)} %bitcast.189, f32[2048]{0:T(1024)S(1)} %bitcast.172, f32[1024]{0:T(1024)S(1)} %copy-done.95, f32[1024]{0:T(1024)S(1)} %copy-done.69), kind=kOutput, calls=%fused_computation.166 | convolution fusion | flops 6455033856 | bytes 19947520 | tf_op jit(solution)/shard_map/dot_general | solution.py:32
  819.9 5.1 convert_reduce_fusion.4
  826.7 1.6 reshape.477
  828.3 15.7 %add_convert_fusion.2 = bf16[1024,2048]{1,0:T(8,128)(2,1)} fusion(f32[1024,2048]{1,0:T(8,128)} %fusion.69, bf16[2048,1024]{1,0:T(8,128)(2,1)} %get-tuple-element.72, bf16[2048,2048]{1,0:T(8,128)(2,1)} %get-tuple-element.73), kind=kOutput, calls=%fused_computation.27 | convolution fusion | flops 8594128896 | bytes 25165824 | tf_op jit(solution)/shard_map/dot_general | solution.py:32
  844.1 4.9 all-gather.16.cloned.1.call-done
  849.0 5.2 convolution_convert_fusion.2.g_ref
  854.2 34.7 %attend_back.3 = bf16[1024,1536]{1,0:T(8,128)(2,1)S(1)} custom-call(s32[4]{0:T(128)S(1)} %copy-done.4, bf16[1024,1536]{1,0:T(8,128)(2,1)} %copy-done.11, bf16[1024,1536]{1,0:T(8,128)(2,1)} %copy-done.11, bf16[1024,1536]{1,0:T(8,128)(2,1)} %copy-done.11, bf16[1024,512]{1,0:T(8,128)(2,1)S(1)} %convolution_convert_fusion.2.g_ref), custom_call_target="tpu_custom_call" | custom-call | flops 40265318400 | bytes 7340032 | tf_op jit(solution)/shard_map/attend_back/pallas_call | solution.py:865
  888.9 12.3 %convert_reduce_fusion = (f32[2048]{0:T(1024)S(1)}, f32[2048]{0:T(1024)S(1)}, bf16[1024,2048]{1,0:T(8,128)(2,1)}) fusion(f32[1024]{0:T(1024)S(1)} %copy-done.97, f32[1024]{0:T(1024)S(1)} %copy-done.71, bf16[1024,2048]{1,0:T(8,128)(2,1)S(1)} %copy-done.30, bf16[1024,1536]{1,0:T(8,128)(2,1)S(1)} %attend_back.3, bf16[2048,2048]{1,0:T(8,128)(2,1)} %get-tuple-element.54), kind=kOutput, calls=%fused_computation.1 | convolution fusion | flops 6459224064 | bytes 17850368 | tf_op jit(solution)/shard_map/dot_general | solution.py:32
  902.8 14.0 %add_convert_fusion = bf16[2048,1536]{1,0:T(8,128)(2,1)} fusion(f32[2048,1536]{1,0:T(8,128)} %fusion.59, bf16[1024,1536]{1,0:T(8,128)(2,1)} %copy-done.2, bf16[1024,2048]{1,0:T(8,128)(2,1)} %all-gather.8.cloned.1.call-done, f32[1024]{0:T(1024)S(1)} %copy-done.97, f32[1024]{0:T(1024)S(1)} %copy-done.71, f32[2048]{0:T(1024)S(1)} %bitcast.190, f32[2048]{0:T(1024)S(1)} %bitcast.173), kind=kOutput, calls=%fused_computation | convolution fusion | flops 6461325312 | bytes 26238976 | tf_op jit(solution)/shard_map/dot_general | solution.py:32
  916.8 2.6 add_convert_fusion.5
  920.1 7.5 pad_maximum_fusion.refs_1_
  927.6 141.9 %exchange.6 = (f32[256,2048]{1,0:T(8,128)}, f32[256,2048]{1,0:T(8,128)}, f32[256,2048]{1,0:T(8,128)}, bf16[2048,256]{1,0:T(8,128)(2,1)}, f32[24,128]{1,0:T(8,128)}) custom-call(bf16[1024,2048]{1,0:T(8,128)(2,1)} %get-tuple-element.209.refs_0_, bf16[2048,2048]{1,0:T(8,128)(2,1)} %pad_maximum_fusion.refs_1_, bf16[2048,2048]{1,0:T(8,128)(2,1)} %get-tuple-element.76.refs_2_, ...), custom_call_target="tpu_custom_call" | custom-call | flops 80000000000 | bytes 10000000 | tf_op jit(solution)/shard_map/exchange/pallas_call | solution.py:708
  1070.9 1.4 slice_bitcast_fusion.4
  1072.3 15.9 %exchange.7 = bf16[2048,256]{1,0:T(8,128)(2,1)} custom-call(bf16[256,2048]{1,0:T(8,128)(2,1)} %reduce-scatter.8.cloned.1.call-done.refs_0_), custom_call_target="tpu_custom_call" | custom-call | flops 80000000000 | bytes 10000000 | tf_op jit(solution)/shard_map/exchange/pallas_call | solution.py:708
  1088.2 2.7 convert_bitcast_fusion.1
  1090.9 3.2 copy.74
  1094.2 3.5 fusion.36
  1097.7 1.5 fusion.55
  1099.3 1.2 slice_bitcast_fusion.3
  1100.5 1.0 copy.73
  1101.5 2.7 convert_element_type.293
  1105.1 5.2 fusion.45
  1110.3 1.5 maximum_bitcast_fusion.1
  1114.1 1.5 maximum_bitcast_fusion
  (338 shorter events, 22.0 us)
Async XLA Ops:
  7.2 4.0 copy-start.102
  7.2 4.0 copy-start.103
  7.3 4.0 copy-start.104
  7.3 4.7 copy-start.46
  7.3 4.7 copy-start.45
  7.3 4.7 copy-start.44
  7.3 120.8 %all-gather.18.cloned.1.call-start = ((), (), s32[]{:S(2)}) async-start(), calls=%async_computation.11 | async-start | bytes 9437184 | tf_op jit(solution)/shard_map/all_gather | solution.py:1244
  10.7 284.6 %all-gather.12.cloned.1.call-start = ((), (), s32[]{:S(2)}) async-start(), calls=%async_computation.5 | async-start | bytes 5242880 | tf_op jit(solution)/shard_map/all_gather | solution.py:1261
  111.7 5.2 copy-start.47
  112.2 4.8 copy-start.86
  112.2 4.7 copy-start.89
  116.9 11.1 copy-start.93
  128.1 216.6 %all-gather.10.cloned.1.call-start = ((), (), s32[]{:S(2)}) async-start(), calls=%async_computation.4 | async-start | bytes 5242880 | tf_op jit(solution)/shard_map/all_gather | solution.py:1247
  128.8 317.5 %all-gather.8.cloned.1.call-start = ((), (), s32[]{:S(2)}) async-start(), calls=%async_computation.3 | async-start | bytes 5242880 | tf_op jit(solution)/shard_map/all_gather | solution.py:1265
  128.9 16.1 %copy-start.5 = (s32[4]{0:T(128)}, s32[4]{0:T(128)S(1)}, u32[]{:S(2)}) copy-start(s32[4]{0:T(128)S(1)} %get-tuple-element.206.parents_ref) | copy-start | bytes 52
  128.9 332.0 %copy-start.3 = (s32[4]{0:T(128)}, s32[4]{0:T(128)S(1)}, u32[]{:S(2)}) copy-start(s32[4]{0:T(128)S(1)} %get-tuple-element.207.parents_ref) | copy-start | bytes 52
  145.0 6.4 copy-start.7
  151.4 507.4 %reduce-scatter.4.cloned.1.call-start = ((), (), s32[]{:S(2)}) async-start(), calls=%async_computation.6 | async-start | bytes 9437184 | tf_op jit(solution)/shard_map/reduce_scatter | solution.py:1292
  151.5 124.0 %copy-start.20 = (bf16[2,1,256,2048]{3,2,1,0:T(8,128)(2,1)S(1)}, bf16[2,1,256,2048]{3,2,1,0:T(8,128)(2,1)}, u32[]{:S(2)}) copy-start(bf16[2,1,256,2048]{3,2,1,0:T(8,128)(2,1)} %param.18) | copy-start | bytes 6291460
  278.2 17.0 %copy-start.61 = (f32[256]{0:T(256)}, f32[256]{0:T(256)S(1)}, u32[]{:S(2)}) copy-start(f32[256]{0:T(256)S(1)} %broadcast_multiply_fusion.5) | copy-start | bytes 3076
  279.9 158.5 %copy-start.76 = (f32[256]{0:T(256)}, f32[256]{0:T(256)S(1)}, u32[]{:S(2)}) copy-start(f32[256]{0:T(256)S(1)} %multiply_reduce_fusion.5) | copy-start | bytes 3076
  279.9 158.5 %copy-start.72 = (f32[256]{0:T(256)}, f32[256]{0:T(256)S(1)}, u32[]{:S(2)}) copy-start(f32[256]{0:T(256)S(1)} %fusion.49) | copy-start | bytes 3076
  279.9 12.3 %copy-start.40 = (f32[1,2,8,128]{3,1,2,0:T(2,128)}, f32[1,2,8,128]{3,1,2,0:T(2,128)S(1)}, u32[]{:S(2)}) copy-start(f32[1,2,8,128]{3,1,2,0:T(2,128)S(1)} %copy.82) | copy-start | bytes 24580
  280.0 15.3 %copy-start.53 = (f32[1,2,8,128]{3,1,2,0:T(2,128)}, f32[1,2,8,128]{3,1,2,0:T(2,128)S(1)}, u32[]{:S(2)}) copy-start(f32[1,2,8,128]{3,1,2,0:T(2,128)S(1)} %copy.83) | copy-start | bytes 24580
  344.7 93.7 %copy-start.41 = (f32[1,2,8,128]{3,1,2,0:T(2,128)S(1)}, f32[1,2,8,128]{3,1,2,0:T(2,128)}, u32[]{:S(2)}) copy-start(f32[1,2,8,128]{3,1,2,0:T(2,128)} %copy-done.40) | copy-start | bytes 24580
  344.7 93.7 %copy-start.62 = (f32[256]{0:T(256)S(1)}, f32[256]{0:T(256)}, u32[]{:S(2)}) copy-start(f32[256]{0:T(256)} %copy-done.61) | copy-start | bytes 3076
  451.1 9.8 copy-start.96
  460.9 14.2 %copy-start.11 = (bf16[1024,1536]{1,0:T(8,128)(2,1)}, bf16[1024,1536]{1,0:T(8,128)(2,1)S(1)}, u32[]{:S(2)}) copy-start(bf16[1024,1536]{1,0:T(8,128)(2,1)S(1)} %add_convert_fusion.3.q_ref.k_ref.v_ref) | copy-start | bytes 9437188
  475.1 183.7 %all-gather.14.cloned.1.call-start = ((), (), s32[]{:S(2)}) async-start(), calls=%async_computation.7 | async-start | bytes 9437184 | tf_op jit(solution)/shard_map/all_gather | solution.py:1275
  475.7 373.3 %all-gather.16.cloned.1.call-start = ((), (), s32[]{:S(2)}) async-start(), calls=%async_computation.8 | async-start | bytes 5242880 | tf_op jit(solution)/shard_map/all_gather | solution.py:1327
  482.0 119.7 %copy-start.21 = (bf16[2,1,256,2048]{3,2,1,0:T(8,128)(2,1)S(1)}, bf16[2,1,256,2048]{3,2,1,0:T(8,128)(2,1)}, u32[]{:S(2)}) copy-start(bf16[2,1,256,2048]{3,2,1,0:T(8,128)(2,1)} %param.18) | copy-start | bytes 6291460
  482.0 119.7 %copy-start.52 = (f32[1,2,8,128]{3,1,2,0:T(2,128)S(1)}, f32[1,2,8,128]{3,1,2,0:T(2,128)}, u32[]{:S(2)}) copy-start(f32[1,2,8,128]{3,1,2,0:T(2,128)} %copy-done.51) | copy-start | bytes 24580
  611.0 36.0 %copy-start.32 = (bf16[1024,2048]{1,0:T(8,128)(2,1)S(1)}, bf16[1024,2048]{1,0:T(8,128)(2,1)}, u32[]{:S(2)}) copy-start(bf16[1024,2048]{1,0:T(8,128)(2,1)} %get-tuple-element.52) | copy-start | bytes 12582916
  611.0 36.0 %copy-start.68 = (f32[1024]{0:T(1024)S(1)}, f32[1024]{0:T(1024)}, u32[]{:S(2)}) copy-start(f32[1024]{0:T(1024)} %copy-done.67) | copy-start | bytes 12292
  611.0 36.0 %copy-start.94 = (f32[1024]{0:T(1024)S(1)}, f32[1024]{0:T(1024)}, u32[]{:S(2)}) copy-start(f32[1024]{0:T(1024)} %copy-done.93) | copy-start | bytes 12292
  658.9 93.8 %copy-start.42 = (f32[1,2,8,128]{3,1,2,0:T(2,128)S(1)}, f32[1,2,8,128]{3,1,2,0:T(2,128)}, u32[]{:S(2)}) copy-start(f32[1,2,8,128]{3,1,2,0:T(2,128)} %copy-done.40) | copy-start | bytes 24580
  658.9 93.8 %copy-start.64 = (f32[256]{0:T(256)S(1)}, f32[256]{0:T(256)}, u32[]{:S(2)}) copy-start(f32[256]{0:T(256)} %copy-done.63) | copy-start | bytes 3076
  658.9 93.8 %copy-start.75 = (f32[256]{0:T(256)S(1)}, f32[256]{0:T(256)}, u32[]{:S(2)}) copy-start(f32[256]{0:T(256)} %copy-done.74) | copy-start | bytes 3076
  759.2 168.4 %reduce-scatter.6.cloned.1.call-start = ((), (), s32[]{:S(2)}) async-start(), calls=%async_computation.9 | async-start | bytes 5242880 | tf_op jit(solution)/shard_map/reduce_scatter | solution.py:1329
  760.2 12.8 %copy-start.111 = (bf16[2048,1024]{1,0:T(8,128)(2,1)S(1)}, bf16[2048,1024]{1,0:T(8,128)(2,1)}, u32[]{:S(2)}) copy-start(bf16[2048,1024]{1,0:T(8,128)(2,1)} %get-tuple-element.78) | copy-start | bytes 12582916
  786.2 286.1 %reduce-scatter.8.cloned.1.call-start = ((), (), s32[]{:S(2)}) async-start(), calls=%async_computation.10 | async-start | bytes 5242880 | tf_op jit(solution)/shard_map/reduce_scatter | solution.py:1331
  787.4 6.7 copy-start.36
  794.2 14.0 %copy-start.1 = (bf16[1024,1536]{1,0:T(8,128)(2,1)S(1)}, bf16[1024,1536]{1,0:T(8,128)(2,1)}, u32[]{:S(2)}) copy-start(bf16[1024,1536]{1,0:T(8,128)(2,1)} %copy-done) | copy-start | bytes 9437188
  794.2 14.0 %copy-start.33 = (bf16[1024,2048]{1,0:T(8,128)(2,1)S(1)}, bf16[1024,2048]{1,0:T(8,128)(2,1)}, u32[]{:S(2)}) copy-start(bf16[1024,2048]{1,0:T(8,128)(2,1)} %get-tuple-element.52) | copy-start | bytes 12582916
  794.2 14.0 %copy-start.49 = (f32[1,2,8,128]{3,1,2,0:T(2,128)S(1)}, f32[1,2,8,128]{3,1,2,0:T(2,128)}, u32[]{:S(2)}) copy-start(f32[1,2,8,128]{3,1,2,0:T(2,128)} %copy-done.47) | copy-start | bytes 24580
  794.2 14.0 %copy-start.69 = (f32[1024]{0:T(1024)S(1)}, f32[1024]{0:T(1024)}, u32[]{:S(2)}) copy-start(f32[1024]{0:T(1024)} %copy-done.67) | copy-start | bytes 12292
  794.2 14.0 %copy-start.88 = (f32[1,2,8,128]{3,1,2,0:T(2,128)S(1)}, f32[1,2,8,128]{3,1,2,0:T(2,128)}, u32[]{:S(2)}) copy-start(f32[1,2,8,128]{3,1,2,0:T(2,128)} %copy-done.86) | copy-start | bytes 24580
  794.2 14.0 %copy-start.95 = (f32[1024]{0:T(1024)S(1)}, f32[1024]{0:T(1024)}, u32[]{:S(2)}) copy-start(f32[1024]{0:T(1024)} %copy-done.93) | copy-start | bytes 12292
  808.2 11.6 %copy-start.57 = (f32[2048]{0:T(1024)S(1)}, f32[2048]{0:T(1024)}, u32[]{:S(2)}) copy-start(f32[2048]{0:T(1024)} %get-tuple-element.158) | copy-start | bytes 24580
  808.2 11.6 %copy-start.56 = (f32[2048]{0:T(1024)S(1)}, f32[2048]{0:T(1024)}, u32[]{:S(2)}) copy-start(f32[2048]{0:T(1024)} %get-tuple-element.140) | copy-start | bytes 24580
  808.2 11.7 %copy-start.55 = (f32[2048]{0:T(1024)S(1)}, f32[2048]{0:T(1024)}, u32[]{:S(2)}) copy-start(f32[2048]{0:T(1024)} %get-tuple-element.155) | copy-start | bytes 24580
  844.0 10.1 copy-start.4
  854.2 34.7 %copy-start.30 = (bf16[1024,2048]{1,0:T(8,128)(2,1)S(1)}, bf16[1024,2048]{1,0:T(8,128)(2,1)}, u32[]{:S(2)}) copy-start(bf16[1024,2048]{1,0:T(8,128)(2,1)} %all-gather.8.cloned.1.call-done) | copy-start | bytes 12582916
  854.2 34.7 %copy-start.71 = (f32[1024]{0:T(1024)S(1)}, f32[1024]{0:T(1024)}, u32[]{:S(2)}) copy-start(f32[1024]{0:T(1024)} %copy-done.70) | copy-start | bytes 12292
  854.2 34.7 %copy-start.97 = (f32[1024]{0:T(1024)S(1)}, f32[1024]{0:T(1024)}, u32[]{:S(2)}) copy-start(f32[1024]{0:T(1024)} %copy-done.96) | copy-start | bytes 12292
  888.9 12.3 %copy-start.2 = (bf16[1024,1536]{1,0:T(8,128)(2,1)}, bf16[1024,1536]{1,0:T(8,128)(2,1)S(1)}, u32[]{:S(2)}) copy-start(bf16[1024,1536]{1,0:T(8,128)(2,1)S(1)} %attend_back.3) | copy-start | bytes 9437188
  902.7 14.1 %copy-start.10 = (bf16[1024,512]{1,0:T(8,128)(2,1)S(1)}, bf16[1024,512]{1,0:T(8,128)(2,1)}, u32[]{:S(2)}) copy-start(bf16[1024,512]{1,0:T(8,128)(2,1)} %copy-done.9) | copy-start | bytes 3145732
  902.7 14.1 %copy-start.108 = (bf16[1024,2048]{1,0:T(8,128)(2,1)S(1)}, bf16[1024,2048]{1,0:T(8,128)(2,1)}, u32[]{:S(2)}) copy-start(bf16[1024,2048]{1,0:T(8,128)(2,1)} %all-gather.16.cloned.1.call-done) | copy-start | bytes 12582916
  902.8 14.1 %copy-start.109 = (f32[2048,512]{1,0:T(8,128)S(1)}, f32[2048,512]{1,0:T(8,128)}, u32[]{:S(2)}) copy-start(f32[2048,512]{1,0:T(8,128)} %fusion.70) | copy-start | bytes 12582916
  1100.5 4.6 copy-start.81
  1100.5 4.6 copy-start.83
  1105.1 6.8 copy-start.38
  1105.1 6.7 copy-start.39
  1105.1 6.7 copy-start.60
  (57 other events, 137.8 us)
Sparse Core Ops, SparseCore 0:
  10.8 90.9 all-gather.17
  128.2 129.9 all-gather.11
  259.8 84.8 all-gather.9
  346.7 80.2 all-gather.7
  475.3 70.0 reduce-scatter.3
  547.3 54.3 all-gather.13
  759.3 89.6 all-gather.15
  851.4 75.2 reduce-scatter.5
  929.0 140.3 reduce-scatter.7

commit v5 on v4

--- a/solution.py
+++ b/solution.py
@@ -218,6 +218,12 @@
                                 + self.come[way, step - 2, part].astype(F32)
                             ).astype(BF16)
 
+                if step > 1:
+
+                    @pl.when(self.sends(step - 1, up))
+                    def _():
+                        self.hop(step - 1, up).wait_send()
+
                 self.hop(step, up).start()
 
     def finish(self):
@@ -241,11 +247,10 @@
                     part = window(i, 16)
                     self.out[part] += self.come[way, n - 2, part].astype(F32)
 
-        for step in range(1, n):
-            for up in (True, False):
-                @pl.when(self.sends(step, up))
-                def _():
-                    self.hop(step, up).wait_send()
+        for up in (True, False):
+            @pl.when(self.sends(n - 1, up))
+            def _():
+                self.hop(n - 1, up).wait_send()
 
 
 class Cube:
@@ -589,7 +594,7 @@
 
 
 def sum_kernel(counts, *refs):
-    lines, planes, gathers, swaps, small = counts
+    lines, planes, gathers, cubes, swaps, small = counts
     line, cube = Line(), Cube()
     count = sum(counts)
     ins, outs, scratch = refs[:count], refs[count : 2 * count], list(refs[2 * count :])
@@ -603,6 +608,7 @@
     sums = [LineScatter(line, *pairs.pop(0), take(7)) for _ in range(lines)]
     folds = [CubeScatter(cube, *pairs.pop(0), take(8)) for _ in range(planes)]
     lanes = [LineGather(line, *pairs.pop(0), take(5)) for _ in range(gathers)]
+    wholes = [CubeGather(cube, *pairs.pop(0), take(5)) for _ in range(cubes)]
     moves = []
     for _ in range(swaps):
         src, dst = pairs.pop(0)
@@ -632,7 +638,7 @@
                 barrier, inc=1, device_id=cube.at((cube.me + k) % cube.dp), device_id_type=MESH
             )
         peers = peers + cube.dp - 1
-    elif planes:
+    elif planes or cubes:
         cube.greet(barrier)
         peers = peers + cube.peers()
     for s in sums:
@@ -640,14 +646,18 @@
     pl.semaphore_wait(barrier, peers)
     if small:
         little.swap.start()
+    for s in sums:
+        s.step(1)
     for lane in lanes:
         lane.start()
+    for whole in wholes[:1]:
+        whole.start()
     pieces = [p for p in folds[0].order() if p] if planes else []
     per = -(-len(pieces) // (line.n - 1))
     for step in range(1, line.n):
-        for s in sums:
-            s.step(step)
         if step > 1:
+            for s in sums:
+                s.step(step)
             for lane in lanes:
                 lane.take(step - 1)
         if step == 1:
@@ -661,6 +671,10 @@
         pieces = pieces[per:]
         if step == 1 and swaps:
             swap.start()
+        for whole in wholes[step - 1 : step]:
+            whole.finish()
+        for whole in wholes[step : step + 1]:
+            whole.start()
     for f in folds:
         f.finish()
     for lane in lanes:
@@ -674,7 +688,7 @@
         little.finish()
 
 
-def exchange(collective_id, lines=(), planes=(), gathers=(), swaps=(), small=()):
+def exchange(collective_id, lines=(), planes=(), gathers=(), cubes=(), swaps=(), small=()):
     dp, n = lax.axis_size("dp"), lax.axis_size("tensor")
     out_shape, out_specs, scratch = [], [], []
     for part in lines:
@@ -692,6 +706,11 @@
         out_shape.append(jax.ShapeDtypeStruct((n * rows, d), BF16))
         out_specs.append(ANY)
         scratch += LineGather.sems(n)
+    for part in cubes:
+        rows, d = part.shape
+        out_shape.append(jax.ShapeDtypeStruct((dp * rows, d), BF16))
+        out_specs.append(ANY)
+        scratch += CubeGather.sems(dp // 2)
     for part in swaps:
         rows, d = part.shape
         out_shape.append(jax.ShapeDtypeStruct((dp * rows, d // dp), BF16))
@@ -703,8 +722,8 @@
         out_shape.append(jax.ShapeDtypeStruct((rows, d), F32))
         out_specs.append(VMEM)
         scratch += SmallSum.scratch(dp, n, rows, d)
-    counts = tuple(len(g) for g in (lines, planes, gathers, swaps, small))
-    operands = [part for group in (lines, planes, gathers, swaps, small) for part in group]
+    counts = tuple(len(g) for g in (lines, planes, gathers, cubes, swaps, small))
+    operands = [part for group in (lines, planes, gathers, cubes, swaps, small) for part in group]
     return pl.pallas_call(
         functools.partial(sum_kernel, counts),
         out_shape=tuple(out_shape),
@@ -1241,14 +1260,14 @@
     bias_e = lax.all_gather(bias_e.transpose(1, 0, 2).reshape(1, mine), "tensor", axis=1, tiled=True)
     bias_e = bias_e.astype(F32)
 
-    seq_grad = [lax.all_gather(dy_low[0], "dp", axis=0, tiled=True)]
     seq_x = [seq_x0]
-    side = 0 if mine % 128 == 0 else 1
-    w_e = lax.all_gather(after(w_e, seq_grad[0]), "tensor", axis=side, tiled=True)
+    w_r = lax.all_gather(w_r, "tensor", axis=0, tiled=True)
+    if mine % 128:
+        w_e = lax.all_gather(w_e, "tensor", axis=1, tiled=True)
 
     normal_one, seq_one, qkv, attended, hidden, normed_two = [], [], [], [], [], []
     out_part, seq_two, activated, d_pre, d_hidden, d_branch, seq_branch = [], [], [], [], [], [], []
-    d_qkv, d_one, out_sum = [], [], []
+    d_qkv, d_one = [], []
     g_gain_two = g_shift_two = g_bias_red = g_bias_out = g_bias_e = 0.0
     g_gain_one = g_shift_one = g_bias_qkv = 0.0
     for m in micros:
@@ -1257,23 +1276,20 @@
         qkv.append(
             (jnp.dot(seq_one[m], w_qkv, preferred_element_type=F32) + bias_qkv).astype(BF16)
         )
-        if m == 0:
-            w_r = lax.all_gather(after(w_r, qkv[m]), "tensor", axis=0, tiled=True)
         attended.append(attend(parents[m, 0], qkv[m], width))
         branch = over(attended[m], w_ot, 1, 1).astype(BF16)
+        if m == 0:
+            others = [w_e] if mine % 128 == 0 else []
+            branch, *full = exchange(3, lines=[branch], gathers=others, cubes=dy_low)
+            w_e = full[0] if others else w_e
+            seq_grad = full[len(others) :]
+        else:
+            branch = lax.psum_scatter(branch, "tensor", scatter_dimension=0, tiled=True).astype(F32)
         if m < last:
-            next_x = lax.all_gather(after(x_low[m + 1], branch), "tensor", axis=0, tiled=True)
-        if m == 0:
-            (branch,) = exchange(3, lines=[branch])
-        else:
-            branch, full = exchange(4, lines=[branch], gathers=[d_branch[m - 1]])
-            seq_branch.append(full)
+            next_x, branch = lax.optimization_barrier((x_low[m + 1], branch))
+            next_x = lax.all_gather(next_x, "tensor", axis=0, tiled=True)
         hidden.append(x_low[m].astype(F32) + (branch + bias_out))
         normed_two.append(layer_norm(hidden[m], gain_two, shift_two).astype(BF16))
-        if m < last:
-            seq_grad.append(
-                lax.all_gather(after(dy_low[m + 1], normed_two[m]), "dp", axis=0, tiled=True)
-            )
 
         def attention_back(k):
             d_att = jnp.dot(seq_branch[k], w_ot, preferred_element_type=F32).astype(BF16)
@@ -1288,10 +1304,10 @@
 
         own = None
         if m:
-            part, attended[m] = lax.optimization_barrier((out_part[m - 1], attended[m]))
-            part = lax.psum_scatter(part, "dp", scatter_dimension=0, tiled=True)
-            normed_two[m], part = lax.optimization_barrier((normed_two[m], part))
-            out_sum.append(part.astype(F32))
+            seq_branch.append(lax.all_gather(d_branch[m - 1], "tensor", axis=0, tiled=True))
+            g_r = over(activated[m - 1], seq_grad[m - 1], 0, 0) + (g_r if m > 1 else 0.0)
+            g_et = over(d_pre[m - 1], seq_two[m - 1], 0, 0) + (g_et if m > 1 else 0.0)
+            normed_two[m], g_r, g_et = lax.optimization_barrier((normed_two[m], g_r, g_et))
             gain, shift, bias = attention_back(m - 1)
             g_gain_one, g_shift_one = g_gain_one + gain, g_shift_one + shift
             g_bias_qkv = g_bias_qkv + bias
@@ -1315,7 +1331,8 @@
         g_bias_out = g_bias_out + jnp.sum(d_branch[m].astype(F32), 0, keepdims=True)
         g_bias_e = g_bias_e + jnp.sum(dpre.astype(F32), 0)
         if m < last:
-            seq_x.append(after(next_x, d_branch[m]))
+            next_x, d_branch[m] = lax.optimization_barrier((next_x, d_branch[m]))
+            seq_x.append(next_x)
 
     def outer(left, right):
         out = None
@@ -1324,12 +1341,19 @@
             out = term if out is None else out + term
         return out.astype(BF16)
 
-    seq_branch.append(lax.all_gather(d_branch[last], "tensor", axis=0, tiled=True))
-    g_r = outer(activated, seq_grad)
-    g_r = lax.psum_scatter(after(g_r, d_branch[last]), "tensor", scatter_dimension=0, tiled=True)
-    g_et = outer(d_pre, seq_two)
-    g_et_sum = lax.psum_scatter(g_et, "tensor", scatter_dimension=0, tiled=True)
-    seq_branch[last] = after(seq_branch[last], g_et)
+    def closing(so_far, left, right):
+        term = over(left, right, 0, 0)
+        return (term if last == 0 else so_far + term).astype(BF16)
+
+    g_r = closing(g_r, activated[last], seq_grad[last])
+    branch_last, g_r = lax.optimization_barrier((d_branch[last], g_r))
+    g_r = lax.psum_scatter(g_r, "tensor", scatter_dimension=0, tiled=True)
+    *out_sum, full = exchange(4, planes=out_part, gathers=[branch_last])
+    full, dpre = lax.optimization_barrier((full, d_pre[last]))
+    g_et = closing(g_et, dpre, seq_two[last])
+    full, g_et, g_r = lax.optimization_barrier((full, g_et, g_r))
+    g_et = lax.psum_scatter(g_et, "tensor", scatter_dimension=0, tiled=True)
+    seq_branch.append(full)
     gain, shift, bias = attention_back(last)
     g_gain_one, g_shift_one = g_gain_one + gain, g_shift_one + shift
     g_bias_qkv = g_bias_qkv + bias
@@ -1351,11 +1375,9 @@
     little = jnp.pad(little, ((0, 0), (0, -little.shape[1] % 1024))).reshape(dp, -1, 128)
 
     g_attn = jnp.concatenate([outer(seq_one, d_qkv), outer(seq_branch, attended)], axis=1)
-    d_one[last], g_attn, out_last, g_reduce, little = exchange(
-        5, lines=[d_one[last]], planes=[g_attn, out_part[last]], swaps=[g_r], small=[little]
+    d_one[last], g_attn, g_reduce, g_expand, little = exchange(
+        5, lines=[d_one[last]], planes=[g_attn], swaps=[g_r, g_et], small=[little]
     )
-    out_sum.append(out_last)
-    (g_expand,) = exchange(6, swaps=[after(g_et_sum, little)])
     g_expand = g_expand.T.astype(F32)
     g_reduce = g_reduce.astype(F32)
     g_query, g_key, g_value = [g_attn[:, i * width : (i + 1) * width] for i in range(3)]

time: 1130 us -> 1080 us (0.956)
  waiting for transfers between devices: 55.7 us -> 10.8 us
  Pallas kernels: 782 us -> 754 us
    all_gather x6 -> x3, waiting for transfers between devices: 54.4 us -> 2.87 us  [the longest x1 2.87 us: body(): lax.all_gather(d_branch[m - 1], 'tensor', axis=0, tiled=True)]
    pallas_call x4 -> x3, Pallas kernels: 401 us -> 381 us  [exchange(): pl.pallas_call(functools.partial(sum_kernel, counts), out_shape=tuple(out...]
    pallas_call x1, Pallas kernels: 95.8 us -> 79.2 us  [front(): pl.pallas_call(front_kernel, out_shape=(jax.ShapeDtypeStruct((n * rows, m...]
  transfers between devices with their start and end apart: 9 -> 6, of which waited for: 2 -> 2; matrix products, arithmetic and copies ran while one was open for 17% -> 18% of each run, Pallas kernels for 59% -> 46%
where the time goes in v5:
time: 1080 us; the launch traced here: 1070 us
  Pallas kernels  754 us (70%)
  matrix products  164 us (15%)
  other arithmetic  71.2 us (7%)
  local copies, waits for them, and re-layouts  29.4 us (3%)
  between operations  16.3 us (2%)
  waiting for transfers between devices  10.8 us (1%)
    pallas_call x3, Pallas kernels, exchange(): pl.pallas_call(functools.partial(sum_kernel, counts), out_shape=tuple(out...  381 us
    pallas_call x2, Pallas kernels, ffn(): pl.pallas_call(functools.partial(ffn_kernel, host), out_shape=(jax.ShapeD...  196 us
    dot_general x12, matrix products, over(): lax.dot_general(left, right, (((on_left,), (on_right,)), ((), ())), prefe...  133 us
    pallas_call x1, Pallas kernels, front(): pl.pallas_call(front_kernel, out_shape=(jax.ShapeDtypeStruct((n * rows, m...  79.2 us
    pallas_call x2, Pallas kernels, attend_back(): pl.pallas_call(attend_back_kernel, out_shape=jax.ShapeDtypeStruct((rows,...  69.1 us
    pallas_call x2, Pallas kernels, attend(): pl.pallas_call(attend_kernel, out_shape=jax.ShapeDtypeStruct((rows, width...  28.4 us
  transfers between devices with their start and end apart: 6, of which 2 were waited for; matrix products, arithmetic and copies ran while one was open for 18% of the time, Pallas kernels for 46%

profile of v5, /device:TPU:0, one launch (start us, length us, event | category | flops | bytes accessed | tf_op | source)
XLA Modules:
  0.0 1065.4 jit_solution(13407072218939553129)
XLA Ops:
  7.4 3.3 slice_bitcast_fusion.3
  11.9 1.1 pad_maximum_fusion.1.w_ref
  13.0 79.2 %front.1 = (bf16[1024,2048]{1,0:T(8,128)(2,1)}, bf16[2048,2048]{1,0:T(8,128)(2,1)}, bf16[2048,256]{1,0:T(8,128)(2,1)}, bf16[256,2048]{1,0:T(8,128)(2,1)}, bf16[128,128]{1,0:T(8,128)(2,1)}) custom-call(bf16[256,2048]{1,0:T(8,128)(2,1)} %get-tuple-element.193.x_ref, bf16[256,2048]{1,0:T(8,128)(2,1)} %pad_maximum_fusion.1.w_ref, bf16[256,2048]{1,0:T(8,128)(2,1)} %we_ref.1, ...), custom_call_target="tpu_custom_call" | custom-call | flops 80000000000 | bytes 10000000 | tf_op jit(solution)/shard_map/front/pallas_call | solution.py:526
  92.3 0.8 reshape.472
  93.2 3.0 convert_reduce_fusion.3
  96.7 1.2 fusion.11
  98.5 11.4 %add_convert_fusion.4.q_ref.k_ref.v_ref = bf16[1024,1536]{1,0:T(8,128)(2,1)S(1)} fusion(bf16[2048,2048]{1,0:T(8,128)(2,1)} %get-tuple-element.61, f32[1536]{0:T(1024)S(1)} %fusion.49, bf16[1024,2048]{1,0:T(8,128)(2,1)} %get-tuple-element.59, f32[2048]{0:T(1024)S(1)} %bitcast.200, f32[2048]{0:T(1024)S(1)} %bitcast.185, f32[1024]{0:T(1024)S(1)} %add_rsqrt_fusion.1, ...), kind=kOutput, calls=%fused_computation.31 | convolution fusion | flops 6458179584 | bytes 13662208 | tf_op jit(solution)/shard_map/dot_general | solution.py:1277
  110.0 14.2 %attend.2 = bf16[1024,512]{1,0:T(8,128)(2,1)S(1)} custom-call(s32[4]{0:T(128)S(1)} %get-tuple-element.220.parents_ref, bf16[1024,1536]{1,0:T(8,128)(2,1)S(1)} %add_convert_fusion.4.q_ref.k_ref.v_ref, bf16[1024,1536]{1,0:T(8,128)(2,1)S(1)} %add_convert_fusion.4.q_ref.k_ref.v_ref, bf16[1024,1536]{1,0:T(8,128)(2,1)S(1)} %add_convert_fusion.4.q_ref.k_ref.v_ref), custom_call_target="tpu_custom_call" | custom-call | flops 16106127360 | bytes 4194304 | tf_op jit(solution)/shard_map/attend/pallas_call | solution.py:808
  124.2 6.3 convolution_convert_fusion.1.refs_0_
  130.6 1.5 slice_bitcast_fusion
  132.0 156.2 %exchange.3 = (f32[256,2048]{1,0:T(8,128)}, bf16[8192,256]{1,0:T(8,128)(2,1)}, bf16[2048,2048]{1,0:T(8,128)(2,1)}, bf16[2048,2048]{1,0:T(8,128)(2,1)}) custom-call(bf16[1024,2048]{1,0:T(8,128)(2,1)} %convolution_convert_fusion.1.refs_0_, bf16[2048,256]{1,0:T(8,128)(2,1)} %get-tuple-element.62.refs_1_, bf16[256,2048]{1,0:T(8,128)(2,1)} %get-tuple-element.192.refs_2_, ...), custom_call_target="tpu_custom_call" | custom-call | flops 80000000000 | bytes 10000000 | tf_op jit(solution)/shard_map/exchange/pallas_call | solution.py:727
  288.4 2.0 fusion.65
  290.4 1.3 copy-done.15
  292.4 9.7 all_gather.13
  303.3 3.0 add_convert_fusion.11.n2_ref
  306.4 92.5 %ffn_plane.2 = (f32[256,2048]{1,0:T(8,128)}, bf16[2048,2048]{1,0:T(8,128)(2,1)}, bf16[2048,1024]{1,0:T(8,128)(2,1)}, bf16[2048,1024]{1,0:T(8,128)(2,1)}, bf16[2048,2048]{1,0:T(8,128)(2,1)}) custom-call(bf16[256,2048]{1,0:T(8,128)(2,1)} %add_convert_fusion.11.n2_ref, bf16[2048,2048]{1,0:T(8,128)(2,1)} %get-tuple-element.65.dy_ref, ...), custom_call_target="tpu_custom_call" | custom-call | flops 154618822656 | bytes 50331648 | tf_op jit(solution)/shard_map/ffn_plane/pallas_call | solution.py:1160
  399.0 3.7 multiply_reduce_fusion.1
  403.4 1.3 copy-done.25
  404.7 2.2 convert_reduce_fusion.10
  406.9 10.0 reduce-scatter.4.cloned.1.call-start
  416.9 3.0 convert_reduce_fusion.2
  420.3 1.2 fusion.10
  421.6 9.9 add_convert_fusion.3.q_ref.k_ref.v_ref
  432.2 14.2 %attend.3 = bf16[1024,512]{1,0:T(8,128)(2,1)S(1)} custom-call(s32[4]{0:T(128)S(1)} %get-tuple-element.219.parents_ref, bf16[1024,1536]{1,0:T(8,128)(2,1)S(1)} %add_convert_fusion.3.q_ref.k_ref.v_ref, bf16[1024,1536]{1,0:T(8,128)(2,1)S(1)} %add_convert_fusion.3.q_ref.k_ref.v_ref, bf16[1024,1536]{1,0:T(8,128)(2,1)S(1)} %add_convert_fusion.3.q_ref.k_ref.v_ref), custom_call_target="tpu_custom_call" | custom-call | flops 16106127360 | bytes 4194304 | tf_op jit(solution)/shard_map/attend/pallas_call | solution.py:808
  446.4 1.0 copy-done.8
  447.4 6.0 convolution_convert_fusion
  453.4 14.9 %fusion.67 = f32[1024,2048]{1,0:T(8,128)} fusion(bf16[2048,1024]{1,0:T(8,128)(2,1)} %get-tuple-element.72, bf16[2048,2048]{1,0:T(8,128)(2,1)} %get-tuple-element.65.dy_ref), kind=kOutput, calls=%fused_computation.171 | convolution fusion | flops 8589934592 | bytes 20971520 | tf_op jit(solution)/shard_map/dot_general | solution.py:32
  468.3 13.8 %fusion.68 = f32[1024,2048]{1,0:T(8,128)} fusion(bf16[2048,1024]{1,0:T(8,128)(2,1)S(1)} %copy-done.33, bf16[2048,2048]{1,0:T(8,128)(2,1)} %get-tuple-element.74), kind=kOutput, calls=%fused_computation.172 | convolution fusion | flops 8589934592 | bytes 20971520 | tf_op jit(solution)/shard_map/dot_general | solution.py:32
  482.2 2.9 all-gather.8.cloned.1.call-done
  485.1 5.3 convolution_convert_fusion.3.g_ref
  490.4 4.5 fusion.69
  494.9 34.6 %attend_back.2 = bf16[1024,1536]{1,0:T(8,128)(2,1)S(1)} custom-call(s32[4]{0:T(128)S(1)} %copy-done.5, bf16[1024,1536]{1,0:T(8,128)(2,1)} %copy-done.9, bf16[1024,1536]{1,0:T(8,128)(2,1)} %copy-done.9, bf16[1024,1536]{1,0:T(8,128)(2,1)} %copy-done.9, bf16[1024,512]{1,0:T(8,128)(2,1)S(1)} %convolution_convert_fusion.3.g_ref), custom_call_target="tpu_custom_call" | custom-call | flops 40265318400 | bytes 7340032 | tf_op jit(solution)/shard_map/attend_back/pallas_call | solution.py:884
  529.6 13.1 %convert_reduce_fusion.1 = (f32[2048]{0:T(1024)}, f32[2048]{0:T(1024)}, bf16[1024,2048]{1,0:T(8,128)(2,1)}) fusion(f32[1024]{0:T(1024)S(1)} %copy-done.92, f32[1024]{0:T(1024)S(1)} %copy-done.69, bf16[1024,2048]{1,0:T(8,128)(2,1)S(1)} %copy-done.31, bf16[1024,1536]{1,0:T(8,128)(2,1)S(1)} %attend_back.2, bf16[2048,2048]{1,0:T(8,128)(2,1)} %get-tuple-element.61), kind=kOutput, calls=%fused_computation.3 | convolution fusion | flops 6459224064 | bytes 17850368 | tf_op jit(solution)/shard_map/dot_general | solution.py:32
  542.7 12.0 %fusion.58 = f32[2048,1536]{1,0:T(8,128)} fusion(bf16[1024,1536]{1,0:T(8,128)(2,1)S(1)} %attend_back.2, bf16[1024,2048]{1,0:T(8,128)(2,1)S(1)} %copy-done.31, f32[2048]{0:T(1024)S(1)} %bitcast.202, f32[2048]{0:T(1024)S(1)} %bitcast.187, f32[1024]{0:T(1024)S(1)} %copy-done.92, f32[1024]{0:T(1024)S(1)} %copy-done.69), kind=kOutput, calls=%fused_computation.166 | convolution fusion | flops 6455033856 | bytes 19947520 | tf_op jit(solution)/shard_map/dot_general | solution.py:32
  554.7 7.8 reduce-scatter.4.cloned.1.call-done
  562.5 1.8 fusion.37
  564.9 1.6 add_convert_fusion.10.n2_ref
  566.6 103.0 %ffn_plane.3 = (f32[256,2048]{1,0:T(8,128)}, bf16[2048,2048]{1,0:T(8,128)(2,1)}, bf16[2048,1024]{1,0:T(8,128)(2,1)}, bf16[2048,1024]{1,0:T(8,128)(2,1)}, bf16[20...) custom-call(bf16[256,2048]{1,0:T(8,128)(2,1)} %add_convert_fusion.10.n2_ref, bf16[2048,2048]{1,0:T(8,128)(2,1)} %get-tuple-element.76.dy_ref, ...), custom_call_target="tpu_custom_call" | custom-call | flops 154618822656 | bytes 50331648 | tf_op jit(solution)/shard_map/ffn_plane/pallas_call | solution.py:1160
  669.8 3.8 multiply_reduce_fusion
  674.8 2.6 fusion.63
  677.5 1.6 convert_reduce_fusion.12
  679.7 15.2 %add_convert_fusion.2 = bf16[1024,2048]{1,0:T(8,128)(2,1)} fusion(f32[1024,2048]{1,0:T(8,128)} %fusion.67, bf16[2048,1024]{1,0:T(8,128)(2,1)} %get-tuple-element.81, bf16[2048,2048]{1,0:T(8,128)(2,1)} %get-tuple-element.76.dy_ref), kind=kOutput, calls=%fused_computation.27 | convolution fusion | flops 8594128896 | bytes 25165824 | tf_op jit(solution)/shard_map/dot_general | solution.py:32
  695.0 147.6 %exchange.4 = (f32[256,2048]{1,0:T(8,128)}, f32[256,2048]{1,0:T(8,128)}, bf16[1024,2048]{1,0:T(8,128)(2,1)}) custom-call(bf16[2048,2048]{1,0:T(8,128)(2,1)} %get-tuple-element.68.refs_0_, bf16[2048,2048]{1,0:T(8,128)(2,1)} %get-tuple-element.78.refs_1_, bf16[256,2048]{1,0:T(8,128)(2,1)} %get-tuple-element.82.refs_2_), custom_call_target="tpu_custom_call" | custom-call | flops 80000000000 | bytes 10000000 | tf_op jit(solution)/shard_map/exchange/pallas_call | solution.py:727
  842.6 5.1 convert_reduce_fusion.4
  849.1 15.2 %add_convert_fusion.1 = bf16[1024,2048]{1,0:T(8,128)(2,1)} fusion(f32[1024,2048]{1,0:T(8,128)} %fusion.68, bf16[2048,1024]{1,0:T(8,128)(2,1)} %get-tuple-element.90, bf16[2048,2048]{1,0:T(8,128)(2,1)} %get-tuple-element.91), kind=kOutput, calls=%fused_computation.26 | convolution fusion | flops 8594128896 | bytes 25165824 | tf_op jit(solution)/shard_map/dot_general | solution.py:32
  864.3 5.2 convolution_convert_fusion.2.g_ref
  869.6 34.5 %attend_back.3 = bf16[1024,1536]{1,0:T(8,128)(2,1)S(1)} custom-call(s32[4]{0:T(128)S(1)} %get-tuple-element.219.parents_ref, bf16[1024,1536]{1,0:T(8,128)(2,1)} %copy-done.10, bf16[1024,1536]{1,0:T(8,128)(2,1)} %copy-done.10, bf16[1024,1536]{1,0:T(8,128)(2,1)} %copy-done.10, bf16[1024,512]{1,0:T(8,128)(2,1)S(1)} %convolution_convert_fusion.2.g_ref), custom_call_target="tpu_custom_call" | custom-call | flops 40265318400 | bytes 7340032 | tf_op jit(solution)/shard_map/attend_back/pallas_call | solution.py:884
  904.2 12.7 %convert_reduce_fusion = (f32[2048]{0:T(1024)S(1)}, f32[2048]{0:T(1024)S(1)}, bf16[1024,2048]{1,0:T(8,128)(2,1)}) fusion(f32[1024]{0:T(1024)S(1)} %copy-done.90, f32[1024]{0:T(1024)S(1)} %copy-done.67, bf16[1024,2048]{1,0:T(8,128)(2,1)S(1)} %copy-done.28, bf16[1024,1536]{1,0:T(8,128)(2,1)S(1)} %attend_back.3, bf16[2048,2048]{1,0:T(8,128)(2,1)} %get-tuple-element.61), kind=kOutput, calls=%fused_computation.1 | convolution fusion | flops 6459224064 | bytes 17850368 | tf_op jit(solution)/shard_map/dot_general | solution.py:32
  917.0 3.1 convert_reduce_fusion.6
  921.2 6.3 add_convert_fusion.5
  927.6 12.4 %add_convert_fusion = bf16[2048,1536]{1,0:T(8,128)(2,1)} fusion(f32[2048,1536]{1,0:T(8,128)} %fusion.58, bf16[1024,1536]{1,0:T(8,128)(2,1)S(1)} %copy-done.3, bf16[1024,2048]{1,0:T(8,128)(2,1)S(1)} %copy-done.29, f32[1024]{0:T(1024)S(1)} %copy-done.90, f32[1024]{0:T(1024)S(1)} %copy-done.67, f32[2048]{0:T(1024)S(1)} %bitcast.203, f32[2048]{0:T(1024)S(1)} %bitcast.188), kind=kOutput, calls=%fused_computation | convolution fusion | flops 6461325312 | bytes 26238976 | tf_op jit(solution)/shard_map/dot_general | solution.py:32
  940.0 7.4 pad_maximum_fusion.refs_1_
  947.4 77.5 %exchange.5 = (f32[256,2048]{1,0:T(8,128)}, f32[256,2048]{1,0:T(8,128)}, bf16[2048,256]{1,0:T(8,128)(2,1)}, bf16[2048,256]{1,0:T(8,128)(2,1)}, f32[24,128]{1,0:T(8,128)}) custom-call(bf16[1024,2048]{1,0:T(8,128)(2,1)} %get-tuple-element.222.refs_0_, bf16[2048,2048]{1,0:T(8,128)(2,1)} %pad_maximum_fusion.refs_1_, ...), custom_call_target="tpu_custom_call" | custom-call | flops 80000000000 | bytes 10000000 | tf_op jit(solution)/shard_map/exchange/pallas_call | solution.py:727
  1026.3 1.4 slice_bitcast_fusion.5
  1027.8 3.6 fusion.35
  1031.5 5.0 fusion.55
  1036.5 1.5 convert_bitcast_fusion
  1038.0 2.9 copy.74
  1040.9 2.9 slice_bitcast_fusion.4
  1043.8 2.0 copy.73
  1045.8 2.7 convert_element_type.293
  1049.4 5.1 fusion.46
  1054.5 1.5 maximum_bitcast_fusion.1
  1056.0 1.5 maximum_bitcast_fusion
  (310 shorter events, 14.4 us)
Async XLA Ops:
  7.2 3.9 copy-start.97
  7.3 4.6 copy-start.46
  7.3 4.6 copy-start.45
  7.3 4.6 copy-start.44
  7.3 299.0 %all-gather.4.cloned.1.call-start = ((), (), s32[]{:S(2)}) async-start(), calls=%async_computation.3 | async-start | bytes 5242880 | tf_op jit(solution)/shard_map/all_gather | solution.py:1264
  92.2 314.6 %all-gather.6.cloned.1.call-start = ((), (), s32[]{:S(2)}) async-start(), calls=%async_computation.4 | async-start | bytes 5242880 | tf_op jit(solution)/shard_map/all_gather | solution.py:1290
  98.0 12.0 %copy-start.91 = (f32[1024]{0:T(1024)}, f32[1024]{0:T(1024)S(1)}, u32[]{:S(2)}) copy-start(f32[1024]{0:T(1024)S(1)} %add_rsqrt_fusion.1) | copy-start | bytes 12292
  98.0 11.9 %copy-start.47 = (f32[1,2,8,128]{3,1,2,0:T(2,128)}, f32[1,2,8,128]{3,1,2,0:T(2,128)S(1)}, u32[]{:S(2)}) copy-start(f32[1,2,8,128]{3,1,2,0:T(2,128)S(1)} %copy.79) | copy-start | bytes 24580
  98.4 11.6 %copy-start.84 = (f32[1,2,8,128]{3,1,2,0:T(2,128)}, f32[1,2,8,128]{3,1,2,0:T(2,128)S(1)}, u32[]{:S(2)}) copy-start(f32[1,2,8,128]{3,1,2,0:T(2,128)S(1)} %copy.80) | copy-start | bytes 24580
  98.4 11.6 %copy-start.4 = (s32[4]{0:T(128)}, s32[4]{0:T(128)S(1)}, u32[]{:S(2)}) copy-start(s32[4]{0:T(128)S(1)} %get-tuple-element.220.parents_ref) | copy-start | bytes 52
  98.5 11.5 %copy-start.87 = (f32[1536]{0:T(1024)}, f32[1536]{0:T(1024)S(1)}, u32[]{:S(2)}) copy-start(f32[1536]{0:T(1024)S(1)} %fusion.49) | copy-start | bytes 18436
  110.0 14.2 %copy-start.9 = (bf16[1024,1536]{1,0:T(8,128)(2,1)}, bf16[1024,1536]{1,0:T(8,128)(2,1)S(1)}, u32[]{:S(2)}) copy-start(bf16[1024,1536]{1,0:T(8,128)(2,1)S(1)} %add_convert_fusion.4.q_ref.k_ref.v_ref) | copy-start | bytes 9437188
  124.2 6.4 copy-start.6
  124.2 6.4 copy-start.21
  132.0 156.3 %copy-start.11 = (bf16[2,1,256,2048]{3,2,1,0:T(8,128)(2,1)S(1)}, bf16[2,1,256,2048]{3,2,1,0:T(8,128)(2,1)}, u32[]{:S(2)}) copy-start(bf16[2,1,256,2048]{3,2,1,0:T(8,128)(2,1)} %param.18) | copy-start | bytes 6291460
  288.3 196.8 %all-gather.8.cloned.1.call-start = ((), (), s32[]{:S(2)}) async-start(), calls=%async_computation.6 | async-start | bytes 5242880 | tf_op jit(solution)/shard_map/all_gather | solution.py:1307
  290.4 15.9 %copy-start.60 = (f32[256]{0:T(256)}, f32[256]{0:T(256)S(1)}, u32[]{:S(2)}) copy-start(f32[256]{0:T(256)S(1)} %broadcast_multiply_fusion.5) | copy-start | bytes 3076
  292.1 106.8 %copy-start.74 = (f32[256]{0:T(256)}, f32[256]{0:T(256)S(1)}, u32[]{:S(2)}) copy-start(f32[256]{0:T(256)S(1)} %multiply_reduce_fusion.5) | copy-start | bytes 3076
  292.1 106.8 %copy-start.70 = (f32[256]{0:T(256)}, f32[256]{0:T(256)S(1)}, u32[]{:S(2)}) copy-start(f32[256]{0:T(256)S(1)} %fusion.50) | copy-start | bytes 3076
  292.1 11.2 %copy-start.40 = (f32[1,2,8,128]{3,1,2,0:T(2,128)}, f32[1,2,8,128]{3,1,2,0:T(2,128)S(1)}, u32[]{:S(2)}) copy-start(f32[1,2,8,128]{3,1,2,0:T(2,128)S(1)} %copy.82) | copy-start | bytes 24580
  292.1 14.2 %copy-start.50 = (f32[1,2,8,128]{3,1,2,0:T(2,128)}, f32[1,2,8,128]{3,1,2,0:T(2,128)S(1)}, u32[]{:S(2)}) copy-start(f32[1,2,8,128]{3,1,2,0:T(2,128)S(1)} %copy.83) | copy-start | bytes 24580
  306.4 92.5 %copy-start.41 = (f32[1,2,8,128]{3,1,2,0:T(2,128)S(1)}, f32[1,2,8,128]{3,1,2,0:T(2,128)}, u32[]{:S(2)}) copy-start(f32[1,2,8,128]{3,1,2,0:T(2,128)} %copy-done.40) | copy-start | bytes 24580
  306.4 92.5 %copy-start.61 = (f32[256]{0:T(256)S(1)}, f32[256]{0:T(256)}, u32[]{:S(2)}) copy-start(f32[256]{0:T(256)} %copy-done.60) | copy-start | bytes 3076
  406.9 155.6 %reduce-scatter.4.cloned.1.call-start = ((), (), s32[]{:S(2)}) async-start(), calls=%async_computation.5 | async-start | bytes 5242880 | tf_op jit(solution)/shard_map/reduce_scatter | solution.py:1287
  421.6 9.9 copy-start.89
  431.5 14.9 %copy-start.10 = (bf16[1024,1536]{1,0:T(8,128)(2,1)}, bf16[1024,1536]{1,0:T(8,128)(2,1)S(1)}, u32[]{:S(2)}) copy-start(bf16[1024,1536]{1,0:T(8,128)(2,1)S(1)} %add_convert_fusion.3.q_ref.k_ref.v_ref) | copy-start | bytes 9437188
  453.4 14.9 %copy-start.33 = (bf16[2048,1024]{1,0:T(8,128)(2,1)S(1)}, bf16[2048,1024]{1,0:T(8,128)(2,1)}, u32[]{:S(2)}) copy-start(bf16[2048,1024]{1,0:T(8,128)(2,1)} %get-tuple-element.73) | copy-start | bytes 12582916
  482.1 8.3 copy-start.7
  482.1 382.2 %reduce-scatter.6.cloned.1.call-start = ((), (), s32[]{:S(2)}) async-start(), calls=%async_computation.7 | async-start | bytes 5242880 | tf_op jit(solution)/shard_map/reduce_scatter | solution.py:1350
  485.1 5.3 copy-start.103
  490.4 4.5 copy-start.5
  494.9 34.7 %copy-start.31 = (bf16[1024,2048]{1,0:T(8,128)(2,1)S(1)}, bf16[1024,2048]{1,0:T(8,128)(2,1)}, u32[]{:S(2)}) copy-start(bf16[1024,2048]{1,0:T(8,128)(2,1)} %get-tuple-element.59) | copy-start | bytes 12582916
  494.9 34.7 %copy-start.69 = (f32[1024]{0:T(1024)S(1)}, f32[1024]{0:T(1024)}, u32[]{:S(2)}) copy-start(f32[1024]{0:T(1024)} %copy-done.68) | copy-start | bytes 12292
  494.9 34.7 %copy-start.92 = (f32[1024]{0:T(1024)S(1)}, f32[1024]{0:T(1024)}, u32[]{:S(2)}) copy-start(f32[1024]{0:T(1024)} %copy-done.91) | copy-start | bytes 12292
  529.6 13.1 %copy-start = (bf16[1024,1536]{1,0:T(8,128)(2,1)}, bf16[1024,1536]{1,0:T(8,128)(2,1)S(1)}, u32[]{:S(2)}) copy-start(bf16[1024,1536]{1,0:T(8,128)(2,1)S(1)} %attend_back.2) | copy-start | bytes 9437188
  542.7 19.8 %copy-start.12 = (bf16[2,1,256,2048]{3,2,1,0:T(8,128)(2,1)S(1)}, bf16[2,1,256,2048]{3,2,1,0:T(8,128)(2,1)}, u32[]{:S(2)}) copy-start(bf16[2,1,256,2048]{3,2,1,0:T(8,128)(2,1)} %param.18) | copy-start | bytes 6291460
  542.7 19.8 %copy-start.37 = (f32[1,2,8,128]{3,1,2,0:T(2,128)S(1)}, f32[1,2,8,128]{3,1,2,0:T(2,128)}, u32[]{:S(2)}) copy-start(f32[1,2,8,128]{3,1,2,0:T(2,128)} %copy-done.36) | copy-start | bytes 24580
  554.7 10.2 copy-start.51
  566.6 103.1 %copy-start.19 = (bf16[256,2048]{1,0:T(8,128)(2,1)S(1)}, bf16[256,2048]{1,0:T(8,128)(2,1)}, u32[]{:S(2)}) copy-start(bf16[256,2048]{1,0:T(8,128)(2,1)} %reduce-scatter.4.cloned.1.call-done) | copy-start | bytes 3145732
  566.6 103.1 %copy-start.38 = (f32[1,2,8,128]{3,1,2,0:T(2,128)S(1)}, f32[1,2,8,128]{3,1,2,0:T(2,128)}, u32[]{:S(2)}) copy-start(f32[1,2,8,128]{3,1,2,0:T(2,128)} %copy-done.36) | copy-start | bytes 24580
  566.6 103.1 %copy-start.42 = (f32[1,2,8,128]{3,1,2,0:T(2,128)S(1)}, f32[1,2,8,128]{3,1,2,0:T(2,128)}, u32[]{:S(2)}) copy-start(f32[1,2,8,128]{3,1,2,0:T(2,128)} %copy-done.40) | copy-start | bytes 24580
  566.6 103.1 %copy-start.63 = (f32[256]{0:T(256)S(1)}, f32[256]{0:T(256)}, u32[]{:S(2)}) copy-start(f32[256]{0:T(256)} %copy-done.62) | copy-start | bytes 3076
  566.6 103.1 %copy-start.73 = (f32[256]{0:T(256)S(1)}, f32[256]{0:T(256)}, u32[]{:S(2)}) copy-start(f32[256]{0:T(256)} %copy-done.72) | copy-start | bytes 3076
  669.7 4.4 copy-start.53
  669.7 5.0 copy-start.77
  669.7 5.0 copy-start.13
  695.0 252.4 %reduce-scatter.8.cloned.1.call-start = ((), (), s32[]{:S(2)}) async-start(), calls=%async_computation.8 | async-start | bytes 5242880 | tf_op jit(solution)/shard_map/reduce_scatter | solution.py:1355
  869.6 34.5 %copy-start.28 = (bf16[1024,2048]{1,0:T(8,128)(2,1)S(1)}, bf16[1024,2048]{1,0:T(8,128)(2,1)}, u32[]{:S(2)}) copy-start(bf16[1024,2048]{1,0:T(8,128)(2,1)} %all-gather.6.cloned.1.call-done) | copy-start | bytes 12582916
  869.6 34.5 %copy-start.67 = (f32[1024]{0:T(1024)S(1)}, f32[1024]{0:T(1024)}, u32[]{:S(2)}) copy-start(f32[1024]{0:T(1024)} %copy-done.66) | copy-start | bytes 12292
  869.6 34.5 %copy-start.90 = (f32[1024]{0:T(1024)S(1)}, f32[1024]{0:T(1024)}, u32[]{:S(2)}) copy-start(f32[1024]{0:T(1024)} %copy-done.89) | copy-start | bytes 12292
  904.1 12.7 %copy-start.2 = (bf16[1024,1536]{1,0:T(8,128)(2,1)}, bf16[1024,1536]{1,0:T(8,128)(2,1)S(1)}, u32[]{:S(2)}) copy-start(bf16[1024,1536]{1,0:T(8,128)(2,1)S(1)} %attend_back.3) | copy-start | bytes 9437188
  904.1 12.7 %copy-start.83 = (f32[2048]{0:T(1024)S(1)}, f32[2048]{0:T(1024)}, u32[]{:S(2)}) copy-start(f32[2048]{0:T(1024)} %get-tuple-element.158) | copy-start | bytes 24580
  904.1 12.8 %copy-start.82 = (f32[2048]{0:T(1024)S(1)}, f32[2048]{0:T(1024)}, u32[]{:S(2)}) copy-start(f32[2048]{0:T(1024)} %get-tuple-element.159) | copy-start | bytes 24580
  904.1 12.8 %copy-start.1 = (bf16[1024,1536]{1,0:T(8,128)(2,1)S(1)}, bf16[1024,1536]{1,0:T(8,128)(2,1)}, u32[]{:S(2)}) copy-start(bf16[1024,1536]{1,0:T(8,128)(2,1)} %copy-done) | copy-start | bytes 9437188
  921.2 6.3 copy-start.3
  921.2 6.3 copy-start.29
  921.2 6.3 copy-start.49
  921.2 6.3 copy-start.86
  947.4 80.3 %copy-start.14 = (bf16[2,1,256,2048]{3,2,1,0:T(8,128)(2,1)S(1)}, bf16[2,1,256,2048]{3,2,1,0:T(8,128)(2,1)}, u32[]{:S(2)}) copy-start(bf16[2,1,256,2048]{3,2,1,0:T(8,128)(2,1)} %param.18) | copy-start | bytes 6291460
  947.4 80.3 %copy-start.64 = (f32[256]{0:T(256)S(1)}, f32[256]{0:T(256)}, u32[]{:S(2)}) copy-start(f32[256]{0:T(256)} %get-tuple-element.223) | copy-start | bytes 3076
  947.4 80.3 %copy-start.65 = (f32[256]{0:T(256)S(1)}, f32[256]{0:T(256)}, u32[]{:S(2)}) copy-start(f32[256]{0:T(256)} %get-tuple-element.224) | copy-start | bytes 3076
  1031.5 5.0 copy-start.35
  1043.8 5.6 copy-start.79
  1043.8 5.6 copy-start.81
  (46 other events, 129.1 us)
Sparse Core Ops, SparseCore 0:
  92.4 107.1 all-gather.3
  288.4 80.0 all-gather.5
  407.0 77.9 all-gather.7
  487.2 75.2 reduce-scatter.3
  695.1 111.8 reduce-scatter.5
  869.7 75.9 reduce-scatter.7

commit v6 on v5

--- a/solution.py
+++ b/solution.py
@@ -63,6 +63,16 @@
         def _():
             pl.semaphore_signal(barrier, inc=1, device_id=self.at(self.me + 1), device_id_type=MESH)
 
+    @property
+    def size(self):
+        return self.n
+
+    def greet_all(self, barrier):
+        for k in range(1, self.n):
+            pl.semaphore_signal(
+                barrier, inc=1, device_id=self.at((self.me + k) % self.n), device_id_type=MESH
+            )
+
     def peers(self):
         return (self.me + self.n - 1) // self.n + (2 * self.n - 2 - self.me) // self.n
 
@@ -70,12 +80,17 @@
 class LineGather:
     def __init__(self, line, own, full, sems):
         self.line, self.own, self.full = line, own, full
-        self.rows = own.shape[0]
+        self.side = own.shape[0] == full.shape[0]
         self.local, self.up_send, self.up_recv, self.down_send, self.down_recv = sems
 
     @staticmethod
     def sems(n):
         return [DMA, DMA((n - 1,)), DMA((n - 1,)), DMA((n - 1,)), DMA((n - 1,))]
+
+    def slot(self, index):
+        if self.side:
+            return self.full.at[:, window(index, self.own.shape[1])]
+        return self.full.at[window(index, self.own.shape[0])]
 
     def hop(self, step, up):
         line = self.line
@@ -85,7 +100,7 @@
         else:
             shard, to = line.me + (step - 1), line.me - 1
             send, recv = self.down_send, self.down_recv
-        there = self.full.at[window(shard, self.rows)]
+        there = self.slot(shard)
         src = self.own if step == 1 else there
         return remote(src, there, send.at[step - 1], recv.at[step - 1], line.at(to))
 
@@ -106,10 +121,7 @@
                 self.hop(step, up).start()
 
     def start(self):
-        self.place = pltpu.make_async_copy(
-            self.own, self.full.at[window(self.line.me, self.rows)], self.local
-        )
-        self.place.start()
+        pltpu.make_async_copy(self.own, self.slot(self.line.me), self.local).start()
         self.send(1)
 
     def take(self, step):
@@ -118,7 +130,7 @@
             def _():
                 line = self.line
                 shard = (line.me - step) if up else (line.me + step)
-                here = self.full.at[window(shard, self.rows)]
+                here = self.slot(shard)
                 send, recv = (
                     (self.up_send, self.up_recv) if up else (self.down_send, self.down_recv)
                 )
@@ -134,9 +146,7 @@
                 @pl.when(self.sends(step, up))
                 def _():
                     self.hop(step, up).wait_send()
-        pltpu.make_async_copy(
-            self.own, self.full.at[window(self.line.me, self.rows)], self.local
-        ).wait()
+        pltpu.make_async_copy(self.own, self.slot(self.line.me), self.local).wait()
 
 
 class LineScatter:
@@ -286,6 +296,16 @@
                 barrier, inc=1, device_id=self.at(self.me + step), device_id_type=MESH
             )
 
+    @property
+    def size(self):
+        return self.dp
+
+    def greet_all(self, barrier):
+        for k in range(1, self.dp):
+            pl.semaphore_signal(
+                barrier, inc=1, device_id=self.at((self.me + k) % self.dp), device_id_type=MESH
+            )
+
     def peers(self):
         return self.levels + 1
 
@@ -436,29 +456,29 @@
                 self.hop(piece).wait_send()
 
 
-class CubeExchange:
-    def __init__(self, cube, moves, sems):
-        self.cube, self.moves = cube, moves
+class Swap:
+    def __init__(self, place, moves, sems):
+        self.place, self.moves = place, moves
         self.send_sem, self.recv_sem, self.local = sems
 
     @staticmethod
-    def sems(dp, moves):
-        return [DMA((moves, dp)), DMA((moves, dp)), DMA((moves,))]
+    def sems(size, moves):
+        return [DMA((moves, size)), DMA((moves, size)), DMA((moves,))]
 
     def copies(self):
-        cube = self.cube
+        place = self.place
         out = []
-        for k in range(1, cube.dp):
-            to = (cube.me + k) % cube.dp
+        for k in range(1, place.size):
+            to = (place.me + k) % place.size
             for m, (src, dst) in enumerate(self.moves):
                 out.append(
-                    remote(src(to), dst(cube.me), self.send_sem.at[m, k], self.recv_sem.at[m, k], cube.at(to))
+                    remote(src(to), dst(place.me), self.send_sem.at[m, k], self.recv_sem.at[m, k], place.at(to))
                 )
         return out
 
     def locals(self):
         return [
-            pltpu.make_async_copy(src(self.cube.me), dst(self.cube.me), self.local.at[m])
+            pltpu.make_async_copy(src(self.place.me), dst(self.place.me), self.local.at[m])
             for m, (src, dst) in enumerate(self.moves)
         ]
 
@@ -467,82 +487,104 @@
             copy.start()
 
     def finish(self):
-        cube = self.cube
+        place = self.place
         for copy in self.copies():
             copy.wait_send()
-        for k in range(1, cube.dp):
-            of = (cube.me - k + cube.dp) % cube.dp
+        for k in range(1, place.size):
+            of = (place.me - k + place.size) % place.size
             for m, (src, dst) in enumerate(self.moves):
                 here = dst(of)
-                remote(here, here, self.send_sem.at[m, k], self.recv_sem.at[m, k], cube.at(of)).wait_recv()
+                remote(here, here, self.send_sem.at[m, k], self.recv_sem.at[m, k], place.at(of)).wait_recv()
         for copy in self.locals():
             copy.wait()
 
 
+def rows_to_side(src, dst):
+    rows, cols = dst.shape[0], src.shape[1]
+    return (lambda d: src.at[window(d, rows)], lambda d: dst.at[:, window(d, cols)])
+
+
+def side_to_rows(src, dst):
+    rows, cols = src.shape[0], dst.shape[1]
+    return (lambda d: src.at[:, window(d, cols)], lambda d: dst.at[window(d, rows)])
+
+
 ANY = pl.BlockSpec(memory_space=pl.ANY)
 VMEM = pl.BlockSpec(memory_space=pltpu.VMEM)
 
 
-def front_kernel(x_ref, w_ref, we_ref, wr_ref, small_ref, seq_ref, w_out, we_out, wr_out, small_out, *sems):
+def front_kernel(
+    x_ref, w_ref, wo_ref, we_ref, wr_ref, small_ref,
+    seq_ref, w_out, wo_line, wo_out, we_out, wr_out, small_out, *sems
+):
     line, cube = Line(), Cube()
     gather = LineGather(line, x_ref, seq_ref, sems[:5])
-    weights = CubeGather(cube, w_ref, w_out, sems[5:10])
-    mine = wr_out.shape[0]
-    rows, cols = we_ref.shape[0], wr_ref.shape[1]
+    wide = LineGather(line, wo_ref, wo_line, sems[5:10])
+    weights = CubeGather(cube, w_ref, w_out, sems[10:15])
+    outer = CubeGather(cube, wo_line, wo_out, sems[15:20])
     tile = small_ref.shape[0]
     moves = [
         (lambda d: small_ref, lambda d: small_out.at[window(d, tile)]),
-        (lambda d: wr_ref.at[window(d, mine)], lambda d: wr_out.at[:, window(d, cols)]),
-        (lambda d: we_ref.at[:, window(d, mine)], lambda d: we_out.at[window(d, rows)]),
+        rows_to_side(wr_ref, wr_out),
     ]
-    swap = CubeExchange(cube, moves if mine % 128 == 0 else moves[:2], sems[10:13])
+    if wr_out.shape[0] % 128 == 0:
+        moves.append(side_to_rows(we_ref, we_out))
+    swap = Swap(cube, moves, sems[20:23])
     barrier = pltpu.get_barrier_semaphore()
     line.greet(barrier)
-    for k in range(1, cube.dp):
-        pl.semaphore_signal(
-            barrier, inc=1, device_id=cube.at((cube.me + k) % cube.dp), device_id_type=MESH
-        )
+    cube.greet_all(barrier)
     pl.semaphore_wait(barrier, cube.dp - 1 + line.peers())
+    wide.start()
     gather.start()
     weights.start()
+    wide.take(1)
+    wide.take(2)
     gather.take(1)
+    for step in range(3, line.n):
+        wide.take(step)
     for piece in range(1, cube.count):
         if piece.bit_length() < cube.levels:
             weights.take(piece)
+    wide.finish()
+    outer.start()
     swap.start()
     gather.take(2)
     for piece in range(1, cube.count):
         weights.take(piece)
+    for piece in range(1, cube.count):
+        outer.take(piece)
     for step in range(3, line.n):
         gather.take(step)
     weights.finish()
+    outer.finish()
     swap.finish()
     gather.finish()
 
 
-def front(x, w, w_e, w_r, small):
+def front(x, w, w_o, w_e, w_r, small):
     dp, n = lax.axis_size("dp"), lax.axis_size("tensor")
     rows, model = x.shape
-    outs = pl.pallas_call(
+    seq, w_all, _, o_all, e_all, r_all, small_all = pl.pallas_call(
         front_kernel,
         out_shape=(
             jax.ShapeDtypeStruct((n * rows, model), BF16),
             jax.ShapeDtypeStruct((dp * w.shape[0], w.shape[1]), BF16),
+            jax.ShapeDtypeStruct((w_o.shape[0], n * w_o.shape[1]), BF16),
+            jax.ShapeDtypeStruct((dp * w_o.shape[0], n * w_o.shape[1]), BF16),
             jax.ShapeDtypeStruct((dp * w_e.shape[0], w_e.shape[1] // dp), BF16),
             jax.ShapeDtypeStruct((w_r.shape[0] // dp, w_r.shape[1] * dp), BF16),
             jax.ShapeDtypeStruct((dp * small.shape[0], small.shape[1]), BF16),
         ),
-        in_specs=[ANY] * 5,
-        out_specs=(ANY,) * 5,
-        scratch_shapes=LineGather.sems(n) + CubeGather.sems(dp // 2) + CubeExchange.sems(dp, 3),
+        in_specs=[ANY] * 6,
+        out_specs=(ANY,) * 7,
+        scratch_shapes=2 * LineGather.sems(n) + 2 * CubeGather.sems(dp // 2) + Swap.sems(dp, 3),
         compiler_params=pltpu.CompilerParams(collective_id=0, has_side_effects=True),
         cost_estimate=pl.CostEstimate(flops=80 * 10**9, bytes_accessed=10**7, transcendentals=0),
         name="front",
-    )(x, w, w_e, w_r, small)
-    seq, w_all, e_all, r_all, small_all = outs
+    )(x, w, w_o, w_e, w_r, small)
     if r_all.shape[0] % 128:
         e_all = lax.all_to_all(w_e, "dp", split_axis=1, concat_axis=0, tiled=True)
-    return seq, w_all, e_all, r_all, small_all
+    return seq, w_all, o_all, e_all, r_all, small_all
 
 
 class SmallSum:
@@ -552,14 +594,14 @@
             scratch[0], scratch[1], scratch[2:5], scratch[5], scratch[6]
         )
         moves = [(lambda d: parts.at[d], lambda d: self.come.at[d])]
-        self.swap = CubeExchange(cube, moves, self.sems)
+        self.swap = Swap(cube, moves, self.sems)
 
     @staticmethod
     def scratch(dp, n, rows, d):
         return [
             pltpu.VMEM((dp, rows, d), F32),
             pltpu.VMEM((n, rows, d), F32),
-            *CubeExchange.sems(dp, 1),
+            *Swap.sems(dp, 1),
             DMA((n,)), DMA((n,)),
         ]
 
@@ -593,50 +635,37 @@
         self.out[...] = total
 
 
-def sum_kernel(counts, *refs):
-    lines, planes, gathers, cubes, swaps, small = counts
+def exchange_kernel(counts, *refs):
+    lines, planes, gathers, cubes, swaps, outs, backs, small = counts
     line, cube = Line(), Cube()
     count = sum(counts)
-    ins, outs, scratch = refs[:count], refs[count : 2 * count], list(refs[2 * count :])
+    pairs, scratch = list(zip(refs[:count], refs[count : 2 * count])), list(refs[2 * count :])
 
     def take(number):
         taken = tuple(scratch[:number])
         del scratch[:number]
         return taken
 
-    pairs = list(zip(ins, outs))
     sums = [LineScatter(line, *pairs.pop(0), take(7)) for _ in range(lines)]
     folds = [CubeScatter(cube, *pairs.pop(0), take(8)) for _ in range(planes)]
     lanes = [LineGather(line, *pairs.pop(0), take(5)) for _ in range(gathers)]
     wholes = [CubeGather(cube, *pairs.pop(0), take(5)) for _ in range(cubes)]
-    moves = []
-    for _ in range(swaps):
-        src, dst = pairs.pop(0)
-        rows, cols = src.shape[0], dst.shape[1]
-        moves.append(
-            (
-                lambda d, src=src, cols=cols: src.at[:, window(d, cols)],
-                lambda d, dst=dst, rows=rows: dst.at[window(d, rows)],
-            )
-        )
-    swap = CubeExchange(cube, moves, take(3)) if swaps else None
+    moves = [side_to_rows(*pairs.pop(0)) for _ in range(swaps)]
+    swap = Swap(cube, moves, take(3)) if swaps else None
+    turns = [rows_to_side(*pairs.pop(0)) for _ in range(outs)]
+    turns += [side_to_rows(*pairs.pop(0)) for _ in range(backs)]
+    turn = Swap(line, turns, take(3)) if turns else None
     little = SmallSum(line, cube, *pairs.pop(0), take(7)) if small else None
     barrier = pltpu.get_barrier_semaphore()
     peers = 0
-    if small:
-        for k in range(1, line.n):
-            pl.semaphore_signal(
-                barrier, inc=1, device_id=line.at((line.me + k) % line.n), device_id_type=MESH
-            )
+    if small or turns:
+        line.greet_all(barrier)
         peers = line.n - 1
     elif lines or gathers:
         line.greet(barrier)
         peers = line.peers()
     if small or swaps:
-        for k in range(1, cube.dp):
-            pl.semaphore_signal(
-                barrier, inc=1, device_id=cube.at((cube.me + k) % cube.dp), device_id_type=MESH
-            )
+        cube.greet_all(barrier)
         peers = peers + cube.dp - 1
     elif planes or cubes:
         cube.greet(barrier)
@@ -644,6 +673,8 @@
     for s in sums:
         s.prepare()
     pl.semaphore_wait(barrier, peers)
+    if turns:
+        turn.start()
     if small:
         little.swap.start()
     for s in sums:
@@ -652,19 +683,22 @@
         lane.start()
     for whole in wholes[:1]:
         whole.start()
+    for f in folds:
+        f.start()
+    if small:
+        little.middle()
     pieces = [p for p in folds[0].order() if p] if planes else []
     per = -(-len(pieces) // (line.n - 1))
     for step in range(1, line.n):
+        for whole in wholes[step - 1 : step]:
+            for piece in range(1, cube.count):
+                if piece.bit_length() < cube.levels:
+                    whole.take(piece)
         if step > 1:
             for s in sums:
                 s.step(step)
             for lane in lanes:
                 lane.take(step - 1)
-        if step == 1:
-            for f in folds:
-                f.start()
-            if small:
-                little.middle()
         for piece in pieces[:per]:
             for f in folds:
                 f.fold(piece)
@@ -682,50 +716,57 @@
         lane.finish()
     for s in sums:
         s.finish()
+    if turns:
+        turn.finish()
     if swaps:
         swap.finish()
     if small:
         little.finish()
 
 
-def exchange(collective_id, lines=(), planes=(), gathers=(), cubes=(), swaps=(), small=()):
+def exchange(
+    collective_id, lines=(), planes=(), gathers=(), cubes=(), swaps=(), outs=(), backs=(), small=()
+):
     dp, n = lax.axis_size("dp"), lax.axis_size("tensor")
+    groups = (lines, planes, gathers, cubes, swaps, outs, backs, small)
+    counts = tuple(len(group) for group in groups)
+    operands = [part for group in groups for part in group]
     out_shape, out_specs, scratch = [], [], []
+
+    def result(rows, d, kind, spec):
+        out_shape.append(jax.ShapeDtypeStruct((rows, d), kind))
+        out_specs.append(spec)
+
     for part in lines:
         rows, d = part.shape[0] // n, part.shape[1]
-        out_shape.append(jax.ShapeDtypeStruct((rows, d), F32))
-        out_specs.append(VMEM)
+        result(rows, d, F32, VMEM)
         scratch += LineScatter.scratch(n, rows, d)
     for part in planes:
         rows, d = part.shape[0] // dp, part.shape[1]
-        out_shape.append(jax.ShapeDtypeStruct((rows, d), F32))
-        out_specs.append(VMEM)
+        result(rows, d, F32, VMEM)
         scratch += CubeScatter.scratch(dp // 2, rows, d)
     for part in gathers:
-        rows, d = part.shape
-        out_shape.append(jax.ShapeDtypeStruct((n * rows, d), BF16))
-        out_specs.append(ANY)
+        result(n * part.shape[0], part.shape[1], BF16, ANY)
         scratch += LineGather.sems(n)
     for part in cubes:
-        rows, d = part.shape
-        out_shape.append(jax.ShapeDtypeStruct((dp * rows, d), BF16))
-        out_specs.append(ANY)
+        result(dp * part.shape[0], part.shape[1], BF16, ANY)
         scratch += CubeGather.sems(dp // 2)
     for part in swaps:
-        rows, d = part.shape
-        out_shape.append(jax.ShapeDtypeStruct((dp * rows, d // dp), BF16))
-        out_specs.append(ANY)
+        result(dp * part.shape[0], part.shape[1] // dp, BF16, ANY)
     if swaps:
-        scratch += CubeExchange.sems(dp, len(swaps))
+        scratch += Swap.sems(dp, len(swaps))
+    for part in outs:
+        result(part.shape[0] // n, part.shape[1] * n, BF16, ANY)
+    for part in backs:
+        result(part.shape[0] * n, part.shape[1] // n, BF16, ANY)
+    if outs or backs:
+        scratch += Swap.sems(n, len(outs) + len(backs))
     for part in small:
         rows, d = part.shape[1:]
-        out_shape.append(jax.ShapeDtypeStruct((rows, d), F32))
-        out_specs.append(VMEM)
+        result(rows, d, F32, VMEM)
         scratch += SmallSum.scratch(dp, n, rows, d)
-    counts = tuple(len(g) for g in (lines, planes, gathers, cubes, swaps, small))
-    operands = [part for group in (lines, planes, gathers, cubes, swaps, small) for part in group]
     return pl.pallas_call(
-        functools.partial(sum_kernel, counts),
+        functools.partial(exchange_kernel, counts),
         out_shape=tuple(out_shape),
         in_specs=[ANY] * len(operands),
         out_specs=tuple(out_specs),
@@ -1240,10 +1281,10 @@
     )
     used = small.shape[0]
     small = jnp.pad(small, (0, -used % 2048)).reshape(-1, 128)
-    w_attn = jnp.concatenate([w_query, w_key, w_value, w_out.T], axis=1)
-    seq_x0, w_attn, w_e, w_r, small = front(x_low[0], w_attn, w_expand, w_reduce, small)
-    w_qkv = w_attn[:, : 3 * width]
-    w_ot = w_attn[:, 3 * width :]
+    w_qkv = jnp.concatenate([w_query, w_key, w_value], axis=1)
+    seq_x0, w_qkv, w_ot, w_e, w_r, small = front(
+        x_low[0], w_qkv, w_out.T, w_expand, w_reduce, small
+    )
     small = small.reshape(dp, -1)[:, :used]
     gain_one, shift_one, bias_out, gain_two, shift_two, bias_red = [
         small[:, i * cut : (i + 1) * cut].reshape(1, model).astype(F32) for i in range(6)
@@ -1257,17 +1298,16 @@
     bias_qkv = jnp.concatenate([bias_qkv[0], jnp.zeros((1, width), F32), bias_qkv[1]], 1)
     bias_e = small[:, at:].reshape(dp, dp, be_rows // dp, be_cols)
     bias_e = lax.dynamic_index_in_dim(bias_e, dp_me, 1, keepdims=False)
-    bias_e = lax.all_gather(bias_e.transpose(1, 0, 2).reshape(1, mine), "tensor", axis=1, tiled=True)
-    bias_e = bias_e.astype(F32)
+    bias_e = bias_e.transpose(1, 0, 2).reshape(mine)
+    bias_e = jnp.pad(bias_e, (0, -mine % 2048)).reshape(-1, 128)
 
     seq_x = [seq_x0]
     w_r = lax.all_gather(w_r, "tensor", axis=0, tiled=True)
-    if mine % 128:
-        w_e = lax.all_gather(w_e, "tensor", axis=1, tiled=True)
+    w_e = lax.all_gather(w_e, "tensor", axis=1 if mine % 128 else 0, tiled=True)
 
     normal_one, seq_one, qkv, attended, hidden, normed_two = [], [], [], [], [], []
-    out_part, seq_two, activated, d_pre, d_hidden, d_branch, seq_branch = [], [], [], [], [], [], []
-    d_qkv, d_one = [], []
+    out_part, seq_two, activated, d_pre, d_hidden, d_branch, out_sum = [], [], [], [], [], [], []
+    d_qkv, d_one, d_att, row_attended = [], [], [], []
     g_gain_two = g_shift_two = g_bias_red = g_bias_out = g_bias_e = 0.0
     g_gain_one = g_shift_one = g_bias_qkv = 0.0
     for m in micros:
@@ -1277,23 +1317,27 @@
             (jnp.dot(seq_one[m], w_qkv, preferred_element_type=F32) + bias_qkv).astype(BF16)
         )
         attended.append(attend(parents[m, 0], qkv[m], width))
-        branch = over(attended[m], w_ot, 1, 1).astype(BF16)
         if m == 0:
-            others = [w_e] if mine % 128 == 0 else []
-            branch, *full = exchange(3, lines=[branch], gathers=others, cubes=dy_low)
-            w_e = full[0] if others else w_e
-            seq_grad = full[len(others) :]
+            bias_e, *seq_grad, row_att = exchange(
+                3, gathers=[bias_e], cubes=dy_low, outs=[attended[m]]
+            )
+            bias_e = bias_e.reshape(tn, -1)[:, :mine].reshape(1, tn * mine).astype(F32)
         else:
-            branch = lax.psum_scatter(branch, "tensor", scatter_dimension=0, tiled=True).astype(F32)
+            part, row_att, col_grad = exchange(
+                4, planes=[out_part[m - 1]], outs=[attended[m]], backs=[d_att[m - 1]]
+            )
+            out_sum.append(part)
+            d_att[m - 1] = col_grad
         if m < last:
-            next_x, branch = lax.optimization_barrier((x_low[m + 1], branch))
+            next_x, row_att = lax.optimization_barrier((x_low[m + 1], row_att))
             next_x = lax.all_gather(next_x, "tensor", axis=0, tiled=True)
+        row_attended.append(row_att)
+        branch = over(row_att, w_ot, 1, 1)
         hidden.append(x_low[m].astype(F32) + (branch + bias_out))
         normed_two.append(layer_norm(hidden[m], gain_two, shift_two).astype(BF16))
 
         def attention_back(k):
-            d_att = jnp.dot(seq_branch[k], w_ot, preferred_element_type=F32).astype(BF16)
-            d_qkv.append(attend_back(parents[k, 0], qkv[k], d_att, width))
+            d_qkv.append(attend_back(parents[k, 0], qkv[k], d_att[k], width))
             d_one.append(over(d_qkv[k], w_qkv, 1, 1).astype(BF16))
             part = d_one[k].astype(F32)
             return (
@@ -1304,10 +1348,6 @@
 
         own = None
         if m:
-            seq_branch.append(lax.all_gather(d_branch[m - 1], "tensor", axis=0, tiled=True))
-            g_r = over(activated[m - 1], seq_grad[m - 1], 0, 0) + (g_r if m > 1 else 0.0)
-            g_et = over(d_pre[m - 1], seq_two[m - 1], 0, 0) + (g_et if m > 1 else 0.0)
-            normed_two[m], g_r, g_et = lax.optimization_barrier((normed_two[m], g_r, g_et))
             gain, shift, bias = attention_back(m - 1)
             g_gain_one, g_shift_one = g_gain_one + gain, g_shift_one + shift
             g_bias_qkv = g_bias_qkv + bias
@@ -1325,6 +1365,7 @@
         d_norm, g_gain, g_shift = norm_pull(d_two)
         d_hidden.append(grad32 + d_norm)
         d_branch.append(d_hidden[m].astype(BF16))
+        d_att.append(jnp.dot(d_branch[m], w_ot, preferred_element_type=F32).astype(BF16))
         g_gain_two = g_gain_two + g_gain
         g_shift_two = g_shift_two + g_shift
         g_bias_red = g_bias_red + jnp.sum(grad32, 0, keepdims=True)
@@ -1341,19 +1382,14 @@
             out = term if out is None else out + term
         return out.astype(BF16)
 
-    def closing(so_far, left, right):
-        term = over(left, right, 0, 0)
-        return (term if last == 0 else so_far + term).astype(BF16)
-
-    g_r = closing(g_r, activated[last], seq_grad[last])
-    branch_last, g_r = lax.optimization_barrier((d_branch[last], g_r))
+    g_r = outer(activated, seq_grad)
+    d_att[last], g_r = lax.optimization_barrier((d_att[last], g_r))
     g_r = lax.psum_scatter(g_r, "tensor", scatter_dimension=0, tiled=True)
-    *out_sum, full = exchange(4, planes=out_part, gathers=[branch_last])
-    full, dpre = lax.optimization_barrier((full, d_pre[last]))
-    g_et = closing(g_et, dpre, seq_two[last])
-    full, g_et, g_r = lax.optimization_barrier((full, g_et, g_r))
+    g_ot = outer(d_branch, row_attended)
+    g_ot, d_att[last] = exchange(6, planes=[g_ot], backs=[d_att[last]])
+    g_et = outer(d_pre, seq_two)
+    g_et, g_r = lax.optimization_barrier((g_et, g_r))
     g_et = lax.psum_scatter(g_et, "tensor", scatter_dimension=0, tiled=True)
-    seq_branch.append(full)
     gain, shift, bias = attention_back(last)
     g_gain_one, g_shift_one = g_gain_one + gain, g_shift_one + shift
     g_bias_qkv = g_bias_qkv + bias
@@ -1374,14 +1410,20 @@
     little = jnp.concatenate([rows, row_qv, row_e], 1)
     little = jnp.pad(little, ((0, 0), (0, -little.shape[1] % 1024))).reshape(dp, -1, 128)
 
-    g_attn = jnp.concatenate([outer(seq_one, d_qkv), outer(seq_branch, attended)], axis=1)
-    d_one[last], g_attn, g_reduce, g_expand, little = exchange(
-        5, lines=[d_one[last]], planes=[g_attn], swaps=[g_r, g_et], small=[little]
+    g_qkv = outer(seq_one, d_qkv)
+    g_ot = g_ot.astype(BF16).reshape(-1, tn, width).transpose(1, 0, 2).reshape(-1, width)
+    d_one[last], g_ot, g_qkv, out_last, g_reduce, g_expand, little = exchange(
+        5,
+        lines=[d_one[last], g_ot],
+        planes=[g_qkv, out_part[last]],
+        swaps=[g_r, g_et],
+        small=[little],
     )
+    out_sum.append(out_last)
+    g_query, g_key, g_value = [g_qkv[:, i * width : (i + 1) * width] for i in range(3)]
+    g_out = g_ot.T
     g_expand = g_expand.T.astype(F32)
     g_reduce = g_reduce.astype(F32)
-    g_query, g_key, g_value = [g_attn[:, i * width : (i + 1) * width] for i in range(3)]
-    g_out = g_attn[:, 3 * width :].T
     layer_out = [(hidden[m] + (out_sum[m] + bias_red)).astype(BF16) for m in micros]
     little = little.reshape(-1)
     six = little[: 6 * cut].reshape(6, cut)

time: 1080 us -> 1050 us (0.972)
  waiting for transfers between devices: 10.8 us -> 75.1 us
  Pallas kernels: 754 us -> 694 us
  other arithmetic: 71.2 us -> 55.8 us
  local copies, waits for them, and re-layouts: 29.4 us -> 40.6 us
    pallas_call x3 -> x4, Pallas kernels: 381 us -> 282 us  [exchange(): pl.pallas_call(functools.partial(exchange_kernel, counts), out_shape=tupl...]
    all_gather x1, waiting for transfers between devices: 0.01 us -> 42.8 us  [body(): w_r = lax.all_gather(w_r, 'tensor', axis=0, tiled=True)]
    pallas_call x1, Pallas kernels: 79.2 us -> 118 us  [front(): pl.pallas_call(front_kernel, out_shape=(jax.ShapeDtypeStruct((n * rows, m...]
    reduce_scatter x1, waiting for transfers between devices: 0.01 us -> 31.5 us  [body(): g_et = lax.psum_scatter(g_et, 'tensor', scatter_dimension=0, tiled=True)]
    unnamed x224 -> x263, local copies, waits for them, and re-layouts: 11.7 us -> 21.7 us
  transfers between devices with their start and end apart: 6 -> 5, of which waited for: 2 -> 2; matrix products, arithmetic and copies ran while one was open for 18% -> 11% of each run, Pallas kernels for 46% -> 27%
where the time goes in v6:
time: 1050 us; the launch traced here: 1040 us
  Pallas kernels  694 us (66%)
  matrix products  161 us (15%)
  waiting for transfers between devices  75.1 us (7%)
  other arithmetic  55.8 us (5%)
  local copies, waits for them, and re-layouts  40.6 us (4%)
  between operations  15.9 us (2%)
    pallas_call x4, Pallas kernels, exchange(): pl.pallas_call(functools.partial(exchange_kernel, counts), out_shape=tupl...  282 us
    pallas_call x2, Pallas kernels, ffn(): pl.pallas_call(functools.partial(ffn_kernel, host), out_shape=(jax.ShapeD...  198 us
    dot_general x12, matrix products, over(): lax.dot_general(left, right, (((on_left,), (on_right,)), ((), ())), prefe...  135 us
    pallas_call x1, Pallas kernels, front(): pl.pallas_call(front_kernel, out_shape=(jax.ShapeDtypeStruct((n * rows, m...  118 us
    pallas_call x2, Pallas kernels, attend_back(): pl.pallas_call(attend_back_kernel, out_shape=jax.ShapeDtypeStruct((rows,...  68.5 us
    all_gather x1, waiting for transfers between devices, body(): w_r = lax.all_gather(w_r, 'tensor', axis=0, tiled=True)  42.8 us
    reduce_scatter x1, waiting for transfers between devices, body(): g_et = lax.psum_scatter(g_et, 'tensor', scatter_dimension=0, tiled=True)  31.5 us
    pallas_call x2, Pallas kernels, attend(): pl.pallas_call(attend_kernel, out_shape=jax.ShapeDtypeStruct((rows, width...  28.6 us
  transfers between devices with their start and end apart: 5, of which 2 were waited for; matrix products, arithmetic and copies ran while one was open for 11% of the time, Pallas kernels for 27%

profile of v6, /device:TPU:0, one launch (start us, length us, event | category | flops | bytes accessed | tf_op | source)
XLA Modules:
  0.0 1043.4 jit_solution(5850354022942384309)
XLA Ops:
  7.4 3.3 slice_bitcast_fusion.3
  13.5 117.8 %front.1 = (bf16[1024,2048]{1,0:T(8,128)(2,1)}, bf16[2048,1536]{1,0:T(8,128)(2,1)}, bf16[256,2048]{1,0:T(8,128)(2,1)}, bf16[2048,2048]{1,0:T(8,128)(2,1)}, bf16[...) custom-call(bf16[256,2048]{1,0:T(8,128)(2,1)} %get-tuple-element.184.x_ref, ...), custom_call_target="tpu_custom_call" | custom-call | flops 80000000000 | bytes 10000000 | tf_op jit(solution)/shard_map/front/pallas_call | solution.py:567
  132.3 3.0 convert_reduce_fusion.3
  135.7 1.2 fusion.11
  138.3 3.4 slice_bitcast_fusion
  141.8 9.8 add_convert_fusion.5.q_ref.k_ref.v_ref
  151.7 14.2 %attend.2.refs_3_ = bf16[1024,512]{1,0:T(8,128)(2,1)S(1)} custom-call(s32[4]{0:T(128)S(1)} %get-tuple-element.215.parents_ref, bf16[1024,1536]{1,0:T(8,128)(2,1)S(1)} %add_convert_fusion.5.q_ref.k_ref.v_ref, bf16[1024,1536]{1,0:T(8,128)(2,1)S(1)} %add_convert_fusion.5.q_ref.k_ref.v_ref, bf16[1024,1536]{1,0:T(8,128)(2,1)S(1)} %add_convert_fusion.5.q_ref.k_ref.v_ref), custom_call_target="tpu_custom_call" | custom-call | flops 16106127360 | bytes 4194304 | tf_op jit(solution)/shard_map/attend/pallas_call | solution.py:849
  166.8 88.1 %exchange.4 = (bf16[64,128]{1,0:T(8,128)(2,1)}, bf16[2048,2048]{1,0:T(8,128)(2,1)}, bf16[2048,2048]{1,0:T(8,128)(2,1)}, bf16[256,2048]{1,0:T(8,128)(2,1)}) custom-call(bf16[16,128]{1,0:T(8,128)(2,1)} %pad_bitcast_fusion.refs_0_, bf16[256,2048]{1,0:T(8,128)(2,1)} %get-tuple-element.183.refs_1_, bf16[256,2048]{1,0:T(8,128)(2,1)} %get-tuple-element.182.refs_2_, ...), custom_call_target="tpu_custom_call" | custom-call | flops 80000000000 | bytes 10000000 | tf_op jit(solution)/shard_map/exchange/pallas_call | solution.py:768
  255.5 1.9 convert_reduce_fusion.9
  258.0 6.2 fusion.49
  264.3 1.3 copy-done.14
  267.8 3.0 add_convert_fusion.11.n2_ref
  270.8 42.8 %all-gather.6.cloned.1.call-done.wr_ref = bf16[1024,2048]{1,0:T(8,128)(2,1)} async-done(((bf16[256,2048]{1,0:T(8,128)(2,1)}), bf16[1024,2048]{1,0:T(8,128)(2,1)}) %all-gather.6.cloned.1.call-update) | async-done | bytes 4194320 | tf_op jit(solution)/shard_map/all_gather | solution.py:1305
  313.6 93.5 %ffn_plane.2 = (f32[256,2048]{1,0:T(8,128)}, bf16[2048,2048]{1,0:T(8,128)(2,1)}, bf16[2048,1024]{1,0:T(8,128)(2,1)}, bf16[2048,1024]{1,0:T(8,128)(2,1)}, bf16[2048,2048]{1,0:T(8,128)(2,1)}) custom-call(bf16[256,2048]{1,0:T(8,128)(2,1)} %add_convert_fusion.11.n2_ref, bf16[2048,2048]{1,0:T(8,128)(2,1)} %get-tuple-element.64.dy_ref, ...), custom_call_target="tpu_custom_call" | custom-call | flops 154618822656 | bytes 50331648 | tf_op jit(solution)/shard_map/ffn_plane/pallas_call | solution.py:1201
  407.2 3.7 multiply_reduce_fusion.1
  412.5 1.3 convert_reduce_fusion.10
  413.8 1.0 copy-done.35
  414.8 1.3 copy-done.117
  416.1 3.4 convolution_convert_fusion.3.refs_2_
  419.5 3.0 convert_reduce_fusion.2
  422.9 1.2 fusion.10
  424.2 9.8 add_convert_fusion.4.q_ref.k_ref.v_ref
  434.0 14.4 %attend.3.refs_1_ = bf16[1024,512]{1,0:T(8,128)(2,1)S(1)} custom-call(s32[4]{0:T(128)S(1)} %get-tuple-element.214.parents_ref, bf16[1024,1536]{1,0:T(8,128)(2,1)S(1)} %add_convert_fusion.4.q_ref.k_ref.v_ref, bf16[1024,1536]{1,0:T(8,128)(2,1)S(1)} %add_convert_fusion.4.q_ref.k_ref.v_ref, bf16[1024,1536]{1,0:T(8,128)(2,1)S(1)} %add_convert_fusion.4.q_ref.k_ref.v_ref), custom_call_target="tpu_custom_call" | custom-call | flops 16106127360 | bytes 4194304 | tf_op jit(solution)/shard_map/attend/pallas_call | solution.py:849
  449.4 44.5 %exchange.5 = (f32[256,2048]{1,0:T(8,128)}, bf16[256,2048]{1,0:T(8,128)(2,1)}, bf16[1024,512]{1,0:T(8,128)(2,1)}) custom-call(bf16[2048,2048]{1,0:T(8,128)(2,1)} %get-tuple-element.68.refs_0_, bf16[1024,512]{1,0:T(8,128)(2,1)} %copy-done.9, bf16[256,2048]{1,0:T(8,128)(2,1)} %convolution_convert_fusion.3.refs_2_), custom_call_target="tpu_custom_call" | custom-call | flops 80000000000 | bytes 10000000 | tf_op jit(solution)/shard_map/exchange/pallas_call | solution.py:768
  494.0 1.2 copy-done.11
  495.2 34.2 %attend_back.2 = bf16[1024,1536]{1,0:T(8,128)(2,1)S(1)} custom-call(s32[4]{0:T(128)S(1)} %copy-done.5, bf16[1024,1536]{1,0:T(8,128)(2,1)} %copy-done.6, bf16[1024,1536]{1,0:T(8,128)(2,1)} %copy-done.6, bf16[1024,1536]{1,0:T(8,128)(2,1)} %copy-done.6, bf16[1024,512]{1,0:T(8,128)(2,1)S(1)} %copy-done.11), custom_call_target="tpu_custom_call" | custom-call | flops 40265318400 | bytes 7340032 | tf_op jit(solution)/shard_map/attend_back/pallas_call | solution.py:925
  529.5 13.3 %convert_reduce_fusion.1 = (f32[2048]{0:T(1024)}, f32[2048]{0:T(1024)}, bf16[1024,2048]{1,0:T(8,128)(2,1)}) fusion(f32[1024]{0:T(1024)S(1)} %copy-done.103, f32[1024]{0:T(1024)S(1)} %copy-done.77, bf16[1024,2048]{1,0:T(8,128)(2,1)S(1)} %copy-done.28, bf16[1024,1536]{1,0:T(8,128)(2,1)S(1)} %attend_back.2, bf16[2048,1536]{1,0:T(8,128)(2,1)} %get-tuple-element.60), kind=kOutput, calls=%fused_computation.4 | convolution fusion | flops 6459224064 | bytes 17850368 | tf_op jit(solution)/shard_map/dot_general | solution.py:32
  542.8 5.9 fusion.50
  549.5 1.4 add_convert_fusion.9.n2_ref
  550.9 104.2 %ffn_plane.3 = (f32[256,2048]{1,0:T(8,128)}, bf16[2048,2048]{1,0:T(8,128)(2,1)}, bf16[2048,1024]{1,0:T(8,128)(2,1)}, bf16[2048,1024]{1,0:T(8,128)(2,1)}, bf16[20...) custom-call(bf16[256,2048]{1,0:T(8,128)(2,1)} %add_convert_fusion.9.n2_ref, bf16[2048,2048]{1,0:T(8,128)(2,1)} %get-tuple-element.75.dy_ref, ...), custom_call_target="tpu_custom_call" | custom-call | flops 154618822656 | bytes 50331648 | tf_op jit(solution)/shard_map/ffn_plane/pallas_call | solution.py:1201
  655.2 3.7 multiply_reduce_fusion
  659.9 12.9 %fusion.52 = f32[1024,2048]{1,0:T(8,128)S(1)} fusion(bf16[2048,1024]{1,0:T(8,128)(2,1)S(1)} %copy-done.118, bf16[2048,2048]{1,0:T(8,128)(2,1)} %get-tuple-element.64.dy_ref), kind=kOutput, calls=%fused_computation.163 | convolution fusion | flops 8589934592 | bytes 20971520 | tf_op jit(solution)/shard_map/dot_general | solution.py:32
  672.8 1.0 convert_reduce_fusion.12
  673.8 3.4 convolution_convert_fusion.2.refs_1_
  677.2 13.1 %add_convert_fusion.3 = bf16[1024,2048]{1,0:T(8,128)(2,1)} fusion(f32[1024,2048]{1,0:T(8,128)S(1)} %fusion.52, bf16[2048,1024]{1,0:T(8,128)(2,1)} %get-tuple-element.79, bf16[2048,2048]{1,0:T(8,128)(2,1)S(1)} %bitcast.214), kind=kOutput, calls=%fused_computation.27 | convolution fusion | flops 8594128896 | bytes 25165824 | tf_op jit(solution)/shard_map/dot_general | solution.py:32
  690.3 9.5 fusion.51
  699.8 11.5 %add_convert_fusion.refs_0_ = bf16[2048,2048]{1,0:T(8,128)(2,1)} fusion(f32[2048,2048]{1,0:T(8,128)} %fusion.51, bf16[256,2048]{1,0:T(8,128)(2,1)S(1)} %get-tuple-element.171, bf16[256,2048]{1,0:T(8,128)(2,1)S(1)} %copy-done.44), kind=kOutput, calls=%fused_computation | convolution fusion | flops 2155872256 | bytes 27262976 | tf_op jit(solution)/shard_map/dot_general | solution.py:32
  711.4 50.2 %exchange.6 = (f32[256,2048]{1,0:T(8,128)}, bf16[1024,512]{1,0:T(8,128)(2,1)}) custom-call(bf16[2048,2048]{1,0:T(8,128)(2,1)} %add_convert_fusion.refs_0_, bf16[256,2048]{1,0:T(8,128)(2,1)} %convolution_convert_fusion.2.refs_1_), custom_call_target="tpu_custom_call" | custom-call | flops 80000000000 | bytes 10000000 | tf_op jit(solution)/shard_map/exchange/pallas_call | solution.py:768
  761.6 12.9 %fusion.53 = f32[1024,2048]{1,0:T(8,128)S(1)} fusion(bf16[2048,1024]{1,0:T(8,128)(2,1)} %get-tuple-element.84, bf16[2048,2048]{1,0:T(8,128)(2,1)} %get-tuple-element.85), kind=kOutput, calls=%fused_computation.164 | convolution fusion | flops 8589934592 | bytes 20971520 | tf_op jit(solution)/shard_map/dot_general | solution.py:32
  774.5 12.9 %add_convert_fusion.2 = bf16[1024,2048]{1,0:T(8,128)(2,1)} fusion(f32[1024,2048]{1,0:T(8,128)S(1)} %fusion.53, bf16[2048,1024]{1,0:T(8,128)(2,1)S(1)} %copy-done.34, bf16[2048,2048]{1,0:T(8,128)(2,1)} %get-tuple-element.87), kind=kOutput, calls=%fused_computation.26 | convolution fusion | flops 8594128896 | bytes 25165824 | tf_op jit(solution)/shard_map/dot_general | solution.py:32
  787.4 34.3 %attend_back.3 = bf16[1024,1536]{1,0:T(8,128)(2,1)S(1)} custom-call(s32[4]{0:T(128)S(1)} %get-tuple-element.214.parents_ref, bf16[1024,1536]{1,0:T(8,128)(2,1)} %copy-done.7, bf16[1024,1536]{1,0:T(8,128)(2,1)} %copy-done.7, bf16[1024,1536]{1,0:T(8,128)(2,1)} %copy-done.7, bf16[1024,512]{1,0:T(8,128)(2,1)S(1)} %copy-done.10), custom_call_target="tpu_custom_call" | custom-call | flops 40265318400 | bytes 7340032 | tf_op jit(solution)/shard_map/attend_back/pallas_call | solution.py:925
  821.7 1.7 copy-done.2
  824.2 12.3 %convert_reduce_fusion = (f32[2048]{0:T(1024)S(1)}, f32[2048]{0:T(1024)S(1)}, bf16[1024,2048]{1,0:T(8,128)(2,1)}) fusion(f32[1024]{0:T(1024)S(1)} %copy-done.106, f32[1024]{0:T(1024)S(1)} %copy-done.80, bf16[1024,2048]{1,0:T(8,128)(2,1)} %all-gather.8.cloned.1.call-done, bf16[1024,1536]{1,0:T(8,128)(2,1)} %copy-done.2, bf16[2048,1536]{1,0:T(8,128)(2,1)} %get-tuple-element.60), kind=kOutput, calls=%fused_computation.2 | convolution fusion | flops 6459224064 | bytes 17850368 | tf_op jit(solution)/shard_map/dot_general | solution.py:32
  836.8 3.6 convert_reduce_fusion.6
  840.8 5.1 convert_reduce_fusion.4
  847.6 1.6 reshape.508
  849.9 1.9 convert_element_type.274
  851.8 1.1 copy.79
  852.9 11.6 %fusion.40 = f32[2048,1536]{1,0:T(8,128)} fusion(bf16[1024,1536]{1,0:T(8,128)(2,1)S(1)} %copy-done.1, bf16[1024,2048]{1,0:T(8,128)(2,1)S(1)} %copy-done.29, f32[2048]{0:T(1024)S(1)} %bitcast.204, f32[2048]{0:T(1024)S(1)} %bitcast.189, f32[1024]{0:T(1024)S(1)} %copy-done.104, f32[1024]{0:T(1024)S(1)} %copy-done.78), kind=kOutput, calls=%fused_computation.155 | convolution fusion | flops 6455033856 | bytes 19947520 | tf_op jit(solution)/shard_map/dot_general | solution.py:32
  864.5 12.6 %add_convert_fusion.1.refs_2_ = bf16[2048,1536]{1,0:T(8,128)(2,1)} fusion(f32[2048,1536]{1,0:T(8,128)} %fusion.40, bf16[1024,1536]{1,0:T(8,128)(2,1)S(1)} %copy-done.3, bf16[1024,2048]{1,0:T(8,128)(2,1)S(1)} %copy-done.31, f32[1024]{0:T(1024)S(1)} %copy-done.106, f32[1024]{0:T(1024)S(1)} %copy-done.80, f32[2048]{0:T(1024)S(1)} %bitcast.205, ...), kind=kOutput, calls=%fused_computation.1 | convolution fusion | flops 6461325312 | bytes 26238976 | tf_op jit(solution)/shard_map/dot_general | solution.py:32
  877.1 31.5 %reduce-scatter.5.cloned.1.call-done.refs_5_ = bf16[256,2048]{1,0:T(8,128)(2,1)} async-done(((bf16[1024,2048]{1,0:T(8,128)(2,1)}), bf16[256,2048]{1,0:T(8,128)(2,1)}) %reduce-scatter.5.cloned.1.call-update) | async-done | bytes 1048592 | tf_op jit(solution)/shard_map/reduce_scatter | solution.py:1392
  908.6 99.1 %exchange.7 = (f32[256,2048]{1,0:T(8,128)}, f32[256,512]{1,0:T(8,128)}, f32[256,1536]{1,0:T(8,128)}, f32[256,2048]{1,0:T(8,128)}, bf16[2048,256]{1,0:T(8,128)(2,...) custom-call(bf16[1024,2048]{1,0:T(8,128)(2,1)} %get-tuple-element.221.refs_0_, bf16[1024,512]{1,0:T(8,128)(2,1)} %bitcast.177, ...), custom_call_target="tpu_custom_call" | custom-call | flops 80000000000 | bytes 10000000 | tf_op jit(solution)/shard_map/exchange/pallas_call | solution.py:768
  1009.1 1.4 slice_bitcast_fusion.4
  1010.6 3.5 fusion.23
  1014.1 1.5 fusion.36
  1015.6 1.5 convert_bitcast_fusion
  1017.1 3.0 copy.64
  1020.1 1.5 convert_element_type.290
  1022.2 1.2 fusion.47
  1023.4 1.0 copy.63
  1025.3 5.2 fusion.28
  1030.5 1.5 maximum_bitcast_fusion.1
  1033.5 1.0 fusion.26
  1034.5 1.5 maximum_bitcast_fusion
  (351 shorter events, 23.4 us)
Async XLA Ops:
  7.3 5.3 copy-start.53
  7.3 5.3 copy-start.52
  7.3 5.3 copy-start.51
  7.3 263.5 %all-gather.4.cloned.1.call-start = ((), (), s32[]{:S(2)}) async-start(), calls=%async_computation.2 | async-start | bytes 5242880 | tf_op jit(solution)/shard_map/all_gather | solution.py:1306
  131.3 182.3 %all-gather.6.cloned.1.call-start = ((), (), s32[]{:S(2)}) async-start(), calls=%async_computation.3 | async-start | bytes 5242880 | tf_op jit(solution)/shard_map/all_gather | solution.py:1305
  132.1 287.4 %all-gather.8.cloned.1.call-start = ((), (), s32[]{:S(2)}) async-start(), calls=%async_computation.4 | async-start | bytes 5242880 | tf_op jit(solution)/shard_map/all_gather | solution.py:1333
  135.7 6.1 copy-start.76
  137.0 4.8 copy-start.102
  137.0 4.8 copy-start.54
  137.4 14.3 %copy-start.4 = (s32[4]{0:T(128)}, s32[4]{0:T(128)S(1)}, u32[]{:S(2)}) copy-start(s32[4]{0:T(128)S(1)} %get-tuple-element.215.parents_ref) | copy-start | bytes 52
  141.8 9.9 copy-start.98
  151.6 14.2 %copy-start.6 = (bf16[1024,1536]{1,0:T(8,128)(2,1)}, bf16[1024,1536]{1,0:T(8,128)(2,1)S(1)}, u32[]{:S(2)}) copy-start(bf16[1024,1536]{1,0:T(8,128)(2,1)S(1)} %add_convert_fusion.5.q_ref.k_ref.v_ref) | copy-start | bytes 9437188
  255.0 568.4 %reduce-scatter.3.cloned.1.call-start = ((), (), s32[]{:S(2)}) async-start(), calls=%async_computation.5 | async-start | bytes 5242880 | tf_op jit(solution)/shard_map/reduce_scatter | solution.py:1387
  264.2 6.6 copy-start.69
  265.9 47.7 %copy-start.85 = (f32[256]{0:T(256)}, f32[256]{0:T(256)S(1)}, u32[]{:S(2)}) copy-start(f32[256]{0:T(256)S(1)} %multiply_reduce_fusion.5) | copy-start | bytes 3076
  265.9 47.7 %copy-start.81 = (f32[256]{0:T(256)}, f32[256]{0:T(256)S(1)}, u32[]{:S(2)}) copy-start(f32[256]{0:T(256)S(1)} %fusion.32) | copy-start | bytes 3076
  266.0 47.6 %copy-start.57 = (f32[1,2,8,128]{3,1,2,0:T(2,128)}, f32[1,2,8,128]{3,1,2,0:T(2,128)S(1)}, u32[]{:S(2)}) copy-start(f32[1,2,8,128]{3,1,2,0:T(2,128)S(1)} %copy.70) | copy-start | bytes 24580
  313.6 93.5 %copy-start.47 = (f32[1,2,8,128]{3,1,2,0:T(2,128)S(1)}, f32[1,2,8,128]{3,1,2,0:T(2,128)}, u32[]{:S(2)}) copy-start(f32[1,2,8,128]{3,1,2,0:T(2,128)} %copy-done.46) | copy-start | bytes 24580
  313.6 93.5 %copy-start.70 = (f32[256]{0:T(256)S(1)}, f32[256]{0:T(256)}, u32[]{:S(2)}) copy-start(f32[256]{0:T(256)} %copy-done.69) | copy-start | bytes 3076
  313.6 93.5 %copy-start.82 = (f32[256]{0:T(256)S(1)}, f32[256]{0:T(256)}, u32[]{:S(2)}) copy-start(f32[256]{0:T(256)} %copy-done.81) | copy-start | bytes 3076
  410.9 5.2 copy-start.117
  424.2 9.8 copy-start.105
  434.0 14.4 %copy-start.7 = (bf16[1024,1536]{1,0:T(8,128)(2,1)}, bf16[1024,1536]{1,0:T(8,128)(2,1)S(1)}, u32[]{:S(2)}) copy-start(bf16[1024,1536]{1,0:T(8,128)(2,1)S(1)} %add_convert_fusion.4.q_ref.k_ref.v_ref) | copy-start | bytes 9437188
  449.4 44.5 %copy-start.5 = (s32[4]{0:T(128)S(1)}, s32[4]{0:T(128)}, u32[]{:S(2)}) copy-start(s32[4]{0:T(128)} %copy-done.4) | copy-start | bytes 52
  495.2 34.2 %copy-start.28 = (bf16[1024,2048]{1,0:T(8,128)(2,1)S(1)}, bf16[1024,2048]{1,0:T(8,128)(2,1)}, u32[]{:S(2)}) copy-start(bf16[1024,2048]{1,0:T(8,128)(2,1)} %get-tuple-element.59) | copy-start | bytes 12582916
  495.2 34.2 %copy-start.77 = (f32[1024]{0:T(1024)S(1)}, f32[1024]{0:T(1024)}, u32[]{:S(2)}) copy-start(f32[1024]{0:T(1024)} %copy-done.76) | copy-start | bytes 12292
  495.2 34.2 %copy-start.103 = (f32[1024]{0:T(1024)S(1)}, f32[1024]{0:T(1024)}, u32[]{:S(2)}) copy-start(f32[1024]{0:T(1024)} %copy-done.102) | copy-start | bytes 12292
  529.4 13.3 %copy-start = (bf16[1024,1536]{1,0:T(8,128)(2,1)}, bf16[1024,1536]{1,0:T(8,128)(2,1)S(1)}, u32[]{:S(2)}) copy-start(bf16[1024,1536]{1,0:T(8,128)(2,1)S(1)} %attend_back.2) | copy-start | bytes 9437188
  529.5 13.3 %copy-start.12 = (bf16[2,1,256,2048]{3,2,1,0:T(8,128)(2,1)S(1)}, bf16[2,1,256,2048]{3,2,1,0:T(8,128)(2,1)}, u32[]{:S(2)}) copy-start(bf16[2,1,256,2048]{3,2,1,0:T(8,128)(2,1)} %param.18) | copy-start | bytes 6291460
  529.5 13.3 %copy-start.43 = (bf16[256,2048]{1,0:T(8,128)(2,1)S(1)}, bf16[256,2048]{1,0:T(8,128)(2,1)}, u32[]{:S(2)}) copy-start(bf16[256,2048]{1,0:T(8,128)(2,1)} %get-tuple-element.73) | copy-start | bytes 3145732
  529.5 13.3 %copy-start.101 = (f32[1,2,8,128]{3,1,2,0:T(2,128)S(1)}, f32[1,2,8,128]{3,1,2,0:T(2,128)}, u32[]{:S(2)}) copy-start(f32[1,2,8,128]{3,1,2,0:T(2,128)} %copy-done.100) | copy-start | bytes 24580
  550.9 104.2 %copy-start.49 = (f32[1,2,8,128]{3,1,2,0:T(2,128)S(1)}, f32[1,2,8,128]{3,1,2,0:T(2,128)}, u32[]{:S(2)}) copy-start(f32[1,2,8,128]{3,1,2,0:T(2,128)} %copy-done.46) | copy-start | bytes 24580
  550.9 104.2 %copy-start.72 = (f32[256]{0:T(256)S(1)}, f32[256]{0:T(256)}, u32[]{:S(2)}) copy-start(f32[256]{0:T(256)} %copy-done.71) | copy-start | bytes 3076
  550.9 104.2 %copy-start.84 = (f32[256]{0:T(256)S(1)}, f32[256]{0:T(256)}, u32[]{:S(2)}) copy-start(f32[256]{0:T(256)} %copy-done.83) | copy-start | bytes 3076
  655.2 4.7 copy-start.118
  658.9 15.0 %slice-start = ((s8[8388608]{0:T(1024)(128)(4,1)}), s8[4194304]{0:T(1024)(128)(4,1)S(1)}, s32[]{:S(2)}) async-start(s8[8388608]{0:T(1024)(128)(4,1)} %bitcast.211), calls=%async_computation.7 | async-start | bytes 8388608
  659.5 13.3 %copy-start.25 = (f32[256,2048]{1,0:T(8,128)}, f32[256,2048]{1,0:T(8,128)S(1)}, u32[]{:S(2)}) copy-start(f32[256,2048]{1,0:T(8,128)S(1)} %get-tuple-element.175) | copy-start | bytes 6291460
  659.5 13.3 %copy-start.89 = (f32[256]{0:T(256)}, f32[256]{0:T(256)S(1)}, u32[]{:S(2)}) copy-start(f32[256]{0:T(256)S(1)} %negate_multiply_fusion.2) | copy-start | bytes 3076
  659.9 12.9 %copy-start.21 = (bf16[2,1,256,2048]{3,2,1,0:T(8,128)(2,1)S(1)}, bf16[2,1,256,2048]{3,2,1,0:T(8,128)(2,1)}, u32[]{:S(2)}) copy-start(bf16[2,1,256,2048]{3,2,1,0:T(8,128)(2,1)} %param.20) | copy-start | bytes 6291460
  659.9 14.0 %slice-start.1 = ((s8[8388608]{0:T(1024)(128)(4,1)}), s8[4194304]{0:T(1024)(128)(4,1)S(1)}, s32[]{:S(2)}) async-start(s8[8388608]{0:T(1024)(128)(4,1)} %bitcast.211), calls=%async_computation.8 | async-start | bytes 8388608
  677.2 13.1 %copy-start.36 = (bf16[256,2048]{1,0:T(8,128)(2,1)S(1)}, bf16[256,2048]{1,0:T(8,128)(2,1)}, u32[]{:S(2)}) copy-start(bf16[256,2048]{1,0:T(8,128)(2,1)} %copy-done.35) | copy-start | bytes 3145732
  690.3 9.5 copy-start.44
  711.3 197.3 %reduce-scatter.5.cloned.1.call-start = ((), (), s32[]{:S(2)}) async-start(), calls=%async_computation.6 | async-start | bytes 5242880 | tf_op jit(solution)/shard_map/reduce_scatter | solution.py:1392
  761.6 12.9 %copy-start.34 = (bf16[2048,1024]{1,0:T(8,128)(2,1)S(1)}, bf16[2048,1024]{1,0:T(8,128)(2,1)}, u32[]{:S(2)}) copy-start(bf16[2048,1024]{1,0:T(8,128)(2,1)} %get-tuple-element.86) | copy-start | bytes 12582916
  774.5 12.9 %copy-start.10 = (bf16[1024,512]{1,0:T(8,128)(2,1)S(1)}, bf16[1024,512]{1,0:T(8,128)(2,1)}, u32[]{:S(2)}) copy-start(bf16[1024,512]{1,0:T(8,128)(2,1)} %get-tuple-element.81.g_ref) | copy-start | bytes 3145732
  824.1 12.4 %copy-start.62 = (f32[2048]{0:T(1024)S(1)}, f32[2048]{0:T(1024)}, u32[]{:S(2)}) copy-start(f32[2048]{0:T(1024)} %get-tuple-element.169) | copy-start | bytes 24580
  824.1 12.4 %copy-start.65 = (f32[2048]{0:T(1024)S(1)}, f32[2048]{0:T(1024)}, u32[]{:S(2)}) copy-start(f32[2048]{0:T(1024)} %get-tuple-element.168) | copy-start | bytes 24580
  824.1 12.4 %copy-start.61 = (f32[2048]{0:T(1024)S(1)}, f32[2048]{0:T(1024)}, u32[]{:S(2)}) copy-start(f32[2048]{0:T(1024)} %get-tuple-element.152) | copy-start | bytes 24580
  824.1 12.5 %copy-start.64 = (f32[2048]{0:T(1024)S(1)}, f32[2048]{0:T(1024)}, u32[]{:S(2)}) copy-start(f32[2048]{0:T(1024)} %get-tuple-element.150) | copy-start | bytes 24580
  824.1 12.5 %copy-start.63 = (f32[2048]{0:T(1024)S(1)}, f32[2048]{0:T(1024)}, u32[]{:S(2)}) copy-start(f32[2048]{0:T(1024)} %get-tuple-element.180) | copy-start | bytes 24580
  824.1 12.5 %copy-start.66 = (f32[2048]{0:T(1024)S(1)}, f32[2048]{0:T(1024)}, u32[]{:S(2)}) copy-start(f32[2048]{0:T(1024)} %get-tuple-element.170) | copy-start | bytes 24580
  824.1 12.5 %copy-start.94 = (f32[2048]{0:T(1024)S(1)}, f32[2048]{0:T(1024)}, u32[]{:S(2)}) copy-start(f32[2048]{0:T(1024)} %get-tuple-element.156) | copy-start | bytes 24580
  824.2 12.5 %copy-start.93 = (f32[2048]{0:T(1024)S(1)}, f32[2048]{0:T(1024)}, u32[]{:S(2)}) copy-start(f32[2048]{0:T(1024)} %get-tuple-element.157) | copy-start | bytes 24580
  824.2 12.6 %copy-start.59 = (f32[2048]{0:T(1024)S(1)}, f32[2048]{0:T(1024)}, u32[]{:S(2)}) copy-start(f32[2048]{0:T(1024)} %get-tuple-element.166) | copy-start | bytes 24580
  824.2 12.6 %copy-start.60 = (f32[2048]{0:T(1024)S(1)}, f32[2048]{0:T(1024)}, u32[]{:S(2)}) copy-start(f32[2048]{0:T(1024)} %get-tuple-element.167) | copy-start | bytes 24580
  824.2 12.6 %copy-start.1 = (bf16[1024,1536]{1,0:T(8,128)(2,1)S(1)}, bf16[1024,1536]{1,0:T(8,128)(2,1)}, u32[]{:S(2)}) copy-start(bf16[1024,1536]{1,0:T(8,128)(2,1)} %copy-done) | copy-start | bytes 9437188
  852.9 11.6 %copy-start.3 = (bf16[1024,1536]{1,0:T(8,128)(2,1)S(1)}, bf16[1024,1536]{1,0:T(8,128)(2,1)}, u32[]{:S(2)}) copy-start(bf16[1024,1536]{1,0:T(8,128)(2,1)} %copy-done.2) | copy-start | bytes 9437188
  852.9 11.6 %copy-start.31 = (bf16[1024,2048]{1,0:T(8,128)(2,1)S(1)}, bf16[1024,2048]{1,0:T(8,128)(2,1)}, u32[]{:S(2)}) copy-start(bf16[1024,2048]{1,0:T(8,128)(2,1)} %all-gather.8.cloned.1.call-done) | copy-start | bytes 12582916
  908.6 101.9 %copy-start.13 = (bf16[2,1,256,2048]{3,2,1,0:T(8,128)(2,1)S(1)}, bf16[2,1,256,2048]{3,2,1,0:T(8,128)(2,1)}, u32[]{:S(2)}) copy-start(bf16[2,1,256,2048]{3,2,1,0:T(8,128)(2,1)} %param.18) | copy-start | bytes 6291460
  908.6 101.9 %copy-start.73 = (f32[256]{0:T(256)S(1)}, f32[256]{0:T(256)}, u32[]{:S(2)}) copy-start(f32[256]{0:T(256)} %get-tuple-element.226) | copy-start | bytes 3076
  908.6 101.9 %copy-start.74 = (f32[256]{0:T(256)S(1)}, f32[256]{0:T(256)}, u32[]{:S(2)}) copy-start(f32[256]{0:T(256)} %get-tuple-element.227) | copy-start | bytes 3076
  1025.3 6.8 copy-start.37
  1025.3 6.7 copy-start.38
  1025.3 6.7 copy-start.68
  (64 other events, 169.7 us)
Sparse Core Ops, SparseCore 0:
  131.5 101.2 all-gather.3
  234.3 79.2 all-gather.5
  315.7 79.2 all-gather.7
  711.5 92.9 reduce-scatter.2
  823.6 85.0 reduce-scatter.4

commit v7 on v6

--- a/solution.py
+++ b/solution.py
@@ -515,13 +515,12 @@
 
 def front_kernel(
     x_ref, w_ref, wo_ref, we_ref, wr_ref, small_ref,
-    seq_ref, w_out, wo_line, wo_out, we_out, wr_out, small_out, *sems
+    seq_ref, w_out, wo_line, we_out, wr_out, small_out, *sems
 ):
     line, cube = Line(), Cube()
     gather = LineGather(line, x_ref, seq_ref, sems[:5])
     wide = LineGather(line, wo_ref, wo_line, sems[5:10])
     weights = CubeGather(cube, w_ref, w_out, sems[10:15])
-    outer = CubeGather(cube, wo_line, wo_out, sems[15:20])
     tile = small_ref.shape[0]
     moves = [
         (lambda d: small_ref, lambda d: small_out.at[window(d, tile)]),
@@ -529,62 +528,56 @@
     ]
     if wr_out.shape[0] % 128 == 0:
         moves.append(side_to_rows(we_ref, we_out))
-    swap = Swap(cube, moves, sems[20:23])
+    swap = Swap(cube, moves, sems[15:18])
     barrier = pltpu.get_barrier_semaphore()
     line.greet(barrier)
     cube.greet_all(barrier)
     pl.semaphore_wait(barrier, cube.dp - 1 + line.peers())
-    wide.start()
     gather.start()
     weights.start()
-    wide.take(1)
-    wide.take(2)
     gather.take(1)
-    for step in range(3, line.n):
-        wide.take(step)
     for piece in range(1, cube.count):
         if piece.bit_length() < cube.levels:
             weights.take(piece)
-    wide.finish()
-    outer.start()
     swap.start()
     gather.take(2)
+    wide.start()
     for piece in range(1, cube.count):
         weights.take(piece)
-    for piece in range(1, cube.count):
-        outer.take(piece)
+    wide.take(1)
     for step in range(3, line.n):
         gather.take(step)
+        wide.take(step - 1)
+    wide.take(line.n - 1)
     weights.finish()
-    outer.finish()
     swap.finish()
     gather.finish()
+    wide.finish()
 
 
 def front(x, w, w_o, w_e, w_r, small):
     dp, n = lax.axis_size("dp"), lax.axis_size("tensor")
     rows, model = x.shape
-    seq, w_all, _, o_all, e_all, r_all, small_all = pl.pallas_call(
+    seq, w_all, o_line, e_all, r_all, small_all = pl.pallas_call(
         front_kernel,
         out_shape=(
             jax.ShapeDtypeStruct((n * rows, model), BF16),
             jax.ShapeDtypeStruct((dp * w.shape[0], w.shape[1]), BF16),
             jax.ShapeDtypeStruct((w_o.shape[0], n * w_o.shape[1]), BF16),
-            jax.ShapeDtypeStruct((dp * w_o.shape[0], n * w_o.shape[1]), BF16),
             jax.ShapeDtypeStruct((dp * w_e.shape[0], w_e.shape[1] // dp), BF16),
             jax.ShapeDtypeStruct((w_r.shape[0] // dp, w_r.shape[1] * dp), BF16),
             jax.ShapeDtypeStruct((dp * small.shape[0], small.shape[1]), BF16),
         ),
         in_specs=[ANY] * 6,
-        out_specs=(ANY,) * 7,
-        scratch_shapes=2 * LineGather.sems(n) + 2 * CubeGather.sems(dp // 2) + Swap.sems(dp, 3),
+        out_specs=(ANY,) * 6,
+        scratch_shapes=2 * LineGather.sems(n) + CubeGather.sems(dp // 2) + Swap.sems(dp, 3),
         compiler_params=pltpu.CompilerParams(collective_id=0, has_side_effects=True),
         cost_estimate=pl.CostEstimate(flops=80 * 10**9, bytes_accessed=10**7, transcendentals=0),
         name="front",
     )(x, w, w_o, w_e, w_r, small)
     if r_all.shape[0] % 128:
         e_all = lax.all_to_all(w_e, "dp", split_axis=1, concat_axis=0, tiled=True)
-    return seq, w_all, o_all, e_all, r_all, small_all
+    return seq, w_all, o_line, e_all, r_all, small_all
 
 
 class SmallSum:
@@ -1318,9 +1311,10 @@
         )
         attended.append(attend(parents[m, 0], qkv[m], width))
         if m == 0:
-            bias_e, *seq_grad, row_att = exchange(
-                3, gathers=[bias_e], cubes=dy_low, outs=[attended[m]]
+            bias_e, w_ot, grad, row_att = exchange(
+                3, gathers=[bias_e], cubes=[w_ot, dy_low[m]], outs=[attended[m]]
             )
+            seq_grad = [grad]
             bias_e = bias_e.reshape(tn, -1)[:, :mine].reshape(1, tn * mine).astype(F32)
         else:
             part, row_att, col_grad = exchange(
@@ -1335,20 +1329,26 @@
         branch = over(row_att, w_ot, 1, 1)
         hidden.append(x_low[m].astype(F32) + (branch + bias_out))
         normed_two.append(layer_norm(hidden[m], gain_two, shift_two).astype(BF16))
-
-        def attention_back(k):
+        if m < last:
+            grad, normed_two[m] = lax.optimization_barrier((dy_low[m + 1], normed_two[m]))
+            seq_grad.append(lax.all_gather(grad, "dp", axis=0, tiled=True))
+
+        def attention_back(k, awaited=None):
             d_qkv.append(attend_back(parents[k, 0], qkv[k], d_att[k], width))
+            if awaited is not None:
+                d_qkv[k], awaited = lax.optimization_barrier((d_qkv[k], awaited))
             d_one.append(over(d_qkv[k], w_qkv, 1, 1).astype(BF16))
             part = d_one[k].astype(F32)
             return (
                 jnp.sum(part * normal_one[k], 0, keepdims=True),
                 jnp.sum(part, 0, keepdims=True),
                 jnp.sum(d_qkv[k].astype(F32), 0),
+                awaited,
             )
 
         own = None
         if m:
-            gain, shift, bias = attention_back(m - 1)
+            gain, shift, bias, _ = attention_back(m - 1)
             g_gain_one, g_shift_one = g_gain_one + gain, g_shift_one + shift
             g_bias_qkv = g_bias_qkv + bias
             own = d_one[m - 1]
@@ -1385,12 +1385,12 @@
     g_r = outer(activated, seq_grad)
     d_att[last], g_r = lax.optimization_barrier((d_att[last], g_r))
     g_r = lax.psum_scatter(g_r, "tensor", scatter_dimension=0, tiled=True)
-    g_ot = outer(d_branch, row_attended)
+    g_ot = outer([jnp.concatenate(d_branch, 0)], [jnp.concatenate(row_attended, 0)])
     g_ot, d_att[last] = exchange(6, planes=[g_ot], backs=[d_att[last]])
+    d_pre[last], d_att[last] = lax.optimization_barrier((d_pre[last], d_att[last]))
     g_et = outer(d_pre, seq_two)
-    g_et, g_r = lax.optimization_barrier((g_et, g_r))
     g_et = lax.psum_scatter(g_et, "tensor", scatter_dimension=0, tiled=True)
-    gain, shift, bias = attention_back(last)
+    gain, shift, bias, g_r = attention_back(last, g_r)
     g_gain_one, g_shift_one = g_gain_one + gain, g_shift_one + shift
     g_bias_qkv = g_bias_qkv + bias
 
@@ -1412,11 +1412,11 @@
 
     g_qkv = outer(seq_one, d_qkv)
     g_ot = g_ot.astype(BF16).reshape(-1, tn, width).transpose(1, 0, 2).reshape(-1, width)
-    d_one[last], g_ot, g_qkv, out_last, g_reduce, g_expand, little = exchange(
+    d_one[last], g_ot, g_qkv, out_last, g_expand, g_reduce, little = exchange(
         5,
         lines=[d_one[last], g_ot],
         planes=[g_qkv, out_part[last]],
-        swaps=[g_r, g_et],
+        swaps=[g_et, g_r],
         small=[little],
     )
     out_sum.append(out_last)

time: 1050 us -> 1020 us (0.971)
  Pallas kernels: 694 us -> 673 us
  matrix products: 161 us -> 149 us
    pallas_call x1, Pallas kernels: 118 us -> 96.2 us  [front(): pl.pallas_call(front_kernel, out_shape=(jax.ShapeDtypeStruct((n * rows, m...]
    dot_general x12 -> x11, matrix products: 135 us -> 123 us  [over(): lax.dot_general(left, right, (((on_left,), (on_right,)), ((), ())), prefe...]
    unnamed x263 -> x271, local copies, waits for them, and re-layouts: 21.7 us -> 25.7 us
  transfers between devices with their start and end apart: 5 -> 6, of which waited for: 2 -> 2; matrix products, arithmetic and copies ran while one was open for 11% -> 16% of each run, Pallas kernels for 27% -> 37%
where the time goes in v7:
time: 1020 us; the launch traced here: 1010 us
  Pallas kernels  673 us (66%)
  matrix products  149 us (15%)
  waiting for transfers between devices  82.5 us (8%)
  other arithmetic  47.1 us (5%)
  local copies, waits for them, and re-layouts  44 us (4%)
  between operations  16.2 us (2%)
    pallas_call x4, Pallas kernels, exchange(): pl.pallas_call(functools.partial(exchange_kernel, counts), out_shape=tupl...  282 us
    pallas_call x2, Pallas kernels, ffn(): pl.pallas_call(functools.partial(ffn_kernel, host), out_shape=(jax.ShapeD...  197 us
    dot_general x11, matrix products, over(): lax.dot_general(left, right, (((on_left,), (on_right,)), ((), ())), prefe...  123 us
    pallas_call x1, Pallas kernels, front(): pl.pallas_call(front_kernel, out_shape=(jax.ShapeDtypeStruct((n * rows, m...  96.2 us
    pallas_call x2, Pallas kernels, attend_back(): pl.pallas_call(attend_back_kernel, out_shape=jax.ShapeDtypeStruct((rows,...  68.6 us
    all_gather x1, waiting for transfers between devices, body(): w_r = lax.all_gather(w_r, 'tensor', axis=0, tiled=True)  47.1 us
    reduce_scatter x1, waiting for transfers between devices, body(): g_et = lax.psum_scatter(g_et, 'tensor', scatter_dimension=0, tiled=True)  34.5 us
    pallas_call x2, Pallas kernels, attend(): pl.pallas_call(attend_kernel, out_shape=jax.ShapeDtypeStruct((rows, width...  28.8 us
  transfers between devices with their start and end apart: 6, of which 2 were waited for; matrix products, arithmetic and copies ran while one was open for 16% of the time, Pallas kernels for 37%

profile of v7, /device:TPU:0, one launch (start us, length us, event | category | flops | bytes accessed | tf_op | source)
XLA Modules:
  0.0 1012.7 jit_solution(12891677891434998191)
XLA Ops:
  7.4 3.3 slice_bitcast_fusion.3
  13.5 96.2 %front.1 = (bf16[1024,2048]{1,0:T(8,128)(2,1)}, bf16[2048,1536]{1,0:T(8,128)(2,1)}, bf16[256,2048]{1,0:T(8,128)(2,1)}, bf16[2048,256]{1,0:T(8,128)(2,1)}, bf16[2...) custom-call(bf16[256,2048]{1,0:T(8,128)(2,1)} %get-tuple-element.192.x_ref, bf16[256,1536]{1,0:T(8,128)(2,1)} %pad_maximum_fusion.w_ref, ...), custom_call_target="tpu_custom_call" | custom-call | flops 80000000000 | bytes 10000000 | tf_op jit(solution)/shard_map/front/pallas_call | solution.py:561
  112.3 1.5 slice_bitcast_fusion.1
  114.2 3.3 convert_reduce_fusion.3
  118.3 1.2 fusion.11
  119.6 9.9 add_convert_fusion.4.q_ref.k_ref.v_ref
  129.5 14.2 %attend.2.refs_3_ = bf16[1024,512]{1,0:T(8,128)(2,1)S(1)} custom-call(s32[4]{0:T(128)S(1)} %get-tuple-element.223.parents_ref, bf16[1024,1536]{1,0:T(8,128)(2,1)S(1)} %add_convert_fusion.4.q_ref.k_ref.v_ref, bf16[1024,1536]{1,0:T(8,128)(2,1)S(1)} %add_convert_fusion.4.q_ref.k_ref.v_ref, bf16[1024,1536]{1,0:T(8,128)(2,1)S(1)} %add_convert_fusion.4.q_ref.k_ref.v_ref), custom_call_target="tpu_custom_call" | custom-call | flops 16106127360 | bytes 4194304 | tf_op jit(solution)/shard_map/attend/pallas_call | solution.py:842
  143.8 1.0 copy-done.8
  144.7 87.2 %exchange.4 = (bf16[64,128]{1,0:T(8,128)(2,1)}, bf16[2048,2048]{1,0:T(8,128)(2,1)}, bf16[2048,2048]{1,0:T(8,128)(2,1)}, bf16[256,2048]{1,0:T(8,128)(2,1)}) custom-call(bf16[16,128]{1,0:T(8,128)(2,1)} %pad_bitcast_fusion.refs_0_, bf16[256,2048]{1,0:T(8,128)(2,1)} %get-tuple-element.63.refs_1_, bf16[256,2048]{1,0:T(8,128)(2,1)} %get-tuple-element.190.refs_2_, ...), custom_call_target="tpu_custom_call" | custom-call | flops 80000000000 | bytes 10000000 | tf_op jit(solution)/shard_map/exchange/pallas_call | solution.py:761
  232.3 6.3 fusion.56
  239.8 1.4 add_convert_fusion.10.n2_ref
  243.7 47.1 %all-gather.7.cloned.1.call-done.wr_ref = bf16[1024,2048]{1,0:T(8,128)(2,1)} async-done(((bf16[256,2048]{1,0:T(8,128)(2,1)}), bf16[1024,2048]{1,0:T(8,128)(2,1)}) %all-gather.7.cloned.1.call-update) | async-done | bytes 4194320 | tf_op jit(solution)/shard_map/all_gather | solution.py:1298
  290.9 93.6 %ffn_plane.2 = (f32[256,2048]{1,0:T(8,128)}, bf16[2048,2048]{1,0:T(8,128)(2,1)}, bf16[2048,1024]{1,0:T(8,128)(2,1)}, bf16[2048,1024]{1,0:T(8,128)(2,1)}, bf16[2048,2048]{1,0:T(8,128)(2,1)}) custom-call(bf16[256,2048]{1,0:T(8,128)(2,1)} %add_convert_fusion.10.n2_ref, bf16[2048,2048]{1,0:T(8,128)(2,1)} %get-tuple-element.70.dy_ref, ...), custom_call_target="tpu_custom_call" | custom-call | flops 154618822656 | bytes 50331648 | tf_op jit(solution)/shard_map/ffn_plane/pallas_call | solution.py:1194
  384.5 3.7 multiply_reduce_fusion.1
  389.8 1.3 convert_reduce_fusion.10
  391.1 1.0 copy-done.44
  392.1 1.3 copy-done.114
  393.4 3.4 convolution_convert_fusion.4.refs_2_
  396.8 3.0 convert_reduce_fusion.2
  400.3 1.2 fusion.10
  401.6 9.9 add_convert_fusion.3.q_ref.k_ref.v_ref
  411.5 14.6 %attend.3.refs_1_ = bf16[1024,512]{1,0:T(8,128)(2,1)S(1)} custom-call(s32[4]{0:T(128)S(1)} %get-tuple-element.222.parents_ref, bf16[1024,1536]{1,0:T(8,128)(2,1)S(1)} %add_convert_fusion.3.q_ref.k_ref.v_ref, bf16[1024,1536]{1,0:T(8,128)(2,1)S(1)} %add_convert_fusion.3.q_ref.k_ref.v_ref, bf16[1024,1536]{1,0:T(8,128)(2,1)S(1)} %add_convert_fusion.3.q_ref.k_ref.v_ref), custom_call_target="tpu_custom_call" | custom-call | flops 16106127360 | bytes 4194304 | tf_op jit(solution)/shard_map/attend/pallas_call | solution.py:842
  426.1 1.0 copy-done.9
  427.1 45.3 %exchange.5 = (f32[256,2048]{1,0:T(8,128)}, bf16[256,2048]{1,0:T(8,128)(2,1)}, bf16[1024,512]{1,0:T(8,128)(2,1)}) custom-call(bf16[2048,2048]{1,0:T(8,128)(2,1)} %get-tuple-element.74.refs_0_, bf16[1024,512]{1,0:T(8,128)(2,1)} %copy-done.9, bf16[256,2048]{1,0:T(8,128)(2,1)} %convolution_convert_fusion.4.refs_2_), custom_call_target="tpu_custom_call" | custom-call | flops 80000000000 | bytes 10000000 | tf_op jit(solution)/shard_map/exchange/pallas_call | solution.py:761
  473.0 6.4 fusion.57
  480.3 1.4 add_convert_fusion.8.n2_ref
  481.8 13.9 %fusion.58 = f32[1024,2048]{1,0:T(8,128)} fusion(bf16[2048,1024]{1,0:T(8,128)(2,1)S(1)} %copy-done.118, bf16[2048,2048]{1,0:T(8,128)(2,1)} %get-tuple-element.70.dy_ref), kind=kOutput, calls=%fused_computation.169 | convolution fusion | flops 8589934592 | bytes 20971520 | tf_op jit(solution)/shard_map/dot_general | solution.py:32
  495.7 11.8 %fusion.59 = f32[1024,2048]{1,0:T(8,128)} fusion(bf16[2048,1024]{1,0:T(8,128)(2,1)S(1)} %copy-done.37, bf16[2048,2048]{1,0:T(8,128)(2,1)S(1)} %bitcast.212), kind=kOutput, calls=%fused_computation.170 | convolution fusion | flops 8589934592 | bytes 20971520 | tf_op jit(solution)/shard_map/dot_general | solution.py:32
  507.6 34.2 %attend_back.2 = bf16[1024,1536]{1,0:T(8,128)(2,1)S(1)} custom-call(s32[4]{0:T(128)S(1)} %copy-done.5, bf16[1024,1536]{1,0:T(8,128)(2,1)} %copy-done.6, bf16[1024,1536]{1,0:T(8,128)(2,1)} %copy-done.6, bf16[1024,1536]{1,0:T(8,128)(2,1)} %copy-done.6, bf16[1024,512]{1,0:T(8,128)(2,1)S(1)} %copy-done.10), custom_call_target="tpu_custom_call" | custom-call | flops 40265318400 | bytes 7340032 | tf_op jit(solution)/shard_map/attend_back/pallas_call | solution.py:918
  541.9 9.7 convert_reduce_fusion.1
  551.7 11.7 %fusion.47 = f32[2048,1536]{1,0:T(8,128)} fusion(bf16[1024,1536]{1,0:T(8,128)(2,1)S(1)} %attend_back.2, bf16[1024,2048]{1,0:T(8,128)(2,1)S(1)} %copy-done.34, f32[2048]{0:T(1024)S(1)} %bitcast.200, f32[2048]{0:T(1024)S(1)} %bitcast.185, f32[1024]{0:T(1024)S(1)} %copy-done.103, f32[1024]{0:T(1024)S(1)} %copy-done.77), kind=kOutput, calls=%fused_computation.162 | convolution fusion | flops 6455033856 | bytes 19947520 | tf_op jit(solution)/shard_map/dot_general | solution.py:32
  563.4 103.8 %ffn_plane.3 = (f32[256,2048]{1,0:T(8,128)}, bf16[2048,2048]{1,0:T(8,128)(2,1)}, bf16[2048,1024]{1,0:T(8,128)(2,1)}, bf16[2048,1024]{1,0:T(8,128)(2,1)}, bf16[20...) custom-call(bf16[256,2048]{1,0:T(8,128)(2,1)} %add_convert_fusion.8.n2_ref, ...), custom_call_target="tpu_custom_call" | custom-call | flops 154618822656 | bytes 50331648 | tf_op jit(solution)/shard_map/ffn_plane/pallas_call | solution.py:1194
  667.3 3.7 multiply_reduce_fusion
  672.6 1.0 convert_reduce_fusion.12
  673.6 2.2 copy-done.115
  675.8 3.4 convolution_convert_fusion.3.refs_1_
  679.2 6.8 convolution_convert_fusion.refs_0_
  686.1 12.9 %add_convert_fusion.2 = bf16[1024,2048]{1,0:T(8,128)(2,1)} fusion(f32[1024,2048]{1,0:T(8,128)S(1)} %bitcast.210, bf16[2048,1024]{1,0:T(8,128)(2,1)} %get-tuple-element.86, bf16[2048,2048]{1,0:T(8,128)(2,1)S(1)} %bitcast.208), kind=kOutput, calls=%fused_computation.26 | convolution fusion | flops 8594128896 | bytes 25165824 | tf_op jit(solution)/shard_map/dot_general | solution.py:32
  699.0 50.9 %exchange.6 = (f32[256,2048]{1,0:T(8,128)}, bf16[1024,512]{1,0:T(8,128)(2,1)}) custom-call(bf16[2048,2048]{1,0:T(8,128)(2,1)} %convolution_convert_fusion.refs_0_, bf16[256,2048]{1,0:T(8,128)(2,1)} %convolution_convert_fusion.3.refs_1_), custom_call_target="tpu_custom_call" | custom-call | flops 80000000000 | bytes 10000000 | tf_op jit(solution)/shard_map/exchange/pallas_call | solution.py:761
  749.9 15.4 %add_convert_fusion.1 = bf16[1024,2048]{1,0:T(8,128)(2,1)} fusion(f32[1024,2048]{1,0:T(8,128)} %fusion.59, bf16[2048,1024]{1,0:T(8,128)(2,1)} %get-tuple-element.96, bf16[2048,2048]{1,0:T(8,128)(2,1)} %get-tuple-element.97), kind=kOutput, calls=%fused_computation.25 | convolution fusion | flops 8594128896 | bytes 25165824 | tf_op jit(solution)/shard_map/dot_general | solution.py:32
  765.3 1.2 copy-done.11
  766.5 34.4 %attend_back.3 = bf16[1024,1536]{1,0:T(8,128)(2,1)S(1)} custom-call(s32[4]{0:T(128)S(1)} %get-tuple-element.222.parents_ref, bf16[1024,1536]{1,0:T(8,128)(2,1)} %copy-done.7, bf16[1024,1536]{1,0:T(8,128)(2,1)} %copy-done.7, bf16[1024,1536]{1,0:T(8,128)(2,1)} %copy-done.7, bf16[1024,512]{1,0:T(8,128)(2,1)S(1)} %copy-done.11), custom_call_target="tpu_custom_call" | custom-call | flops 40265318400 | bytes 7340032 | tf_op jit(solution)/shard_map/attend_back/pallas_call | solution.py:918
  801.1 1.1 copy.79
  803.1 1.6 copy-done.38
  804.7 1.7 convert_reduce_fusion.4
  808.1 1.6 reshape.508
  809.8 3.0 convert_reduce_fusion.6
  813.4 13.4 %convert_reduce_fusion = (f32[2048]{0:T(1024)S(1)}, f32[2048]{0:T(1024)S(1)}, bf16[1024,2048]{1,0:T(8,128)(2,1)}) fusion(f32[1024]{0:T(1024)S(1)} %copy-done.101, f32[1024]{0:T(1024)S(1)} %copy-done.75, bf16[1024,2048]{1,0:T(8,128)(2,1)} %all-gather.9.cloned.1.call-done, bf16[1024,1536]{1,0:T(8,128)(2,1)} %copy-done.2, bf16[2048,1536]{1,0:T(8,128)(2,1)} %get-tuple-element.65), kind=kOutput, calls=%fused_computation.1 | convolution fusion | flops 6459224064 | bytes 17850368 | tf_op jit(solution)/shard_map/dot_general | solution.py:32
  827.6 14.3 %add_convert_fusion.refs_2_ = bf16[2048,1536]{1,0:T(8,128)(2,1)} fusion(f32[2048,1536]{1,0:T(8,128)} %fusion.47, bf16[1024,1536]{1,0:T(8,128)(2,1)S(1)} %copy-done.3, bf16[1024,2048]{1,0:T(8,128)(2,1)} %all-gather.9.cloned.1.call-done, f32[1024]{0:T(1024)S(1)} %copy-done.101, f32[1024]{0:T(1024)S(1)} %copy-done.75, f32[2048]{0:T(1024)S(1)} %bitcast.201, ...), kind=kOutput, calls=%fused_computation | convolution fusion | flops 6461325312 | bytes 26238976 | tf_op jit(solution)/shard_map/dot_general | solution.py:32
  841.9 34.5 %reduce-scatter.5.cloned.1.call-done.refs_4_ = bf16[256,2048]{1,0:T(8,128)(2,1)} async-done(((bf16[1024,2048]{1,0:T(8,128)(2,1)}), bf16[256,2048]{1,0:T(8,128)(2,1)}) %reduce-scatter.5.cloned.1.call-update) | async-done | bytes 1048592 | tf_op jit(solution)/shard_map/reduce_scatter | solution.py:1392
  876.5 99.0 %exchange.7 = (f32[256,2048]{1,0:T(8,128)}, f32[256,512]{1,0:T(8,128)}, f32[256,1536]{1,0:T(8,128)}, f32[256,2048]{1,0:T(8,128)}, bf16[2048,256]{1,0:T(8,128)(2,...) custom-call(bf16[1024,2048]{1,0:T(8,128)(2,1)} %get-tuple-element.229.refs_0_, bf16[1024,512]{1,0:T(8,128)(2,1)} %bitcast.173, ...), custom_call_target="tpu_custom_call" | custom-call | flops 80000000000 | bytes 10000000 | tf_op jit(solution)/shard_map/exchange/pallas_call | solution.py:761
  975.5 1.4 slice_bitcast_fusion.4
  978.3 3.6 fusion.23
  982.0 1.5 fusion.43
  983.5 1.2 fusion.54
  984.7 2.0 copy.63
  986.8 1.5 convert_bitcast_fusion
  988.3 3.0 copy.64
  992.0 1.5 convert_element_type.290
  994.4 3.8 fusion.32
  998.2 1.5 maximum_bitcast_fusion
  999.7 1.0 copy-done.23
  1001.3 2.1 fusion.34
  1003.5 1.5 maximum_bitcast_fusion.1
  (363 shorter events, 24.3 us)
Async XLA Ops:
  7.3 5.3 copy-start.50
  7.3 5.3 copy-start.51
  7.3 5.3 copy-start.52
  7.3 236.4 %all-gather.5.cloned.1.call-start = ((), (), s32[]{:S(2)}) async-start(), calls=%async_computation.2 | async-start | bytes 5242880 | tf_op jit(solution)/shard_map/all_gather | solution.py:1299
  109.7 181.1 %all-gather.7.cloned.1.call-start = ((), (), s32[]{:S(2)}) async-start(), calls=%async_computation.3 | async-start | bytes 5242880 | tf_op jit(solution)/shard_map/all_gather | solution.py:1298
  110.5 286.3 %all-gather.9.cloned.1.call-start = ((), (), s32[]{:S(2)}) async-start(), calls=%async_computation.4 | async-start | bytes 5242880 | tf_op jit(solution)/shard_map/all_gather | solution.py:1327
  113.8 15.8 %copy-start.4 = (s32[4]{0:T(128)}, s32[4]{0:T(128)S(1)}, u32[]{:S(2)}) copy-start(s32[4]{0:T(128)S(1)} %get-tuple-element.223.parents_ref) | copy-start | bytes 52
  114.1 5.5 copy-start.92
  114.2 5.4 copy-start.53
  119.5 10.0 copy-start.102
  119.6 9.9 copy-start.96
  129.5 14.2 %copy-start.6 = (bf16[1024,1536]{1,0:T(8,128)(2,1)}, bf16[1024,1536]{1,0:T(8,128)(2,1)S(1)}, u32[]{:S(2)}) copy-start(bf16[1024,1536]{1,0:T(8,128)(2,1)S(1)} %add_convert_fusion.4.q_ref.k_ref.v_ref) | copy-start | bytes 9437188
  144.7 87.5 %copy-start.12 = (bf16[2,1,256,2048]{3,2,1,0:T(8,128)(2,1)S(1)}, bf16[2,1,256,2048]{3,2,1,0:T(8,128)(2,1)}, u32[]{:S(2)}) copy-start(bf16[2,1,256,2048]{3,2,1,0:T(8,128)(2,1)} %param.18) | copy-start | bytes 6291460
  232.0 331.4 %all-gather.11.cloned.1.call-start = ((), (), s32[]{:S(2)}) async-start(), calls=%async_computation.5 | async-start | bytes 9437184 | tf_op jit(solution)/shard_map/all_gather | solution.py:1334
  232.2 6.3 copy-start.98
  232.2 6.7 copy-start.57
  232.2 6.7 copy-start.46
  241.2 568.6 %reduce-scatter.3.cloned.1.call-start = ((), (), s32[]{:S(2)}) async-start(), calls=%async_computation.6 | async-start | bytes 5242880 | tf_op jit(solution)/shard_map/reduce_scatter | solution.py:1387
  290.9 93.6 %copy-start.47 = (f32[1,2,8,128]{3,1,2,0:T(2,128)S(1)}, f32[1,2,8,128]{3,1,2,0:T(2,128)}, u32[]{:S(2)}) copy-start(f32[1,2,8,128]{3,1,2,0:T(2,128)} %copy-done.46) | copy-start | bytes 24580
  290.9 93.6 %copy-start.68 = (f32[256]{0:T(256)S(1)}, f32[256]{0:T(256)}, u32[]{:S(2)}) copy-start(f32[256]{0:T(256)} %copy-done.67) | copy-start | bytes 3076
  290.9 93.6 %copy-start.79 = (f32[256]{0:T(256)S(1)}, f32[256]{0:T(256)}, u32[]{:S(2)}) copy-start(f32[256]{0:T(256)} %copy-done.78) | copy-start | bytes 3076
  388.3 5.2 copy-start.114
  401.5 9.9 copy-start.100
  411.5 14.6 %copy-start.7 = (bf16[1024,1536]{1,0:T(8,128)(2,1)}, bf16[1024,1536]{1,0:T(8,128)(2,1)S(1)}, u32[]{:S(2)}) copy-start(bf16[1024,1536]{1,0:T(8,128)(2,1)S(1)} %add_convert_fusion.3.q_ref.k_ref.v_ref) | copy-start | bytes 9437188
  427.1 45.9 %copy-start.13 = (bf16[2,1,256,2048]{3,2,1,0:T(8,128)(2,1)S(1)}, bf16[2,1,256,2048]{3,2,1,0:T(8,128)(2,1)}, u32[]{:S(2)}) copy-start(bf16[2,1,256,2048]{3,2,1,0:T(8,128)(2,1)} %param.18) | copy-start | bytes 6291460
  427.1 45.9 %copy-start.99 = (f32[1,2,8,128]{3,1,2,0:T(2,128)S(1)}, f32[1,2,8,128]{3,1,2,0:T(2,128)}, u32[]{:S(2)}) copy-start(f32[1,2,8,128]{3,1,2,0:T(2,128)} %copy-done.98) | copy-start | bytes 24580
  473.0 8.8 copy-start.118
  479.4 16.3 %slice-start.4 = ((s8[8388608]{0:T(1024)(128)(4,1)}), s8[4194304]{0:T(1024)(128)(4,1)S(1)}, s32[]{:S(2)}) async-start(s8[8388608]{0:T(1024)(128)(4,1)} %bitcast.211), calls=%async_computation.12 | async-start | bytes 8388608
  481.8 13.9 %copy-start.37 = (bf16[2048,1024]{1,0:T(8,128)(2,1)S(1)}, bf16[2048,1024]{1,0:T(8,128)(2,1)}, u32[]{:S(2)}) copy-start(bf16[2048,1024]{1,0:T(8,128)(2,1)} %get-tuple-element.94) | copy-start | bytes 12582916
  481.8 13.9 %slice-start.5 = ((s8[8388608]{0:T(1024)(128)(4,1)}), s8[4194304]{0:T(1024)(128)(4,1)S(1)}, s32[]{:S(2)}) async-start(s8[8388608]{0:T(1024)(128)(4,1)} %bitcast.211), calls=%async_computation.13 | async-start | bytes 8388608
  495.7 11.9 %copy-start.5 = (s32[4]{0:T(128)S(1)}, s32[4]{0:T(128)}, u32[]{:S(2)}) copy-start(s32[4]{0:T(128)} %copy-done.4) | copy-start | bytes 52
  495.7 11.9 %copy-start.10 = (bf16[1024,512]{1,0:T(8,128)(2,1)S(1)}, bf16[1024,512]{1,0:T(8,128)(2,1)}, u32[]{:S(2)}) copy-start(bf16[1024,512]{1,0:T(8,128)(2,1)} %get-tuple-element.81.g_ref) | copy-start | bytes 3145732
  495.7 46.1 %slice-start.6 = ((s8[6291456]{0:T(1024)(128)(4,1)}), s8[4194304]{0:T(1024)(128)(4,1)S(1)}, s32[]{:S(2)}) async-start(s8[6291456]{0:T(1024)(128)(4,1)} %bitcast.213), calls=%async_computation.14 | async-start | bytes 8388608
  507.6 34.3 %copy-start.34 = (bf16[1024,2048]{1,0:T(8,128)(2,1)S(1)}, bf16[1024,2048]{1,0:T(8,128)(2,1)}, u32[]{:S(2)}) copy-start(bf16[1024,2048]{1,0:T(8,128)(2,1)} %get-tuple-element.64) | copy-start | bytes 12582916
  507.6 34.3 %copy-start.77 = (f32[1024]{0:T(1024)S(1)}, f32[1024]{0:T(1024)}, u32[]{:S(2)}) copy-start(f32[1024]{0:T(1024)} %copy-done.76) | copy-start | bytes 12292
  507.6 34.3 %copy-start.103 = (f32[1024]{0:T(1024)S(1)}, f32[1024]{0:T(1024)}, u32[]{:S(2)}) copy-start(f32[1024]{0:T(1024)} %copy-done.102) | copy-start | bytes 12292
  507.6 34.3 %slice-start.7 = ((s8[6291456]{0:T(1024)(128)(4,1)}), s8[2097152]{0:T(1024)(128)(4,1)S(1)}, s32[]{:S(2)}) async-start(s8[6291456]{0:T(1024)(128)(4,1)} %bitcast.213), calls=%async_computation.15 | async-start | bytes 4194304
  541.9 9.8 copy-start
  541.9 9.7 copy-start.55
  541.9 9.7 copy-start.94
  563.3 103.9 %copy-start.48 = (f32[1,2,8,128]{3,1,2,0:T(2,128)S(1)}, f32[1,2,8,128]{3,1,2,0:T(2,128)}, u32[]{:S(2)}) copy-start(f32[1,2,8,128]{3,1,2,0:T(2,128)} %copy-done.46) | copy-start | bytes 24580
  563.4 103.9 %copy-start.70 = (f32[256]{0:T(256)S(1)}, f32[256]{0:T(256)}, u32[]{:S(2)}) copy-start(f32[256]{0:T(256)} %copy-done.69) | copy-start | bytes 3076
  563.4 103.9 %copy-start.81 = (f32[256]{0:T(256)S(1)}, f32[256]{0:T(256)}, u32[]{:S(2)}) copy-start(f32[256]{0:T(256)} %copy-done.80) | copy-start | bytes 3076
  675.8 10.3 %slice-start = ((s8[8388608]{0:T(1024)(128)(4,1)}), s8[4194304]{0:T(1024)(128)(4,1)S(1)}, s32[]{:S(2)}) async-start(s8[8388608]{0:T(1024)(128)(4,1)} %bitcast.207), calls=%async_computation.8 | async-start | bytes 8388608
  675.8 10.3 %slice-start.2 = ((s8[8388608]{0:T(1024)(128)(4,1)}), s8[4194304]{0:T(1024)(128)(4,1)S(1)}, s32[]{:S(2)}) async-start(s8[8388608]{0:T(1024)(128)(4,1)} %bitcast.209), calls=%async_computation.10 | async-start | bytes 8388608
  679.2 6.9 slice-start.1
  679.2 6.9 slice-start.3
  699.0 177.5 %reduce-scatter.5.cloned.1.call-start = ((), (), s32[]{:S(2)}) async-start(), calls=%async_computation.7 | async-start | bytes 5242880 | tf_op jit(solution)/shard_map/reduce_scatter | solution.py:1392
  766.5 34.4 %copy-start.40 = (f32[256,2048]{1,0:T(8,128)S(1)}, f32[256,2048]{1,0:T(8,128)}, u32[]{:S(2)}) copy-start(f32[256,2048]{1,0:T(8,128)} %get-tuple-element.92) | copy-start | bytes 6291460
  766.5 36.6 %copy-start.39 = (bf16[2048,1024]{1,0:T(8,128)(2,1)S(1)}, bf16[2048,1024]{1,0:T(8,128)(2,1)}, u32[]{:S(2)}) copy-start(bf16[2048,1024]{1,0:T(8,128)(2,1)} %get-tuple-element.96) | copy-start | bytes 12582916
  813.3 13.5 %copy-start.91 = (f32[2048]{0:T(1024)S(1)}, f32[2048]{0:T(1024)}, u32[]{:S(2)}) copy-start(f32[2048]{0:T(1024)} %get-tuple-element.165) | copy-start | bytes 24580
  813.3 13.5 %copy-start.90 = (f32[2048]{0:T(1024)S(1)}, f32[2048]{0:T(1024)}, u32[]{:S(2)}) copy-start(f32[2048]{0:T(1024)} %get-tuple-element.164) | copy-start | bytes 24580
  813.3 13.6 %copy-start.65 = (f32[1,8,256]{2,1,0:T(8,128)S(1)}, f32[1,8,256]{2,1,0:T(8,128)}, u32[]{:S(2)}) copy-start(f32[1,8,256]{2,1,0:T(8,128)} %add.325) | copy-start | bytes 24580
  813.3 14.2 %copy-start.3 = (bf16[1024,1536]{1,0:T(8,128)(2,1)S(1)}, bf16[1024,1536]{1,0:T(8,128)(2,1)}, u32[]{:S(2)}) copy-start(bf16[1024,1536]{1,0:T(8,128)(2,1)} %copy-done.2) | copy-start | bytes 9437188
  813.4 14.2 %copy-start.56 = (f32[1,2,8,128]{3,1,2,0:T(2,128)S(1)}, f32[1,2,8,128]{3,1,2,0:T(2,128)}, u32[]{:S(2)}) copy-start(f32[1,2,8,128]{3,1,2,0:T(2,128)} %copy-done.53) | copy-start | bytes 24580
  813.4 14.2 %copy-start.95 = (f32[1,2,8,128]{3,1,2,0:T(2,128)S(1)}, f32[1,2,8,128]{3,1,2,0:T(2,128)}, u32[]{:S(2)}) copy-start(f32[1,2,8,128]{3,1,2,0:T(2,128)} %copy-done.92) | copy-start | bytes 24580
  876.5 101.8 %copy-start.14 = (bf16[2,1,256,2048]{3,2,1,0:T(8,128)(2,1)S(1)}, bf16[2,1,256,2048]{3,2,1,0:T(8,128)(2,1)}, u32[]{:S(2)}) copy-start(bf16[2,1,256,2048]{3,2,1,0:T(8,128)(2,1)} %param.18) | copy-start | bytes 6291460
  876.5 101.8 %copy-start.71 = (f32[256]{0:T(256)S(1)}, f32[256]{0:T(256)}, u32[]{:S(2)}) copy-start(f32[256]{0:T(256)} %get-tuple-element.234) | copy-start | bytes 3076
  876.5 101.8 %copy-start.72 = (f32[256]{0:T(256)S(1)}, f32[256]{0:T(256)}, u32[]{:S(2)}) copy-start(f32[256]{0:T(256)} %get-tuple-element.235) | copy-start | bytes 3076
  994.4 5.3 copy-start.27
  994.4 5.3 copy-start.29
  994.4 5.3 copy-start.31
  994.4 5.3 copy-start.87
  994.4 5.3 copy-start.89
  (69 other events, 204.8 us)
Sparse Core Ops, SparseCore 0:
  109.9 100.1 all-gather.4
  211.7 79.1 all-gather.6
  293.0 79.2 all-gather.8
  374.1 52.9 all-gather.10
  699.1 93.4 reduce-scatter.2
  794.8 81.5 reduce-scatter.4

commit v8 on v7

--- a/solution.py
+++ b/solution.py
@@ -718,7 +718,8 @@
 
 
 def exchange(
-    collective_id, lines=(), planes=(), gathers=(), cubes=(), swaps=(), outs=(), backs=(), small=()
+    collective_id, lines=(), planes=(), gathers=(), cubes=(), swaps=(), outs=(), backs=(), small=(),
+    weight=80,
 ):
     dp, n = lax.axis_size("dp"), lax.axis_size("tensor")
     groups = (lines, planes, gathers, cubes, swaps, outs, backs, small)
@@ -767,7 +768,7 @@
         compiler_params=pltpu.CompilerParams(
             collective_id=collective_id, has_side_effects=True, vmem_limit_bytes=60 << 20
         ),
-        cost_estimate=pl.CostEstimate(flops=80 * 10**9, bytes_accessed=10**7, transcendentals=0),
+        cost_estimate=pl.CostEstimate(flops=weight * 10**9, bytes_accessed=10**7, transcendentals=0),
         name="exchange",
     )(*operands)
 
@@ -945,29 +946,23 @@
 def ffn_kernel(host, n2_ref, dy_ref, we_ref, wr_ref, be_ref, *refs):
     if host:
         line_own, refs = refs[0], refs[1:]
-    sum_ref, seq_ref, act_ref, dpre_ref, part_ref = refs[:5]
-    refs = refs[5:]
+    sum_ref, act_ref, dpre_ref, part_ref = refs[:4]
+    refs = refs[4:]
     if host:
         line_full, refs = refs[0], refs[1:]
-    we, wr, seq, dy_st, act_st, dpre_st, part_st, keep, give, core_in, fold_in = refs[:11]
-    refs = refs[1:]
-    w_sem, own_sem, dy_sem, seq_sem, st_sem = refs[10:15]
-    ag_send, ag_recv, agc_send, agc_recv, rsc_send, rsc_recv, fold_send, fold_recv = refs[15:23]
+    we, wr, seq_st, dy_st, act_st, dpre_st, part_st, keep, give, core_in, fold_in = refs[:11]
+    w_sem, load_sem, st_sem, rsc_send, rsc_recv, fold_send, fold_recv = refs[11:18]
     cube = Cube()
-    levels, me, steps, core_step = cube.levels, cube.me, cube.steps, cube.core_step
-    count, at, owner = cube.count, cube.at, cube.owner
-    rows, model = n2_ref.shape
+    levels, count, owner = cube.levels, cube.count, cube.owner
+    rows, model = sum_ref.shape
     units = wr_ref.shape[0]
     barrier = pltpu.get_barrier_semaphore()
     cube.greet(barrier)
-    hosted = []
     if host:
         line = Line()
         line.greet(barrier)
-        aside = LineScatter(line, line_own, line_full, refs[23:])
+        aside = LineScatter(line, line_own, line_full, refs[18:])
         aside.prepare()
-    load_own = pltpu.make_async_copy(n2_ref, seq.at[0, pl.ds(0, rows)], own_sem)
-    load_own.start()
     parts = we_ref.shape[0] // model
     mine_units = we_ref.shape[1]
     loads_w = [pltpu.make_async_copy(wr_ref, wr, w_sem.at[parts])]
@@ -979,124 +974,70 @@
                 w_sem.at[part],
             )
         )
-    for c in loads_w:
+
+    def load(piece, slot):
+        out = []
+        for half, index in enumerate(owner(piece)):
+            for kind, (ref, stage) in enumerate(((n2_ref, seq_st), (dy_ref, dy_st))):
+                out.append(
+                    pltpu.make_async_copy(
+                        ref.at[window(index, rows)],
+                        stage.at[slot, pl.ds(half * rows, rows)],
+                        load_sem.at[kind, slot, half],
+                    )
+                )
+        return out
+
+    order = sorted(range(count), key=lambda p: (-(p.bit_length()), p))
+    slots = {piece: i % 2 for i, piece in enumerate(order)}
+    loads = {order[0]: load(order[0], 0)}
+    for c in loads[order[0]] + loads_w:
         c.start()
-
-    def load_dy(piece, slot):
-        mine, other = owner(piece)
-        out = []
-        for half, index in enumerate((mine, other)):
-            out.append(
-                pltpu.make_async_copy(
-                    dy_ref.at[pl.ds(pl.multiple_of(index * rows, rows), rows)],
-                    dy_st.at[slot, pl.ds(half * rows, rows)],
-                    dy_sem.at[slot, half],
-                )
-            )
-        return out
-
-    def gather_copy(piece, level):
-        there = piece + (1 << level)
-        return remote(
-            seq.at[piece, pl.ds(0, rows)], seq.at[there, pl.ds(0, rows)],
-            ag_send.at[there], ag_recv.at[there], at(me + steps[level]),
-        )
-
-    def gather_core(piece):
-        return remote(
-            seq.at[piece, pl.ds(0, rows)], seq.at[piece, pl.ds(rows, rows)],
-            agc_send.at[piece], agc_recv.at[piece], at(me + core_step),
-        )
-
-    order = [0] + sorted(range(1, count), key=lambda p: (-(p.bit_length()), p))
-    slots = {piece: i % 2 for i, piece in enumerate(order)}
-    loads = {order[0]: load_dy(order[0], 0)}
-    for c in loads[order[0]]:
-        c.start()
-
-    load_own.wait()
     pl.semaphore_wait(barrier, cube.peers() + (line.peers() if host else 0))
     if host:
         aside.step(1)
-    sends = []
-    for level in range(levels):
-        sends.append(gather_copy(0, level))
-        sends[-1].start()
-    sends.append(gather_core(0))
-    sends[-1].start()
     for c in loads_w:
         c.wait()
-
-    arrived = {0}
-
-    def take(piece):
-        if piece in arrived:
-            return
-        low = piece - (1 << (piece.bit_length() - 1))
-        gather_copy(low, piece.bit_length() - 1).wait_recv()
-        arrived.add(piece)
-        for level in range(piece.bit_length(), levels):
-            sends.append(gather_copy(piece, level))
-            sends[-1].start()
-        sends.append(gather_core(piece))
-        sends[-1].start()
-
-    stores = {}
-    outs = {}
-    core_sends = {}
-    folds = {}
-    done_core = set()
+    stores, core_sends, folds = {}, {}, {}
 
     def add(piece, other):
         @pl.loop(0, rows // 16)
         def _(i):
-            part = pl.ds(pl.multiple_of(i * 16, 16), 16)
+            part = window(i, 16)
             keep[piece, part] = (
                 keep[piece, part].astype(F32) + other[part].astype(F32)
             ).astype(BF16)
 
-    def add_core(piece):
-        if piece in done_core:
-            return
-        core_copy(piece).wait_recv()
-        add(piece, core_in.at[piece])
-        done_core.add(piece)
-
     def core_copy(piece):
         return remote(
             give.at[slots[piece]], core_in.at[piece],
-            rsc_send.at[piece], rsc_recv.at[piece], at(me + core_step),
+            rsc_send.at[piece], rsc_recv.at[piece], cube.at(cube.me + cube.core_step),
         )
 
     def fold_copy(piece):
-        level = piece.bit_length() - 1
-        low = piece - (1 << level)
         return remote(
-            keep.at[piece], fold_in.at[piece - 1],
-            fold_send.at[piece - 1], fold_recv.at[piece - 1], at(me + steps[level]),
+            keep.at[piece], fold_in.at[piece - 1], fold_send.at[piece - 1], fold_recv.at[piece - 1],
+            cube.at(cube.me + cube.steps[piece.bit_length() - 1]),
         )
 
     def fold(piece):
-        add_core(piece)
+        core_copy(piece).wait_recv()
+        add(piece, core_in.at[piece])
         for level in range(levels - 1, piece.bit_length() - 1, -1):
             above = piece + (1 << level)
             fold_copy(above).wait_recv()
             add(piece, fold_in.at[above - 1])
-        if piece:
-            folds[piece] = fold_copy(piece)
-            folds[piece].start()
+        folds[piece] = fold_copy(piece)
+        folds[piece].start()
 
     chunk = 256
     wide = 512
     for turn, piece in enumerate(order):
         slot = turn % 2
-        for earlier in range(1, piece + 1):
-            take(earlier)
-        gather_core(piece).wait_recv()
         for c in loads[piece]:
             c.wait()
         if turn + 1 < count:
-            loads[order[turn + 1]] = load_dy(order[turn + 1], 1 - slot)
+            loads[order[turn + 1]] = load(order[turn + 1], 1 - slot)
             for c in loads[order[turn + 1]]:
                 c.start()
         if turn >= 2:
@@ -1106,8 +1047,8 @@
 
         @pl.loop(0, units // chunk)
         def _(i):
-            cols = pl.ds(pl.multiple_of(i * chunk, chunk), chunk)
-            pre = over(seq[piece], we[:, cols], 1, 0) + be_ref[:, cols]
+            cols = window(i, chunk)
+            pre = over(seq_st[slot], we[:, cols], 1, 0) + be_ref[:, cols]
             d_act = over(dy_st[slot], wr[cols, :], 1, 1)
             square = pre * pre
             t = jnp.tanh(GELU * pre * (1.0 + 0.044715 * square))
@@ -1117,51 +1058,40 @@
             )
             dpre_st[slot, :, cols] = (d_act * slope).astype(BF16)
 
+        if turn:
+            fold(order[turn - 1])
+
         @pl.loop(0, model // wide)
         def _(i):
-            cols = pl.ds(pl.multiple_of(i * wide, wide), wide)
+            cols = window(i, wide)
             d_two = over(dpre_st[slot], we[cols, :], 1, 1).astype(BF16)
             keep[piece, :, cols] = d_two[:rows]
             give[slot, :, cols] = d_two[rows:]
-            out = over(act_st[slot], wr[:, cols], 1, 0).astype(BF16)
-            part_st[slot, :, cols] = out
-
+            part_st[slot, :, cols] = over(act_st[slot], wr[:, cols], 1, 0).astype(BF16)
+
+        core_sends[piece] = core_copy(piece)
+        core_sends[piece].start()
+        stores[turn] = []
+        for half, index in enumerate(owner(piece)):
+            to, part = window(index, rows), pl.ds(half * rows, rows)
+            for kind, (stage, ref) in enumerate(
+                ((act_st, act_ref), (dpre_st, dpre_ref), (part_st, part_ref))
+            ):
+                stores[turn].append(
+                    pltpu.make_async_copy(stage.at[slot, part], ref.at[to], st_sem.at[kind, slot, half])
+                )
+        for c in stores[turn]:
+            c.start()
         if host and turn < line.n - 2:
             aside.step(turn + 2)
-        core_sends[piece] = core_copy(piece)
-        core_sends[piece].start()
-        mine, other = owner(piece)
-        stores[turn] = []
-        for half, index in enumerate((mine, other)):
-            to = pl.ds(pl.multiple_of(index * rows, rows), rows)
-            part = pl.ds(half * rows, rows)
-            stores[turn].append(
-                pltpu.make_async_copy(act_st.at[slot, part], act_ref.at[to], st_sem.at[0, slot, half])
-            )
-            stores[turn].append(
-                pltpu.make_async_copy(dpre_st.at[slot, part], dpre_ref.at[to], st_sem.at[1, slot, half])
-            )
-            stores[turn].append(
-                pltpu.make_async_copy(part_st.at[slot, part], part_ref.at[to], st_sem.at[2, slot, half])
-            )
-            stores[turn].append(
-                pltpu.make_async_copy(seq.at[piece, part], seq_ref.at[to], seq_sem.at[piece, half])
-            )
-        for c in stores[turn]:
-            c.start()
-        if piece.bit_length() == levels:
-            fold(piece)
-    for level in range(levels - 2, -1, -1):
-        for piece in range((1 << level), 2 << level):
-            fold(piece)
-    add_core(0)
+    core_copy(0).wait_recv()
     for level in range(levels):
         fold_copy(1 << level).wait_recv()
 
     @pl.loop(0, rows // 16)
     def _(i):
-        part = pl.ds(pl.multiple_of(i * 16, 16), 16)
-        total = keep[0, part].astype(F32)
+        part = window(i, 16)
+        total = keep[0, part].astype(F32) + core_in[0, part].astype(F32)
         for level in range(levels):
             total = total + fold_in[(1 << level) - 1, part].astype(F32)
         sum_ref[part] = total
@@ -1170,8 +1100,6 @@
         for step in range(count + 2, line.n):
             aside.step(step)
         aside.finish()
-    for s in sends:
-        s.wait_send()
     for turn in range(max(0, count - 2), count):
         for c in stores[turn]:
             c.wait()
@@ -1180,33 +1108,28 @@
         s.wait_send()
 
 
-def ffn(n2, dy_all, we, wr, bias_e, own=None):
+def ffn(n2, dy, we, wr, bias_e, own=None):
     host = own is not None
-    n = lax.axis_size("tensor")
-    rows, model = n2.shape
-    units = wr.shape[0]
-    dp = lax.axis_size("dp")
-    count = dp // 2
-    dma, anywhere, vmem = DMA, ANY, VMEM
-    operands = [n2, dy_all, we, wr, bias_e] + [own] * host
-    lines = [jax.ShapeDtypeStruct((rows, model), F32)] * host
-    flops = 36 * dp * rows * model * units
+    n, dp = lax.axis_size("tensor"), lax.axis_size("dp")
+    rows, model = n2.shape[0] // dp, n2.shape[1]
+    units, count = wr.shape[0], dp // 2
+    operands = [n2, dy, we, wr, bias_e] + [own] * host
+    flops = 30 * dp * rows * model * units
     return pl.pallas_call(
         functools.partial(ffn_kernel, host),
         out_shape=(
             jax.ShapeDtypeStruct((rows, model), F32),
-            jax.ShapeDtypeStruct((dp * rows, model), BF16),
             jax.ShapeDtypeStruct((dp * rows, units), BF16),
             jax.ShapeDtypeStruct((dp * rows, units), BF16),
             jax.ShapeDtypeStruct((dp * rows, model), BF16),
-            *lines,
+            *[jax.ShapeDtypeStruct((rows, model), F32)] * host,
         ),
-        in_specs=[anywhere, anywhere, anywhere, anywhere, vmem] + [anywhere] * host,
-        out_specs=(vmem, anywhere, anywhere, anywhere, anywhere) + (vmem,) * host,
+        in_specs=[ANY] * 4 + [VMEM] + [ANY] * host,
+        out_specs=(VMEM, ANY, ANY, ANY) + (VMEM,) * host,
         scratch_shapes=[
             pltpu.VMEM((model, units), BF16),
             pltpu.VMEM((units, model), BF16),
-            pltpu.VMEM((count, 2 * rows, model), BF16),
+            pltpu.VMEM((2, 2 * rows, model), BF16),
             pltpu.VMEM((2, 2 * rows, model), BF16),
             pltpu.VMEM((2, 2 * rows, units), BF16),
             pltpu.VMEM((2, 2 * rows, units), BF16),
@@ -1215,9 +1138,8 @@
             pltpu.VMEM((2, rows, model), BF16),
             pltpu.VMEM((count, rows, model), BF16),
             pltpu.VMEM((count - 1, rows, model), BF16),
-            dma((n + 1,)), dma, dma((2, 2)), dma((count, 2)), dma((3, 2, 2)),
-            dma((count,)), dma((count,)), dma((count,)), dma((count,)),
-            dma((count,)), dma((count,)), dma((count - 1,)), dma((count - 1,)),
+            DMA((n + 1,)), DMA((2, 2, 2)), DMA((3, 2, 2)),
+            DMA((count,)), DMA((count,)), DMA((count - 1,)), DMA((count - 1,)),
         ]
         + (LineScatter.scratch(n, rows, model) if host else []),
         compiler_params=pltpu.CompilerParams(
@@ -1298,6 +1220,13 @@
     w_r = lax.all_gather(w_r, "tensor", axis=0, tiled=True)
     w_e = lax.all_gather(w_e, "tensor", axis=1 if mine % 128 else 0, tiled=True)
 
+    def outer(left, right):
+        out = None
+        for a, b in zip(left, right):
+            term = over(a, b, 0, 0)
+            out = term if out is None else out + term
+        return out.astype(BF16)
+
     normal_one, seq_one, qkv, attended, hidden, normed_two = [], [], [], [], [], []
     out_part, seq_two, activated, d_pre, d_hidden, d_branch, out_sum = [], [], [], [], [], [], []
     d_qkv, d_one, d_att, row_attended = [], [], [], []
@@ -1333,33 +1262,38 @@
             grad, normed_two[m] = lax.optimization_barrier((dy_low[m + 1], normed_two[m]))
             seq_grad.append(lax.all_gather(grad, "dp", axis=0, tiled=True))
 
-        def attention_back(k, awaited=None):
+        def attention_back(k):
             d_qkv.append(attend_back(parents[k, 0], qkv[k], d_att[k], width))
-            if awaited is not None:
-                d_qkv[k], awaited = lax.optimization_barrier((d_qkv[k], awaited))
             d_one.append(over(d_qkv[k], w_qkv, 1, 1).astype(BF16))
             part = d_one[k].astype(F32)
             return (
                 jnp.sum(part * normal_one[k], 0, keepdims=True),
                 jnp.sum(part, 0, keepdims=True),
                 jnp.sum(d_qkv[k].astype(F32), 0),
-                awaited,
             )
 
         own = None
         if m:
-            gain, shift, bias, _ = attention_back(m - 1)
+            gain, shift, bias = attention_back(m - 1)
             g_gain_one, g_shift_one = g_gain_one + gain, g_shift_one + shift
             g_bias_qkv = g_bias_qkv + bias
             own = d_one[m - 1]
 
-        d_two, seq, act, dpre, part, *line = ffn(normed_two[m], seq_grad[m], w_e, w_r, bias_e, own)
+        if m == 0:
+            (seq,) = exchange(7, cubes=[normed_two[m]])
+        else:
+            seq = lax.all_gather(normed_two[m], "dp", axis=0, tiled=True)
+        d_two, act, dpre, part, *line = ffn(seq, seq_grad[m], w_e, w_r, bias_e, own)
         if m:
             d_one[m - 1] = line[0]
         seq_two.append(seq)
         activated.append(act)
         d_pre.append(dpre)
         out_part.append(part)
+        if m == last:
+            g_r = outer(activated, seq_grad)
+            d_two, g_r = lax.optimization_barrier((d_two, g_r))
+            g_r = lax.psum_scatter(g_r, "tensor", scatter_dimension=0, tiled=True)
         grad32 = dy_low[m].astype(F32)
         norm_value, norm_pull = jax.vjp(layer_norm, hidden[m], gain_two, shift_two)
         d_norm, g_gain, g_shift = norm_pull(d_two)
@@ -1375,22 +1309,13 @@
             next_x, d_branch[m] = lax.optimization_barrier((next_x, d_branch[m]))
             seq_x.append(next_x)
 
-    def outer(left, right):
-        out = None
-        for a, b in zip(left, right):
-            term = over(a, b, 0, 0)
-            out = term if out is None else out + term
-        return out.astype(BF16)
-
-    g_r = outer(activated, seq_grad)
+    g_ot = outer([jnp.concatenate(d_branch, 0)], [jnp.concatenate(row_attended, 0)])
+    g_ot, d_att[last] = exchange(6, planes=[g_ot], backs=[d_att[last]], weight=15)
+    d_att[last], *d_pre = lax.optimization_barrier((d_att[last], *d_pre))
+    g_et = outer(d_pre, seq_two)
     d_att[last], g_r = lax.optimization_barrier((d_att[last], g_r))
-    g_r = lax.psum_scatter(g_r, "tensor", scatter_dimension=0, tiled=True)
-    g_ot = outer([jnp.concatenate(d_branch, 0)], [jnp.concatenate(row_attended, 0)])
-    g_ot, d_att[last] = exchange(6, planes=[g_ot], backs=[d_att[last]])
-    d_pre[last], d_att[last] = lax.optimization_barrier((d_pre[last], d_att[last]))
-    g_et = outer(d_pre, seq_two)
     g_et = lax.psum_scatter(g_et, "tensor", scatter_dimension=0, tiled=True)
-    gain, shift, bias, g_r = attention_back(last, g_r)
+    gain, shift, bias = attention_back(last)
     g_gain_one, g_shift_one = g_gain_one + gain, g_shift_one + shift
     g_bias_qkv = g_bias_qkv + bias
 

time: 1020 us -> 988 us (0.969)
  waiting for transfers between devices: 82.5 us -> 37.5 us
    pallas_call x4 -> x5, Pallas kernels: 282 us -> 337 us  [exchange(): pl.pallas_call(functools.partial(exchange_kernel, counts), out_shape=tupl...]
    pallas_call x2, Pallas kernels: 197 us -> 152 us  [ffn(): pl.pallas_call(functools.partial(ffn_kernel, host), out_shape=(jax.ShapeD...]
    all_gather x1, waiting for transfers between devices: 47.1 us -> 5.35 us  [body(): w_r = lax.all_gather(w_r, 'tensor', axis=0, tiled=True)]
    reduce_scatter x1, waiting for transfers between devices: 34.5 us -> 22.8 us  [body(): g_et = lax.psum_scatter(g_et, 'tensor', scatter_dimension=0, tiled=True)]
    unnamed x271 -> x255, local copies, waits for them, and re-layouts: 25.7 us -> 21.5 us
  transfers between devices with their start and end apart: 6 -> 7, of which waited for: 2 -> 3; matrix products, arithmetic and copies ran while one was open for 16% -> 18% of each run, Pallas kernels for 37% -> 41%
where the time goes in v8:
time: 988 us; the launch traced here: 979 us
  Pallas kernels  683 us (69%)
  matrix products  153 us (15%)
  other arithmetic  52.6 us (5%)
  waiting for transfers between devices  37.5 us (4%)
  local copies, waits for them, and re-layouts  36.6 us (4%)
  between operations  16.1 us (2%)
    pallas_call x5, Pallas kernels, exchange(): pl.pallas_call(functools.partial(exchange_kernel, counts), out_shape=tupl...  337 us
    pallas_call x2, Pallas kernels, ffn(): pl.pallas_call(functools.partial(ffn_kernel, host), out_shape=(jax.ShapeD...  152 us
    dot_general x11, matrix products, over(): lax.dot_general(left, right, (((on_left,), (on_right,)), ((), ())), prefe...  121 us
    pallas_call x1, Pallas kernels, front(): pl.pallas_call(front_kernel, out_shape=(jax.ShapeDtypeStruct((n * rows, m...  96.2 us
    pallas_call x2, Pallas kernels, attend_back(): pl.pallas_call(attend_back_kernel, out_shape=jax.ShapeDtypeStruct((rows,...  68.9 us
    pallas_call x2, Pallas kernels, attend(): pl.pallas_call(attend_kernel, out_shape=jax.ShapeDtypeStruct((rows, width...  28.4 us
    reduce_scatter x1, waiting for transfers between devices, body(): g_et = lax.psum_scatter(g_et, 'tensor', scatter_dimension=0, tiled=True)  22.8 us
    unnamed x255, local copies, waits for them, and re-layouts  21.5 us
  transfers between devices with their start and end apart: 7, of which 3 were waited for; matrix products, arithmetic and copies ran while one was open for 18% of the time, Pallas kernels for 41%

profile of v8, /device:TPU:0, one launch (start us, length us, event | category | flops | bytes accessed | tf_op | source)
XLA Modules:
  0.0 979.1 jit_solution(16394834309254122830)
XLA Ops:
  7.4 3.3 slice_bitcast_fusion.3
  13.5 96.2 %front.1 = (bf16[1024,2048]{1,0:T(8,128)(2,1)}, bf16[2048,1536]{1,0:T(8,128)(2,1)}, bf16[256,2048]{1,0:T(8,128)(2,1)}, bf16[2048,256]{1,0:T(8,128)(2,1)}, bf16[2...) custom-call(bf16[256,2048]{1,0:T(8,128)(2,1)} %get-tuple-element.190.x_ref, bf16[256,1536]{1,0:T(8,128)(2,1)} %pad_maximum_fusion.w_ref, ...), custom_call_target="tpu_custom_call" | custom-call | flops 80000000000 | bytes 10000000 | tf_op jit(solution)/shard_map/front/pallas_call | solution.py:561
  111.3 3.0 convert_reduce_fusion.3
  115.1 1.2 fusion.11
  117.7 1.5 slice_bitcast_fusion.1
  119.2 1.4 copy-done.29
  120.6 9.9 %add_convert_fusion.4.q_ref.k_ref.v_ref = bf16[1024,1536]{1,0:T(8,128)(2,1)S(1)} fusion(bf16[2048,1536]{1,0:T(8,128)(2,1)} %get-tuple-element.64, f32[1536]{0:T(1024)S(1)} %fusion.37, bf16[1024,2048]{1,0:T(8,128)(2,1)S(1)} %copy-done.29, f32[2048]{0:T(1024)S(1)} %bitcast.198, f32[2048]{0:T(1024)S(1)} %bitcast.183, f32[1024]{0:T(1024)S(1)} %add_rsqrt_fusion.1, ...), kind=kOutput, calls=%fused_computation.31 | convolution fusion | flops 6458179584 | bytes 13662208 | tf_op jit(solution)/shard_map/dot_general | solution.py:1239
  130.5 14.2 %attend.2.refs_3_ = bf16[1024,512]{1,0:T(8,128)(2,1)S(1)} custom-call(s32[4]{0:T(128)S(1)} %get-tuple-element.221.parents_ref, bf16[1024,1536]{1,0:T(8,128)(2,1)S(1)} %add_convert_fusion.4.q_ref.k_ref.v_ref, bf16[1024,1536]{1,0:T(8,128)(2,1)S(1)} %add_convert_fusion.4.q_ref.k_ref.v_ref, bf16[1024,1536]{1,0:T(8,128)(2,1)S(1)} %add_convert_fusion.4.q_ref.k_ref.v_ref), custom_call_target="tpu_custom_call" | custom-call | flops 16106127360 | bytes 4194304 | tf_op jit(solution)/shard_map/attend/pallas_call | solution.py:843
  144.7 1.0 copy-done.8
  145.7 89.3 %exchange.5 = (bf16[64,128]{1,0:T(8,128)(2,1)}, bf16[2048,2048]{1,0:T(8,128)(2,1)}, bf16[2048,2048]{1,0:T(8,128)(2,1)}, bf16[256,2048]{1,0:T(8,128)(2,1)}) custom-call(bf16[16,128]{1,0:T(8,128)(2,1)} %pad_bitcast_fusion.refs_0_, bf16[256,2048]{1,0:T(8,128)(2,1)} %get-tuple-element.62.refs_1_, bf16[256,2048]{1,0:T(8,128)(2,1)} %get-tuple-element.188.refs_2_, ...), custom_call_target="tpu_custom_call" | custom-call | flops 80000000000 | bytes 10000000 | tf_op jit(solution)/shard_map/exchange/pallas_call | solution.py:762
  235.4 6.3 fusion.56
  243.0 1.4 add_convert_fusion.10.refs_0_
  244.5 40.5 %exchange.6.n2_ref = bf16[2048,2048]{1,0:T(8,128)(2,1)} custom-call(bf16[256,2048]{1,0:T(8,128)(2,1)} %add_convert_fusion.10.refs_0_), custom_call_target="tpu_custom_call" | custom-call | flops 80000000000 | bytes 10000000 | tf_op jit(solution)/shard_map/exchange/pallas_call | solution.py:762
  285.6 5.3 all-gather.8.cloned.1.call-done.wr_ref
  290.9 65.9 %ffn_plane.2 = (f32[256,2048]{1,0:T(8,128)}, bf16[2048,1024]{1,0:T(8,128)(2,1)}, bf16[2048,1024]{1,0:T(8,128)(2,1)}, bf16[2048,2048]{1,0:T(8,128)(2,1)}) custom-call(bf16[2048,2048]{1,0:T(8,128)(2,1)} %exchange.6.n2_ref, bf16[2048,2048]{1,0:T(8,128)(2,1)} %get-tuple-element.69.dy_ref, bf16[8192,256]{1,0:T(8,128)(2,1)} %all-gather.6.cloned.1.call-done.we_ref, ...), custom_call_target="tpu_custom_call" | custom-call | flops 128849018880 | bytes 50331648 | tf_op jit(solution)/shard_map/ffn_plane/pallas_call | solution.py:1118
  356.9 3.7 multiply_reduce_fusion.1
  361.3 1.3 copy-done.25
  362.6 1.3 convert_reduce_fusion.10
  363.9 8.5 all-gather.10.cloned.1.call-done
  372.4 3.0 convert_reduce_fusion.2
  375.8 1.2 fusion.10
  377.2 7.3 convolution_convert_fusion.4.refs_2_
  384.5 7.4 add_convert_fusion.3.q_ref.k_ref.v_ref
  391.9 14.2 %attend.3.refs_1_ = bf16[1024,512]{1,0:T(8,128)(2,1)S(1)} custom-call(s32[4]{0:T(128)S(1)} %get-tuple-element.220.parents_ref, bf16[1024,1536]{1,0:T(8,128)(2,1)S(1)} %add_convert_fusion.3.q_ref.k_ref.v_ref, bf16[1024,1536]{1,0:T(8,128)(2,1)S(1)} %add_convert_fusion.3.q_ref.k_ref.v_ref, bf16[1024,1536]{1,0:T(8,128)(2,1)S(1)} %add_convert_fusion.3.q_ref.k_ref.v_ref), custom_call_target="tpu_custom_call" | custom-call | flops 16106127360 | bytes 4194304 | tf_op jit(solution)/shard_map/attend/pallas_call | solution.py:843
  407.0 58.0 %exchange.7 = (f32[256,2048]{1,0:T(8,128)}, bf16[256,2048]{1,0:T(8,128)(2,1)}, bf16[1024,512]{1,0:T(8,128)(2,1)}) custom-call(bf16[2048,2048]{1,0:T(8,128)(2,1)} %get-tuple-element.73.refs_0_, bf16[1024,512]{1,0:T(8,128)(2,1)} %copy-done.9, bf16[256,2048]{1,0:T(8,128)(2,1)} %convolution_convert_fusion.4.refs_2_), custom_call_target="tpu_custom_call" | custom-call | flops 80000000000 | bytes 10000000 | tf_op jit(solution)/shard_map/exchange/pallas_call | solution.py:762
  465.1 6.2 fusion.57
  473.2 1.4 add_convert_fusion.8
  476.9 14.8 %fusion.58 = f32[1024,2048]{1,0:T(8,128)} fusion(bf16[2048,1024]{1,0:T(8,128)(2,1)} %get-tuple-element.83, bf16[2048,2048]{1,0:T(8,128)(2,1)} %get-tuple-element.69.dy_ref), kind=kOutput, calls=%fused_computation.169 | convolution fusion | flops 8589934592 | bytes 20971520 | tf_op jit(solution)/shard_map/dot_general | solution.py:32
  491.7 34.4 %attend_back.2 = bf16[1024,1536]{1,0:T(8,128)(2,1)S(1)} custom-call(s32[4]{0:T(128)S(1)} %copy-done.4, bf16[1024,1536]{1,0:T(8,128)(2,1)} %copy-done.6, bf16[1024,1536]{1,0:T(8,128)(2,1)} %copy-done.6, bf16[1024,1536]{1,0:T(8,128)(2,1)} %copy-done.6, bf16[1024,512]{1,0:T(8,128)(2,1)S(1)} %copy-done.10), custom_call_target="tpu_custom_call" | custom-call | flops 40265318400 | bytes 7340032 | tf_op jit(solution)/shard_map/attend_back/pallas_call | solution.py:919
  526.3 9.6 convert_reduce_fusion.1
  535.9 11.7 %fusion.47 = f32[2048,1536]{1,0:T(8,128)} fusion(bf16[1024,1536]{1,0:T(8,128)(2,1)S(1)} %attend_back.2, bf16[1024,2048]{1,0:T(8,128)(2,1)S(1)} %copy-done.30, f32[2048]{0:T(1024)S(1)} %bitcast.200, f32[2048]{0:T(1024)S(1)} %bitcast.185, f32[1024]{0:T(1024)S(1)} %copy-done.100, f32[1024]{0:T(1024)S(1)} %copy-done.74), kind=kOutput, calls=%fused_computation.162 | convolution fusion | flops 6455033856 | bytes 19947520 | tf_op jit(solution)/shard_map/dot_general | solution.py:32
  547.6 86.5 %ffn_plane.3 = (f32[256,2048]{1,0:T(8,128)}, bf16[2048,1024]{1,0:T(8,128)(2,1)}, bf16[2048,1024]{1,0:T(8,128)(2,1)}, bf16[2048,2048]{1,0:T(8,128)(2,1)}, f32[256,2048]{1,0:T(8,128)}) custom-call(bf16[2048,2048]{1,0:T(8,128)(2,1)} %all-gather.12.cloned.1.call-done.n2_ref, bf16[2048,2048]{1,0:T(8,128)(2,1)} %all-gather.14.cloned.1.call-done.dy_ref, ...), custom_call_target="tpu_custom_call" | custom-call | flops 128849018880 | bytes 50331648 | tf_op jit(solution)/shard_map/ffn_plane/pallas_call | solution.py:1118
  634.2 15.4 %add_convert_fusion.2 = bf16[1024,2048]{1,0:T(8,128)(2,1)} fusion(f32[1024,2048]{1,0:T(8,128)} %fusion.58, bf16[2048,1024]{1,0:T(8,128)(2,1)} %get-tuple-element.84, bf16[2048,2048]{1,0:T(8,128)(2,1)} %all-gather.14.cloned.1.call-done.dy_ref), kind=kOutput, calls=%fused_computation.26 | convolution fusion | flops 8594128896 | bytes 25165824 | tf_op jit(solution)/shard_map/dot_general | solution.py:32
  649.6 2.5 multiply_reduce_fusion
  652.2 1.9 fusion.52
  654.6 1.1 copy-done.22
  655.7 2.0 convert_reduce_fusion.12
  657.8 6.9 convolution_convert_fusion.3.refs_1_
  664.7 6.9 convolution_convert_fusion.refs_0_
  671.6 50.4 %exchange.8 = (f32[256,2048]{1,0:T(8,128)}, bf16[1024,512]{1,0:T(8,128)(2,1)}) custom-call(bf16[2048,2048]{1,0:T(8,128)(2,1)} %convolution_convert_fusion.refs_0_, bf16[256,2048]{1,0:T(8,128)(2,1)} %convolution_convert_fusion.3.refs_1_), custom_call_target="tpu_custom_call" | custom-call | flops 15000000512 | bytes 10000000 | tf_op jit(solution)/shard_map/exchange/pallas_call | solution.py:762
  722.0 5.2 convert_reduce_fusion.4
  728.2 1.1 copy.79
  729.3 1.4 copy-done.33
  730.6 12.1 %fusion.59 = f32[1024,2048]{1,0:T(8,128)S(1)} fusion(bf16[2048,1024]{1,0:T(8,128)(2,1)S(1)} %copy-done.33, bf16[2048,2048]{1,0:T(8,128)(2,1)} %exchange.6.n2_ref), kind=kOutput, calls=%fused_computation.170 | convolution fusion | flops 8589934592 | bytes 20971520 | tf_op jit(solution)/shard_map/dot_general | solution.py:32
  742.8 11.5 %add_convert_fusion.1 = bf16[1024,2048]{1,0:T(8,128)(2,1)} fusion(f32[1024,2048]{1,0:T(8,128)S(1)} %fusion.59, bf16[2048,1024]{1,0:T(8,128)(2,1)S(1)} %copy-done.34, bf16[2048,2048]{1,0:T(8,128)(2,1)S(1)} %bitcast.208), kind=kOutput, calls=%fused_computation.25 | convolution fusion | flops 8594128896 | bytes 25165824 | tf_op jit(solution)/shard_map/dot_general | solution.py:32
  754.4 1.1 copy-done.7
  755.5 34.5 %attend_back.3 = bf16[1024,1536]{1,0:T(8,128)(2,1)S(1)} custom-call(s32[4]{0:T(128)S(1)} %get-tuple-element.220.parents_ref, bf16[1024,1536]{1,0:T(8,128)(2,1)} %copy-done.5, bf16[1024,1536]{1,0:T(8,128)(2,1)} %copy-done.5, bf16[1024,1536]{1,0:T(8,128)(2,1)} %copy-done.5, bf16[1024,512]{1,0:T(8,128)(2,1)S(1)} %copy-done.7), custom_call_target="tpu_custom_call" | custom-call | flops 40265318400 | bytes 7340032 | tf_op jit(solution)/shard_map/attend_back/pallas_call | solution.py:919
  790.1 13.2 %convert_reduce_fusion = (f32[2048]{0:T(1024)S(1)}, f32[2048]{0:T(1024)S(1)}, bf16[1024,2048]{1,0:T(8,128)(2,1)}) fusion(f32[1024]{0:T(1024)S(1)} %copy-done.98, f32[1024]{0:T(1024)S(1)} %copy-done.72, bf16[1024,2048]{1,0:T(8,128)(2,1)S(1)} %copy-done.27, bf16[1024,1536]{1,0:T(8,128)(2,1)S(1)} %attend_back.3, bf16[2048,1536]{1,0:T(8,128)(2,1)} %get-tuple-element.64), kind=kOutput, calls=%fused_computation.1 | convolution fusion | flops 6459224064 | bytes 17850368 | tf_op jit(solution)/shard_map/dot_general | solution.py:32
  803.4 3.0 convert_reduce_fusion.6
  807.6 13.7 %add_convert_fusion.refs_2_ = bf16[2048,1536]{1,0:T(8,128)(2,1)} fusion(f32[2048,1536]{1,0:T(8,128)} %fusion.47, bf16[1024,1536]{1,0:T(8,128)(2,1)} %copy-done.2, bf16[1024,2048]{1,0:T(8,128)(2,1)} %all-gather.10.cloned.1.call-done, f32[1024]{0:T(1024)S(1)} %copy-done.98, f32[1024]{0:T(1024)S(1)} %copy-done.72, f32[2048]{0:T(1024)S(1)} %bitcast.201, ...), kind=kOutput, calls=%fused_computation | convolution fusion | flops 6461325312 | bytes 26238976 | tf_op jit(solution)/shard_map/dot_general | solution.py:32
  821.3 22.8 %reduce-scatter.5.cloned.1.call-done.refs_4_ = bf16[256,2048]{1,0:T(8,128)(2,1)} async-done(((bf16[1024,2048]{1,0:T(8,128)(2,1)}), bf16[256,2048]{1,0:T(8,128)(2,1)}) %reduce-scatter.5.cloned.1.call-update) | async-done | bytes 1048592 | tf_op jit(solution)/shard_map/reduce_scatter | solution.py:1317
  844.1 98.8 %exchange.9 = (f32[256,2048]{1,0:T(8,128)}, f32[256,512]{1,0:T(8,128)}, f32[256,1536]{1,0:T(8,128)}, f32[256,2048]{1,0:T(8,128)}, bf16[2048,256]{1,0:T(8,128)(2,...) custom-call(bf16[1024,2048]{1,0:T(8,128)(2,1)} %get-tuple-element.227.refs_0_, bf16[1024,512]{1,0:T(8,128)(2,1)} %bitcast.173, ...), custom_call_target="tpu_custom_call" | custom-call | flops 80000000000 | bytes 10000000 | tf_op jit(solution)/shard_map/exchange/pallas_call | solution.py:762
  944.3 1.4 slice_bitcast_fusion.4
  945.7 3.6 fusion.23
  949.4 1.7 fusion.43
  951.0 1.5 convert_bitcast_fusion
  952.5 3.0 copy.64
  955.5 1.5 convert_element_type.290
  957.6 1.2 fusion.54
  958.8 1.0 copy.63
  960.7 5.2 fusion.34
  966.0 1.5 maximum_bitcast_fusion.1
  969.0 1.0 fusion.32
  970.0 1.5 maximum_bitcast_fusion
  (350 shorter events, 22.8 us)
Async XLA Ops:
  7.3 5.3 copy-start.50
  7.3 278.2 %all-gather.6.cloned.1.call-start = ((), (), s32[]{:S(2)}) async-start(), calls=%async_computation.2 | async-start | bytes 5242880 | tf_op jit(solution)/shard_map/all_gather | solution.py:1221
  109.7 181.2 %all-gather.8.cloned.1.call-start = ((), (), s32[]{:S(2)}) async-start(), calls=%async_computation.3 | async-start | bytes 5242880 | tf_op jit(solution)/shard_map/all_gather | solution.py:1220
  110.5 261.9 %all-gather.10.cloned.1.call-start = ((), (), s32[]{:S(2)}) async-start(), calls=%async_computation.4 | async-start | bytes 5242880 | tf_op jit(solution)/shard_map/all_gather | solution.py:1256
  116.8 13.7 %copy-start.3 = (s32[4]{0:T(128)}, s32[4]{0:T(128)S(1)}, u32[]{:S(2)}) copy-start(s32[4]{0:T(128)S(1)} %get-tuple-element.221.parents_ref) | copy-start | bytes 52
  119.2 11.3 %copy-start.93 = (f32[1536]{0:T(1024)}, f32[1536]{0:T(1024)S(1)}, u32[]{:S(2)}) copy-start(f32[1536]{0:T(1024)S(1)} %fusion.37) | copy-start | bytes 18436
  130.5 14.2 %copy-start.6 = (bf16[1024,1536]{1,0:T(8,128)(2,1)}, bf16[1024,1536]{1,0:T(8,128)(2,1)S(1)}, u32[]{:S(2)}) copy-start(bf16[1024,1536]{1,0:T(8,128)(2,1)S(1)} %add_convert_fusion.4.q_ref.k_ref.v_ref) | copy-start | bytes 9437188
  145.7 89.7 %copy-start.11 = (bf16[2,1,256,2048]{3,2,1,0:T(8,128)(2,1)S(1)}, bf16[2,1,256,2048]{3,2,1,0:T(8,128)(2,1)}, u32[]{:S(2)}) copy-start(bf16[2,1,256,2048]{3,2,1,0:T(8,128)(2,1)} %param.18) | copy-start | bytes 6291460
  235.0 312.5 %all-gather.14.cloned.1.call-start = ((), (), s32[]{:S(2)}) async-start(), calls=%async_computation.6 | async-start | bytes 9437184 | tf_op jit(solution)/shard_map/all_gather | solution.py:1263
  235.3 6.4 copy-start.95
  235.3 7.6 copy-start.44
  235.4 7.6 copy-start.55
  244.4 40.5 %copy-start.70 = (bf16[64,128]{1,0:T(8,128)(2,1)S(1)}, bf16[64,128]{1,0:T(8,128)(2,1)}, u32[]{:S(2)}) copy-start(bf16[64,128]{1,0:T(8,128)(2,1)} %get-tuple-element.72) | copy-start | bytes 49156
  244.4 303.2 %all-gather.12.cloned.1.call-start = ((), (), s32[]{:S(2)}) async-start(), calls=%async_computation.5 | async-start | bytes 9437184 | tf_op jit(solution)/shard_map/all_gather | solution.py:1285
  290.9 65.9 %copy-start.45 = (f32[1,2,8,128]{3,1,2,0:T(2,128)S(1)}, f32[1,2,8,128]{3,1,2,0:T(2,128)}, u32[]{:S(2)}) copy-start(f32[1,2,8,128]{3,1,2,0:T(2,128)} %copy-done.44) | copy-start | bytes 24580
  290.9 65.9 %copy-start.67 = (f32[256]{0:T(256)S(1)}, f32[256]{0:T(256)}, u32[]{:S(2)}) copy-start(f32[256]{0:T(256)} %copy-done.66) | copy-start | bytes 3076
  290.9 65.9 %copy-start.78 = (f32[256]{0:T(256)S(1)}, f32[256]{0:T(256)}, u32[]{:S(2)}) copy-start(f32[256]{0:T(256)} %copy-done.77) | copy-start | bytes 3076
  363.8 13.2 %copy-start.41 = (bf16[256,2048]{1,0:T(8,128)(2,1)}, bf16[256,2048]{1,0:T(8,128)(2,1)S(1)}, u32[]{:S(2)}) copy-start(bf16[256,2048]{1,0:T(8,128)(2,1)S(1)} %get-tuple-element.79) | copy-start | bytes 3145732
  372.4 12.0 %slice-start.2 = ((s8[6291456]{0:T(1024)(128)(4,1)}), s8[4194304]{0:T(1024)(128)(4,1)S(1)}, s32[]{:S(2)}) async-start(s8[6291456]{0:T(1024)(128)(4,1)} %bitcast.209), calls=%async_computation.11 | async-start | bytes 8388608
  375.8 8.6 copy-start.71
  377.1 7.3 copy-start.97
  377.1 7.3 copy-start.52
  377.1 7.3 copy-start.90
  377.1 7.3 copy-start.94
  377.1 7.3 slice-start.3
  391.9 14.2 %copy-start.5 = (bf16[1024,1536]{1,0:T(8,128)(2,1)}, bf16[1024,1536]{1,0:T(8,128)(2,1)S(1)}, u32[]{:S(2)}) copy-start(bf16[1024,1536]{1,0:T(8,128)(2,1)S(1)} %add_convert_fusion.3.q_ref.k_ref.v_ref) | copy-start | bytes 9437188
  407.0 58.0 %copy-start.12 = (bf16[2,1,256,2048]{3,2,1,0:T(8,128)(2,1)S(1)}, bf16[2,1,256,2048]{3,2,1,0:T(8,128)(2,1)}, u32[]{:S(2)}) copy-start(bf16[2,1,256,2048]{3,2,1,0:T(8,128)(2,1)} %param.18) | copy-start | bytes 6291460
  407.0 58.0 %copy-start.96 = (f32[1,2,8,128]{3,1,2,0:T(2,128)S(1)}, f32[1,2,8,128]{3,1,2,0:T(2,128)}, u32[]{:S(2)}) copy-start(f32[1,2,8,128]{3,1,2,0:T(2,128)} %copy-done.95) | copy-start | bytes 24580
  474.7 279.7 %reduce-scatter.3.cloned.1.call-start = ((), (), s32[]{:S(2)}) async-start(), calls=%async_computation.7 | async-start | bytes 5242880 | tf_op jit(solution)/shard_map/reduce_scatter | solution.py:1296
  476.9 14.8 %copy-start.4 = (s32[4]{0:T(128)S(1)}, s32[4]{0:T(128)}, u32[]{:S(2)}) copy-start(s32[4]{0:T(128)} %copy-done.3) | copy-start | bytes 52
  476.9 14.8 %copy-start.10 = (bf16[1024,512]{1,0:T(8,128)(2,1)S(1)}, bf16[1024,512]{1,0:T(8,128)(2,1)}, u32[]{:S(2)}) copy-start(bf16[1024,512]{1,0:T(8,128)(2,1)} %get-tuple-element.81.g_ref) | copy-start | bytes 3145732
  476.9 49.3 %slice-start.4 = ((s8[6291456]{0:T(1024)(128)(4,1)}), s8[4194304]{0:T(1024)(128)(4,1)S(1)}, s32[]{:S(2)}) async-start(s8[6291456]{0:T(1024)(128)(4,1)} %bitcast.211), calls=%async_computation.13 | async-start | bytes 8388608
  491.7 34.5 %copy-start.30 = (bf16[1024,2048]{1,0:T(8,128)(2,1)S(1)}, bf16[1024,2048]{1,0:T(8,128)(2,1)}, u32[]{:S(2)}) copy-start(bf16[1024,2048]{1,0:T(8,128)(2,1)} %get-tuple-element.63) | copy-start | bytes 12582916
  491.7 34.5 %copy-start.74 = (f32[1024]{0:T(1024)S(1)}, f32[1024]{0:T(1024)}, u32[]{:S(2)}) copy-start(f32[1024]{0:T(1024)} %copy-done.73) | copy-start | bytes 12292
  491.7 34.5 %copy-start.100 = (f32[1024]{0:T(1024)S(1)}, f32[1024]{0:T(1024)}, u32[]{:S(2)}) copy-start(f32[1024]{0:T(1024)} %copy-done.99) | copy-start | bytes 12292
  491.7 34.5 %slice-start.5 = ((s8[6291456]{0:T(1024)(128)(4,1)}), s8[2097152]{0:T(1024)(128)(4,1)S(1)}, s32[]{:S(2)}) async-start(s8[6291456]{0:T(1024)(128)(4,1)} %bitcast.211), calls=%async_computation.14 | async-start | bytes 4194304
  526.2 9.7 copy-start
  526.2 9.6 copy-start.53
  526.3 9.6 copy-start.91
  634.2 15.4 %copy-start.18 = (f32[256,2048]{1,0:T(8,128)S(1)}, f32[256,2048]{1,0:T(8,128)}, u32[]{:S(2)}) copy-start(f32[256,2048]{1,0:T(8,128)} %copy-done.17) | copy-start | bytes 6291460
  634.2 15.4 %copy-start.46 = (f32[1,2,8,128]{3,1,2,0:T(2,128)S(1)}, f32[1,2,8,128]{3,1,2,0:T(2,128)}, u32[]{:S(2)}) copy-start(f32[1,2,8,128]{3,1,2,0:T(2,128)} %copy-done.44) | copy-start | bytes 24580
  634.2 15.4 %copy-start.65 = (f32[256]{0:T(256)S(1)}, f32[256]{0:T(256)}, u32[]{:S(2)}) copy-start(f32[256]{0:T(256)} %copy-done.64) | copy-start | bytes 3076
  634.2 15.4 %copy-start.76 = (f32[256]{0:T(256)S(1)}, f32[256]{0:T(256)}, u32[]{:S(2)}) copy-start(f32[256]{0:T(256)} %copy-done.75) | copy-start | bytes 3076
  654.1 190.0 %reduce-scatter.5.cloned.1.call-start = ((), (), s32[]{:S(2)}) async-start(), calls=%async_computation.8 | async-start | bytes 5242880 | tf_op jit(solution)/shard_map/reduce_scatter | solution.py:1317
  657.8 6.9 copy-start.42
  657.8 6.9 copy-start.111
  657.8 6.9 copy-start.112
  722.0 6.0 copy-start.35
  728.2 14.5 %slice-start = ((s8[8388608]{0:T(1024)(128)(4,1)}), s8[4194304]{0:T(1024)(128)(4,1)S(1)}, s32[]{:S(2)}) async-start(s8[8388608]{0:T(1024)(128)(4,1)} %bitcast.207), calls=%async_computation.9 | async-start | bytes 8388608
  730.6 12.1 %copy-start.34 = (bf16[2048,1024]{1,0:T(8,128)(2,1)S(1)}, bf16[2048,1024]{1,0:T(8,128)(2,1)}, u32[]{:S(2)}) copy-start(bf16[2048,1024]{1,0:T(8,128)(2,1)} %get-tuple-element.95) | copy-start | bytes 12582916
  730.6 12.1 %slice-start.1 = ((s8[8388608]{0:T(1024)(128)(4,1)}), s8[4194304]{0:T(1024)(128)(4,1)S(1)}, s32[]{:S(2)}) async-start(s8[8388608]{0:T(1024)(128)(4,1)} %bitcast.207), calls=%async_computation.10 | async-start | bytes 8388608
  754.3 35.7 %copy-start.72 = (f32[1024]{0:T(1024)S(1)}, f32[1024]{0:T(1024)}, u32[]{:S(2)}) copy-start(f32[1024]{0:T(1024)} %copy-done.71) | copy-start | bytes 12292
  754.3 35.7 %copy-start.98 = (f32[1024]{0:T(1024)S(1)}, f32[1024]{0:T(1024)}, u32[]{:S(2)}) copy-start(f32[1024]{0:T(1024)} %copy-done.97) | copy-start | bytes 12292
  755.5 34.5 %copy-start.27 = (bf16[1024,2048]{1,0:T(8,128)(2,1)S(1)}, bf16[1024,2048]{1,0:T(8,128)(2,1)}, u32[]{:S(2)}) copy-start(bf16[1024,2048]{1,0:T(8,128)(2,1)} %all-gather.10.cloned.1.call-done) | copy-start | bytes 12582916
  790.0 13.3 %copy-start.2 = (bf16[1024,1536]{1,0:T(8,128)(2,1)}, bf16[1024,1536]{1,0:T(8,128)(2,1)S(1)}, u32[]{:S(2)}) copy-start(bf16[1024,1536]{1,0:T(8,128)(2,1)S(1)} %attend_back.3) | copy-start | bytes 9437188
  790.0 13.3 %copy-start.88 = (f32[2048]{0:T(1024)S(1)}, f32[2048]{0:T(1024)}, u32[]{:S(2)}) copy-start(f32[2048]{0:T(1024)} %get-tuple-element.162) | copy-start | bytes 24580
  790.0 13.3 %copy-start.87 = (f32[2048]{0:T(1024)S(1)}, f32[2048]{0:T(1024)}, u32[]{:S(2)}) copy-start(f32[2048]{0:T(1024)} %get-tuple-element.163) | copy-start | bytes 24580
  790.0 13.3 %copy-start.1 = (bf16[1024,1536]{1,0:T(8,128)(2,1)S(1)}, bf16[1024,1536]{1,0:T(8,128)(2,1)}, u32[]{:S(2)}) copy-start(bf16[1024,1536]{1,0:T(8,128)(2,1)} %copy-done) | copy-start | bytes 9437188
  844.1 101.6 %copy-start.13 = (bf16[2,1,256,2048]{3,2,1,0:T(8,128)(2,1)S(1)}, bf16[2,1,256,2048]{3,2,1,0:T(8,128)(2,1)}, u32[]{:S(2)}) copy-start(bf16[2,1,256,2048]{3,2,1,0:T(8,128)(2,1)} %param.18) | copy-start | bytes 6291460
  844.1 101.6 %copy-start.68 = (f32[256]{0:T(256)S(1)}, f32[256]{0:T(256)}, u32[]{:S(2)}) copy-start(f32[256]{0:T(256)} %get-tuple-element.232) | copy-start | bytes 3076
  844.1 101.6 %copy-start.69 = (f32[256]{0:T(256)S(1)}, f32[256]{0:T(256)}, u32[]{:S(2)}) copy-start(f32[256]{0:T(256)} %get-tuple-element.233) | copy-start | bytes 3076
  960.7 6.8 copy-start.36
  960.7 6.8 copy-start.37
  960.7 6.8 copy-start.63
  (62 other events, 173.0 us)
Sparse Core Ops, SparseCore 0:
  109.9 100.1 all-gather.5
  211.7 79.2 all-gather.7
  293.1 79.2 all-gather.9
  374.7 59.0 all-gather.13
  474.8 53.4 all-gather.11
  654.2 96.9 reduce-scatter.2
  754.4 89.6 reduce-scatter.4

commit v9 on v8

--- a/solution.py
+++ b/solution.py
@@ -514,13 +514,11 @@
 
 
 def front_kernel(
-    x_ref, w_ref, wo_ref, we_ref, wr_ref, small_ref,
-    seq_ref, w_out, wo_line, we_out, wr_out, small_out, *sems
+    x_ref, w_ref, we_ref, wr_ref, small_ref, seq_ref, w_out, we_out, wr_out, small_out, *sems
 ):
     line, cube = Line(), Cube()
     gather = LineGather(line, x_ref, seq_ref, sems[:5])
-    wide = LineGather(line, wo_ref, wo_line, sems[5:10])
-    weights = CubeGather(cube, w_ref, w_out, sems[10:15])
+    weights = CubeGather(cube, w_ref, w_out, sems[5:10])
     tile = small_ref.shape[0]
     moves = [
         (lambda d: small_ref, lambda d: small_out.at[window(d, tile)]),
@@ -528,7 +526,7 @@
     ]
     if wr_out.shape[0] % 128 == 0:
         moves.append(side_to_rows(we_ref, we_out))
-    swap = Swap(cube, moves, sems[15:18])
+    swap = Swap(cube, moves, sems[10:13])
     barrier = pltpu.get_barrier_semaphore()
     line.greet(barrier)
     cube.greet_all(barrier)
@@ -541,43 +539,37 @@
             weights.take(piece)
     swap.start()
     gather.take(2)
-    wide.start()
     for piece in range(1, cube.count):
         weights.take(piece)
-    wide.take(1)
     for step in range(3, line.n):
         gather.take(step)
-        wide.take(step - 1)
-    wide.take(line.n - 1)
     weights.finish()
     swap.finish()
     gather.finish()
-    wide.finish()
-
-
-def front(x, w, w_o, w_e, w_r, small):
+
+
+def front(x, w, w_e, w_r, small):
     dp, n = lax.axis_size("dp"), lax.axis_size("tensor")
     rows, model = x.shape
-    seq, w_all, o_line, e_all, r_all, small_all = pl.pallas_call(
+    seq, w_all, e_all, r_all, small_all = pl.pallas_call(
         front_kernel,
         out_shape=(
             jax.ShapeDtypeStruct((n * rows, model), BF16),
             jax.ShapeDtypeStruct((dp * w.shape[0], w.shape[1]), BF16),
-            jax.ShapeDtypeStruct((w_o.shape[0], n * w_o.shape[1]), BF16),
             jax.ShapeDtypeStruct((dp * w_e.shape[0], w_e.shape[1] // dp), BF16),
             jax.ShapeDtypeStruct((w_r.shape[0] // dp, w_r.shape[1] * dp), BF16),
             jax.ShapeDtypeStruct((dp * small.shape[0], small.shape[1]), BF16),
         ),
-        in_specs=[ANY] * 6,
-        out_specs=(ANY,) * 6,
-        scratch_shapes=2 * LineGather.sems(n) + CubeGather.sems(dp // 2) + Swap.sems(dp, 3),
+        in_specs=[ANY] * 5,
+        out_specs=(ANY,) * 5,
+        scratch_shapes=LineGather.sems(n) + CubeGather.sems(dp // 2) + Swap.sems(dp, 3),
         compiler_params=pltpu.CompilerParams(collective_id=0, has_side_effects=True),
         cost_estimate=pl.CostEstimate(flops=80 * 10**9, bytes_accessed=10**7, transcendentals=0),
         name="front",
-    )(x, w, w_o, w_e, w_r, small)
+    )(x, w, w_e, w_r, small)
     if r_all.shape[0] % 128:
         e_all = lax.all_to_all(w_e, "dp", split_axis=1, concat_axis=0, tiled=True)
-    return seq, w_all, o_line, e_all, r_all, small_all
+    return seq, w_all, e_all, r_all, small_all
 
 
 class SmallSum:
@@ -629,10 +621,11 @@
 
 
 def exchange_kernel(counts, *refs):
-    lines, planes, gathers, cubes, swaps, outs, backs, small = counts
+    lines, planes, gathers, cubes, swaps, outs, backs, small, spreads = counts
     line, cube = Line(), Cube()
     count = sum(counts)
     pairs, scratch = list(zip(refs[:count], refs[count : 2 * count])), list(refs[2 * count :])
+    whole_refs = [scratch.pop(0) for _ in range(spreads)]
 
     def take(number):
         taken = tuple(scratch[:number])
@@ -649,18 +642,22 @@
     turns += [side_to_rows(*pairs.pop(0)) for _ in range(backs)]
     turn = Swap(line, turns, take(3)) if turns else None
     little = SmallSum(line, cube, *pairs.pop(0), take(7)) if small else None
+    for whole_ref in whole_refs:
+        own, side = pairs.pop(0)
+        lanes.append(LineGather(line, own, side, take(5)))
+        wholes.append(CubeGather(cube, side, whole_ref, take(5)))
     barrier = pltpu.get_barrier_semaphore()
     peers = 0
     if small or turns:
         line.greet_all(barrier)
         peers = line.n - 1
-    elif lines or gathers:
+    elif lanes or lines:
         line.greet(barrier)
         peers = line.peers()
     if small or swaps:
         cube.greet_all(barrier)
         peers = peers + cube.dp - 1
-    elif planes or cubes:
+    elif planes or wholes:
         cube.greet(barrier)
         peers = peers + cube.peers()
     for s in sums:
@@ -680,6 +677,15 @@
         f.start()
     if small:
         little.middle()
+    if spreads:
+        for step in range(1, line.n):
+            for lane in lanes:
+                lane.take(step)
+        for lane in lanes:
+            lane.finish()
+        for whole in wholes[1:]:
+            whole.start()
+        lanes = []
     pieces = [p for p in folds[0].order() if p] if planes else []
     per = -(-len(pieces) // (line.n - 1))
     for step in range(1, line.n):
@@ -701,7 +707,8 @@
         for whole in wholes[step - 1 : step]:
             whole.finish()
         for whole in wholes[step : step + 1]:
-            whole.start()
+            if not spreads:
+                whole.start()
     for f in folds:
         f.finish()
     for lane in lanes:
@@ -719,10 +726,10 @@
 
 def exchange(
     collective_id, lines=(), planes=(), gathers=(), cubes=(), swaps=(), outs=(), backs=(), small=(),
-    weight=80,
+    spreads=(), weight=80,
 ):
     dp, n = lax.axis_size("dp"), lax.axis_size("tensor")
-    groups = (lines, planes, gathers, cubes, swaps, outs, backs, small)
+    groups = (lines, planes, gathers, cubes, swaps, outs, backs, small, spreads)
     counts = tuple(len(group) for group in groups)
     operands = [part for group in groups for part in group]
     out_shape, out_specs, scratch = [], [], []
@@ -759,6 +766,11 @@
         rows, d = part.shape[1:]
         result(rows, d, F32, VMEM)
         scratch += SmallSum.scratch(dp, n, rows, d)
+    for part in spreads:
+        result(part.shape[0], n * part.shape[1], BF16, ANY)
+        scratch += LineGather.sems(n) + CubeGather.sems(dp // 2)
+    for part in spreads:
+        result(dp * part.shape[0], n * part.shape[1], BF16, ANY)
     return pl.pallas_call(
         functools.partial(exchange_kernel, counts),
         out_shape=tuple(out_shape),
@@ -943,13 +955,9 @@
     )(parents, qkv, qkv, qkv, grad)
 
 
-def ffn_kernel(host, n2_ref, dy_ref, we_ref, wr_ref, be_ref, *refs):
-    if host:
-        line_own, refs = refs[0], refs[1:]
+def ffn_kernel(n2_ref, dy_ref, we_ref, wr_ref, be_ref, *refs):
     sum_ref, act_ref, dpre_ref, part_ref = refs[:4]
     refs = refs[4:]
-    if host:
-        line_full, refs = refs[0], refs[1:]
     we, wr, seq_st, dy_st, act_st, dpre_st, part_st, keep, give, core_in, fold_in = refs[:11]
     w_sem, load_sem, st_sem, rsc_send, rsc_recv, fold_send, fold_recv = refs[11:18]
     cube = Cube()
@@ -958,11 +966,6 @@
     units = wr_ref.shape[0]
     barrier = pltpu.get_barrier_semaphore()
     cube.greet(barrier)
-    if host:
-        line = Line()
-        line.greet(barrier)
-        aside = LineScatter(line, line_own, line_full, refs[18:])
-        aside.prepare()
     parts = we_ref.shape[0] // model
     mine_units = we_ref.shape[1]
     loads_w = [pltpu.make_async_copy(wr_ref, wr, w_sem.at[parts])]
@@ -993,9 +996,7 @@
     loads = {order[0]: load(order[0], 0)}
     for c in loads[order[0]] + loads_w:
         c.start()
-    pl.semaphore_wait(barrier, cube.peers() + (line.peers() if host else 0))
-    if host:
-        aside.step(1)
+    pl.semaphore_wait(barrier, cube.peers())
     for c in loads_w:
         c.wait()
     stores, core_sends, folds = {}, {}, {}
@@ -1082,8 +1083,6 @@
                 )
         for c in stores[turn]:
             c.start()
-        if host and turn < line.n - 2:
-            aside.step(turn + 2)
     core_copy(0).wait_recv()
     for level in range(levels):
         fold_copy(1 << level).wait_recv()
@@ -1096,10 +1095,6 @@
             total = total + fold_in[(1 << level) - 1, part].astype(F32)
         sum_ref[part] = total
 
-    if host:
-        for step in range(count + 2, line.n):
-            aside.step(step)
-        aside.finish()
     for turn in range(max(0, count - 2), count):
         for c in stores[turn]:
             c.wait()
@@ -1108,24 +1103,21 @@
         s.wait_send()
 
 
-def ffn(n2, dy, we, wr, bias_e, own=None):
-    host = own is not None
+def ffn(n2, dy, we, wr, bias_e):
     n, dp = lax.axis_size("tensor"), lax.axis_size("dp")
     rows, model = n2.shape[0] // dp, n2.shape[1]
     units, count = wr.shape[0], dp // 2
-    operands = [n2, dy, we, wr, bias_e] + [own] * host
     flops = 30 * dp * rows * model * units
     return pl.pallas_call(
-        functools.partial(ffn_kernel, host),
+        ffn_kernel,
         out_shape=(
             jax.ShapeDtypeStruct((rows, model), F32),
             jax.ShapeDtypeStruct((dp * rows, units), BF16),
             jax.ShapeDtypeStruct((dp * rows, units), BF16),
             jax.ShapeDtypeStruct((dp * rows, model), BF16),
-            *[jax.ShapeDtypeStruct((rows, model), F32)] * host,
         ),
-        in_specs=[ANY] * 4 + [VMEM] + [ANY] * host,
-        out_specs=(VMEM, ANY, ANY, ANY) + (VMEM,) * host,
+        in_specs=[ANY] * 4 + [VMEM],
+        out_specs=(VMEM, ANY, ANY, ANY),
         scratch_shapes=[
             pltpu.VMEM((model, units), BF16),
             pltpu.VMEM((units, model), BF16),
@@ -1140,16 +1132,15 @@
             pltpu.VMEM((count - 1, rows, model), BF16),
             DMA((n + 1,)), DMA((2, 2, 2)), DMA((3, 2, 2)),
             DMA((count,)), DMA((count,)), DMA((count - 1,)), DMA((count - 1,)),
-        ]
-        + (LineScatter.scratch(n, rows, model) if host else []),
+        ],
         compiler_params=pltpu.CompilerParams(
-            collective_id=2 if host else 1, has_side_effects=True, vmem_limit_bytes=62 << 20
+            collective_id=1, has_side_effects=True, vmem_limit_bytes=62 << 20
         ),
         cost_estimate=pl.CostEstimate(
             flops=flops, bytes_accessed=8 * dp * rows * (model + units), transcendentals=dp * rows * units
         ),
         name="ffn_plane",
-    )(*operands)
+    )(n2, dy, we, wr, bias_e)
 
 
 def body(
@@ -1197,9 +1188,7 @@
     used = small.shape[0]
     small = jnp.pad(small, (0, -used % 2048)).reshape(-1, 128)
     w_qkv = jnp.concatenate([w_query, w_key, w_value], axis=1)
-    seq_x0, w_qkv, w_ot, w_e, w_r, small = front(
-        x_low[0], w_qkv, w_out.T, w_expand, w_reduce, small
-    )
+    seq_x0, w_qkv, w_e, w_r, small = front(x_low[0], w_qkv, w_expand, w_reduce, small)
     small = small.reshape(dp, -1)[:, :used]
     gain_one, shift_one, bias_out, gain_two, shift_two, bias_red = [
         small[:, i * cut : (i + 1) * cut].reshape(1, model).astype(F32) for i in range(6)
@@ -1240,8 +1229,8 @@
         )
         attended.append(attend(parents[m, 0], qkv[m], width))
         if m == 0:
-            bias_e, w_ot, grad, row_att = exchange(
-                3, gathers=[bias_e], cubes=[w_ot, dy_low[m]], outs=[attended[m]]
+            bias_e, grad, row_att, _, w_ot = exchange(
+                3, gathers=[bias_e], cubes=[dy_low[m]], outs=[attended[m]], spreads=[w_out.T]
             )
             seq_grad = [grad]
             bias_e = bias_e.reshape(tn, -1)[:, :mine].reshape(1, tn * mine).astype(F32)
@@ -1272,27 +1261,29 @@
                 jnp.sum(d_qkv[k].astype(F32), 0),
             )
 
-        own = None
         if m:
+            normed_two[m], seq_grad[m] = lax.optimization_barrier((normed_two[m], seq_grad[m]))
+            next_two = lax.all_gather(normed_two[m], "dp", axis=0, tiled=True)
             gain, shift, bias = attention_back(m - 1)
             g_gain_one, g_shift_one = g_gain_one + gain, g_shift_one + shift
             g_bias_qkv = g_bias_qkv + bias
-            own = d_one[m - 1]
+            next_two, d_one[m - 1] = lax.optimization_barrier((next_two, d_one[m - 1]))
+            d_one[m - 1] = lax.psum_scatter(
+                d_one[m - 1], "tensor", scatter_dimension=0, tiled=True
+            )
 
         if m == 0:
             (seq,) = exchange(7, cubes=[normed_two[m]])
         else:
-            seq = lax.all_gather(normed_two[m], "dp", axis=0, tiled=True)
-        d_two, act, dpre, part, *line = ffn(seq, seq_grad[m], w_e, w_r, bias_e, own)
-        if m:
-            d_one[m - 1] = line[0]
+            seq = next_two
+        d_two, act, dpre, part = ffn(seq, seq_grad[m], w_e, w_r, bias_e)
         seq_two.append(seq)
         activated.append(act)
         d_pre.append(dpre)
         out_part.append(part)
         if m == last:
             g_r = outer(activated, seq_grad)
-            d_two, g_r = lax.optimization_barrier((d_two, g_r))
+            d_two, g_r, *d_one = lax.optimization_barrier((d_two, g_r, *d_one))
             g_r = lax.psum_scatter(g_r, "tensor", scatter_dimension=0, tiled=True)
         grad32 = dy_low[m].astype(F32)
         norm_value, norm_pull = jax.vjp(layer_norm, hidden[m], gain_two, shift_two)
@@ -1335,6 +1326,7 @@
     little = jnp.concatenate([rows, row_qv, row_e], 1)
     little = jnp.pad(little, ((0, 0), (0, -little.shape[1] % 1024))).reshape(dp, -1, 128)
 
+    d_one[last], *d_qkv = lax.optimization_barrier((d_one[last], *d_qkv))
     g_qkv = outer(seq_one, d_qkv)
     g_ot = g_ot.astype(BF16).reshape(-1, tn, width).transpose(1, 0, 2).reshape(-1, width)
     d_one[last], g_ot, g_qkv, out_last, g_expand, g_reduce, little = exchange(
@@ -1364,7 +1356,7 @@
         first_value, first_pull = jax.vjp(
             lambda rows: layer_norm(rows, gain_one, shift_one), x_low[m].astype(F32)
         )
-        input_grad.append((d_hidden[m] + first_pull(d_one[m])[0]).astype(BF16))
+        input_grad.append((d_hidden[m] + first_pull(d_one[m].astype(F32))[0]).astype(BF16))
 
     return (
         jnp.stack(layer_out, 0)[:, None],

time: 988 us -> 985 us (level)
  waiting for transfers between devices: 37.5 us -> 10.9 us
  Pallas kernels: 683 us -> 702 us
    pallas_call x5, Pallas kernels: 337 us -> 375 us  [exchange(): pl.pallas_call(functools.partial(exchange_kernel, counts), out_shape=tupl...]
    pallas_call x1, Pallas kernels: 96.2 us -> 79.2 us  [front(): pl.pallas_call(front_kernel, out_shape=(jax.ShapeDtypeStruct((n * rows, m...]
    reduce_scatter x1, waiting for transfers between devices: 22.8 us -> 10 us  [body(): g_et = lax.psum_scatter(g_et, 'tensor', scatter_dimension=0, tiled=True)]
    unnamed x255 -> x231, local copies, waits for them, and re-layouts: 21.5 us -> 23.8 us
  transfers between devices with their start and end apart: 7 -> 8, of which waited for: 3 -> 1; matrix products, arithmetic and copies ran while one was open for 18% -> 20% of each run, Pallas kernels for 41% -> 53%
where the time goes in v9:
time: 985 us; the launch traced here: 982 us
  Pallas kernels  702 us (71%)
  matrix products  154 us (16%)
  other arithmetic  51.4 us (5%)
  local copies, waits for them, and re-layouts  46.3 us (5%)
  between operations  16 us (2%)
  waiting for transfers between devices  10.9 us (1%)
    pallas_call x5, Pallas kernels, exchange(): pl.pallas_call(functools.partial(exchange_kernel, counts), out_shape=tupl...  375 us
    pallas_call x2, Pallas kernels, ffn(): pl.pallas_call(ffn_kernel, out_shape=(jax.ShapeDtypeStruct((rows, model),...  151 us
    dot_general x11, matrix products, over(): lax.dot_general(left, right, (((on_left,), (on_right,)), ((), ())), prefe...  122 us
    pallas_call x1, Pallas kernels, front(): pl.pallas_call(front_kernel, out_shape=(jax.ShapeDtypeStruct((n * rows, m...  79.2 us
    pallas_call x2, Pallas kernels, attend_back(): pl.pallas_call(attend_back_kernel, out_shape=jax.ShapeDtypeStruct((rows,...  68.7 us
    pallas_call x2, Pallas kernels, attend(): pl.pallas_call(attend_kernel, out_shape=jax.ShapeDtypeStruct((rows, width...  28.4 us
    unnamed x231, local copies, waits for them, and re-layouts  23.8 us
  transfers between devices with their start and end apart: 8, of which 1 were waited for; matrix products, arithmetic and copies ran while one was open for 20% of the time, Pallas kernels for 53%

profile of v9, /device:TPU:0, one launch (start us, length us, event | category | flops | bytes accessed | tf_op | source)
XLA Modules:
  0.0 981.8 jit_solution(16996121748989782728)
XLA Ops:
  9.6 4.1 concatenate.27
  14.3 3.2 slice_bitcast_fusion.3
  17.5 0.9 pad_maximum_fusion.w_ref
  18.5 79.2 %front.1 = (bf16[1024,2048]{1,0:T(8,128)(2,1)}, bf16[2048,1536]{1,0:T(8,128)(2,1)}, bf16[2048,256]{1,0:T(8,128)(2,1)}, bf16[256,2048]{1,0:T(8,128)(2,1)}, bf16[128,128]{1,0:T(8,128)(2,1)}) custom-call(bf16[256,2048]{1,0:T(8,128)(2,1)} %get-tuple-element.202.x_ref, bf16[256,1536]{1,0:T(8,128)(2,1)} %pad_maximum_fusion.w_ref, bf16[256,2048]{1,0:T(8,128)(2,1)} %we_ref.1, ...), custom_call_target="tpu_custom_call" | custom-call | flops 80000000000 | bytes 10000000 | tf_op jit(solution)/shard_map/front/pallas_call | solution.py:554
  100.8 1.5 slice_bitcast_fusion.1
  102.3 1.9 copy-done.30
  104.8 1.2 fusion.11
  107.4 10.6 %add_convert_fusion.4.q_ref.k_ref.v_ref = bf16[1024,1536]{1,0:T(8,128)(2,1)S(1)} fusion(bf16[2048,1536]{1,0:T(8,128)(2,1)} %get-tuple-element.69, f32[1536]{0:T(1024)S(1)} %fusion.38, bf16[1024,2048]{1,0:T(8,128)(2,1)} %get-tuple-element.68, f32[2048]{0:T(1024)S(1)} %bitcast.196, f32[2048]{0:T(1024)S(1)} %bitcast.183, f32[1024]{0:T(1024)S(1)} %add_rsqrt_fusion.1, ...), kind=kOutput, calls=%fused_computation.31 | convolution fusion | flops 6458179584 | bytes 13662208 | tf_op jit(solution)/shard_map/dot_general | solution.py:1228
  118.1 14.2 %attend.2.refs_2_ = bf16[1024,512]{1,0:T(8,128)(2,1)S(1)} custom-call(s32[4]{0:T(128)S(1)} %get-tuple-element.233.parents_ref, bf16[1024,1536]{1,0:T(8,128)(2,1)S(1)} %add_convert_fusion.4.q_ref.k_ref.v_ref, bf16[1024,1536]{1,0:T(8,128)(2,1)S(1)} %add_convert_fusion.4.q_ref.k_ref.v_ref, bf16[1024,1536]{1,0:T(8,128)(2,1)S(1)} %add_convert_fusion.4.q_ref.k_ref.v_ref), custom_call_target="tpu_custom_call" | custom-call | flops 16106127360 | bytes 4194304 | tf_op jit(solution)/shard_map/attend/pallas_call | solution.py:855
  132.3 1.0 copy-done.9
  133.2 138.3 %exchange.5 = (bf16[64,128]{1,0:T(8,128)(2,1)}, bf16[2048,2048]{1,0:T(8,128)(2,1)}, bf16[256,2048]{1,0:T(8,128)(2,1)}, bf16[256,2048]{1,0:T(8,128)(2,1)}, bf16[2048,2048]{1,0:T(8,128)(2,1)}) custom-call(bf16[16,128]{1,0:T(8,128)(2,1)} %pad_bitcast_fusion.refs_0_, bf16[256,2048]{1,0:T(8,128)(2,1)} %get-tuple-element.200.refs_1_, bf16[1024,512]{1,0:T(8,128)(2,1)} %copy-done.9, ...), custom_call_target="tpu_custom_call" | custom-call | flops 80000000000 | bytes 10000000 | tf_op jit(solution)/shard_map/exchange/pallas_call | solution.py:774
  271.9 6.2 fusion.56
  279.4 1.4 add_convert_fusion.10.refs_0_
  281.6 42.6 %exchange.6.n2_ref = bf16[2048,2048]{1,0:T(8,128)(2,1)} custom-call(bf16[256,2048]{1,0:T(8,128)(2,1)} %add_convert_fusion.10.refs_0_), custom_call_target="tpu_custom_call" | custom-call | flops 80000000000 | bytes 10000000 | tf_op jit(solution)/shard_map/exchange/pallas_call | solution.py:774
  324.3 86.6 %ffn_plane.2 = (f32[256,2048]{1,0:T(8,128)}, bf16[2048,1024]{1,0:T(8,128)(2,1)}, bf16[2048,1024]{1,0:T(8,128)(2,1)}, bf16[2048,2048]{1,0:T(8,128)(2,1)}) custom-call(bf16[2048,2048]{1,0:T(8,128)(2,1)} %exchange.6.n2_ref, bf16[2048,2048]{1,0:T(8,128)(2,1)} %get-tuple-element.74.dy_ref, bf16[8192,256]{1,0:T(8,128)(2,1)} %all-gather.6.cloned.1.call-done.we_ref, ...), custom_call_target="tpu_custom_call" | custom-call | flops 128849018880 | bytes 50331648 | tf_op jit(solution)/shard_map/ffn_plane/pallas_call | solution.py:1111
  411.0 3.7 multiply_reduce_fusion.1
  415.4 1.3 copy-done.24
  416.7 1.3 convert_reduce_fusion.10
  418.0 3.2 convert_reduce_fusion.2
  421.9 1.2 fusion.10
  423.3 7.0 convolution_convert_fusion.4.refs_2_
  430.3 7.4 add_convert_fusion.3.q_ref.k_ref.v_ref
  437.7 14.2 %attend.3.refs_1_ = bf16[1024,512]{1,0:T(8,128)(2,1)S(1)} custom-call(s32[4]{0:T(128)S(1)} %get-tuple-element.232.parents_ref, bf16[1024,1536]{1,0:T(8,128)(2,1)S(1)} %add_convert_fusion.3.q_ref.k_ref.v_ref, bf16[1024,1536]{1,0:T(8,128)(2,1)S(1)} %add_convert_fusion.3.q_ref.k_ref.v_ref, bf16[1024,1536]{1,0:T(8,128)(2,1)S(1)} %add_convert_fusion.3.q_ref.k_ref.v_ref), custom_call_target="tpu_custom_call" | custom-call | flops 16106127360 | bytes 4194304 | tf_op jit(solution)/shard_map/attend/pallas_call | solution.py:855
  451.9 1.0 copy-done.10
  452.9 44.5 %exchange.7 = (f32[256,2048]{1,0:T(8,128)}, bf16[256,2048]{1,0:T(8,128)(2,1)}, bf16[1024,512]{1,0:T(8,128)(2,1)}) custom-call(bf16[2048,2048]{1,0:T(8,128)(2,1)} %get-tuple-element.78.refs_0_, bf16[1024,512]{1,0:T(8,128)(2,1)} %copy-done.10, bf16[256,2048]{1,0:T(8,128)(2,1)} %convolution_convert_fusion.4.refs_2_), custom_call_target="tpu_custom_call" | custom-call | flops 80000000000 | bytes 10000000 | tf_op jit(solution)/shard_map/exchange/pallas_call | solution.py:774
  497.4 6.2 fusion.57
  505.6 1.4 add_convert_fusion.8
  509.2 15.2 %fusion.58 = f32[1024,2048]{1,0:T(8,128)} fusion(bf16[2048,1024]{1,0:T(8,128)(2,1)} %get-tuple-element.91, bf16[2048,2048]{1,0:T(8,128)(2,1)} %get-tuple-element.74.dy_ref), kind=kOutput, calls=%fused_computation.170 | convolution fusion | flops 8589934592 | bytes 20971520 | tf_op jit(solution)/shard_map/dot_general | solution.py:32
  524.4 34.2 %attend_back.2 = bf16[1024,1536]{1,0:T(8,128)(2,1)S(1)} custom-call(s32[4]{0:T(128)S(1)} %copy-done.5, bf16[1024,1536]{1,0:T(8,128)(2,1)} %copy-done.7, bf16[1024,1536]{1,0:T(8,128)(2,1)} %copy-done.7, bf16[1024,1536]{1,0:T(8,128)(2,1)} %copy-done.7, bf16[1024,512]{1,0:T(8,128)(2,1)S(1)} %copy-done.11), custom_call_target="tpu_custom_call" | custom-call | flops 40265318400 | bytes 7340032 | tf_op jit(solution)/shard_map/attend_back/pallas_call | solution.py:931
  558.6 1.8 copy-done
  560.4 9.2 convert_reduce_fusion.1
  569.7 64.6 %ffn_plane.3 = (f32[256,2048]{1,0:T(8,128)}, bf16[2048,1024]{1,0:T(8,128)(2,1)}, bf16[2048,1024]{1,0:T(8,128)(2,1)}, bf16[2048,2048]{1,0:T(8,128)(2,1)}) custom-call(bf16[2048,2048]{1,0:T(8,128)(2,1)} %all-gather.14.cloned.1.call-done.n2_ref, bf16[2048,2048]{1,0:T(8,128)(2,1)} %all-gather.12.cloned.1.call-done.dy_ref, ...), custom_call_target="tpu_custom_call" | custom-call | flops 128849018880 | bytes 50331648 | tf_op jit(solution)/shard_map/ffn_plane/pallas_call | solution.py:1111
  634.3 5.1 convert_reduce_fusion.4
  640.2 15.6 %add_convert_fusion.2 = bf16[1024,2048]{1,0:T(8,128)(2,1)} fusion(f32[1024,2048]{1,0:T(8,128)} %fusion.58, bf16[2048,1024]{1,0:T(8,128)(2,1)} %get-tuple-element.92, bf16[2048,2048]{1,0:T(8,128)(2,1)} %all-gather.12.cloned.1.call-done.dy_ref), kind=kOutput, calls=%fused_computation.26 | convolution fusion | flops 8594128896 | bytes 25165824 | tf_op jit(solution)/shard_map/dot_general | solution.py:32
  655.9 1.5 copy-done.19
  657.4 2.4 multiply_reduce_fusion
  659.8 2.4 fusion.52
  663.6 7.6 convolution_convert_fusion.3.refs_1_
  671.2 7.3 convolution_convert_fusion.refs_0_
  678.5 49.2 %exchange.8 = (f32[256,2048]{1,0:T(8,128)}, bf16[1024,512]{1,0:T(8,128)(2,1)}) custom-call(bf16[2048,2048]{1,0:T(8,128)(2,1)} %convolution_convert_fusion.refs_0_, bf16[256,2048]{1,0:T(8,128)(2,1)} %convolution_convert_fusion.3.refs_1_), custom_call_target="tpu_custom_call" | custom-call | flops 15000000512 | bytes 10000000 | tf_op jit(solution)/shard_map/exchange/pallas_call | solution.py:774
  727.7 1.9 convert_element_type.277
  729.7 1.1 copy.79
  730.7 12.4 %fusion.59 = f32[1024,2048]{1,0:T(8,128)S(1)} fusion(bf16[2048,1024]{1,0:T(8,128)(2,1)S(1)} %copy-done.37, bf16[2048,2048]{1,0:T(8,128)(2,1)} %exchange.6.n2_ref), kind=kOutput, calls=%fused_computation.171 | convolution fusion | flops 8589934592 | bytes 20971520 | tf_op jit(solution)/shard_map/dot_general | solution.py:32
  743.2 11.2 %add_convert_fusion.1 = bf16[1024,2048]{1,0:T(8,128)(2,1)} fusion(f32[1024,2048]{1,0:T(8,128)S(1)} %fusion.59, bf16[2048,1024]{1,0:T(8,128)(2,1)S(1)} %copy-done.38, bf16[2048,2048]{1,0:T(8,128)(2,1)S(1)} %bitcast.206), kind=kOutput, calls=%fused_computation.25 | convolution fusion | flops 8594128896 | bytes 25165824 | tf_op jit(solution)/shard_map/dot_general | solution.py:32
  754.5 1.1 copy-done.8
  755.6 34.5 %attend_back.3 = bf16[1024,1536]{1,0:T(8,128)(2,1)S(1)} custom-call(s32[4]{0:T(128)S(1)} %get-tuple-element.232.parents_ref, bf16[1024,1536]{1,0:T(8,128)(2,1)} %copy-done.6, bf16[1024,1536]{1,0:T(8,128)(2,1)} %copy-done.6, bf16[1024,1536]{1,0:T(8,128)(2,1)} %copy-done.6, bf16[1024,512]{1,0:T(8,128)(2,1)S(1)} %copy-done.8), custom_call_target="tpu_custom_call" | custom-call | flops 40265318400 | bytes 7340032 | tf_op jit(solution)/shard_map/attend_back/pallas_call | solution.py:931
  790.2 12.6 %convert_reduce_fusion = (f32[2048]{0:T(1024)S(1)}, f32[2048]{0:T(1024)S(1)}, bf16[1024,2048]{1,0:T(8,128)(2,1)}) fusion(f32[1024]{0:T(1024)S(1)} %copy-done.97, f32[1024]{0:T(1024)S(1)} %copy-done.69, bf16[1024,2048]{1,0:T(8,128)(2,1)S(1)} %copy-done.33, bf16[1024,1536]{1,0:T(8,128)(2,1)S(1)} %attend_back.3, bf16[2048,1536]{1,0:T(8,128)(2,1)} %get-tuple-element.69), kind=kOutput, calls=%fused_computation.1 | convolution fusion | flops 6459224064 | bytes 17850368 | tf_op jit(solution)/shard_map/dot_general | solution.py:32
  802.9 3.0 convert_reduce_fusion.6
  807.1 13.4 %fusion.47 = f32[2048,1536]{1,0:T(8,128)} fusion(bf16[1024,1536]{1,0:T(8,128)(2,1)S(1)} %copy-done.1, bf16[1024,2048]{1,0:T(8,128)(2,1)} %get-tuple-element.68, f32[2048]{0:T(1024)S(1)} %bitcast.198, f32[2048]{0:T(1024)S(1)} %bitcast.185, f32[1024]{0:T(1024)S(1)} %copy-done.95, f32[1024]{0:T(1024)S(1)} %copy-done.67), kind=kOutput, calls=%fused_computation.163 | convolution fusion | flops 6455033856 | bytes 19947520 | tf_op jit(solution)/shard_map/dot_general | solution.py:32
  820.5 12.4 %add_convert_fusion.refs_2_ = bf16[2048,1536]{1,0:T(8,128)(2,1)} fusion(f32[2048,1536]{1,0:T(8,128)} %fusion.47, bf16[1024,1536]{1,0:T(8,128)(2,1)S(1)} %copy-done.3, bf16[1024,2048]{1,0:T(8,128)(2,1)S(1)} %copy-done.34, f32[1024]{0:T(1024)S(1)} %copy-done.97, f32[1024]{0:T(1024)S(1)} %copy-done.69, f32[2048]{0:T(1024)S(1)} %bitcast.199, f32[2048]{0:T(1024)S(1)} %bitcast.186), kind=kOutput, calls=%fused_computation | convolution fusion | flops 6461325312 | bytes 26238976 | tf_op jit(solution)/shard_map/dot_general | solution.py:32
  832.9 10.0 %reduce-scatter.8.cloned.1.call-done.refs_4_ = bf16[256,2048]{1,0:T(8,128)(2,1)} async-done(((bf16[1024,2048]{1,0:T(8,128)(2,1)}), bf16[256,2048]{1,0:T(8,128)(2,1)}) %reduce-scatter.8.cloned.1.call-update) | async-done | bytes 1048592 | tf_op jit(solution)/shard_map/reduce_scatter | solution.py:1308
  842.9 100.3 %exchange.9 = (f32[256,2048]{1,0:T(8,128)}, f32[256,512]{1,0:T(8,128)}, f32[256,1536]{1,0:T(8,128)}, f32[256,2048]{1,0:T(8,128)}, bf16[2048,256]{1,0:T(8,128)(2,...) custom-call(bf16[1024,2048]{1,0:T(8,128)(2,1)} %get-tuple-element.101.refs_0_, bf16[1024,512]{1,0:T(8,128)(2,1)} %bitcast.171, ...), custom_call_target="tpu_custom_call" | custom-call | flops 80000000000 | bytes 10000000 | tf_op jit(solution)/shard_map/exchange/pallas_call | solution.py:774
  944.5 1.4 slice_bitcast_fusion.4
  946.0 3.0 fusion.23
  949.0 1.8 fusion.30
  951.7 2.0 copy.63
  953.8 2.6 fusion.54
  956.4 1.5 convert_bitcast_fusion
  957.9 2.9 copy.64
  960.7 2.9 convert_element_type.294
  963.6 3.8 fusion.33
  967.4 1.5 maximum_bitcast_fusion
  970.5 2.2 fusion.36
  972.6 1.5 maximum_bitcast_fusion.1
  (329 shorter events, 23.7 us)
Async XLA Ops:
  7.2 317.0 %all-gather.6.cloned.1.call-start = ((), (), s32[]{:S(2)}) async-start(), calls=%async_computation.3 | async-start | bytes 5242880 | tf_op jit(solution)/shard_map/all_gather | solution.py:1210
  18.5 81.5 %copy-start.45 = (bf16[512,256]{1,0:T(8,128)(2,1)S(1)}, bf16[512,256]{1,0:T(8,128)(2,1)}, u32[]{:S(2)}) copy-start(bf16[512,256]{1,0:T(8,128)(2,1)} %param.28) | copy-start | bytes 786436
  97.7 226.6 %all-gather.8.cloned.1.call-start = ((), (), s32[]{:S(2)}) async-start(), calls=%async_computation.4 | async-start | bytes 5242880 | tf_op jit(solution)/shard_map/all_gather | solution.py:1209
  98.4 319.5 %all-gather.10.cloned.1.call-start = ((), (), s32[]{:S(2)}) async-start(), calls=%async_computation.5 | async-start | bytes 5242880 | tf_op jit(solution)/shard_map/all_gather | solution.py:1245
  100.0 18.1 %copy-start.4 = (s32[4]{0:T(128)}, s32[4]{0:T(128)S(1)}, u32[]{:S(2)}) copy-start(s32[4]{0:T(128)S(1)} %get-tuple-element.233.parents_ref) | copy-start | bytes 52
  106.0 12.0 %copy-start.93 = (f32[1024]{0:T(1024)}, f32[1024]{0:T(1024)S(1)}, u32[]{:S(2)}) copy-start(f32[1024]{0:T(1024)S(1)} %add_rsqrt_fusion.1) | copy-start | bytes 12292
  106.0 12.0 %copy-start.86 = (f32[1,2,8,128]{3,1,2,0:T(2,128)}, f32[1,2,8,128]{3,1,2,0:T(2,128)S(1)}, u32[]{:S(2)}) copy-start(f32[1,2,8,128]{3,1,2,0:T(2,128)S(1)} %copy.67) | copy-start | bytes 24580
  106.1 12.0 %copy-start.49 = (f32[1,2,8,128]{3,1,2,0:T(2,128)}, f32[1,2,8,128]{3,1,2,0:T(2,128)S(1)}, u32[]{:S(2)}) copy-start(f32[1,2,8,128]{3,1,2,0:T(2,128)S(1)} %copy.66) | copy-start | bytes 24580
  107.3 10.7 %copy-start.89 = (f32[1536]{0:T(1024)}, f32[1536]{0:T(1024)S(1)}, u32[]{:S(2)}) copy-start(f32[1536]{0:T(1024)S(1)} %fusion.38) | copy-start | bytes 18436
  118.0 14.2 %copy-start.7 = (bf16[1024,1536]{1,0:T(8,128)(2,1)}, bf16[1024,1536]{1,0:T(8,128)(2,1)S(1)}, u32[]{:S(2)}) copy-start(bf16[1024,1536]{1,0:T(8,128)(2,1)S(1)} %add_convert_fusion.4.q_ref.k_ref.v_ref) | copy-start | bytes 9437188
  133.2 138.7 %copy-start.12 = (bf16[2,1,256,2048]{3,2,1,0:T(8,128)(2,1)S(1)}, bf16[2,1,256,2048]{3,2,1,0:T(8,128)(2,1)}, u32[]{:S(2)}) copy-start(bf16[2,1,256,2048]{3,2,1,0:T(8,128)(2,1)} %param.18) | copy-start | bytes 6291460
  271.5 235.4 %all-gather.12.cloned.1.call-start = ((), (), s32[]{:S(2)}) async-start(), calls=%async_computation.6 | async-start | bytes 9437184 | tf_op jit(solution)/shard_map/all_gather | solution.py:1252
  271.9 7.6 copy-start.52
  271.9 7.5 copy-start.42
  271.9 6.3 copy-start.91
  280.9 288.8 %all-gather.14.cloned.1.call-start = ((), (), s32[]{:S(2)}) async-start(), calls=%async_computation.7 | async-start | bytes 9437184 | tf_op jit(solution)/shard_map/all_gather | solution.py:1266
  324.3 86.6 %copy-start.43 = (f32[1,2,8,128]{3,1,2,0:T(2,128)S(1)}, f32[1,2,8,128]{3,1,2,0:T(2,128)}, u32[]{:S(2)}) copy-start(f32[1,2,8,128]{3,1,2,0:T(2,128)} %copy-done.42) | copy-start | bytes 24580
  324.3 86.6 %copy-start.63 = (f32[256]{0:T(256)S(1)}, f32[256]{0:T(256)}, u32[]{:S(2)}) copy-start(f32[256]{0:T(256)} %copy-done.62) | copy-start | bytes 3076
  324.3 86.6 %copy-start.73 = (f32[256]{0:T(256)S(1)}, f32[256]{0:T(256)}, u32[]{:S(2)}) copy-start(f32[256]{0:T(256)} %copy-done.72) | copy-start | bytes 3076
  418.0 5.2 copy-start.40
  418.0 12.3 %slice-start.2 = ((s8[6291456]{0:T(1024)(128)(4,1)}), s8[4194304]{0:T(1024)(128)(4,1)S(1)}, s32[]{:S(2)}) async-start(s8[6291456]{0:T(1024)(128)(4,1)} %bitcast.207), calls=%async_computation.13 | async-start | bytes 8388608
  421.9 8.3 copy-start.68
  423.2 7.1 copy-start.96
  423.2 7.1 copy-start.50
  423.2 7.1 copy-start.87
  423.2 7.1 copy-start.90
  423.2 7.1 slice-start.3
  437.7 14.2 %copy-start.6 = (bf16[1024,1536]{1,0:T(8,128)(2,1)}, bf16[1024,1536]{1,0:T(8,128)(2,1)S(1)}, u32[]{:S(2)}) copy-start(bf16[1024,1536]{1,0:T(8,128)(2,1)S(1)} %add_convert_fusion.3.q_ref.k_ref.v_ref) | copy-start | bytes 9437188
  452.9 44.5 %copy-start.13 = (bf16[2,1,256,2048]{3,2,1,0:T(8,128)(2,1)S(1)}, bf16[2,1,256,2048]{3,2,1,0:T(8,128)(2,1)}, u32[]{:S(2)}) copy-start(bf16[2,1,256,2048]{3,2,1,0:T(8,128)(2,1)} %param.18) | copy-start | bytes 6291460
  452.9 44.5 %copy-start.92 = (f32[1,2,8,128]{3,1,2,0:T(2,128)S(1)}, f32[1,2,8,128]{3,1,2,0:T(2,128)}, u32[]{:S(2)}) copy-start(f32[1,2,8,128]{3,1,2,0:T(2,128)} %copy-done.91) | copy-start | bytes 24580
  507.0 148.8 %reduce-scatter.4.cloned.1.call-start = ((), (), s32[]{:S(2)}) async-start(), calls=%async_computation.8 | async-start | bytes 5242880 | tf_op jit(solution)/shard_map/reduce_scatter | solution.py:1271
  509.2 15.2 %copy-start.5 = (s32[4]{0:T(128)S(1)}, s32[4]{0:T(128)}, u32[]{:S(2)}) copy-start(s32[4]{0:T(128)} %copy-done.4) | copy-start | bytes 52
  509.2 15.2 %copy-start.11 = (bf16[1024,512]{1,0:T(8,128)(2,1)S(1)}, bf16[1024,512]{1,0:T(8,128)(2,1)}, u32[]{:S(2)}) copy-start(bf16[1024,512]{1,0:T(8,128)(2,1)} %get-tuple-element.87.g_ref) | copy-start | bytes 3145732
  509.2 51.2 %slice-start.4 = ((s8[6291456]{0:T(1024)(128)(4,1)}), s8[4194304]{0:T(1024)(128)(4,1)S(1)}, s32[]{:S(2)}) async-start(s8[6291456]{0:T(1024)(128)(4,1)} %bitcast.209), calls=%async_computation.15 | async-start | bytes 8388608
  524.4 36.0 %copy-start.31 = (bf16[1024,2048]{1,0:T(8,128)(2,1)S(1)}, bf16[1024,2048]{1,0:T(8,128)(2,1)}, u32[]{:S(2)}) copy-start(bf16[1024,2048]{1,0:T(8,128)(2,1)} %get-tuple-element.68) | copy-start | bytes 12582916
  524.4 36.0 %copy-start.66 = (f32[1024]{0:T(1024)S(1)}, f32[1024]{0:T(1024)}, u32[]{:S(2)}) copy-start(f32[1024]{0:T(1024)} %copy-done.65) | copy-start | bytes 12292
  524.4 36.0 %copy-start.94 = (f32[1024]{0:T(1024)S(1)}, f32[1024]{0:T(1024)}, u32[]{:S(2)}) copy-start(f32[1024]{0:T(1024)} %copy-done.93) | copy-start | bytes 12292
  524.4 36.0 %slice-start.5 = ((s8[6291456]{0:T(1024)(128)(4,1)}), s8[2097152]{0:T(1024)(128)(4,1)S(1)}, s32[]{:S(2)}) async-start(s8[6291456]{0:T(1024)(128)(4,1)} %bitcast.209), calls=%async_computation.16 | async-start | bytes 4194304
  569.7 184.8 %reduce-scatter.6.cloned.1.call-start = ((), (), s32[]{:S(2)}) async-start(), calls=%async_computation.9 | async-start | bytes 5242880 | tf_op jit(solution)/shard_map/reduce_scatter | solution.py:1287
  655.9 187.1 %reduce-scatter.8.cloned.1.call-start = ((), (), s32[]{:S(2)}) async-start(), calls=%async_computation.10 | async-start | bytes 5242880 | tf_op jit(solution)/shard_map/reduce_scatter | solution.py:1308
  663.6 7.6 copy-start.41
  663.6 7.6 copy-start.99
  663.6 7.6 copy-start.100
  729.7 13.5 %slice-start = ((s8[8388608]{0:T(1024)(128)(4,1)}), s8[4194304]{0:T(1024)(128)(4,1)S(1)}, s32[]{:S(2)}) async-start(s8[8388608]{0:T(1024)(128)(4,1)} %bitcast.205), calls=%async_computation.11 | async-start | bytes 8388608
  730.7 12.4 %copy-start.38 = (bf16[2048,1024]{1,0:T(8,128)(2,1)S(1)}, bf16[2048,1024]{1,0:T(8,128)(2,1)}, u32[]{:S(2)}) copy-start(bf16[2048,1024]{1,0:T(8,128)(2,1)} %get-tuple-element.107) | copy-start | bytes 12582916
  730.7 12.4 %slice-start.1 = ((s8[8388608]{0:T(1024)(128)(4,1)}), s8[4194304]{0:T(1024)(128)(4,1)S(1)}, s32[]{:S(2)}) async-start(s8[8388608]{0:T(1024)(128)(4,1)} %bitcast.205), calls=%async_computation.12 | async-start | bytes 8388608
  754.4 35.7 %copy-start.69 = (f32[1024]{0:T(1024)S(1)}, f32[1024]{0:T(1024)}, u32[]{:S(2)}) copy-start(f32[1024]{0:T(1024)} %copy-done.68) | copy-start | bytes 12292
  754.5 35.7 %copy-start.97 = (f32[1024]{0:T(1024)S(1)}, f32[1024]{0:T(1024)}, u32[]{:S(2)}) copy-start(f32[1024]{0:T(1024)} %copy-done.96) | copy-start | bytes 12292
  755.6 34.5 %copy-start.33 = (bf16[1024,2048]{1,0:T(8,128)(2,1)S(1)}, bf16[1024,2048]{1,0:T(8,128)(2,1)}, u32[]{:S(2)}) copy-start(bf16[1024,2048]{1,0:T(8,128)(2,1)} %all-gather.10.cloned.1.call-done) | copy-start | bytes 12582916
  790.2 12.6 %copy-start.2 = (bf16[1024,1536]{1,0:T(8,128)(2,1)}, bf16[1024,1536]{1,0:T(8,128)(2,1)S(1)}, u32[]{:S(2)}) copy-start(bf16[1024,1536]{1,0:T(8,128)(2,1)S(1)} %attend_back.3) | copy-start | bytes 9437188
  790.2 12.6 %copy-start.85 = (f32[2048]{0:T(1024)S(1)}, f32[2048]{0:T(1024)}, u32[]{:S(2)}) copy-start(f32[2048]{0:T(1024)} %get-tuple-element.174) | copy-start | bytes 24580
  790.2 12.6 %copy-start.84 = (f32[2048]{0:T(1024)S(1)}, f32[2048]{0:T(1024)}, u32[]{:S(2)}) copy-start(f32[2048]{0:T(1024)} %get-tuple-element.175) | copy-start | bytes 24580
  790.2 12.6 %copy-start.1 = (bf16[1024,1536]{1,0:T(8,128)(2,1)S(1)}, bf16[1024,1536]{1,0:T(8,128)(2,1)}, u32[]{:S(2)}) copy-start(bf16[1024,1536]{1,0:T(8,128)(2,1)} %copy-done) | copy-start | bytes 9437188
  802.8 4.3 copy-start.51
  807.1 13.4 %copy-start.3 = (bf16[1024,1536]{1,0:T(8,128)(2,1)S(1)}, bf16[1024,1536]{1,0:T(8,128)(2,1)}, u32[]{:S(2)}) copy-start(bf16[1024,1536]{1,0:T(8,128)(2,1)} %copy-done.2) | copy-start | bytes 9437188
  807.1 13.4 %copy-start.34 = (bf16[1024,2048]{1,0:T(8,128)(2,1)S(1)}, bf16[1024,2048]{1,0:T(8,128)(2,1)}, u32[]{:S(2)}) copy-start(bf16[1024,2048]{1,0:T(8,128)(2,1)} %all-gather.10.cloned.1.call-done) | copy-start | bytes 12582916
  842.9 103.1 %copy-start.14 = (bf16[2,1,256,2048]{3,2,1,0:T(8,128)(2,1)S(1)}, bf16[2,1,256,2048]{3,2,1,0:T(8,128)(2,1)}, u32[]{:S(2)}) copy-start(bf16[2,1,256,2048]{3,2,1,0:T(8,128)(2,1)} %param.18) | copy-start | bytes 6291460
  842.9 103.1 %copy-start.35 = (bf16[256,2048]{1,0:T(8,128)(2,1)S(1)}, bf16[256,2048]{1,0:T(8,128)(2,1)}, u32[]{:S(2)}) copy-start(bf16[256,2048]{1,0:T(8,128)(2,1)} %reduce-scatter.4.cloned.1.call-done) | copy-start | bytes 3145732
  842.9 103.1 %copy-start.74 = (f32[256]{0:T(256)S(1)}, f32[256]{0:T(256)}, u32[]{:S(2)}) copy-start(f32[256]{0:T(256)} %get-tuple-element.244) | copy-start | bytes 3076
  842.9 103.1 %copy-start.75 = (f32[256]{0:T(256)S(1)}, f32[256]{0:T(256)}, u32[]{:S(2)}) copy-start(f32[256]{0:T(256)} %get-tuple-element.245) | copy-start | bytes 3076
  963.6 5.3 copy-start.27
  963.6 5.3 copy-start.29
  963.6 5.3 copy-start.81
  963.6 5.3 copy-start.83
  (51 other events, 125.1 us)
Sparse Core Ops, SparseCore 0:
  97.8 107.7 all-gather.5
  207.2 80.3 all-gather.7
  289.7 79.2 all-gather.9
  370.8 56.0 all-gather.11
  507.1 57.2 all-gather.13
  569.8 79.6 reduce-scatter.3
  655.9 98.0 reduce-scatter.5
  756.3 86.5 reduce-scatter.7

commit v10 on v8

--- a/solution.py
+++ b/solution.py
@@ -534,21 +534,21 @@
     cube.greet_all(barrier)
     pl.semaphore_wait(barrier, cube.dp - 1 + line.peers())
     gather.start()
+    wide.start()
     weights.start()
     gather.take(1)
+    wide.take(1)
     for piece in range(1, cube.count):
         if piece.bit_length() < cube.levels:
             weights.take(piece)
     swap.start()
     gather.take(2)
-    wide.start()
+    wide.take(2)
     for piece in range(1, cube.count):
         weights.take(piece)
-    wide.take(1)
     for step in range(3, line.n):
         gather.take(step)
-        wide.take(step - 1)
-    wide.take(line.n - 1)
+        wide.take(step)
     weights.finish()
     swap.finish()
     gather.finish()
@@ -943,13 +943,9 @@
     )(parents, qkv, qkv, qkv, grad)
 
 
-def ffn_kernel(host, n2_ref, dy_ref, we_ref, wr_ref, be_ref, *refs):
-    if host:
-        line_own, refs = refs[0], refs[1:]
+def ffn_kernel(n2_ref, dy_ref, we_ref, wr_ref, be_ref, *refs):
     sum_ref, act_ref, dpre_ref, part_ref = refs[:4]
     refs = refs[4:]
-    if host:
-        line_full, refs = refs[0], refs[1:]
     we, wr, seq_st, dy_st, act_st, dpre_st, part_st, keep, give, core_in, fold_in = refs[:11]
     w_sem, load_sem, st_sem, rsc_send, rsc_recv, fold_send, fold_recv = refs[11:18]
     cube = Cube()
@@ -958,11 +954,6 @@
     units = wr_ref.shape[0]
     barrier = pltpu.get_barrier_semaphore()
     cube.greet(barrier)
-    if host:
-        line = Line()
-        line.greet(barrier)
-        aside = LineScatter(line, line_own, line_full, refs[18:])
-        aside.prepare()
     parts = we_ref.shape[0] // model
     mine_units = we_ref.shape[1]
     loads_w = [pltpu.make_async_copy(wr_ref, wr, w_sem.at[parts])]
@@ -993,9 +984,7 @@
     loads = {order[0]: load(order[0], 0)}
     for c in loads[order[0]] + loads_w:
         c.start()
-    pl.semaphore_wait(barrier, cube.peers() + (line.peers() if host else 0))
-    if host:
-        aside.step(1)
+    pl.semaphore_wait(barrier, cube.peers())
     for c in loads_w:
         c.wait()
     stores, core_sends, folds = {}, {}, {}
@@ -1082,8 +1071,6 @@
                 )
         for c in stores[turn]:
             c.start()
-        if host and turn < line.n - 2:
-            aside.step(turn + 2)
     core_copy(0).wait_recv()
     for level in range(levels):
         fold_copy(1 << level).wait_recv()
@@ -1096,10 +1083,6 @@
             total = total + fold_in[(1 << level) - 1, part].astype(F32)
         sum_ref[part] = total
 
-    if host:
-        for step in range(count + 2, line.n):
-            aside.step(step)
-        aside.finish()
     for turn in range(max(0, count - 2), count):
         for c in stores[turn]:
             c.wait()
@@ -1108,24 +1091,21 @@
         s.wait_send()
 
 
-def ffn(n2, dy, we, wr, bias_e, own=None):
-    host = own is not None
+def ffn(n2, dy, we, wr, bias_e):
     n, dp = lax.axis_size("tensor"), lax.axis_size("dp")
     rows, model = n2.shape[0] // dp, n2.shape[1]
     units, count = wr.shape[0], dp // 2
-    operands = [n2, dy, we, wr, bias_e] + [own] * host
     flops = 30 * dp * rows * model * units
     return pl.pallas_call(
-        functools.partial(ffn_kernel, host),
+        ffn_kernel,
         out_shape=(
             jax.ShapeDtypeStruct((rows, model), F32),
             jax.ShapeDtypeStruct((dp * rows, units), BF16),
             jax.ShapeDtypeStruct((dp * rows, units), BF16),
             jax.ShapeDtypeStruct((dp * rows, model), BF16),
-            *[jax.ShapeDtypeStruct((rows, model), F32)] * host,
         ),
-        in_specs=[ANY] * 4 + [VMEM] + [ANY] * host,
-        out_specs=(VMEM, ANY, ANY, ANY) + (VMEM,) * host,
+        in_specs=[ANY] * 4 + [VMEM],
+        out_specs=(VMEM, ANY, ANY, ANY),
         scratch_shapes=[
             pltpu.VMEM((model, units), BF16),
             pltpu.VMEM((units, model), BF16),
@@ -1140,16 +1120,15 @@
             pltpu.VMEM((count - 1, rows, model), BF16),
             DMA((n + 1,)), DMA((2, 2, 2)), DMA((3, 2, 2)),
             DMA((count,)), DMA((count,)), DMA((count - 1,)), DMA((count - 1,)),
-        ]
-        + (LineScatter.scratch(n, rows, model) if host else []),
+        ],
         compiler_params=pltpu.CompilerParams(
-            collective_id=2 if host else 1, has_side_effects=True, vmem_limit_bytes=62 << 20
+            collective_id=1, has_side_effects=True, vmem_limit_bytes=62 << 20
         ),
         cost_estimate=pl.CostEstimate(
             flops=flops, bytes_accessed=8 * dp * rows * (model + units), transcendentals=dp * rows * units
         ),
         name="ffn_plane",
-    )(*operands)
+    )(n2, dy, we, wr, bias_e)
 
 
 def body(
@@ -1272,27 +1251,29 @@
                 jnp.sum(d_qkv[k].astype(F32), 0),
             )
 
-        own = None
         if m:
+            normed_two[m], seq_grad[m] = lax.optimization_barrier((normed_two[m], seq_grad[m]))
+            next_two = lax.all_gather(normed_two[m], "dp", axis=0, tiled=True)
             gain, shift, bias = attention_back(m - 1)
             g_gain_one, g_shift_one = g_gain_one + gain, g_shift_one + shift
             g_bias_qkv = g_bias_qkv + bias
-            own = d_one[m - 1]
+            next_two, d_one[m - 1] = lax.optimization_barrier((next_two, d_one[m - 1]))
+            d_one[m - 1] = lax.psum_scatter(
+                d_one[m - 1], "tensor", scatter_dimension=0, tiled=True
+            )
 
         if m == 0:
             (seq,) = exchange(7, cubes=[normed_two[m]])
         else:
-            seq = lax.all_gather(normed_two[m], "dp", axis=0, tiled=True)
-        d_two, act, dpre, part, *line = ffn(seq, seq_grad[m], w_e, w_r, bias_e, own)
-        if m:
-            d_one[m - 1] = line[0]
+            seq = next_two
+        d_two, act, dpre, part = ffn(seq, seq_grad[m], w_e, w_r, bias_e)
         seq_two.append(seq)
         activated.append(act)
         d_pre.append(dpre)
         out_part.append(part)
         if m == last:
             g_r = outer(activated, seq_grad)
-            d_two, g_r = lax.optimization_barrier((d_two, g_r))
+            d_two, g_r, *d_one = lax.optimization_barrier((d_two, g_r, *d_one))
             g_r = lax.psum_scatter(g_r, "tensor", scatter_dimension=0, tiled=True)
         grad32 = dy_low[m].astype(F32)
         norm_value, norm_pull = jax.vjp(layer_norm, hidden[m], gain_two, shift_two)
@@ -1335,7 +1316,21 @@
     little = jnp.concatenate([rows, row_qv, row_e], 1)
     little = jnp.pad(little, ((0, 0), (0, -little.shape[1] % 1024))).reshape(dp, -1, 128)
 
+    layer_out, input_grad = [], []
+
+    def done(m):
+        layer_out.append((hidden[m] + (out_sum[m] + bias_red)).astype(BF16))
+        first_value, first_pull = jax.vjp(
+            lambda rows: layer_norm(rows, gain_one, shift_one), x_low[m].astype(F32)
+        )
+        input_grad.append((d_hidden[m] + first_pull(d_one[m].astype(F32))[0]).astype(BF16))
+
+    d_one[last], *d_qkv = lax.optimization_barrier((d_one[last], *d_qkv))
     g_qkv = outer(seq_one, d_qkv)
+    for m in micros[:last]:
+        done(m)
+    d_one[last], *finished = lax.optimization_barrier((d_one[last], *layer_out, *input_grad))
+    layer_out, input_grad = finished[:last], finished[last:]
     g_ot = g_ot.astype(BF16).reshape(-1, tn, width).transpose(1, 0, 2).reshape(-1, width)
     d_one[last], g_ot, g_qkv, out_last, g_expand, g_reduce, little = exchange(
         5,
@@ -1349,7 +1344,6 @@
     g_out = g_ot.T
     g_expand = g_expand.T.astype(F32)
     g_reduce = g_reduce.astype(F32)
-    layer_out = [(hidden[m] + (out_sum[m] + bias_red)).astype(BF16) for m in micros]
     little = little.reshape(-1)
     six = little[: 6 * cut].reshape(6, cut)
     at = 6 * cut
@@ -1359,12 +1353,7 @@
     at += tn * 2 * bq_rows * bq_cols
     g_be = little[at : at + tn * be_rows * be_cols].reshape(tn, be_rows, be_cols)
     g_be = lax.dynamic_index_in_dim(g_be, tn_me, 0, keepdims=False)
-    input_grad = []
-    for m in micros:
-        first_value, first_pull = jax.vjp(
-            lambda rows: layer_norm(rows, gain_one, shift_one), x_low[m].astype(F32)
-        )
-        input_grad.append((d_hidden[m] + first_pull(d_one[m])[0]).astype(BF16))
+    done(last)
 
     return (
         jnp.stack(layer_out, 0)[:, None],

time: 988 us -> 956 us (0.968)
  Pallas kernels: 683 us -> 661 us
  waiting for transfers between devices: 37.5 us -> 18.2 us
    reduce_scatter x1, waiting for transfers between devices: 22.8 us -> 9.94 us  [body(): g_et = lax.psum_scatter(g_et, 'tensor', scatter_dimension=0, tiled=True)]
    pallas_call x2, Pallas kernels: 152 us -> 140 us  [ffn(): pl.pallas_call(ffn_kernel, out_shape=(jax.ShapeDtypeStruct((rows, model),...]
    unnamed x255 -> x249, local copies, waits for them, and re-layouts: 21.5 us -> 24.5 us
  transfers between devices with their start and end apart: 7 -> 8, of which waited for: 3 -> 2; matrix products, arithmetic and copies ran while one was open for 18% -> 21% of each run, Pallas kernels for 41% -> 50%
where the time goes in v10:
time: 956 us; the launch traced here: 947 us
  Pallas kernels  661 us (69%)
  matrix products  153 us (16%)
  other arithmetic  52.8 us (6%)
  local copies, waits for them, and re-layouts  45.6 us (5%)
  waiting for transfers between devices  18.2 us (2%)
  between operations  16.2 us (2%)
    pallas_call x5, Pallas kernels, exchange(): pl.pallas_call(functools.partial(exchange_kernel, counts), out_shape=tupl...  332 us
    pallas_call x2, Pallas kernels, ffn(): pl.pallas_call(ffn_kernel, out_shape=(jax.ShapeDtypeStruct((rows, model),...  140 us
    dot_general x11, matrix products, over(): lax.dot_general(left, right, (((on_left,), (on_right,)), ((), ())), prefe...  120 us
    pallas_call x1, Pallas kernels, front(): pl.pallas_call(front_kernel, out_shape=(jax.ShapeDtypeStruct((n * rows, m...  92 us
    pallas_call x2, Pallas kernels, attend_back(): pl.pallas_call(attend_back_kernel, out_shape=jax.ShapeDtypeStruct((rows,...  68.8 us
    pallas_call x2, Pallas kernels, attend(): pl.pallas_call(attend_kernel, out_shape=jax.ShapeDtypeStruct((rows, width...  28.4 us
    unnamed x249, local copies, waits for them, and re-layouts  24.5 us
  transfers between devices with their start and end apart: 8, of which 2 were waited for; matrix products, arithmetic and copies ran while one was open for 21% of the time, Pallas kernels for 50%

profile of v10, /device:TPU:0, one launch (start us, length us, event | category | flops | bytes accessed | tf_op | source)
XLA Modules:
  0.0 947.3 jit_solution(957877211532192957)
XLA Ops:
  9.6 4.1 concatenate.27
  14.3 1.8 copy.52
  16.1 3.2 slice_bitcast_fusion.2
  20.2 92.0 %front.1 = (bf16[1024,2048]{1,0:T(8,128)(2,1)}, bf16[2048,1536]{1,0:T(8,128)(2,1)}, bf16[256,2048]{1,0:T(8,128)(2,1)}, bf16[2048,256]{1,0:T(8,128)(2,1)}, bf16[2...) custom-call(bf16[256,2048]{1,0:T(8,128)(2,1)} %get-tuple-element.206.x_ref, bf16[256,1536]{1,0:T(8,128)(2,1)} %pad_maximum_fusion.w_ref, ...), custom_call_target="tpu_custom_call" | custom-call | flops 80000000000 | bytes 10000000 | tf_op jit(solution)/shard_map/front/pallas_call | solution.py:561
  114.6 1.5 slice_bitcast_fusion.1
  116.1 1.5 copy-done.29
  118.2 1.2 fusion.11
  120.8 10.7 %add_convert_fusion.4.q_ref.k_ref.v_ref = bf16[1024,1536]{1,0:T(8,128)(2,1)S(1)} fusion(bf16[2048,1536]{1,0:T(8,128)(2,1)} %get-tuple-element.74, f32[1536]{0:T(1024)S(1)} %fusion.36, bf16[1024,2048]{1,0:T(8,128)(2,1)} %get-tuple-element.73, f32[2048]{0:T(1024)S(1)} %bitcast.200, f32[2048]{0:T(1024)S(1)} %bitcast.179, f32[1024]{0:T(1024)S(1)} %add_rsqrt_fusion.1, ...), kind=kOutput, calls=%fused_computation.31 | convolution fusion | flops 6458179584 | bytes 13662208 | tf_op jit(solution)/shard_map/dot_general | solution.py:1218
  131.6 14.2 %attend.2.refs_3_ = bf16[1024,512]{1,0:T(8,128)(2,1)S(1)} custom-call(s32[4]{0:T(128)S(1)} %get-tuple-element.235.parents_ref, bf16[1024,1536]{1,0:T(8,128)(2,1)S(1)} %add_convert_fusion.4.q_ref.k_ref.v_ref, bf16[1024,1536]{1,0:T(8,128)(2,1)S(1)} %add_convert_fusion.4.q_ref.k_ref.v_ref, bf16[1024,1536]{1,0:T(8,128)(2,1)S(1)} %add_convert_fusion.4.q_ref.k_ref.v_ref), custom_call_target="tpu_custom_call" | custom-call | flops 16106127360 | bytes 4194304 | tf_op jit(solution)/shard_map/attend/pallas_call | solution.py:843
  146.8 88.3 %exchange.5 = (bf16[64,128]{1,0:T(8,128)(2,1)}, bf16[2048,2048]{1,0:T(8,128)(2,1)}, bf16[2048,2048]{1,0:T(8,128)(2,1)}, bf16[256,2048]{1,0:T(8,128)(2,1)}) custom-call(bf16[16,128]{1,0:T(8,128)(2,1)} %pad_bitcast_fusion.refs_0_, bf16[256,2048]{1,0:T(8,128)(2,1)} %get-tuple-element.72.refs_1_, bf16[256,2048]{1,0:T(8,128)(2,1)} %get-tuple-element.204.refs_2_, ...), custom_call_target="tpu_custom_call" | custom-call | flops 80000000000 | bytes 10000000 | tf_op jit(solution)/shard_map/exchange/pallas_call | solution.py:762
  235.5 6.3 fusion.54
  243.0 1.4 add_convert_fusion.10.refs_0_
  245.2 42.3 %exchange.6.n2_ref = bf16[2048,2048]{1,0:T(8,128)(2,1)} custom-call(bf16[256,2048]{1,0:T(8,128)(2,1)} %add_convert_fusion.10.refs_0_), custom_call_target="tpu_custom_call" | custom-call | flops 80000000000 | bytes 10000000 | tf_op jit(solution)/shard_map/exchange/pallas_call | solution.py:762
  287.6 7.4 all-gather.10.cloned.1.call-done.wr_ref
  295.0 76.3 %ffn_plane.2 = (f32[256,2048]{1,0:T(8,128)}, bf16[2048,1024]{1,0:T(8,128)(2,1)}, bf16[2048,1024]{1,0:T(8,128)(2,1)}, bf16[2048,2048]{1,0:T(8,128)(2,1)}) custom-call(bf16[2048,2048]{1,0:T(8,128)(2,1)} %exchange.6.n2_ref, bf16[2048,2048]{1,0:T(8,128)(2,1)} %get-tuple-element.80.dy_ref, bf16[8192,256]{1,0:T(8,128)(2,1)} %all-gather.8.cloned.1.call-done.we_ref, ...), custom_call_target="tpu_custom_call" | custom-call | flops 128849018880 | bytes 50331648 | tf_op jit(solution)/shard_map/ffn_plane/pallas_call | solution.py:1099
  371.3 3.7 multiply_reduce_fusion.1
  375.7 1.3 copy-done.26
  377.0 1.3 convert_reduce_fusion.10
  378.3 3.2 convert_reduce_fusion.2
  382.1 1.2 fusion.10
  383.4 7.7 convolution_convert_fusion.4.refs_2_
  391.2 7.4 add_convert_fusion.3.q_ref.k_ref.v_ref
  398.6 14.2 %attend.3.refs_1_ = bf16[1024,512]{1,0:T(8,128)(2,1)S(1)} custom-call(s32[4]{0:T(128)S(1)} %get-tuple-element.234.parents_ref, bf16[1024,1536]{1,0:T(8,128)(2,1)S(1)} %add_convert_fusion.3.q_ref.k_ref.v_ref, bf16[1024,1536]{1,0:T(8,128)(2,1)S(1)} %add_convert_fusion.3.q_ref.k_ref.v_ref, bf16[1024,1536]{1,0:T(8,128)(2,1)S(1)} %add_convert_fusion.3.q_ref.k_ref.v_ref), custom_call_target="tpu_custom_call" | custom-call | flops 16106127360 | bytes 4194304 | tf_op jit(solution)/shard_map/attend/pallas_call | solution.py:843
  413.8 55.3 %exchange.7 = (f32[256,2048]{1,0:T(8,128)}, bf16[256,2048]{1,0:T(8,128)(2,1)}, bf16[1024,512]{1,0:T(8,128)(2,1)}) custom-call(bf16[2048,2048]{1,0:T(8,128)(2,1)} %get-tuple-element.87.refs_0_, bf16[1024,512]{1,0:T(8,128)(2,1)} %copy-done.10, bf16[256,2048]{1,0:T(8,128)(2,1)} %convolution_convert_fusion.4.refs_2_), custom_call_target="tpu_custom_call" | custom-call | flops 80000000000 | bytes 10000000 | tf_op jit(solution)/shard_map/exchange/pallas_call | solution.py:762
  469.1 6.3 fusion.55
  477.2 1.4 add_convert_fusion.9
  480.2 34.6 %attend_back.2 = bf16[1024,1536]{1,0:T(8,128)(2,1)S(1)} custom-call(s32[4]{0:T(128)S(1)} %copy-done.5, bf16[1024,1536]{1,0:T(8,128)(2,1)} %copy-done.7, bf16[1024,1536]{1,0:T(8,128)(2,1)} %copy-done.7, bf16[1024,1536]{1,0:T(8,128)(2,1)} %copy-done.7, bf16[1024,512]{1,0:T(8,128)(2,1)S(1)} %copy-done.11), custom_call_target="tpu_custom_call" | custom-call | flops 40265318400 | bytes 7340032 | tf_op jit(solution)/shard_map/attend_back/pallas_call | solution.py:919
  514.8 1.1 convert_reduce_fusion.7
  515.9 1.6 copy-done.17
  517.5 1.3 add_convert_fusion.8
  518.9 1.2 copy-done.109
  520.1 13.8 %fusion.56 = f32[1024,2048]{1,0:T(8,128)} fusion(bf16[2048,1024]{1,0:T(8,128)(2,1)S(1)} %copy-done.109, bf16[2048,2048]{1,0:T(8,128)(2,1)} %get-tuple-element.80.dy_ref), kind=kOutput, calls=%fused_computation.168 | convolution fusion | flops 8589934592 | bytes 20971520 | tf_op jit(solution)/shard_map/dot_general | solution.py:32
  534.0 9.3 convert_reduce_fusion.1
  543.4 63.4 %ffn_plane.3 = (f32[256,2048]{1,0:T(8,128)}, bf16[2048,1024]{1,0:T(8,128)(2,1)}, bf16[2048,1024]{1,0:T(8,128)(2,1)}, bf16[2048,2048]{1,0:T(8,128)(2,1)}) custom-call(bf16[2048,2048]{1,0:T(8,128)(2,1)} %all-gather.14.cloned.1.call-done.n2_ref, bf16[2048,2048]{1,0:T(8,128)(2,1)} %all-gather.12.cloned.1.call-done.dy_ref, ...), custom_call_target="tpu_custom_call" | custom-call | flops 128849018880 | bytes 50331648 | tf_op jit(solution)/shard_map/ffn_plane/pallas_call | solution.py:1099
  606.8 5.2 convert_reduce_fusion.4
  612.7 15.7 %add_convert_fusion.2 = bf16[1024,2048]{1,0:T(8,128)(2,1)} fusion(f32[1024,2048]{1,0:T(8,128)} %fusion.56, bf16[2048,1024]{1,0:T(8,128)(2,1)} %get-tuple-element.96, bf16[2048,2048]{1,0:T(8,128)(2,1)} %all-gather.12.cloned.1.call-done.dy_ref), kind=kOutput, calls=%fused_computation.26 | convolution fusion | flops 8594128896 | bytes 25165824 | tf_op jit(solution)/shard_map/dot_general | solution.py:32
  628.6 1.4 copy-done.13
  630.4 3.6 fusion.22
  634.0 1.9 fusion.50
  636.8 1.0 copy-done.21
  637.8 4.4 convert_reduce_fusion.12
  642.3 7.2 convolution_convert_fusion.3.refs_1_
  649.5 6.9 convolution_convert_fusion.refs_0_
  656.4 47.4 %exchange.8 = (f32[256,2048]{1,0:T(8,128)}, bf16[1024,512]{1,0:T(8,128)(2,1)}) custom-call(bf16[2048,2048]{1,0:T(8,128)(2,1)} %convolution_convert_fusion.refs_0_, bf16[256,2048]{1,0:T(8,128)(2,1)} %convolution_convert_fusion.3.refs_1_), custom_call_target="tpu_custom_call" | custom-call | flops 15000000512 | bytes 10000000 | tf_op jit(solution)/shard_map/exchange/pallas_call | solution.py:762
  703.8 1.9 convert_element_type.279
  705.7 1.1 copy.79
  707.3 12.0 %fusion.57 = f32[1024,2048]{1,0:T(8,128)S(1)} fusion(bf16[2048,1024]{1,0:T(8,128)(2,1)S(1)} %copy-done.37, bf16[2048,2048]{1,0:T(8,128)(2,1)} %exchange.6.n2_ref), kind=kOutput, calls=%fused_computation.169 | convolution fusion | flops 8589934592 | bytes 20971520 | tf_op jit(solution)/shard_map/dot_general | solution.py:32
  719.4 11.4 %add_convert_fusion.1 = bf16[1024,2048]{1,0:T(8,128)(2,1)} fusion(f32[1024,2048]{1,0:T(8,128)S(1)} %fusion.57, bf16[2048,1024]{1,0:T(8,128)(2,1)S(1)} %copy-done.38, bf16[2048,2048]{1,0:T(8,128)(2,1)S(1)} %bitcast.210), kind=kOutput, calls=%fused_computation.25 | convolution fusion | flops 8594128896 | bytes 25165824 | tf_op jit(solution)/shard_map/dot_general | solution.py:32
  730.8 1.1 copy-done.8
  732.0 34.2 %attend_back.3 = bf16[1024,1536]{1,0:T(8,128)(2,1)S(1)} custom-call(s32[4]{0:T(128)S(1)} %get-tuple-element.234.parents_ref, bf16[1024,1536]{1,0:T(8,128)(2,1)} %copy-done.6, bf16[1024,1536]{1,0:T(8,128)(2,1)} %copy-done.6, bf16[1024,1536]{1,0:T(8,128)(2,1)} %copy-done.6, bf16[1024,512]{1,0:T(8,128)(2,1)S(1)} %copy-done.8), custom_call_target="tpu_custom_call" | custom-call | flops 40265318400 | bytes 7340032 | tf_op jit(solution)/shard_map/attend_back/pallas_call | solution.py:919
  766.3 12.4 %convert_reduce_fusion = (f32[2048]{0:T(1024)S(1)}, f32[2048]{0:T(1024)S(1)}, bf16[1024,2048]{1,0:T(8,128)(2,1)}) fusion(f32[1024]{0:T(1024)S(1)} %copy-done.105, f32[1024]{0:T(1024)S(1)} %copy-done.78, bf16[1024,2048]{1,0:T(8,128)(2,1)S(1)} %copy-done.32, bf16[1024,1536]{1,0:T(8,128)(2,1)S(1)} %attend_back.3, bf16[2048,1536]{1,0:T(8,128)(2,1)} %get-tuple-element.74), kind=kOutput, calls=%fused_computation.1 | convolution fusion | flops 6459224064 | bytes 17850368 | tf_op jit(solution)/shard_map/dot_general | solution.py:32
  778.8 2.5 convert_reduce_fusion.6
  782.6 13.2 %fusion.45 = f32[2048,1536]{1,0:T(8,128)} fusion(bf16[1024,1536]{1,0:T(8,128)(2,1)S(1)} %copy-done.1, bf16[1024,2048]{1,0:T(8,128)(2,1)} %get-tuple-element.73, f32[2048]{0:T(1024)S(1)} %bitcast.202, f32[2048]{0:T(1024)S(1)} %bitcast.184, f32[1024]{0:T(1024)S(1)} %copy-done.103, f32[1024]{0:T(1024)S(1)} %copy-done.76), kind=kOutput, calls=%fused_computation.161 | convolution fusion | flops 6455033856 | bytes 19947520 | tf_op jit(solution)/shard_map/dot_general | solution.py:32
  795.7 12.3 %add_convert_fusion.refs_2_ = bf16[2048,1536]{1,0:T(8,128)(2,1)} fusion(f32[2048,1536]{1,0:T(8,128)} %fusion.45, bf16[1024,1536]{1,0:T(8,128)(2,1)S(1)} %copy-done.3, bf16[1024,2048]{1,0:T(8,128)(2,1)S(1)} %copy-done.33, f32[1024]{0:T(1024)S(1)} %copy-done.105, f32[1024]{0:T(1024)S(1)} %copy-done.78, f32[2048]{0:T(1024)S(1)} %bitcast.203, f32[2048]{0:T(1024)S(1)} %bitcast.185), kind=kOutput, calls=%fused_computation | convolution fusion | flops 6461325312 | bytes 26238976 | tf_op jit(solution)/shard_map/dot_general | solution.py:32
  808.1 9.9 %reduce-scatter.8.cloned.1.call-done.refs_4_ = bf16[256,2048]{1,0:T(8,128)(2,1)} async-done(((bf16[1024,2048]{1,0:T(8,128)(2,1)}), bf16[256,2048]{1,0:T(8,128)(2,1)}) %reduce-scatter.8.cloned.1.call-update) | async-done | bytes 1048592 | tf_op jit(solution)/shard_map/reduce_scatter | solution.py:1298
  818.0 99.1 %exchange.9 = (f32[256,2048]{1,0:T(8,128)}, f32[256,512]{1,0:T(8,128)}, f32[256,1536]{1,0:T(8,128)}, f32[256,2048]{1,0:T(8,128)}, bf16[2048,256]{1,0:T(8,128)(2,...) custom-call(bf16[1024,2048]{1,0:T(8,128)(2,1)} %get-tuple-element.109.refs_0_, bf16[1024,512]{1,0:T(8,128)(2,1)} %bitcast.171, ...), custom_call_target="tpu_custom_call" | custom-call | flops 80000000000 | bytes 10000000 | tf_op jit(solution)/shard_map/exchange/pallas_call | solution.py:762
  918.5 1.4 slice_bitcast_fusion.4
  920.0 2.2 fusion.33
  925.3 1.9 fusion.34
  929.1 1.2 fusion.52
  931.0 1.8 copy.64
  932.9 2.8 convert_element_type.294
  935.7 1.5 maximum_bitcast_fusion
  938.0 1.5 maximum_bitcast_fusion.1
  (351 shorter events, 29.2 us)
Async XLA Ops:
  7.2 280.4 %all-gather.8.cloned.1.call-start = ((), (), s32[]{:S(2)}) async-start(), calls=%async_computation.4 | async-start | bytes 5242880 | tf_op jit(solution)/shard_map/all_gather | solution.py:1200
  112.3 182.6 %all-gather.10.cloned.1.call-start = ((), (), s32[]{:S(2)}) async-start(), calls=%async_computation.5 | async-start | bytes 5242880 | tf_op jit(solution)/shard_map/all_gather | solution.py:1199
  113.1 265.2 %all-gather.6.cloned.1.call-start = ((), (), s32[]{:S(2)}) async-start(), calls=%async_computation.3 | async-start | bytes 5242880 | tf_op jit(solution)/shard_map/all_gather | solution.py:1235
  114.6 17.0 %copy-start.4 = (s32[4]{0:T(128)}, s32[4]{0:T(128)S(1)}, u32[]{:S(2)}) copy-start(s32[4]{0:T(128)S(1)} %get-tuple-element.235.parents_ref) | copy-start | bytes 52
  119.5 12.1 %copy-start.101 = (f32[1024]{0:T(1024)}, f32[1024]{0:T(1024)S(1)}, u32[]{:S(2)}) copy-start(f32[1024]{0:T(1024)S(1)} %add_rsqrt_fusion.1) | copy-start | bytes 12292
  119.5 12.0 %copy-start.94 = (f32[1,2,8,128]{3,1,2,0:T(2,128)}, f32[1,2,8,128]{3,1,2,0:T(2,128)S(1)}, u32[]{:S(2)}) copy-start(f32[1,2,8,128]{3,1,2,0:T(2,128)S(1)} %copy.67) | copy-start | bytes 24580
  119.5 12.0 %copy-start.52 = (f32[1,2,8,128]{3,1,2,0:T(2,128)}, f32[1,2,8,128]{3,1,2,0:T(2,128)S(1)}, u32[]{:S(2)}) copy-start(f32[1,2,8,128]{3,1,2,0:T(2,128)S(1)} %copy.66) | copy-start | bytes 24580
  120.8 10.8 %copy-start.97 = (f32[1536]{0:T(1024)}, f32[1536]{0:T(1024)S(1)}, u32[]{:S(2)}) copy-start(f32[1536]{0:T(1024)S(1)} %fusion.36) | copy-start | bytes 18436
  131.6 14.2 %copy-start.7 = (bf16[1024,1536]{1,0:T(8,128)(2,1)}, bf16[1024,1536]{1,0:T(8,128)(2,1)S(1)}, u32[]{:S(2)}) copy-start(bf16[1024,1536]{1,0:T(8,128)(2,1)S(1)} %add_convert_fusion.4.q_ref.k_ref.v_ref) | copy-start | bytes 9437188
  146.8 88.8 %copy-start.18 = (bf16[2,1,256,2048]{3,2,1,0:T(8,128)(2,1)S(1)}, bf16[2,1,256,2048]{3,2,1,0:T(8,128)(2,1)}, u32[]{:S(2)}) copy-start(bf16[2,1,256,2048]{3,2,1,0:T(8,128)(2,1)} %param.18) | copy-start | bytes 6291460
  235.1 243.5 %all-gather.12.cloned.1.call-start = ((), (), s32[]{:S(2)}) async-start(), calls=%async_computation.6 | async-start | bytes 9437184 | tf_op jit(solution)/shard_map/all_gather | solution.py:1242
  235.5 7.6 copy-start.60
  235.5 7.5 copy-start.49
  235.5 6.3 copy-start.99
  244.5 298.8 %all-gather.14.cloned.1.call-start = ((), (), s32[]{:S(2)}) async-start(), calls=%async_computation.7 | async-start | bytes 9437184 | tf_op jit(solution)/shard_map/all_gather | solution.py:1256
  294.9 76.3 %copy-start.50 = (f32[1,2,8,128]{3,1,2,0:T(2,128)S(1)}, f32[1,2,8,128]{3,1,2,0:T(2,128)}, u32[]{:S(2)}) copy-start(f32[1,2,8,128]{3,1,2,0:T(2,128)} %copy-done.49) | copy-start | bytes 24580
  294.9 76.3 %copy-start.71 = (f32[256]{0:T(256)S(1)}, f32[256]{0:T(256)}, u32[]{:S(2)}) copy-start(f32[256]{0:T(256)} %copy-done.70) | copy-start | bytes 3076
  294.9 76.3 %copy-start.82 = (f32[256]{0:T(256)S(1)}, f32[256]{0:T(256)}, u32[]{:S(2)}) copy-start(f32[256]{0:T(256)} %copy-done.81) | copy-start | bytes 3076
  378.3 5.1 copy-start.45
  378.3 3.8 copy-start.31
  378.3 12.8 %slice-start.2 = ((s8[6291456]{0:T(1024)(128)(4,1)}), s8[4194304]{0:T(1024)(128)(4,1)S(1)}, s32[]{:S(2)}) async-start(s8[6291456]{0:T(1024)(128)(4,1)} %bitcast.211), calls=%async_computation.13 | async-start | bytes 8388608
  382.1 9.0 copy-start.77
  383.4 7.8 copy-start.104
  383.4 7.8 copy-start.53
  383.4 7.8 copy-start.95
  383.4 7.8 copy-start.98
  383.4 7.8 slice-start.3
  398.6 14.2 %copy-start.6 = (bf16[1024,1536]{1,0:T(8,128)(2,1)}, bf16[1024,1536]{1,0:T(8,128)(2,1)S(1)}, u32[]{:S(2)}) copy-start(bf16[1024,1536]{1,0:T(8,128)(2,1)S(1)} %add_convert_fusion.3.q_ref.k_ref.v_ref) | copy-start | bytes 9437188
  413.8 55.3 %copy-start.19 = (bf16[2,1,256,2048]{3,2,1,0:T(8,128)(2,1)S(1)}, bf16[2,1,256,2048]{3,2,1,0:T(8,128)(2,1)}, u32[]{:S(2)}) copy-start(bf16[2,1,256,2048]{3,2,1,0:T(8,128)(2,1)} %param.18) | copy-start | bytes 6291460
  413.8 55.3 %copy-start.100 = (f32[1,2,8,128]{3,1,2,0:T(2,128)S(1)}, f32[1,2,8,128]{3,1,2,0:T(2,128)}, u32[]{:S(2)}) copy-start(f32[1,2,8,128]{3,1,2,0:T(2,128)} %copy-done.99) | copy-start | bytes 24580
  478.7 149.8 %reduce-scatter.4.cloned.1.call-start = ((), (), s32[]{:S(2)}) async-start(), calls=%async_computation.8 | async-start | bytes 5242880 | tf_op jit(solution)/shard_map/reduce_scatter | solution.py:1261
  478.8 37.2 %copy-start.58 = (f32[1,2,8,128]{3,1,2,0:T(2,128)}, f32[1,2,8,128]{3,1,2,0:T(2,128)S(1)}, u32[]{:S(2)}) copy-start(f32[1,2,8,128]{3,1,2,0:T(2,128)S(1)} %copy.72) | copy-start | bytes 24580
  480.2 35.7 %copy-start.42 = (f32[256,2048]{1,0:T(8,128)S(1)}, f32[256,2048]{1,0:T(8,128)}, u32[]{:S(2)}) copy-start(f32[256,2048]{1,0:T(8,128)} %get-tuple-element.106) | copy-start | bytes 6291460
  514.8 19.2 %copy-start = (bf16[1024,1536]{1,0:T(8,128)(2,1)}, bf16[1024,1536]{1,0:T(8,128)(2,1)S(1)}, u32[]{:S(2)}) copy-start(bf16[1024,1536]{1,0:T(8,128)(2,1)S(1)} %attend_back.2) | copy-start | bytes 9437188
  517.5 16.4 %slice-start.4 = ((s8[6291456]{0:T(1024)(128)(4,1)}), s8[2097152]{0:T(1024)(128)(4,1)S(1)}, s32[]{:S(2)}) async-start(s8[6291456]{0:T(1024)(128)(4,1)} %bitcast.213), calls=%async_computation.15 | async-start | bytes 4194304
  520.1 13.9 %copy-start.30 = (bf16[1024,2048]{1,0:T(8,128)(2,1)S(1)}, bf16[1024,2048]{1,0:T(8,128)(2,1)}, u32[]{:S(2)}) copy-start(bf16[1024,2048]{1,0:T(8,128)(2,1)} %get-tuple-element.73) | copy-start | bytes 12582916
  520.1 13.9 %copy-start.75 = (f32[1024]{0:T(1024)S(1)}, f32[1024]{0:T(1024)}, u32[]{:S(2)}) copy-start(f32[1024]{0:T(1024)} %copy-done.74) | copy-start | bytes 12292
  520.1 13.9 %copy-start.102 = (f32[1024]{0:T(1024)S(1)}, f32[1024]{0:T(1024)}, u32[]{:S(2)}) copy-start(f32[1024]{0:T(1024)} %copy-done.101) | copy-start | bytes 12292
  520.1 13.9 %slice-start.5 = ((s8[6291456]{0:T(1024)(128)(4,1)}), s8[4194304]{0:T(1024)(128)(4,1)S(1)}, s32[]{:S(2)}) async-start(s8[6291456]{0:T(1024)(128)(4,1)} %bitcast.213), calls=%async_computation.16 | async-start | bytes 8388608
  543.4 187.5 %reduce-scatter.6.cloned.1.call-start = ((), (), s32[]{:S(2)}) async-start(), calls=%async_computation.9 | async-start | bytes 5242880 | tf_op jit(solution)/shard_map/reduce_scatter | solution.py:1277
  628.6 5.4 copy-start.85
  628.6 189.5 %reduce-scatter.8.cloned.1.call-start = ((), (), s32[]{:S(2)}) async-start(), calls=%async_computation.10 | async-start | bytes 5242880 | tf_op jit(solution)/shard_map/reduce_scatter | solution.py:1298
  635.9 6.3 copy-start.88
  637.8 4.4 copy-start.62
  642.2 7.3 copy-start.46
  642.2 7.3 copy-start.47
  642.3 7.3 copy-start.107
  642.3 7.3 copy-start.108
  703.8 15.5 %slice-start = ((s8[8388608]{0:T(1024)(128)(4,1)}), s8[4194304]{0:T(1024)(128)(4,1)S(1)}, s32[]{:S(2)}) async-start(s8[8388608]{0:T(1024)(128)(4,1)} %bitcast.209), calls=%async_computation.11 | async-start | bytes 8388608
  707.3 12.0 %copy-start.38 = (bf16[2048,1024]{1,0:T(8,128)(2,1)S(1)}, bf16[2048,1024]{1,0:T(8,128)(2,1)}, u32[]{:S(2)}) copy-start(bf16[2048,1024]{1,0:T(8,128)(2,1)} %get-tuple-element.115) | copy-start | bytes 12582916
  707.3 12.0 %slice-start.1 = ((s8[8388608]{0:T(1024)(128)(4,1)}), s8[4194304]{0:T(1024)(128)(4,1)S(1)}, s32[]{:S(2)}) async-start(s8[8388608]{0:T(1024)(128)(4,1)} %bitcast.209), calls=%async_computation.12 | async-start | bytes 8388608
  730.8 35.4 %copy-start.78 = (f32[1024]{0:T(1024)S(1)}, f32[1024]{0:T(1024)}, u32[]{:S(2)}) copy-start(f32[1024]{0:T(1024)} %copy-done.77) | copy-start | bytes 12292
  730.8 35.4 %copy-start.105 = (f32[1024]{0:T(1024)S(1)}, f32[1024]{0:T(1024)}, u32[]{:S(2)}) copy-start(f32[1024]{0:T(1024)} %copy-done.104) | copy-start | bytes 12292
  732.0 34.2 %copy-start.32 = (bf16[1024,2048]{1,0:T(8,128)(2,1)S(1)}, bf16[1024,2048]{1,0:T(8,128)(2,1)}, u32[]{:S(2)}) copy-start(bf16[1024,2048]{1,0:T(8,128)(2,1)} %all-gather.6.cloned.1.call-done) | copy-start | bytes 12582916
  766.2 12.5 %copy-start.2 = (bf16[1024,1536]{1,0:T(8,128)(2,1)}, bf16[1024,1536]{1,0:T(8,128)(2,1)S(1)}, u32[]{:S(2)}) copy-start(bf16[1024,1536]{1,0:T(8,128)(2,1)S(1)} %attend_back.3) | copy-start | bytes 9437188
  766.2 12.5 %copy-start.93 = (f32[2048]{0:T(1024)S(1)}, f32[2048]{0:T(1024)}, u32[]{:S(2)}) copy-start(f32[2048]{0:T(1024)} %get-tuple-element.182) | copy-start | bytes 24580
  766.2 12.5 %copy-start.92 = (f32[2048]{0:T(1024)S(1)}, f32[2048]{0:T(1024)}, u32[]{:S(2)}) copy-start(f32[2048]{0:T(1024)} %get-tuple-element.183) | copy-start | bytes 24580
  778.8 3.8 copy-start.1
  778.8 3.8 copy-start.76
  782.5 13.2 %copy-start.3 = (bf16[1024,1536]{1,0:T(8,128)(2,1)S(1)}, bf16[1024,1536]{1,0:T(8,128)(2,1)}, u32[]{:S(2)}) copy-start(bf16[1024,1536]{1,0:T(8,128)(2,1)} %copy-done.2) | copy-start | bytes 9437188
  782.6 13.2 %copy-start.33 = (bf16[1024,2048]{1,0:T(8,128)(2,1)S(1)}, bf16[1024,2048]{1,0:T(8,128)(2,1)}, u32[]{:S(2)}) copy-start(bf16[1024,2048]{1,0:T(8,128)(2,1)} %all-gather.6.cloned.1.call-done) | copy-start | bytes 12582916
  818.0 101.9 %copy-start.14 = (f32[256,2048]{1,0:T(8,128)S(1)}, f32[256,2048]{1,0:T(8,128)}, u32[]{:S(2)}) copy-start(f32[256,2048]{1,0:T(8,128)} %copy-done.12) | copy-start | bytes 6291460
  818.0 101.9 %copy-start.59 = (f32[1,2,8,128]{3,1,2,0:T(2,128)S(1)}, f32[1,2,8,128]{3,1,2,0:T(2,128)}, u32[]{:S(2)}) copy-start(f32[1,2,8,128]{3,1,2,0:T(2,128)} %copy-done.58) | copy-start | bytes 24580
  925.3 3.8 copy-start.43
  (60 other events, 131.9 us)
Sparse Core Ops, SparseCore 0:
  112.4 101.6 all-gather.7
  215.7 79.1 all-gather.9
  297.1 79.2 all-gather.5
  378.7 58.2 all-gather.11
  478.8 53.4 all-gather.13
  543.5 75.8 reduce-scatter.3
  628.7 94.7 reduce-scatter.5
  730.9 87.0 reduce-scatter.7

commit v11 on v10

--- a/solution.py
+++ b/solution.py
@@ -1019,7 +1019,7 @@
         folds[piece] = fold_copy(piece)
         folds[piece].start()
 
-    chunk = 256
+    chunk = 512
     wide = 512
     for turn, piece in enumerate(order):
         slot = turn % 2
@@ -1209,7 +1209,7 @@
     normal_one, seq_one, qkv, attended, hidden, normed_two = [], [], [], [], [], []
     out_part, seq_two, activated, d_pre, d_hidden, d_branch, out_sum = [], [], [], [], [], [], []
     d_qkv, d_one, d_att, row_attended = [], [], [], []
-    g_gain_two = g_shift_two = g_bias_red = g_bias_out = g_bias_e = 0.0
+    g_gain_two = g_shift_two = g_bias_red = g_bias_out = 0.0
     g_gain_one = g_shift_one = g_bias_qkv = 0.0
     for m in micros:
         normal_one.append(layer_norm(seq_x[m].astype(F32), 1.0, 0.0))
@@ -1285,7 +1285,6 @@
         g_shift_two = g_shift_two + g_shift
         g_bias_red = g_bias_red + jnp.sum(grad32, 0, keepdims=True)
         g_bias_out = g_bias_out + jnp.sum(d_branch[m].astype(F32), 0, keepdims=True)
-        g_bias_e = g_bias_e + jnp.sum(dpre.astype(F32), 0)
         if m < last:
             next_x, d_branch[m] = lax.optimization_barrier((next_x, d_branch[m]))
             seq_x.append(next_x)
@@ -1297,6 +1296,8 @@
     d_att[last], g_r = lax.optimization_barrier((d_att[last], g_r))
     g_et = lax.psum_scatter(g_et, "tensor", scatter_dimension=0, tiled=True)
     gain, shift, bias = attention_back(last)
+    d_one[last], *d_pre = lax.optimization_barrier((d_one[last], *d_pre))
+    g_bias_e = sum(jnp.sum(part.astype(F32), 0) for part in d_pre)
     g_gain_one, g_shift_one = g_gain_one + gain, g_shift_one + shift
     g_bias_qkv = g_bias_qkv + bias
 

time: 956 us -> 953 us (level)
    unnamed x249 -> x253, local copies, waits for them, and re-layouts: 24.5 us -> 23.6 us
  transfers between devices with their start and end apart: 8 -> 8, of which waited for: 2 -> 3; matrix products, arithmetic and copies ran while one was open for 21% -> 21% of each run, Pallas kernels for 50% -> 49%
where the time goes in v11:
time: 953 us; the launch traced here: 945 us
  Pallas kernels  664 us (70%)
  matrix products  152 us (16%)
  other arithmetic  48.7 us (5%)
  local copies, waits for them, and re-layouts  48.2 us (5%)
  between operations  16.2 us (2%)
  waiting for transfers between devices  15.4 us (2%)
    pallas_call x5, Pallas kernels, exchange(): pl.pallas_call(functools.partial(exchange_kernel, counts), out_shape=tupl...  342 us
    pallas_call x2, Pallas kernels, ffn(): pl.pallas_call(ffn_kernel, out_shape=(jax.ShapeDtypeStruct((rows, model),...  134 us
    dot_general x11, matrix products, over(): lax.dot_general(left, right, (((on_left,), (on_right,)), ((), ())), prefe...  119 us
    pallas_call x1, Pallas kernels, front(): pl.pallas_call(front_kernel, out_shape=(jax.ShapeDtypeStruct((n * rows, m...  92 us
    pallas_call x2, Pallas kernels, attend_back(): pl.pallas_call(attend_back_kernel, out_shape=jax.ShapeDtypeStruct((rows,...  68.5 us
    pallas_call x2, Pallas kernels, attend(): pl.pallas_call(attend_kernel, out_shape=jax.ShapeDtypeStruct((rows, width...  28.4 us
    unnamed x253, local copies, waits for them, and re-layouts  23.6 us
  transfers between devices with their start and end apart: 8, of which 3 were waited for; matrix products, arithmetic and copies ran while one was open for 21% of the time, Pallas kernels for 49%

profile of v11, /device:TPU:0, one launch (start us, length us, event | category | flops | bytes accessed | tf_op | source)
XLA Modules:
  0.0 944.8 jit_solution(3042866274934931103)
XLA Ops:
  9.6 4.1 concatenate.27
  14.3 1.8 copy.52
  16.1 3.2 slice_bitcast_fusion.2
  20.2 92.0 %front.1 = (bf16[1024,2048]{1,0:T(8,128)(2,1)}, bf16[2048,1536]{1,0:T(8,128)(2,1)}, bf16[256,2048]{1,0:T(8,128)(2,1)}, bf16[2048,256]{1,0:T(8,128)(2,1)}, bf16[2...) custom-call(bf16[256,2048]{1,0:T(8,128)(2,1)} %get-tuple-element.212.x_ref, bf16[256,1536]{1,0:T(8,128)(2,1)} %pad_maximum_fusion.w_ref, ...), custom_call_target="tpu_custom_call" | custom-call | flops 80000000000 | bytes 10000000 | tf_op jit(solution)/shard_map/front/pallas_call | solution.py:561
  113.9 3.3 slice_bitcast_fusion.1
  117.8 1.2 fusion.11
  120.3 10.8 %add_convert_fusion.4.q_ref.k_ref.v_ref = bf16[1024,1536]{1,0:T(8,128)(2,1)S(1)} fusion(bf16[2048,1536]{1,0:T(8,128)(2,1)} %get-tuple-element.77, f32[1536]{0:T(1024)S(1)} %fusion.36, bf16[1024,2048]{1,0:T(8,128)(2,1)} %get-tuple-element.76, f32[2048]{0:T(1024)S(1)} %bitcast.200, f32[2048]{0:T(1024)S(1)} %bitcast.179, f32[1024]{0:T(1024)S(1)} %add_rsqrt_fusion.1, ...), kind=kOutput, calls=%fused_computation.31 | convolution fusion | flops 6458179584 | bytes 13662208 | tf_op jit(solution)/shard_map/dot_general | solution.py:1218
  131.2 14.2 %attend.2.refs_3_ = bf16[1024,512]{1,0:T(8,128)(2,1)S(1)} custom-call(s32[4]{0:T(128)S(1)} %get-tuple-element.241.parents_ref, bf16[1024,1536]{1,0:T(8,128)(2,1)S(1)} %add_convert_fusion.4.q_ref.k_ref.v_ref, bf16[1024,1536]{1,0:T(8,128)(2,1)S(1)} %add_convert_fusion.4.q_ref.k_ref.v_ref, bf16[1024,1536]{1,0:T(8,128)(2,1)S(1)} %add_convert_fusion.4.q_ref.k_ref.v_ref), custom_call_target="tpu_custom_call" | custom-call | flops 16106127360 | bytes 4194304 | tf_op jit(solution)/shard_map/attend/pallas_call | solution.py:843
  146.4 88.4 %exchange.5 = (bf16[64,128]{1,0:T(8,128)(2,1)}, bf16[2048,2048]{1,0:T(8,128)(2,1)}, bf16[2048,2048]{1,0:T(8,128)(2,1)}, bf16[256,2048]{1,0:T(8,128)(2,1)}) custom-call(bf16[16,128]{1,0:T(8,128)(2,1)} %pad_bitcast_fusion.refs_0_, bf16[256,2048]{1,0:T(8,128)(2,1)} %get-tuple-element.75.refs_1_, bf16[256,2048]{1,0:T(8,128)(2,1)} %get-tuple-element.210.refs_2_, ...), custom_call_target="tpu_custom_call" | custom-call | flops 80000000000 | bytes 10000000 | tf_op jit(solution)/shard_map/exchange/pallas_call | solution.py:762
  235.2 6.4 fusion.54
  242.1 1.4 add_convert_fusion.10.refs_0_
  244.3 42.0 %exchange.6.n2_ref = bf16[2048,2048]{1,0:T(8,128)(2,1)} custom-call(bf16[256,2048]{1,0:T(8,128)(2,1)} %add_convert_fusion.10.refs_0_), custom_call_target="tpu_custom_call" | custom-call | flops 80000000000 | bytes 10000000 | tf_op jit(solution)/shard_map/exchange/pallas_call | solution.py:762
  286.4 8.6 all-gather.10.cloned.1.call-done.wr_ref
  295.0 72.2 %ffn_plane.2 = (f32[256,2048]{1,0:T(8,128)}, bf16[2048,1024]{1,0:T(8,128)(2,1)}, bf16[2048,1024]{1,0:T(8,128)(2,1)}, bf16[2048,2048]{1,0:T(8,128)(2,1)}) custom-call(bf16[2048,2048]{1,0:T(8,128)(2,1)} %exchange.6.n2_ref, bf16[2048,2048]{1,0:T(8,128)(2,1)} %get-tuple-element.83.dy_ref, bf16[8192,256]{1,0:T(8,128)(2,1)} %all-gather.8.cloned.1.call-done.we_ref, ...), custom_call_target="tpu_custom_call" | custom-call | flops 128849018880 | bytes 50331648 | tf_op jit(solution)/shard_map/ffn_plane/pallas_call | solution.py:1099
  367.2 3.7 multiply_reduce_fusion.1
  371.6 1.3 copy-done.26
  372.9 1.3 convert_reduce_fusion.10
  374.2 2.3 all-gather.6.cloned.1.call-done
  376.5 3.0 convert_reduce_fusion.2
  379.9 1.2 fusion.10
  381.2 7.2 convolution_convert_fusion.4.refs_2_
  388.5 7.2 add_convert_fusion.3.q_ref.k_ref.v_ref
  395.8 14.2 %attend.3.refs_1_ = bf16[1024,512]{1,0:T(8,128)(2,1)S(1)} custom-call(s32[4]{0:T(128)S(1)} %get-tuple-element.240.parents_ref, bf16[1024,1536]{1,0:T(8,128)(2,1)S(1)} %add_convert_fusion.3.q_ref.k_ref.v_ref, bf16[1024,1536]{1,0:T(8,128)(2,1)S(1)} %add_convert_fusion.3.q_ref.k_ref.v_ref, bf16[1024,1536]{1,0:T(8,128)(2,1)S(1)} %add_convert_fusion.3.q_ref.k_ref.v_ref), custom_call_target="tpu_custom_call" | custom-call | flops 16106127360 | bytes 4194304 | tf_op jit(solution)/shard_map/attend/pallas_call | solution.py:843
  410.9 58.6 %exchange.7 = (f32[256,2048]{1,0:T(8,128)}, bf16[256,2048]{1,0:T(8,128)(2,1)}, bf16[1024,512]{1,0:T(8,128)(2,1)}) custom-call(bf16[2048,2048]{1,0:T(8,128)(2,1)} %get-tuple-element.90.refs_0_, bf16[1024,512]{1,0:T(8,128)(2,1)} %copy-done.12, bf16[256,2048]{1,0:T(8,128)(2,1)} %convolution_convert_fusion.4.refs_2_), custom_call_target="tpu_custom_call" | custom-call | flops 80000000000 | bytes 10000000 | tf_op jit(solution)/shard_map/exchange/pallas_call | solution.py:762
  469.5 6.2 fusion.55
  477.7 1.4 add_convert_fusion.9
  480.6 34.3 %attend_back.2 = bf16[1024,1536]{1,0:T(8,128)(2,1)S(1)} custom-call(s32[4]{0:T(128)S(1)} %copy-done.7, bf16[1024,1536]{1,0:T(8,128)(2,1)} %copy-done.9, bf16[1024,1536]{1,0:T(8,128)(2,1)} %copy-done.9, bf16[1024,1536]{1,0:T(8,128)(2,1)} %copy-done.9, bf16[1024,512]{1,0:T(8,128)(2,1)S(1)} %copy-done.13), custom_call_target="tpu_custom_call" | custom-call | flops 40265318400 | bytes 7340032 | tf_op jit(solution)/shard_map/attend_back/pallas_call | solution.py:919
  514.9 1.1 convert_reduce_fusion.7
  516.0 1.6 copy-done.19
  517.6 1.3 add_convert_fusion.8
  518.9 1.2 copy-done.111
  520.2 13.7 %fusion.56 = f32[1024,2048]{1,0:T(8,128)} fusion(bf16[2048,1024]{1,0:T(8,128)(2,1)S(1)} %copy-done.111, bf16[2048,2048]{1,0:T(8,128)(2,1)} %get-tuple-element.83.dy_ref), kind=kOutput, calls=%fused_computation.168 | convolution fusion | flops 8589934592 | bytes 20971520 | tf_op jit(solution)/shard_map/dot_general | solution.py:32
  533.9 9.4 convert_reduce_fusion.1
  543.4 61.4 %ffn_plane.3 = (f32[256,2048]{1,0:T(8,128)}, bf16[2048,1024]{1,0:T(8,128)(2,1)}, bf16[2048,1024]{1,0:T(8,128)(2,1)}, bf16[2048,2048]{1,0:T(8,128)(2,1)}) custom-call(bf16[2048,2048]{1,0:T(8,128)(2,1)} %all-gather.14.cloned.1.call-done.n2_ref, bf16[2048,2048]{1,0:T(8,128)(2,1)} %all-gather.12.cloned.1.call-done.dy_ref, ...), custom_call_target="tpu_custom_call" | custom-call | flops 128849018880 | bytes 50331648 | tf_op jit(solution)/shard_map/ffn_plane/pallas_call | solution.py:1099
  604.8 15.8 %add_convert_fusion.2 = bf16[1024,2048]{1,0:T(8,128)(2,1)} fusion(f32[1024,2048]{1,0:T(8,128)} %fusion.56, bf16[2048,1024]{1,0:T(8,128)(2,1)} %get-tuple-element.99, bf16[2048,2048]{1,0:T(8,128)(2,1)} %all-gather.12.cloned.1.call-done.dy_ref), kind=kOutput, calls=%fused_computation.26 | convolution fusion | flops 8594128896 | bytes 25165824 | tf_op jit(solution)/shard_map/dot_general | solution.py:32
  620.7 1.4 copy-done.15
  622.4 3.5 fusion.22
  626.0 1.9 fusion.50
  628.8 1.2 copy-done.22
  629.9 4.4 convert_reduce_fusion.12
  634.4 7.2 convolution_convert_fusion.3.refs_1_
  641.6 6.9 convolution_convert_fusion.refs_0_
  648.5 47.4 %exchange.8 = (f32[256,2048]{1,0:T(8,128)}, bf16[1024,512]{1,0:T(8,128)(2,1)}) custom-call(bf16[2048,2048]{1,0:T(8,128)(2,1)} %convolution_convert_fusion.refs_0_, bf16[256,2048]{1,0:T(8,128)(2,1)} %convolution_convert_fusion.3.refs_1_), custom_call_target="tpu_custom_call" | custom-call | flops 15000000512 | bytes 10000000 | tf_op jit(solution)/shard_map/exchange/pallas_call | solution.py:762
  695.9 1.9 convert_element_type.279
  697.8 1.1 copy.79
  699.4 11.7 %fusion.57 = f32[1024,2048]{1,0:T(8,128)S(1)} fusion(bf16[2048,1024]{1,0:T(8,128)(2,1)S(1)} %copy-done.37, bf16[2048,2048]{1,0:T(8,128)(2,1)} %exchange.6.n2_ref), kind=kOutput, calls=%fused_computation.169 | convolution fusion | flops 8589934592 | bytes 20971520 | tf_op jit(solution)/shard_map/dot_general | solution.py:32
  711.2 10.8 %add_convert_fusion.1 = bf16[1024,2048]{1,0:T(8,128)(2,1)} fusion(f32[1024,2048]{1,0:T(8,128)S(1)} %fusion.57, bf16[2048,1024]{1,0:T(8,128)(2,1)S(1)} %copy-done.38, bf16[2048,2048]{1,0:T(8,128)(2,1)S(1)} %bitcast.210), kind=kOutput, calls=%fused_computation.25 | convolution fusion | flops 8594128896 | bytes 25165824 | tf_op jit(solution)/shard_map/dot_general | solution.py:32
  722.6 1.2 copy-done.10
  723.9 34.2 %attend_back.3 = bf16[1024,1536]{1,0:T(8,128)(2,1)S(1)} custom-call(s32[4]{0:T(128)S(1)} %copy-done.5, bf16[1024,1536]{1,0:T(8,128)(2,1)} %copy-done.8, bf16[1024,1536]{1,0:T(8,128)(2,1)} %copy-done.8, bf16[1024,1536]{1,0:T(8,128)(2,1)} %copy-done.8, bf16[1024,512]{1,0:T(8,128)(2,1)S(1)} %copy-done.10), custom_call_target="tpu_custom_call" | custom-call | flops 40265318400 | bytes 7340032 | tf_op jit(solution)/shard_map/attend_back/pallas_call | solution.py:919
  758.1 12.3 %convert_reduce_fusion = (f32[2048]{0:T(1024)S(1)}, f32[2048]{0:T(1024)S(1)}, bf16[1024,2048]{1,0:T(8,128)(2,1)}) fusion(f32[1024]{0:T(1024)S(1)} %copy-done.107, f32[1024]{0:T(1024)S(1)} %copy-done.80, bf16[1024,2048]{1,0:T(8,128)(2,1)S(1)} %copy-done.32, bf16[1024,1536]{1,0:T(8,128)(2,1)S(1)} %attend_back.3, bf16[2048,1536]{1,0:T(8,128)(2,1)} %get-tuple-element.77), kind=kOutput, calls=%fused_computation.1 | convolution fusion | flops 6459224064 | bytes 17850368 | tf_op jit(solution)/shard_map/dot_general | solution.py:32
  771.6 3.1 convert_reduce_fusion.5
  777.5 1.6 reshape.508
  779.8 13.1 %fusion.45 = f32[2048,1536]{1,0:T(8,128)} fusion(bf16[1024,1536]{1,0:T(8,128)(2,1)S(1)} %copy-done.1, bf16[1024,2048]{1,0:T(8,128)(2,1)} %get-tuple-element.76, f32[2048]{0:T(1024)S(1)} %bitcast.202, f32[2048]{0:T(1024)S(1)} %bitcast.184, f32[1024]{0:T(1024)S(1)} %copy-done.105, f32[1024]{0:T(1024)S(1)} %copy-done.78), kind=kOutput, calls=%fused_computation.161 | convolution fusion | flops 6455033856 | bytes 19947520 | tf_op jit(solution)/shard_map/dot_general | solution.py:32
  792.9 12.8 %add_convert_fusion.refs_2_ = bf16[2048,1536]{1,0:T(8,128)(2,1)} fusion(f32[2048,1536]{1,0:T(8,128)} %fusion.45, bf16[1024,1536]{1,0:T(8,128)(2,1)S(1)} %copy-done.3, bf16[1024,2048]{1,0:T(8,128)(2,1)S(1)} %copy-done.33, f32[1024]{0:T(1024)S(1)} %copy-done.107, f32[1024]{0:T(1024)S(1)} %copy-done.80, f32[2048]{0:T(1024)S(1)} %bitcast.203, f32[2048]{0:T(1024)S(1)} %bitcast.185), kind=kOutput, calls=%fused_computation | convolution fusion | flops 6461325312 | bytes 26238976 | tf_op jit(solution)/shard_map/dot_general | solution.py:32
  805.7 3.7 reduce-scatter.8.cloned.1.call-done.refs_4_
  809.4 105.3 %exchange.9 = (f32[256,2048]{1,0:T(8,128)}, f32[256,512]{1,0:T(8,128)}, f32[256,1536]{1,0:T(8,128)}, f32[256,2048]{1,0:T(8,128)}, bf16[2048,256]{1,0:T(8,128)(2,...) custom-call(bf16[1024,2048]{1,0:T(8,128)(2,1)} %get-tuple-element.115.refs_0_, bf16[1024,512]{1,0:T(8,128)(2,1)} %bitcast.171, ...), custom_call_target="tpu_custom_call" | custom-call | flops 80000000000 | bytes 10000000 | tf_op jit(solution)/shard_map/exchange/pallas_call | solution.py:762
  916.1 1.4 slice_bitcast_fusion.4
  917.5 2.1 fusion.33
  922.8 1.9 fusion.34
  926.5 1.2 fusion.52
  928.5 1.8 copy.64
  930.3 2.8 convert_element_type.294
  933.1 1.5 maximum_bitcast_fusion
  935.4 1.5 maximum_bitcast_fusion.1
  (356 shorter events, 30.8 us)
Async XLA Ops:
  7.2 279.2 %all-gather.8.cloned.1.call-start = ((), (), s32[]{:S(2)}) async-start(), calls=%async_computation.4 | async-start | bytes 5242880 | tf_op jit(solution)/shard_map/all_gather | solution.py:1200
  112.3 182.7 %all-gather.10.cloned.1.call-start = ((), (), s32[]{:S(2)}) async-start(), calls=%async_computation.5 | async-start | bytes 5242880 | tf_op jit(solution)/shard_map/all_gather | solution.py:1199
  113.1 263.4 %all-gather.6.cloned.1.call-start = ((), (), s32[]{:S(2)}) async-start(), calls=%async_computation.3 | async-start | bytes 5242880 | tf_op jit(solution)/shard_map/all_gather | solution.py:1235
  113.8 17.4 %copy-start.6 = (s32[4]{0:T(128)}, s32[4]{0:T(128)S(1)}, u32[]{:S(2)}) copy-start(s32[4]{0:T(128)S(1)} %get-tuple-element.241.parents_ref) | copy-start | bytes 52
  113.8 281.9 %copy-start.4 = (s32[4]{0:T(128)}, s32[4]{0:T(128)S(1)}, u32[]{:S(2)}) copy-start(s32[4]{0:T(128)S(1)} %get-tuple-element.240.parents_ref) | copy-start | bytes 52
  119.0 12.2 %copy-start.103 = (f32[1024]{0:T(1024)}, f32[1024]{0:T(1024)S(1)}, u32[]{:S(2)}) copy-start(f32[1024]{0:T(1024)S(1)} %add_rsqrt_fusion.1) | copy-start | bytes 12292
  119.0 12.2 %copy-start.96 = (f32[1,2,8,128]{3,1,2,0:T(2,128)}, f32[1,2,8,128]{3,1,2,0:T(2,128)S(1)}, u32[]{:S(2)}) copy-start(f32[1,2,8,128]{3,1,2,0:T(2,128)S(1)} %copy.67) | copy-start | bytes 24580
  119.0 12.2 %copy-start.53 = (f32[1,2,8,128]{3,1,2,0:T(2,128)}, f32[1,2,8,128]{3,1,2,0:T(2,128)S(1)}, u32[]{:S(2)}) copy-start(f32[1,2,8,128]{3,1,2,0:T(2,128)S(1)} %copy.66) | copy-start | bytes 24580
  120.3 10.9 %copy-start.99 = (f32[1536]{0:T(1024)}, f32[1536]{0:T(1024)S(1)}, u32[]{:S(2)}) copy-start(f32[1536]{0:T(1024)S(1)} %fusion.36) | copy-start | bytes 18436
  131.2 14.2 %copy-start.9 = (bf16[1024,1536]{1,0:T(8,128)(2,1)}, bf16[1024,1536]{1,0:T(8,128)(2,1)S(1)}, u32[]{:S(2)}) copy-start(bf16[1024,1536]{1,0:T(8,128)(2,1)S(1)} %add_convert_fusion.4.q_ref.k_ref.v_ref) | copy-start | bytes 9437188
  234.9 244.2 %all-gather.12.cloned.1.call-start = ((), (), s32[]{:S(2)}) async-start(), calls=%async_computation.6 | async-start | bytes 9437184 | tf_op jit(solution)/shard_map/all_gather | solution.py:1242
  235.2 6.9 copy-start.61
  235.2 6.9 copy-start.50
  235.2 6.5 copy-start.101
  243.6 299.7 %all-gather.14.cloned.1.call-start = ((), (), s32[]{:S(2)}) async-start(), calls=%async_computation.7 | async-start | bytes 9437184 | tf_op jit(solution)/shard_map/all_gather | solution.py:1256
  295.0 72.2 %copy-start.51 = (f32[1,2,8,128]{3,1,2,0:T(2,128)S(1)}, f32[1,2,8,128]{3,1,2,0:T(2,128)}, u32[]{:S(2)}) copy-start(f32[1,2,8,128]{3,1,2,0:T(2,128)} %copy-done.50) | copy-start | bytes 24580
  295.0 72.2 %copy-start.73 = (f32[256]{0:T(256)S(1)}, f32[256]{0:T(256)}, u32[]{:S(2)}) copy-start(f32[256]{0:T(256)} %copy-done.72) | copy-start | bytes 3076
  295.0 72.2 %copy-start.84 = (f32[256]{0:T(256)S(1)}, f32[256]{0:T(256)}, u32[]{:S(2)}) copy-start(f32[256]{0:T(256)} %copy-done.83) | copy-start | bytes 3076
  374.2 7.0 copy-start.46
  376.5 12.0 %slice-start.2 = ((s8[6291456]{0:T(1024)(128)(4,1)}), s8[4194304]{0:T(1024)(128)(4,1)S(1)}, s32[]{:S(2)}) async-start(s8[6291456]{0:T(1024)(128)(4,1)} %bitcast.211), calls=%async_computation.13 | async-start | bytes 8388608
  379.9 8.5 copy-start.79
  381.2 7.3 copy-start.106
  381.2 7.3 copy-start.54
  381.2 7.3 copy-start.97
  381.2 7.3 copy-start.100
  381.2 7.3 slice-start.3
  395.7 14.2 %copy-start.8 = (bf16[1024,1536]{1,0:T(8,128)(2,1)}, bf16[1024,1536]{1,0:T(8,128)(2,1)S(1)}, u32[]{:S(2)}) copy-start(bf16[1024,1536]{1,0:T(8,128)(2,1)S(1)} %add_convert_fusion.3.q_ref.k_ref.v_ref) | copy-start | bytes 9437188
  410.9 58.6 %copy-start.20 = (bf16[2,1,256,2048]{3,2,1,0:T(8,128)(2,1)S(1)}, bf16[2,1,256,2048]{3,2,1,0:T(8,128)(2,1)}, u32[]{:S(2)}) copy-start(bf16[2,1,256,2048]{3,2,1,0:T(8,128)(2,1)} %param.18) | copy-start | bytes 6291460
  410.9 58.6 %copy-start.102 = (f32[1,2,8,128]{3,1,2,0:T(2,128)S(1)}, f32[1,2,8,128]{3,1,2,0:T(2,128)}, u32[]{:S(2)}) copy-start(f32[1,2,8,128]{3,1,2,0:T(2,128)} %copy-done.101) | copy-start | bytes 24580
  479.1 141.5 %reduce-scatter.4.cloned.1.call-start = ((), (), s32[]{:S(2)}) async-start(), calls=%async_computation.8 | async-start | bytes 5242880 | tf_op jit(solution)/shard_map/reduce_scatter | solution.py:1261
  479.2 36.8 %copy-start.59 = (f32[1,2,8,128]{3,1,2,0:T(2,128)}, f32[1,2,8,128]{3,1,2,0:T(2,128)S(1)}, u32[]{:S(2)}) copy-start(f32[1,2,8,128]{3,1,2,0:T(2,128)S(1)} %copy.72) | copy-start | bytes 24580
  480.6 35.4 %copy-start.43 = (f32[256,2048]{1,0:T(8,128)S(1)}, f32[256,2048]{1,0:T(8,128)}, u32[]{:S(2)}) copy-start(f32[256,2048]{1,0:T(8,128)} %get-tuple-element.112) | copy-start | bytes 6291460
  514.8 19.0 %copy-start = (bf16[1024,1536]{1,0:T(8,128)(2,1)}, bf16[1024,1536]{1,0:T(8,128)(2,1)S(1)}, u32[]{:S(2)}) copy-start(bf16[1024,1536]{1,0:T(8,128)(2,1)S(1)} %attend_back.2) | copy-start | bytes 9437188
  517.6 16.3 %slice-start.4 = ((s8[6291456]{0:T(1024)(128)(4,1)}), s8[2097152]{0:T(1024)(128)(4,1)S(1)}, s32[]{:S(2)}) async-start(s8[6291456]{0:T(1024)(128)(4,1)} %bitcast.213), calls=%async_computation.15 | async-start | bytes 4194304
  520.1 13.7 %copy-start.30 = (bf16[1024,2048]{1,0:T(8,128)(2,1)S(1)}, bf16[1024,2048]{1,0:T(8,128)(2,1)}, u32[]{:S(2)}) copy-start(bf16[1024,2048]{1,0:T(8,128)(2,1)} %get-tuple-element.76) | copy-start | bytes 12582916
  520.2 13.7 %copy-start.77 = (f32[1024]{0:T(1024)S(1)}, f32[1024]{0:T(1024)}, u32[]{:S(2)}) copy-start(f32[1024]{0:T(1024)} %copy-done.76) | copy-start | bytes 12292
  520.2 13.7 %copy-start.104 = (f32[1024]{0:T(1024)S(1)}, f32[1024]{0:T(1024)}, u32[]{:S(2)}) copy-start(f32[1024]{0:T(1024)} %copy-done.103) | copy-start | bytes 12292
  520.2 13.7 %slice-start.5 = ((s8[6291456]{0:T(1024)(128)(4,1)}), s8[4194304]{0:T(1024)(128)(4,1)S(1)}, s32[]{:S(2)}) async-start(s8[6291456]{0:T(1024)(128)(4,1)} %bitcast.213), calls=%async_computation.16 | async-start | bytes 8388608
  543.3 178.7 %reduce-scatter.6.cloned.1.call-start = ((), (), s32[]{:S(2)}) async-start(), calls=%async_computation.9 | async-start | bytes 5242880 | tf_op jit(solution)/shard_map/reduce_scatter | solution.py:1277
  620.6 5.3 copy-start.87
  620.7 188.7 %reduce-scatter.8.cloned.1.call-start = ((), (), s32[]{:S(2)}) async-start(), calls=%async_computation.10 | async-start | bytes 5242880 | tf_op jit(solution)/shard_map/reduce_scatter | solution.py:1297
  627.9 6.4 copy-start.90
  629.9 4.4 copy-start.63
  634.4 7.3 copy-start.47
  634.4 7.3 copy-start.48
  634.4 7.2 copy-start.109
  634.4 7.2 copy-start.110
  697.8 13.4 %slice-start = ((s8[8388608]{0:T(1024)(128)(4,1)}), s8[4194304]{0:T(1024)(128)(4,1)S(1)}, s32[]{:S(2)}) async-start(s8[8388608]{0:T(1024)(128)(4,1)} %bitcast.209), calls=%async_computation.11 | async-start | bytes 8388608
  699.4 11.8 %copy-start.38 = (bf16[2048,1024]{1,0:T(8,128)(2,1)S(1)}, bf16[2048,1024]{1,0:T(8,128)(2,1)}, u32[]{:S(2)}) copy-start(bf16[2048,1024]{1,0:T(8,128)(2,1)} %get-tuple-element.122) | copy-start | bytes 12582916
  699.4 11.8 %slice-start.1 = ((s8[8388608]{0:T(1024)(128)(4,1)}), s8[4194304]{0:T(1024)(128)(4,1)S(1)}, s32[]{:S(2)}) async-start(s8[8388608]{0:T(1024)(128)(4,1)} %bitcast.209), calls=%async_computation.12 | async-start | bytes 8388608
  723.9 34.2 %copy-start.32 = (bf16[1024,2048]{1,0:T(8,128)(2,1)S(1)}, bf16[1024,2048]{1,0:T(8,128)(2,1)}, u32[]{:S(2)}) copy-start(bf16[1024,2048]{1,0:T(8,128)(2,1)} %all-gather.6.cloned.1.call-done) | copy-start | bytes 12582916
  723.9 34.2 %copy-start.80 = (f32[1024]{0:T(1024)S(1)}, f32[1024]{0:T(1024)}, u32[]{:S(2)}) copy-start(f32[1024]{0:T(1024)} %copy-done.79) | copy-start | bytes 12292
  723.9 34.2 %copy-start.107 = (f32[1024]{0:T(1024)S(1)}, f32[1024]{0:T(1024)}, u32[]{:S(2)}) copy-start(f32[1024]{0:T(1024)} %copy-done.106) | copy-start | bytes 12292
  758.1 12.4 %copy-start.2 = (bf16[1024,1536]{1,0:T(8,128)(2,1)}, bf16[1024,1536]{1,0:T(8,128)(2,1)S(1)}, u32[]{:S(2)}) copy-start(bf16[1024,1536]{1,0:T(8,128)(2,1)S(1)} %attend_back.3) | copy-start | bytes 9437188
  758.1 12.3 %copy-start.95 = (f32[2048]{0:T(1024)S(1)}, f32[2048]{0:T(1024)}, u32[]{:S(2)}) copy-start(f32[2048]{0:T(1024)} %get-tuple-element.188) | copy-start | bytes 24580
  758.1 12.3 %copy-start.94 = (f32[2048]{0:T(1024)S(1)}, f32[2048]{0:T(1024)}, u32[]{:S(2)}) copy-start(f32[2048]{0:T(1024)} %get-tuple-element.189) | copy-start | bytes 24580
  775.1 4.7 copy-start.1
  775.1 4.7 copy-start.78
  775.1 4.7 copy-start.98
  775.1 4.7 copy-start.105
  779.8 13.1 %copy-start.3 = (bf16[1024,1536]{1,0:T(8,128)(2,1)S(1)}, bf16[1024,1536]{1,0:T(8,128)(2,1)}, u32[]{:S(2)}) copy-start(bf16[1024,1536]{1,0:T(8,128)(2,1)} %copy-done.2) | copy-start | bytes 9437188
  779.8 13.1 %copy-start.33 = (bf16[1024,2048]{1,0:T(8,128)(2,1)S(1)}, bf16[1024,2048]{1,0:T(8,128)(2,1)}, u32[]{:S(2)}) copy-start(bf16[1024,2048]{1,0:T(8,128)(2,1)} %all-gather.6.cloned.1.call-done) | copy-start | bytes 12582916
  809.4 108.1 %copy-start.16 = (f32[256,2048]{1,0:T(8,128)S(1)}, f32[256,2048]{1,0:T(8,128)}, u32[]{:S(2)}) copy-start(f32[256,2048]{1,0:T(8,128)} %copy-done.14) | copy-start | bytes 6291460
  809.4 108.1 %copy-start.60 = (f32[1,2,8,128]{3,1,2,0:T(2,128)S(1)}, f32[1,2,8,128]{3,1,2,0:T(2,128)}, u32[]{:S(2)}) copy-start(f32[1,2,8,128]{3,1,2,0:T(2,128)} %copy-done.59) | copy-start | bytes 24580
  (62 other events, 132.6 us)
Sparse Core Ops, SparseCore 0:
  112.4 101.6 all-gather.7
  215.7 79.2 all-gather.9
  297.1 79.2 all-gather.5
  378.8 59.2 all-gather.11
  479.2 53.4 all-gather.13
  543.4 75.8 reduce-scatter.3
  621.7 94.1 reduce-scatter.5
  722.1 87.2 reduce-scatter.7
